TPU v7x, 32 devices: a whole 2x2x4 slice. The times are simulated.
32 devices in a mesh: groups: 2 (over y), seq: 8 (over z, x), head: 2 (over core).
Axes of the slice: x: 2, y: 2, z: 4, core: 2. Of those that a mesh axis runs over, the one named last changes fastest.
Arguments:
- queries: bfloat16 [2048, 1024], P(('groups', 'seq'), 'head'), parts along dimension 0, may hold values from -600 to 600
- keys: bfloat16 [2048, 1024], P(('groups', 'seq'), 'head'), parts along dimension 0, may hold values from -600 to 600
- values: bfloat16 [2048, 1024], P(('groups', 'seq'), 'head'), parts along dimension 0, may hold values from -600 to 600
- out_weight: bfloat16 [2048, 1024], P('seq', 'head'), may hold values from -0.1875 to 0.1875
- grad_y: bfloat16 [2048, 2048], P(('groups', 'seq')), parts along dimension 0, may hold values from -6 to 6
Outputs:
- out_y: bfloat16 [2048, 2048], P(('groups', 'seq')), parts along dimension 0
- grad_queries: bfloat16 [2048, 1024], P(('groups', 'seq'), 'head'), parts along dimension 0
- grad_keys: bfloat16 [2048, 1024], P(('groups', 'seq'), 'head'), parts along dimension 0
- grad_values: bfloat16 [2048, 1024], P(('groups', 'seq'), 'head'), parts along dimension 0
- grad_weight: float32 [4096, 1024], P(('groups', 'seq'), 'head'), parts along dimension 0
There are 2 independent parts, one for each index of `groups`. A program takes and returns all parts, laid end to end along the dimension named above; an argument that names none is the same for every part. Nothing has to cross between parts.
All inputs are finite; a program needn't handle non-finite values.
Results may differ from a plain program's by a relative error of at most 0.009.
Values may be sent and summed in bfloat16 or wider, within the bound.
No kernel may reach another device: no remote copies, remote signals or barrier semaphores. Data moves between devices by JAX's collectives and lax.ppermute only.
A program may use at most 192 MiB of HBM per device.

v0:
```python
import jax
import jax.numpy as jnp
from jax import lax
from jax.sharding import PartitionSpec as P

DH = 128
TILE = 128


epsilon = 1e-06


def carried_in(value, axis, join, neutral, backward):
    count, mine = (lax.axis_size(axis), lax.axis_index(axis))
    pieces = lax.all_gather(value, axis)
    if backward:
        pieces = pieces[::-1]
        mine = count - 1 - mine
    so_far = jnp.full_like(value, 0) + jnp.asarray(neutral, value.dtype)

    def turn(position, so_far):
        longer = join(so_far, pieces[position])
        return jnp.where(position < mine, longer, so_far)

    return lax.fori_loop(0, count - 1, turn, so_far)


def add_states(earlier, later):
    return earlier + later


def on_device(queries, keys, values, out_weight, grad_y):
    row_count = queries.shape[0]
    tile_count = row_count // TILE
    head_count = queries.shape[1] // DH

    def tiled(array):
        return array.reshape(tile_count, TILE, head_count, DH)

    query_tiles = tiled(queries)
    key_tiles = tiled(keys)
    value_tiles = tiled(values)
    causal = lax.broadcasted_iota(jnp.int32, (TILE, TILE), 0) >= lax.broadcasted_iota(
        jnp.int32, (TILE, TILE), 1
    )
    raw_scores = jnp.einsum(
        "nthd,nshd->nhts", query_tiles, key_tiles, preferred_element_type=jnp.float32
    )
    scores = jnp.where(causal, raw_scores, 0.0).astype(jnp.bfloat16)
    states = jnp.einsum(
        "nshd,nshe->nhde", key_tiles, value_tiles, preferred_element_type=jnp.float32
    )
    empty_state = jnp.zeros(states.shape[1:], jnp.float32)
    device_prefix = carried_in(jnp.sum(states, axis=0), "seq", add_states, empty_state, False)
    prefix_state = (device_prefix[None] + (jnp.cumsum(states, axis=0) - states)).astype(
        jnp.bfloat16
    )
    attended = jnp.einsum(
        "nhts,nshe->nthe", scores, value_tiles, preferred_element_type=jnp.float32
    )
    attended = attended + jnp.einsum(
        "nthd,nhde->nthe", query_tiles, prefix_state, preferred_element_type=jnp.float32
    )
    inverse_rms = lax.rsqrt(jnp.mean(attended * attended, axis=-1, keepdims=True) + epsilon)
    normed_exact = attended * inverse_rms
    normed = normed_exact.astype(jnp.bfloat16).reshape(row_count, -1)
    contract_last = (((1,), (1,)), ((), ()))
    back_weight = lax.all_gather(out_weight, "seq", axis=0, tiled=True)
    grad_normed = jnp.dot(grad_y, back_weight, preferred_element_type=jnp.float32)
    fore_weight = lax.all_gather(out_weight, "seq", axis=0, tiled=True)
    partial_out = lax.dot_general(
        normed, fore_weight, contract_last, preferred_element_type=jnp.float32
    )
    out_y = lax.psum(partial_out.astype(jnp.bfloat16), "head")
    grad_tiles = tiled(grad_normed)
    projected = jnp.mean(grad_tiles * normed_exact, axis=-1, keepdims=True)
    grad_out = (inverse_rms * (grad_tiles - normed_exact * projected)).astype(jnp.bfloat16)
    raw_grad = jnp.einsum(
        "nthe,nshe->nhts", grad_out, value_tiles, preferred_element_type=jnp.float32
    )
    grad_scores = jnp.where(causal, raw_grad, 0.0).astype(jnp.bfloat16)
    adjoint = jnp.einsum(
        "nthd,nthe->nhde", query_tiles, grad_out, preferred_element_type=jnp.float32
    )
    own_adjoint = jnp.sum(adjoint, axis=0)
    device_suffix = carried_in(own_adjoint, "seq", add_states, empty_state, True)
    later_tiles = jnp.flip(jnp.cumsum(jnp.flip(adjoint, 0), axis=0), 0) - adjoint
    suffix_state = (device_suffix[None] + later_tiles).astype(jnp.bfloat16)
    grad_queries = jnp.einsum(
        "nhts,nshd->nthd", grad_scores, key_tiles, preferred_element_type=jnp.float32
    )
    grad_queries = grad_queries + jnp.einsum(
        "nthe,nhde->nthd", grad_out, prefix_state, preferred_element_type=jnp.float32
    )
    grad_keys = jnp.einsum(
        "nhts,nthd->nshd", grad_scores, query_tiles, preferred_element_type=jnp.float32
    )
    grad_keys = grad_keys + jnp.einsum(
        "nshe,nhde->nshd", value_tiles, suffix_state, preferred_element_type=jnp.float32
    )
    grad_values = jnp.einsum(
        "nhts,nthe->nshe", scores, grad_out, preferred_element_type=jnp.float32
    )
    grad_values = grad_values + jnp.einsum(
        "nshd,nhde->nshe", key_tiles, suffix_state, preferred_element_type=jnp.float32
    )
    grad_weight = lax.psum_scatter(
        lax.dot_general(
            grad_y, normed, (((0,), (0,)), ((), ())), preferred_element_type=jnp.float32
        ),
        "seq",
        scatter_dimension=0,
        tiled=True,
    )
    return (
        out_y,
        grad_queries.reshape(row_count, -1).astype(jnp.bfloat16),
        grad_keys.reshape(row_count, -1).astype(jnp.bfloat16),
        grad_values.reshape(row_count, -1).astype(jnp.bfloat16),
        grad_weight,
    )


def solution(mesh):
    placed = (
        P(("groups", "seq"), "head"),
        P(("groups", "seq"), "head"),
        P(("groups", "seq"), "head"),
        P("seq", "head"),
        P(("groups", "seq"), None),
    )
    return jax.shard_map(
        on_device,
        mesh=mesh,
        in_specs=placed,
        out_specs=(
            P(("groups", "seq"), None),
            P(("groups", "seq"), "head"),
            P(("groups", "seq"), "head"),
            P(("groups", "seq"), "head"),
            P(("groups", "seq"), "head"),
        ),
        check_vma=False,
    )
```

profile of v0, /device:TPU:0, one launch (start us, length us, event | category | flops | bytes accessed | tf_op | source)
XLA Modules:
  0.0 284.6 jit_solution(14528810327368836696)
XLA Ops:
  7.2 1.1 copy.104
  8.3 1.8 fusion.10
  11.0 1.2 fusion.1
  12.8 1.1 convolution_bitcast_fusion.4
  14.0 48.7 %all-gather.8.cloned.1.call-done = f32[32,128,128]{2,1,0:T(8,128)} async-done(((f32[4,128,128]{2,1,0:T(8,128)}), f32[32,128,128]{2,1,0:T(8,128)}) %all-gather.8.cloned.1.call-update) | async-done | bytes 2097168 | tf_op jit(solution)/shard_map/all_gather | solution.py:15
  62.7 7.5 %while.28 = (s32[]{:T(128)}, f32[4,128,128]{2,1,0:T(8,128)S(1)}, s32[]{:T(128)}, f32[8,4,128,128]{3,2,1,0:T(8,128)}, s32[]{:T(128)}, /*index=5*/s32[]{:T(128)}) while((s32[]{:T(128)}, f32[4,128,128]{2,1,0:T(8,128)S(1)}, s32[]{:T(128)}, f32[8,4,128,128]{3,2,1,0:T(8,128)}, s32[]{:T(128)}, /*index=5*/s32[]{:T(128)}) %tuple.84), condition=%wide.region_1.2_spmd.clone, body=%wide.region_0.1_spmd.clone.sunk | while | flops 196612 | bytes 786533 | solution.py:25
  62.7 1.1 add_select_fusion.4
  63.8 1.0 add_select_fusion.4
  64.9 1.0 add_select_fusion.4
  66.0 1.0 add_select_fusion.4
  67.0 1.0 add_select_fusion.4
  68.1 1.0 add_select_fusion.4
  69.2 1.0 add_select_fusion.4
  70.5 42.1 %all-gather.6.cloned.1.call-done = bf16[2048,512]{1,0:T(8,128)(2,1)} async-done(((bf16[256,512]{1,0:T(8,128)(2,1)}), bf16[2048,512]{1,0:T(8,128)(2,1)}) %all-gather.6.cloned.1.call-update) | async-done | bytes 2097168 | tf_op jit(solution)/shard_map/all_gather | solution.py:70
  112.7 2.5 fusion.28
  115.5 0.8 copy.47
  116.4 2.7 convolution_bitcast_fusion
  119.2 0.8 copy-done.3
  120.2 1.2 convolution_bitcast_fusion.3
  121.4 0.8 fusion.3
  122.2 1.7 copy.52
  123.9 1.9 convolution_bitcast_fusion.1
  125.8 1.8 fusion.29
  127.6 2.5 convolution_convert_fusion
  130.2 34.2 %all-gather.10.cloned.1.call-done = f32[32,128,128]{2,1,0:T(8,128)} async-done(((f32[4,128,128]{2,1,0:T(8,128)}), f32[32,128,128]{2,1,0:T(8,128)}) %all-gather.10.cloned.1.call-update) | async-done | bytes 2097168 | tf_op jit(solution)/shard_map/all_gather | solution.py:15
  164.3 1.7 rev.3
  167.1 1.2 fusion.4
  168.2 0.8 copy.53
  170.0 84.8 %reduce-scatter.2.cloned.1.call-done = f32[256,512]{0,1:T(8,128)} async-done(((f32[2048,512]{0,1:T(8,128)}), f32[256,512]{0,1:T(8,128)}) %reduce-scatter.2.cloned.1.call-update) | async-done | bytes 524304 | tf_op jit(solution)/shard_map/reduce_scatter | solution.py:107
  254.8 2.0 copy.55
  256.8 19.4 %all-reduce.2.cloned.1.call-done = bf16[128,2048]{1,0:T(8,128)(2,1)} async-done(((bf16[128,2048]{1,0:T(8,128)(2,1)}), bf16[128,2048]{1,0:T(8,128)(2,1)}) %all-reduce.2.cloned.1.call-update) | async-done | bytes 524304 | tf_op jit(solution)/shard_map/psum | solution.py:74
  276.2 1.9 copy.120
  (54 shorter events, 5.0 us)
Async XLA Ops:
  7.2 105.5 %copy-start = (bf16[128,2048]{1,0:T(8,128)(2,1)S(1)}, bf16[128,2048]{1,0:T(8,128)(2,1)}, u32[]{:S(2)}) copy-start(bf16[128,2048]{1,0:T(8,128)(2,1)} %param.13) | copy-start | bytes 1572868
  7.2 55.6 %all-gather.8.cloned.1.call-start = ((), (), s32[]{:S(2)}) async-start(), calls=%async_computation.4 | async-start | bytes 2359296 | tf_op jit(solution)/shard_map/all_gather | solution.py:15
  8.3 2.6 copy-start.4
  10.2 102.5 %all-gather.6.cloned.1.call-start = ((), (), s32[]{:S(2)}) async-start(), calls=%async_computation.1 | async-start | bytes 2359296 | tf_op jit(solution)/shard_map/all_gather | solution.py:70
  10.9 153.4 %all-gather.10.cloned.1.call-start = ((), (), s32[]{:S(2)}) async-start(), calls=%async_computation.5 | async-start | bytes 2359296 | tf_op jit(solution)/shard_map/all_gather | solution.py:15
  12.2 0.6 copy-start.9
  14.0 56.2 %copy-start.2 = (f32[4,128,128]{2,1,0:T(8,128)S(1)}, f32[4,128,128]{2,1,0:T(8,128)}, u32[]{:S(2)}) copy-start(f32[4,128,128]{2,1,0:T(8,128)} %fusion.10) | copy-start | bytes 786436
  62.7 7.5 %copy-start.5 = (bf16[128,512]{1,0:T(8,128)(2,1)S(1)}, bf16[128,512]{1,0:T(8,128)(2,1)}, u32[]{:S(2)}) copy-start(bf16[128,512]{1,0:T(8,128)(2,1)} %param.9) | copy-start | bytes 393220
  115.3 3.7 %copy-start.6 = (bf16[1,128,4,128]{1,3,2,0:T(8,128)(2,1)}, bf16[1,128,4,128]{1,3,2,0:T(8,128)(2,1)S(1)}, u32[]{:S(2)}) copy-start(bf16[1,128,4,128]{1,3,2,0:T(8,128)(2,1)S(1)} %get-tuple-element.222) | copy-start | bytes 393220
  116.4 138.5 %reduce-scatter.2.cloned.1.call-start = ((), (), s32[]{:S(2)}) async-start(), calls=%async_computation.3 | async-start | bytes 4718592 | tf_op jit(solution)/shard_map/reduce_scatter | solution.py:107
  119.1 0.9 copy-start.3
  119.1 8.5 %copy-start.1 = (bf16[2048,512]{1,0:T(8,128)(2,1)S(1)}, bf16[2048,512]{1,0:T(8,128)(2,1)}, u32[]{:S(2)}) copy-start(bf16[2048,512]{1,0:T(8,128)(2,1)} %all-gather.6.cloned.1.call-done) | copy-start | bytes 6291460
  119.1 157.1 %all-reduce.2.cloned.1.call-start = ((), (), s32[]{:S(2)}) async-start(), calls=%async_computation.2 | async-start | bytes 1048576 | tf_op jit(solution)/shard_map/psum | solution.py:74
  120.2 2.0 copy-start.10
  166.1 2.9 %copy-start.7 = (f32[4,128,128]{2,1,0:T(8,128)S(1)}, f32[4,128,128]{2,1,0:T(8,128)}, u32[]{:S(2)}) copy-start(f32[4,128,128]{2,1,0:T(8,128)} %fusion.29) | copy-start | bytes 786436
  166.9 2.2 copy-start.8
Sparse Core Ops, SparseCore 0:
  10.7 51.9 all-gather.7
  64.9 47.7 all-gather.5
  116.5 47.8 all-gather.9
  167.8 86.9 reduce-scatter.1
  257.7 18.4 all-reduce.1
where the time goes:
time: 285 us
  waiting for transfers between devices  230 us (81%)
  matrix products  19.6 us (7%)
  between operations  14 us (5%)
  local copies, waits for them, and re-layouts  12.4 us (4%)
  other arithmetic  8.1 us (3%)
    reduce_scatter x1, waiting for transfers between devices, on_device(): lax.psum_scatter(lax.dot_general(grad_y, normed, (((0,), (0,)), ((), ()))...  84.8 us
    all_gather x2, waiting for transfers between devices, carried_in(): pieces = lax.all_gather(value, axis)  82.9 us
    all_gather x1, waiting for transfers between devices, on_device(): fore_weight = lax.all_gather(out_weight, 'seq', axis=0, tiled=True)  42.1 us
    psum x1, waiting for transfers between devices, on_device(): out_y = lax.psum(partial_out.astype(jnp.bfloat16), 'head')  19.4 us
    unnamed x27, local copies, waits for them, and re-layouts  8.63 us
    select_n x14, other arithmetic, turn(): return jnp.where(position < mine, longer, so_far)  7.89 us
  transfers between devices with their start and end apart: 5, of which 5 were waited for; matrix products, arithmetic and copies ran while one was open for 11% of the time, Pallas kernels for 0%

commit v1 on v0

--- a/solution.py
+++ b/solution.py
@@ -1,6 +1,8 @@
 import jax
 import jax.numpy as jnp
 from jax import lax
+from jax.experimental import pallas as pl
+from jax.experimental.pallas import tpu as pltpu
 from jax.sharding import PartitionSpec as P
 
 DH = 128
@@ -8,6 +10,11 @@
 
 
 epsilon = 1e-06
+F32 = jnp.float32
+BF16 = jnp.bfloat16
+ROWS_T = (((0,), (0,)), ((), ()))
+LAST_T = (((1,), (1,)), ((), ()))
+PLAIN = (((1,), (0,)), ((), ()))
 
 
 def carried_in(value, axis, join, neutral, backward):
@@ -64,12 +71,11 @@
     inverse_rms = lax.rsqrt(jnp.mean(attended * attended, axis=-1, keepdims=True) + epsilon)
     normed_exact = attended * inverse_rms
     normed = normed_exact.astype(jnp.bfloat16).reshape(row_count, -1)
-    contract_last = (((1,), (1,)), ((), ()))
     back_weight = lax.all_gather(out_weight, "seq", axis=0, tiled=True)
     grad_normed = jnp.dot(grad_y, back_weight, preferred_element_type=jnp.float32)
     fore_weight = lax.all_gather(out_weight, "seq", axis=0, tiled=True)
     partial_out = lax.dot_general(
-        normed, fore_weight, contract_last, preferred_element_type=jnp.float32
+        normed, fore_weight, LAST_T, preferred_element_type=jnp.float32
     )
     out_y = lax.psum(partial_out.astype(jnp.bfloat16), "head")
     grad_tiles = tiled(grad_normed)
@@ -121,6 +127,270 @@
     )
 
 
+def dot(a, b, dims):
+    return lax.dot_general(a, b, dims, preferred_element_type=F32)
+
+
+def call(body, shapes, *args, flops=2**27, moved=2**20):
+    return pl.pallas_call(
+        body,
+        out_shape=[jax.ShapeDtypeStruct(s, d) for s, d in shapes],
+        in_specs=[pl.BlockSpec(memory_space=pltpu.VMEM)] * len(args),
+        out_specs=[pl.BlockSpec(memory_space=pltpu.VMEM)] * len(shapes),
+        cost_estimate=pl.CostEstimate(
+            flops=flops, bytes_accessed=moved, transcendentals=0
+        ),
+        compiler_params=pltpu.CompilerParams(vmem_limit_bytes=24 * 2**20),
+    )(*args)
+
+
+def lanes(i, size):
+    return pl.ds(pl.multiple_of(i * size, size), size)
+
+
+def head_of(i):
+    return slice(i * DH, (i + 1) * DH)
+
+
+def causal_mask():
+    rows = lax.broadcasted_iota(jnp.int32, (TILE, TILE), 0)
+    return rows >= lax.broadcasted_iota(jnp.int32, (TILE, TILE), 1)
+
+
+def place():
+    s = lax.axis_index("seq")
+    return lax.axis_index("groups"), s // 2, s % 2, lax.axis_index("head")
+
+
+def on_short_line(seq, queries, keys, values, out_weight, grad_y):
+    rows, feats = queries.shape
+    heads = feats // DH
+    wrows = out_weight.shape[0]
+    half = wrows // 2
+    line = seq // 2
+    turns = range(1, line)
+    outs = grad_y.shape[1]
+    state = (heads * DH, DH)
+
+    def rotate(array, k):
+        return lax.ppermute(
+            array, "seq", [(i, (i + 2 * k) % seq) for i in range(seq)]
+        )
+
+    def swap_x(array):
+        return lax.ppermute(array, "seq", [(i, i ^ 1) for i in range(seq)])
+
+    def swap_y(array):
+        return lax.ppermute(array, "groups", [(0, 1), (1, 0)])
+
+    def swap_core(array):
+        return lax.ppermute(array, "head", [(0, 1), (1, 0)])
+
+    def first(k_ref, v_ref, w_ref, gy_ref, s_ref, wh_ref, ys_ref, *gz_refs):
+        g, z, x, h = place()
+        for i in range(heads):
+            s_ref[head_of(i), :] = dot(
+                k_ref[:, head_of(i)], v_ref[:, head_of(i)], ROWS_T
+            ).astype(BF16)
+        wh_ref[...] = w_ref[pl.ds(pl.multiple_of(g * half, half), half), :]
+        for i in range(seq):
+            ys_ref[:, i * half : (i + 1) * half] = gy_ref[:, lanes(2 * i + 1 - g, half)]
+        for k, gz_ref in zip(turns, gz_refs):
+            gz_ref[...] = gy_ref[:, lanes(lax.rem(z + k, line) * 2 + h, wrows)]
+
+    states, my_weight, y_send, *gz_send = call(
+        first,
+        [(state, BF16), ((half, feats), BF16), ((rows, seq * half), BF16)]
+        + [((rows, wrows), BF16) for _ in turns],
+        keys, values, out_weight, grad_y,
+    )
+    x_states = swap_x(states)
+    z_weight = [rotate(my_weight, k) for k in turns]
+    y_cols = swap_y(y_send)
+
+    def local(q_ref, k_ref, v_ref, sc_ref, att_ref):
+        mask = causal_mask()
+        for i in range(heads):
+            sc = dot(q_ref[:, head_of(i)], k_ref[:, head_of(i)], LAST_T)
+            sc = jnp.where(mask, sc, 0.0).astype(BF16)
+            sc_ref[:, head_of(i)] = sc
+            att_ref[:, head_of(i)] = dot(sc, v_ref[:, head_of(i)], PLAIN)
+
+    scores, att_local = call(
+        local, [((rows, feats), BF16), ((rows, feats), F32)], queries, keys, values
+    )
+
+    pair_states = (states.astype(F32) + x_states.astype(F32)).astype(BF16)
+    z_states = [rotate(pair_states, k) for k in turns]
+
+    x_weight_a = swap_x(jnp.concatenate([my_weight, z_weight[0]], axis=0))
+    x_weight_b = swap_x(jnp.concatenate(z_weight[1:], axis=0))
+
+    def weight_blocks(refs):
+        own, *others, xa_ref, xb_ref = refs
+        g, z, x, h = place()
+        blocks = []
+        for k in range(line):
+            zk = lax.rem(z - k + line, line)
+            blocks.append((zk * 2 + x, (own, *others)[k][...]))
+            far = xa_ref if k < 2 else xb_ref
+            at = k if k < 2 else k - 2
+            blocks.append((zk * 2 + 1 - x, far[at * half : (at + 1) * half, :]))
+        return blocks
+
+    weight_args = (my_weight, *z_weight, x_weight_a, x_weight_b)
+
+    def back(gy_ref, yc_ref, *refs):
+        *w_refs, own_ref, send_ref = refs
+        g = lax.axis_index("groups")
+        own = jnp.zeros((rows, feats), F32)
+        other = jnp.zeros((rows, feats), F32)
+        for s, block in weight_blocks(w_refs):
+            own += dot(gy_ref[:, lanes(2 * s + g, half)], block, PLAIN)
+            other += dot(yc_ref[:, lanes(s, half)], block, PLAIN)
+        own_ref[...] = own
+        send_ref[...] = other
+
+    grad_own, grad_send = call(
+        back, [((rows, feats), F32), ((rows, feats), F32)],
+        grad_y, y_cols, *weight_args,
+    )
+    grad_other = swap_y(grad_send)
+
+    z_cols = [rotate(a, k) for a, k in zip(gz_send, turns)]
+    h_cols = [swap_core(a) for a in z_cols]
+
+    def forward(q_ref, local_ref, xs_ref, *refs):
+        *z_refs, att_ref, normed_ref, prefix_ref = refs
+        g, z, x, h = place()
+        total = jnp.where(x == 1, xs_ref[...].astype(F32), 0.0)
+        for k, z_ref in zip(turns, z_refs):
+            total += jnp.where(z >= k, z_ref[...].astype(F32), 0.0)
+        prefix = total.astype(BF16)
+        prefix_ref[...] = prefix
+        for i in range(heads):
+            att = local_ref[:, head_of(i)] + dot(
+                q_ref[:, head_of(i)], prefix[head_of(i), :], PLAIN
+            )
+            att_ref[:, head_of(i)] = att
+            inv = lax.rsqrt(jnp.mean(att * att, axis=-1, keepdims=True) + epsilon)
+            normed_ref[:, head_of(i)] = (att * inv).astype(BF16)
+
+    attended, normed, prefix = call(
+        forward,
+        [((rows, feats), F32), ((rows, feats), BF16), (state, BF16)],
+        queries, att_local, x_states, *z_states,
+    )
+    y_normed = swap_y(normed)
+    z_normed = [rotate(normed, k) for k in turns]
+
+    def turn_back(att_ref, own_ref, other_ref, q_ref, go_ref, adj_ref):
+        for i in range(heads):
+            att = att_ref[:, head_of(i)]
+            inv = lax.rsqrt(jnp.mean(att * att, axis=-1, keepdims=True) + epsilon)
+            exact = att * inv
+            grad = own_ref[:, head_of(i)] + other_ref[:, head_of(i)]
+            along = jnp.mean(grad * exact, axis=-1, keepdims=True)
+            go = (inv * (grad - exact * along)).astype(BF16)
+            go_ref[:, head_of(i)] = go
+            adj_ref[head_of(i), :] = dot(q_ref[:, head_of(i)], go, ROWS_T).astype(BF16)
+
+    grad_out, adjoint = call(
+        turn_back, [((rows, feats), BF16), (state, BF16)],
+        attended, grad_own, grad_other, queries,
+    )
+    x_adjoint = swap_x(adjoint)
+
+    def local_grads(go_ref, q_ref, k_ref, v_ref, sc_ref, pre_ref, gq_ref, gk_ref, gv_ref):
+        mask = causal_mask()
+        for i in range(heads):
+            at = head_of(i)
+            go = go_ref[:, at]
+            gs = dot(go, v_ref[:, at], LAST_T)
+            gs = jnp.where(mask, gs, 0.0).astype(BF16)
+            gq = dot(gs, k_ref[:, at], PLAIN) + dot(go, pre_ref[at, :], LAST_T)
+            gq_ref[:, at] = gq.astype(BF16)
+            gk_ref[:, at] = dot(gs, q_ref[:, at], ROWS_T)
+            gv_ref[:, at] = dot(sc_ref[:, at], go, ROWS_T)
+
+    grad_queries, gk_local, gv_local = call(
+        local_grads,
+        [((rows, feats), BF16), ((rows, feats), F32), ((rows, feats), F32)],
+        grad_out, queries, keys, values, scores, prefix,
+    )
+    pair_adjoint = (adjoint.astype(F32) + x_adjoint.astype(F32)).astype(BF16)
+    z_adjoint = [rotate(pair_adjoint, k) for k in turns]
+
+    def project(n_ref, yn_ref, *refs):
+        *w_refs, own_ref, other_ref = refs
+        for s, block in weight_blocks(w_refs):
+            own_ref[:, lanes(s, half)] = dot(n_ref[...], block, LAST_T).astype(BF16)
+            other_ref[:, lanes(s, half)] = dot(yn_ref[...], block, LAST_T).astype(BF16)
+
+    out_own, out_send = call(
+        project, [((rows, seq * half), BF16)] * 2, normed, y_normed, *weight_args
+    )
+    out_other = swap_y(out_send)
+    core_own = swap_core(out_own)
+    core_other = swap_core(out_other)
+
+    def join(a_ref, b_ref, c_ref, d_ref, y_ref):
+        g = lax.axis_index("groups")
+        for i in range(seq):
+            at = slice(i * half, (i + 1) * half)
+            y_ref[:, lanes(2 * i + g, half)] = (
+                a_ref[:, at].astype(F32) + b_ref[:, at].astype(F32)
+            ).astype(BF16)
+            y_ref[:, lanes(2 * i + 1 - g, half)] = (
+                c_ref[:, at].astype(F32) + d_ref[:, at].astype(F32)
+            ).astype(BF16)
+
+    (out_y,) = call(
+        join, [((rows, outs), BF16)], out_own, core_own, out_other, core_other
+    )
+
+    def weight_grad(gy_ref, n_ref, *refs):
+        *ins, keep_ref, send_ref = refs
+        count = line - 1
+        c_refs, o_refs, z_refs = ins[:count], ins[count : 2 * count], ins[2 * count :]
+        g, z, x, h = place()
+        same = dot(gy_ref[:, lanes(z * 2 + h, wrows)], n_ref[...], ROWS_T)
+        other = dot(gy_ref[:, lanes(z * 2 + 1 - h, wrows)], n_ref[...], ROWS_T)
+        for c_ref, o_ref, z_ref in zip(c_refs, o_refs, z_refs):
+            same += dot(c_ref[...], z_ref[...], ROWS_T)
+            other += dot(o_ref[...], z_ref[...], ROWS_T)
+        keep_ref[...] = jnp.where(x == h, same, other)
+        send_ref[...] = jnp.where(x == h, other, same).astype(BF16)
+
+    gw_keep, gw_send = call(
+        weight_grad, [((wrows, feats), F32), ((wrows, feats), BF16)],
+        grad_y, normed, *z_cols, *h_cols, *z_normed,
+    )
+    grad_weight = gw_keep + swap_x(gw_send).astype(F32)
+
+    def last(gk_ref, gv_ref, k_ref, v_ref, xa_ref, *refs):
+        *z_refs, ok_ref, ov_ref = refs
+        g, z, x, h = place()
+        total = jnp.where(x == 0, xa_ref[...].astype(F32), 0.0)
+        for k, z_ref in zip(turns, z_refs):
+            total += jnp.where(z < k, z_ref[...].astype(F32), 0.0)
+        suffix = total.astype(BF16)
+        for i in range(heads):
+            at = head_of(i)
+            ok_ref[:, at] = (
+                gk_ref[:, at] + dot(v_ref[:, at], suffix[at, :], LAST_T)
+            ).astype(BF16)
+            ov_ref[:, at] = (
+                gv_ref[:, at] + dot(k_ref[:, at], suffix[at, :], PLAIN)
+            ).astype(BF16)
+
+    grad_keys, grad_values = call(
+        last, [((rows, feats), BF16)] * 2,
+        gk_local, gv_local, keys, values, x_adjoint, *z_adjoint,
+    )
+    return out_y, grad_queries, grad_keys, grad_values, grad_weight
+
+
 def solution(mesh):
     placed = (
         P(("groups", "seq"), "head"),
@@ -129,8 +399,18 @@
         P("seq", "head"),
         P(("groups", "seq"), None),
     )
+    size = dict(mesh.shape)
+
+    def program(queries, keys, values, out_weight, grad_y):
+        short = size["seq"] == 8 and size["groups"] == 2 and size["head"] == 2
+        if short and queries.shape[0] == TILE and out_weight.shape[0] % 256 == 0:
+            return on_short_line(
+                size["seq"], queries, keys, values, out_weight, grad_y
+            )
+        return on_device(queries, keys, values, out_weight, grad_y)
+
     return jax.shard_map(
-        on_device,
+        program,
         mesh=mesh,
         in_specs=placed,
         out_specs=(

time: 285 us -> 78 us (0.27)
  waiting for transfers between devices: 230 us -> 21.3 us
  starting transfers between devices: 0.2 us -> 43.6 us
  matrix products: 19.6 us -> 0 us
  between operations: 14 us -> 0.77 us
  local copies, waits for them, and re-layouts: 12.4 us -> 3.85 us
  Pallas kernels: 0 us -> 7.16 us
  other arithmetic: 8.1 us -> 0.98 us
    all_gather x3 -> x0, waiting for transfers between devices: 125 us -> none  [the longest x2 82.9 us: carried_in(): pieces = lax.all_gather(value, axis)]
    reduce_scatter x1 -> x0, waiting for transfers between devices: 84.8 us -> none  [on_device(): lax.psum_scatter(lax.dot_general(grad_y, normed, (((0,), (0,)), ((), ()))...]
    ppermute x0 -> x29, starting transfers between devices: none -> 43.6 us  [the longest x15 30.3 us: rotate(): lax.ppermute(array, 'seq', [(i, (i + 2 * k) % seq) for i in range(seq)])]
    ppermute x0 -> x29, waiting for transfers between devices: none -> 21.3 us  [the longest x15 17.9 us: rotate(): lax.ppermute(array, 'seq', [(i, (i + 2 * k) % seq) for i in range(seq)])]
    dot_general x15 -> x0, matrix products: 19.6 us -> none  [the longest x1 2.65 us: on_device(): lax.dot_general(grad_y, normed, (((0,), (0,)), ((), ())), preferred_eleme...]
    psum x1 -> x0, waiting for transfers between devices: 19.4 us -> none  [on_device(): out_y = lax.psum(partial_out.astype(jnp.bfloat16), 'head')]
    select_n x14 -> x0, other arithmetic: 7.89 us -> none  [turn(): return jnp.where(position < mine, longer, so_far)]
    pallas_call x0 -> x10, Pallas kernels: none -> 7.16 us  [call(): pl.pallas_call(body, out_shape=[jax.ShapeDtypeStruct(s, d) for s, d in sh...]
  transfers between devices with their start and end apart: 5 -> 29, of which waited for: 5 -> 12; matrix products, arithmetic and copies ran while one was open for 11% -> 1% of each run, Pallas kernels for 0% -> 8%
where the time goes in v1:
time: 78 us; the launch traced here: 77.7 us
  starting transfers between devices  43.6 us (56%)
  waiting for transfers between devices  21.3 us (27%)
  Pallas kernels  7.16 us (9%)
  local copies, waits for them, and re-layouts  3.85 us (5%)
  other arithmetic  0.98 us (1%)
    ppermute x15, starting transfers between devices, rotate(): lax.ppermute(array, 'seq', [(i, (i + 2 * k) % seq) for i in range(seq)])  30.3 us
    ppermute x15, waiting for transfers between devices, rotate(): lax.ppermute(array, 'seq', [(i, (i + 2 * k) % seq) for i in range(seq)])  17.9 us
    ppermute x5, starting transfers between devices, swap_x(): return lax.ppermute(array, 'seq', [(i, i ^ 1) for i in range(seq)])  7.4 us
    pallas_call x10, Pallas kernels, call(): pl.pallas_call(body, out_shape=[jax.ShapeDtypeStruct(s, d) for s, d in sh...  7.16 us
    ppermute x4, starting transfers between devices, swap_y(): return lax.ppermute(array, 'groups', [(0, 1), (1, 0)])  5.44 us
    unnamed x16, local copies, waits for them, and re-layouts  3.85 us
    ppermute x5, waiting for transfers between devices, swap_x(): return lax.ppermute(array, 'seq', [(i, i ^ 1) for i in range(seq)])  3.38 us
  transfers between devices with their start and end apart: 29, of which 12 were waited for; matrix products, arithmetic and copies ran while one was open for 1% of the time, Pallas kernels for 8%

profile of v1, /device:TPU:0, one launch (start us, length us, event | category | flops | bytes accessed | tf_op | source)
XLA Modules:
  0.0 77.7 jit_solution(982425920554966688)
XLA Ops:
  0.6 1.0 %copy-done = bf16[128,2048]{1,0:T(8,128)(2,1)S(1)} copy-done((bf16[128,2048]{1,0:T(8,128)(2,1)S(1)}, bf16[128,2048]{1,0:T(8,128)(2,1)}, u32[]{:S(2)}) %copy-start) | copy-done | bytes 524312
  2.6 0.9 %copy-done.5 = bf16[128,512]{1,0:T(8,128)(2,1)S(1)} copy-done((bf16[128,512]{1,0:T(8,128)(2,1)S(1)}, bf16[128,512]{1,0:T(8,128)(2,1)}, u32[]{:S(2)}) %copy-start.5) | copy-done | bytes 131096
  3.5 0.9 %copy-done.7 = bf16[256,512]{1,0:T(8,128)(2,1)S(1)} copy-done((bf16[256,512]{1,0:T(8,128)(2,1)S(1)}, bf16[256,512]{1,0:T(8,128)(2,1)}, u32[]{:S(2)}) %copy-start.7) | copy-done | bytes 262168
  4.7 4.1 %collective-permute-start.6 = (bf16[128,512]{1,0:T(8,128)(2,1)S(1)}, bf16[128,512]{1,0:T(8,128)(2,1)S(1)}, u32[]{:S(2)}, u32[]{:S(2)}) collective-permute-start(bf16[128,512]{1,0:T(8,128)(2,1)S(1)} %get-tuple-element.32.refs_0_), channel_id=1, source_target_pairs={{0,8},{2,10},{4,12},{6,14},{8,0},{10,2},{12,4},{14,6},{1,9},{3,11}... | collective-permute-start | bytes 393224 | tf_op jit(solution)/shard_map/ppermute | solution.py:176
  8.8 1.3 %collective-permute-start.7 = (bf16[128,512]{1,0:T(8,128)(2,1)S(1)}, bf16[128,512]{1,0:T(8,128)(2,1)S(1)}, u32[]{:S(2)}, u32[]{:S(2)}) collective-permute-start(bf16[128,512]{1,0:T(8,128)(2,1)S(1)} %get-tuple-element.32.refs_0_), channel_id=1, source_target_pairs={{0,12},{2,14},{4,0},{6,2},{8,4},{10,6},{12,8},{14,10},{1,13},{3,15... | collective-permute-start | bytes 393224 | tf_op jit(solution)/shard_map/ppermute | solution.py:176
  10.8 1.5 %collective-permute-start = (bf16[512,128]{1,0:T(8,128)(2,1)S(1)}, bf16[512,128]{1,0:T(8,128)(2,1)S(1)}, u32[]{:S(2)}, u32[]{:S(2)}) collective-permute-start(bf16[512,128]{1,0:T(8,128)(2,1)S(1)} %get-tuple-element.30), channel_id=1, source_target_pairs={{0,2},{2,0},{4,6},{6,4},{8,10},{10,8},{12,14},{14,12},{1,3},{3,1},... | collective-permute-start | bytes 393224 | tf_op jit(solution)/shard_map/ppermute | solution.py:181
  12.3 1.5 %collective-permute-start.13 = (bf16[128,1024]{1,0:T(8,128)(2,1)S(1)}, bf16[128,1024]{1,0:T(8,128)(2,1)S(1)}, u32[]{:S(2)}, u32[]{:S(2)}) collective-permute-start(bf16[128,1024]{1,0:T(8,128)(2,1)S(1)} %get-tuple-element.36), channel_id=1, source_target_pairs={{0,16},{16,0},{1,17},{17,1},{2,18},{18,2},{3,19},{19,3},{4,20},{20... | collective-permute-start | bytes 786440 | tf_op jit(solution)/shard_map/ppermute | solution.py:184
  13.8 2.9 %collective-permute-done.6.refs_2_ = bf16[128,512]{1,0:T(8,128)(2,1)S(1)} collective-permute-done((bf16[128,512]{1,0:T(8,128)(2,1)S(1)}, bf16[128,512]{1,0:T(8,128)(2,1)S(1)}, u32[]{:S(2)}, u32[]{:S(2)}) %collective-permute-start.6) | collective-permute-done | bytes 131104 | tf_op jit(solution)/shard_map/ppermute | solution.py:176
  16.7 2.2 %collective-permute-start.9 = (bf16[256,512]{1,0:T(8,128)(2,1)S(1)}, bf16[256,512]{1,0:T(8,128)(2,1)S(1)}, u32[]{:S(2)}, u32[]{:S(2)}) collective-permute-start(bf16[256,512]{1,0:T(8,128)(2,1)S(1)} %pad_maximum_fusion.1), channel_id=1, source_target_pairs={{0,2},{2,0},{4,6},{6,4},{8,10},{10,8},{12,14},{14,12},{1,3},{3,1},... | collective-permute-start | bytes 786440 | tf_op jit(solution)/shard_map/ppermute | solution.py:181
  19.1 1.6 %collective-permute-start.8 = (bf16[256,512]{1,0:T(8,128)(2,1)S(1)}, bf16[256,512]{1,0:T(8,128)(2,1)S(1)}, u32[]{:S(2)}, u32[]{:S(2)}) collective-permute-start(bf16[256,512]{1,0:T(8,128)(2,1)S(1)} %pad_maximum_fusion), channel_id=1, source_target_pairs={{0,2},{2,0},{4,6},{6,4},{8,10},{10,8},{12,14},{14,12},{1,3},{3,1},... | collective-permute-start | bytes 786440 | tf_op jit(solution)/shard_map/ppermute | solution.py:181
  20.7 2.8 %collective-permute-start.1 = (bf16[512,128]{1,0:T(8,128)(2,1)S(1)}, bf16[512,128]{1,0:T(8,128)(2,1)S(1)}, u32[]{:S(2)}, u32[]{:S(2)}) collective-permute-start(bf16[512,128]{1,0:T(8,128)(2,1)S(1)} %add_convert_fusion.1), channel_id=1, source_target_pairs={{0,4},{2,6},{4,8},{6,10},{8,12},{10,14},{12,0},{14,2},{1,5},{3,7},... | collective-permute-start | bytes 393224 | tf_op jit(solution)/shard_map/ppermute | solution.py:176
  23.6 1.6 %collective-permute-start.2 = (bf16[512,128]{1,0:T(8,128)(2,1)S(1)}, bf16[512,128]{1,0:T(8,128)(2,1)S(1)}, u32[]{:S(2)}, u32[]{:S(2)}) collective-permute-start(bf16[512,128]{1,0:T(8,128)(2,1)S(1)} %add_convert_fusion.1), channel_id=1, source_target_pairs={{0,8},{2,10},{4,12},{6,14},{8,0},{10,2},{12,4},{14,6},{1,9},{3,11}... | collective-permute-start | bytes 393224 | tf_op jit(solution)/shard_map/ppermute | solution.py:176
  25.1 2.8 %collective-permute-start.3 = (bf16[512,128]{1,0:T(8,128)(2,1)S(1)}, bf16[512,128]{1,0:T(8,128)(2,1)S(1)}, u32[]{:S(2)}, u32[]{:S(2)}) collective-permute-start(bf16[512,128]{1,0:T(8,128)(2,1)S(1)} %add_convert_fusion.1), channel_id=1, source_target_pairs={{0,12},{2,14},{4,0},{6,2},{8,4},{10,6},{12,8},{14,10},{1,13},{3,15... | collective-permute-start | bytes 393224 | tf_op jit(solution)/shard_map/ppermute | solution.py:176
  28.0 0.9 %collective-permute-done.8.refs_4_ = bf16[256,512]{1,0:T(8,128)(2,1)S(1)} collective-permute-done((bf16[256,512]{1,0:T(8,128)(2,1)S(1)}, bf16[256,512]{1,0:T(8,128)(2,1)S(1)}, u32[]{:S(2)}, u32[]{:S(2)}) %collective-permute-start.8) | collective-permute-done | bytes 262176 | tf_op jit(solution)/shard_map/ppermute | solution.py:181
  29.6 1.8 %collective-permute-start.14 = (f32[128,512]{1,0:T(8,128)S(1)}, f32[128,512]{1,0:T(8,128)S(1)}, u32[]{:S(2)}, u32[]{:S(2)}) collective-permute-start(f32[128,512]{1,0:T(8,128)S(1)} %get-tuple-element.38), channel_id=1, source_target_pairs={{0,16},{16,0},{1,17},{17,1},{2,18},{18,2},{3,19},{19,3},{4,20},{20... | collective-permute-start | bytes 786440 | tf_op jit(solution)/shard_map/ppermute | solution.py:184
  32.1 1.6 %collective-permute-done.2.refs_1_ = bf16[512,128]{1,0:T(8,128)(2,1)S(1)} collective-permute-done((bf16[512,128]{1,0:T(8,128)(2,1)S(1)}, bf16[512,128]{1,0:T(8,128)(2,1)S(1)}, u32[]{:S(2)}, u32[]{:S(2)}) %collective-permute-start.2) | collective-permute-done | bytes 131104 | tf_op jit(solution)/shard_map/ppermute | solution.py:176
  34.1 1.6 %collective-permute-start.4 = (bf16[128,512]{1,0:T(8,128)(2,1)S(1)}, bf16[128,512]{1,0:T(8,128)(2,1)S(1)}, u32[]{:S(2)}, u32[]{:S(2)}) collective-permute-start(bf16[128,512]{1,0:T(8,128)(2,1)S(1)} %get-tuple-element.31.n_ref), channel_id=1, source_target_pairs={{0,16},{16,0},{1,17},{17,1},{2,18},{18,2},{3,19},{19,3},{4,20},{20... | collective-permute-start | bytes 393224 | tf_op jit(solution)/shard_map/ppermute | solution.py:184
  35.6 3.0 %collective-permute-start.19 = (bf16[128,256]{1,0:T(8,128)(2,1)S(1)}, bf16[128,256]{1,0:T(8,128)(2,1)S(1)}, u32[]{:S(2)}, u32[]{:S(2)}) collective-permute-start(bf16[128,256]{1,0:T(8,128)(2,1)S(1)} %get-tuple-element.48), channel_id=1, source_target_pairs={{0,4},{2,6},{4,8},{6,10},{8,12},{10,14},{12,0},{14,2},{1,5},{3,7},... | collective-permute-start | bytes 196616 | tf_op jit(solution)/shard_map/ppermute | solution.py:176
  38.7 3.4 %collective-permute-start.20 = (bf16[128,256]{1,0:T(8,128)(2,1)S(1)}, bf16[128,256]{1,0:T(8,128)(2,1)S(1)}, u32[]{:S(2)}, u32[]{:S(2)}) collective-permute-start(bf16[128,256]{1,0:T(8,128)(2,1)S(1)} %get-tuple-element.49), channel_id=1, source_target_pairs={{0,8},{2,10},{4,12},{6,14},{8,0},{10,2},{12,4},{14,6},{1,9},{3,11}... | collective-permute-start | bytes 196616 | tf_op jit(solution)/shard_map/ppermute | solution.py:176
  43.9 2.1 %collective-permute-done.20.refs_1_ = bf16[128,256]{1,0:T(8,128)(2,1)S(1)} collective-permute-done((bf16[128,256]{1,0:T(8,128)(2,1)S(1)}, bf16[128,256]{1,0:T(8,128)(2,1)S(1)}, u32[]{:S(2)}, u32[]{:S(2)}) %collective-permute-start.20) | collective-permute-done | bytes 65568 | tf_op jit(solution)/shard_map/ppermute | solution.py:176
  46.6 1.1 %collective-permute-start.25 = (bf16[128,512]{1,0:T(8,128)(2,1)S(1)}, bf16[128,512]{1,0:T(8,128)(2,1)S(1)}, u32[]{:S(2)}, u32[]{:S(2)}) collective-permute-start(bf16[128,512]{1,0:T(8,128)(2,1)S(1)} %get-tuple-element.31.n_ref), channel_id=1, source_target_pairs={{0,4},{2,6},{4,8},{6,10},{8,12},{10,14},{12,0},{14,2},{1,5},{3,7},... | collective-permute-start | bytes 393224 | tf_op jit(solution)/shard_map/ppermute | solution.py:176
  47.7 2.7 %collective-permute-start.26 = (bf16[128,512]{1,0:T(8,128)(2,1)S(1)}, bf16[128,512]{1,0:T(8,128)(2,1)S(1)}, u32[]{:S(2)}, u32[]{:S(2)}) collective-permute-start(bf16[128,512]{1,0:T(8,128)(2,1)S(1)} %get-tuple-element.31.n_ref), channel_id=1, source_target_pairs={{0,8},{2,10},{4,12},{6,14},{8,0},{10,2},{12,4},{14,6},{1,9},{3,11}... | collective-permute-start | bytes 393224 | tf_op jit(solution)/shard_map/ppermute | solution.py:176
  51.1 1.3 %collective-permute-start.15 = (bf16[512,128]{1,0:T(8,128)(2,1)S(1)}, bf16[512,128]{1,0:T(8,128)(2,1)S(1)}, u32[]{:S(2)}, u32[]{:S(2)}) collective-permute-start(bf16[512,128]{1,0:T(8,128)(2,1)S(1)} %get-tuple-element.45), channel_id=1, source_target_pairs={{0,2},{2,0},{4,6},{6,4},{8,10},{10,8},{12,14},{14,12},{1,3},{3,1},... | collective-permute-start | bytes 393224 | tf_op jit(solution)/shard_map/ppermute | solution.py:181
  52.3 2.4 %collective-permute-done.25.refs_6_ = bf16[128,512]{1,0:T(8,128)(2,1)S(1)} collective-permute-done((bf16[128,512]{1,0:T(8,128)(2,1)S(1)}, bf16[128,512]{1,0:T(8,128)(2,1)S(1)}, u32[]{:S(2)}, u32[]{:S(2)}) %collective-permute-start.25) | collective-permute-done | bytes 131104 | tf_op jit(solution)/shard_map/ppermute | solution.py:176
  54.7 5.2 %collective-permute-done.26.refs_7_ = bf16[128,512]{1,0:T(8,128)(2,1)S(1)} collective-permute-done((bf16[128,512]{1,0:T(8,128)(2,1)S(1)}, bf16[128,512]{1,0:T(8,128)(2,1)S(1)}, u32[]{:S(2)}, u32[]{:S(2)}) %collective-permute-start.26) | collective-permute-done | bytes 131104 | tf_op jit(solution)/shard_map/ppermute | solution.py:176
  62.2 3.3 %collective-permute-start.16 = (bf16[512,128]{1,0:T(8,128)(2,1)S(1)}, bf16[512,128]{1,0:T(8,128)(2,1)S(1)}, u32[]{:S(2)}, u32[]{:S(2)}) collective-permute-start(bf16[512,128]{1,0:T(8,128)(2,1)S(1)} %add_convert_fusion), channel_id=1, source_target_pairs={{0,4},{2,6},{4,8},{6,10},{8,12},{10,14},{12,0},{14,2},{1,5},{3,7},... | collective-permute-start | bytes 393224 | tf_op jit(solution)/shard_map/ppermute | solution.py:176
  65.8 2.4 %collective-permute-done.28 = bf16[256,512]{1,0:T(8,128)(2,1)S(1)} collective-permute-done((bf16[256,512]{1,0:T(8,128)(2,1)S(1)}, bf16[256,512]{1,0:T(8,128)(2,1)S(1)}, u32[]{:S(2)}, u32[]{:S(2)}) %collective-permute-start.28) | collective-permute-done | bytes 262176 | tf_op jit(solution)/shard_map/ppermute | solution.py:181
  68.2 2.8 %collective-permute-start.18 = (bf16[512,128]{1,0:T(8,128)(2,1)S(1)}, bf16[512,128]{1,0:T(8,128)(2,1)S(1)}, u32[]{:S(2)}, u32[]{:S(2)}) collective-permute-start(bf16[512,128]{1,0:T(8,128)(2,1)S(1)} %add_convert_fusion), channel_id=1, source_target_pairs={{0,12},{2,14},{4,0},{6,2},{8,4},{10,6},{12,8},{14,10},{1,13},{3,15... | collective-permute-start | bytes 393224 | tf_op jit(solution)/shard_map/ppermute | solution.py:176
  71.9 1.4 %shard_map.99 = (bf16[128,512]{1,0:T(8,128)(2,1)}, f32[128,512]{1,0:T(8,128)S(1)}, f32[128,512]{1,0:T(8,128)S(1)}) custom-call(bf16[128,512]{1,0:T(8,128)(2,1)S(1)} %get-tuple-element.39.go_ref, bf16[128,512]{1,0:T(8,128)(2,1)S(1)} %copy-done.2, bf16[128,512]{1,0:T(8,128)(2,1)S(1)} %copy-done.3, bf16[128,512]{1,0:T(8,128)(2,1)S(1)} %copy-done.6, ...), custom_call_target="tpu_custom_call" | custom-call | flops 134217728 | bytes 1048576 | tf_op jit(solution)/shard_map/pallas_call | solution.py:135
  73.3 1.0 %shard_map.96 = bf16[128,2048]{1,0:T(8,128)(2,1)} custom-call(bf16[128,1024]{1,0:T(8,128)(2,1)S(1)} %get-tuple-element.33.a_ref, bf16[128,1024]{1,0:T(8,128)(2,1)S(1)} %collective-permute-done.10.b_ref, bf16[128,1024]{1,0:T(8,128)(2,1)S(1)} %collective-permute-done.11.c_ref, bf16[128,1024]{1,0:T(8,128)(2,1)S(1)} %collective-permute-done.12.d_ref), custom_call_target="tpu_custom_call" | custom-call | flops 134217728 | bytes 1048576 | tf_op jit(solution)/shard_map/pallas_call | solution.py:135
  75.2 1.5 %collective-permute-done.18.refs_2_ = bf16[512,128]{1,0:T(8,128)(2,1)S(1)} collective-permute-done((bf16[512,128]{1,0:T(8,128)(2,1)S(1)}, bf16[512,128]{1,0:T(8,128)(2,1)S(1)}, u32[]{:S(2)}, u32[]{:S(2)}) %collective-permute-start.18) | collective-permute-done | bytes 131104 | tf_op jit(solution)/shard_map/ppermute | solution.py:176
  76.7 1.0 %shard_map.100 = (bf16[128,512]{1,0:T(8,128)(2,1)}, bf16[128,512]{1,0:T(8,128)(2,1)}) custom-call(f32[128,512]{1,0:T(8,128)S(1)} %get-tuple-element.43.gk_ref, f32[128,512]{1,0:T(8,128)S(1)} %get-tuple-element.44.gv_ref, bf16[128,512]{1,0:T(8,128)(2,1)S(1)} %copy-done.4, bf16[128,512]{1,0:T(8,128)(2,1)S(1)} %copy-done.6, ...), custom_call_target="tpu_custom_call" | custom-call | flops 134217728 | bytes 1048576 | tf_op jit(solution)/shard_map/pallas_call | solution.py:135
  (57 shorter events, 11.1 us)
Async XLA Ops:
  4.7 12.1 %collective-permute-start.6 = (bf16[128,512]{1,0:T(8,128)(2,1)S(1)}, bf16[128,512]{1,0:T(8,128)(2,1)S(1)}, u32[]{:S(2)}, u32[]{:S(2)}) collective-permute-start(bf16[128,512]{1,0:T(8,128)(2,1)S(1)} %get-tuple-element.32.refs_0_), channel_id=1, source_target_pairs={{0,8},{2,10},{4,12},{6,14},{8,0},{10,2},{12,4},{14,6},{1,9},{3,11}... | collective-permute-start | bytes 393224 | tf_op jit(solution)/shard_map/ppermute | solution.py:176
  8.8 8.0 %collective-permute-start.7 = (bf16[128,512]{1,0:T(8,128)(2,1)S(1)}, bf16[128,512]{1,0:T(8,128)(2,1)S(1)}, u32[]{:S(2)}, u32[]{:S(2)}) collective-permute-start(bf16[128,512]{1,0:T(8,128)(2,1)S(1)} %get-tuple-element.32.refs_0_), channel_id=1, source_target_pairs={{0,12},{2,14},{4,0},{6,2},{8,4},{10,6},{12,8},{14,10},{1,13},{3,15... | collective-permute-start | bytes 393224 | tf_op jit(solution)/shard_map/ppermute | solution.py:176
  10.1 9.0 %collective-permute-start.5 = (bf16[128,512]{1,0:T(8,128)(2,1)S(1)}, bf16[128,512]{1,0:T(8,128)(2,1)S(1)}, u32[]{:S(2)}, u32[]{:S(2)}) collective-permute-start(bf16[128,512]{1,0:T(8,128)(2,1)S(1)} %get-tuple-element.32.refs_0_), channel_id=1, source_target_pairs={{0,4},{2,6},{4,8},{6,10},{8,12},{10,14},{12,0},{14,2},{1,5},{3,7},... | collective-permute-start | bytes 393224 | tf_op jit(solution)/shard_map/ppermute | solution.py:176
  10.8 9.9 %collective-permute-start = (bf16[512,128]{1,0:T(8,128)(2,1)S(1)}, bf16[512,128]{1,0:T(8,128)(2,1)S(1)}, u32[]{:S(2)}, u32[]{:S(2)}) collective-permute-start(bf16[512,128]{1,0:T(8,128)(2,1)S(1)} %get-tuple-element.30), channel_id=1, source_target_pairs={{0,2},{2,0},{4,6},{6,4},{8,10},{10,8},{12,14},{14,12},{1,3},{3,1},... | collective-permute-start | bytes 393224 | tf_op jit(solution)/shard_map/ppermute | solution.py:181
  12.3 12.9 %collective-permute-start.13 = (bf16[128,1024]{1,0:T(8,128)(2,1)S(1)}, bf16[128,1024]{1,0:T(8,128)(2,1)S(1)}, u32[]{:S(2)}, u32[]{:S(2)}) collective-permute-start(bf16[128,1024]{1,0:T(8,128)(2,1)S(1)} %get-tuple-element.36), channel_id=1, source_target_pairs={{0,16},{16,0},{1,17},{17,1},{2,18},{18,2},{3,19},{19,3},{4,20},{20... | collective-permute-start | bytes 786440 | tf_op jit(solution)/shard_map/ppermute | solution.py:184
  16.7 12.2 %copy-start.1 = (bf16[128,2048]{1,0:T(8,128)(2,1)S(1)}, bf16[128,2048]{1,0:T(8,128)(2,1)}, u32[]{:S(2)}) copy-start(bf16[128,2048]{1,0:T(8,128)(2,1)} %gy_ref.5) | copy-start | bytes 1572868
  16.7 11.2 %collective-permute-start.9 = (bf16[256,512]{1,0:T(8,128)(2,1)S(1)}, bf16[256,512]{1,0:T(8,128)(2,1)S(1)}, u32[]{:S(2)}, u32[]{:S(2)}) collective-permute-start(bf16[256,512]{1,0:T(8,128)(2,1)S(1)} %pad_maximum_fusion.1), channel_id=1, source_target_pairs={{0,2},{2,0},{4,6},{6,4},{8,10},{10,8},{12,14},{14,12},{1,3},{3,1},... | collective-permute-start | bytes 786440 | tf_op jit(solution)/shard_map/ppermute | solution.py:181
  19.1 9.8 %collective-permute-start.8 = (bf16[256,512]{1,0:T(8,128)(2,1)S(1)}, bf16[256,512]{1,0:T(8,128)(2,1)S(1)}, u32[]{:S(2)}, u32[]{:S(2)}) collective-permute-start(bf16[256,512]{1,0:T(8,128)(2,1)S(1)} %pad_maximum_fusion), channel_id=1, source_target_pairs={{0,2},{2,0},{4,6},{6,4},{8,10},{10,8},{12,14},{14,12},{1,3},{3,1},... | collective-permute-start | bytes 786440 | tf_op jit(solution)/shard_map/ppermute | solution.py:181
  20.7 10.7 %copy-start.2 = (bf16[128,512]{1,0:T(8,128)(2,1)S(1)}, bf16[128,512]{1,0:T(8,128)(2,1)}, u32[]{:S(2)}) copy-start(bf16[128,512]{1,0:T(8,128)(2,1)} %q_ref.7) | copy-start | bytes 393220
  20.7 11.4 %collective-permute-start.1 = (bf16[512,128]{1,0:T(8,128)(2,1)S(1)}, bf16[512,128]{1,0:T(8,128)(2,1)S(1)}, u32[]{:S(2)}, u32[]{:S(2)}) collective-permute-start(bf16[512,128]{1,0:T(8,128)(2,1)S(1)} %add_convert_fusion.1), channel_id=1, source_target_pairs={{0,4},{2,6},{4,8},{6,10},{8,12},{10,14},{12,0},{14,2},{1,5},{3,7},... | collective-permute-start | bytes 393224 | tf_op jit(solution)/shard_map/ppermute | solution.py:176
  23.6 10.1 %collective-permute-start.2 = (bf16[512,128]{1,0:T(8,128)(2,1)S(1)}, bf16[512,128]{1,0:T(8,128)(2,1)S(1)}, u32[]{:S(2)}, u32[]{:S(2)}) collective-permute-start(bf16[512,128]{1,0:T(8,128)(2,1)S(1)} %add_convert_fusion.1), channel_id=1, source_target_pairs={{0,8},{2,10},{4,12},{6,14},{8,0},{10,2},{12,4},{14,6},{1,9},{3,11}... | collective-permute-start | bytes 393224 | tf_op jit(solution)/shard_map/ppermute | solution.py:176
  25.1 8.6 %collective-permute-start.3 = (bf16[512,128]{1,0:T(8,128)(2,1)S(1)}, bf16[512,128]{1,0:T(8,128)(2,1)S(1)}, u32[]{:S(2)}, u32[]{:S(2)}) collective-permute-start(bf16[512,128]{1,0:T(8,128)(2,1)S(1)} %add_convert_fusion.1), channel_id=1, source_target_pairs={{0,12},{2,14},{4,0},{6,2},{8,4},{10,6},{12,8},{14,10},{1,13},{3,15... | collective-permute-start | bytes 393224 | tf_op jit(solution)/shard_map/ppermute | solution.py:176
  29.6 20.8 %collective-permute-start.14 = (f32[128,512]{1,0:T(8,128)S(1)}, f32[128,512]{1,0:T(8,128)S(1)}, u32[]{:S(2)}, u32[]{:S(2)}) collective-permute-start(f32[128,512]{1,0:T(8,128)S(1)} %get-tuple-element.38), channel_id=1, source_target_pairs={{0,16},{16,0},{1,17},{17,1},{2,18},{18,2},{3,19},{19,3},{4,20},{20... | collective-permute-start | bytes 786440 | tf_op jit(solution)/shard_map/ppermute | solution.py:184
  34.1 8.0 %collective-permute-start.4 = (bf16[128,512]{1,0:T(8,128)(2,1)S(1)}, bf16[128,512]{1,0:T(8,128)(2,1)S(1)}, u32[]{:S(2)}, u32[]{:S(2)}) collective-permute-start(bf16[128,512]{1,0:T(8,128)(2,1)S(1)} %get-tuple-element.31.n_ref), channel_id=1, source_target_pairs={{0,16},{16,0},{1,17},{17,1},{2,18},{18,2},{3,19},{19,3},{4,20},{20... | collective-permute-start | bytes 393224 | tf_op jit(solution)/shard_map/ppermute | solution.py:184
  35.6 8.3 %collective-permute-start.19 = (bf16[128,256]{1,0:T(8,128)(2,1)S(1)}, bf16[128,256]{1,0:T(8,128)(2,1)S(1)}, u32[]{:S(2)}, u32[]{:S(2)}) collective-permute-start(bf16[128,256]{1,0:T(8,128)(2,1)S(1)} %get-tuple-element.48), channel_id=1, source_target_pairs={{0,4},{2,6},{4,8},{6,10},{8,12},{10,14},{12,0},{14,2},{1,5},{3,7},... | collective-permute-start | bytes 196616 | tf_op jit(solution)/shard_map/ppermute | solution.py:176
  38.7 7.4 %collective-permute-start.20 = (bf16[128,256]{1,0:T(8,128)(2,1)S(1)}, bf16[128,256]{1,0:T(8,128)(2,1)S(1)}, u32[]{:S(2)}, u32[]{:S(2)}) collective-permute-start(bf16[128,256]{1,0:T(8,128)(2,1)S(1)} %get-tuple-element.49), channel_id=1, source_target_pairs={{0,8},{2,10},{4,12},{6,14},{8,0},{10,2},{12,4},{14,6},{1,9},{3,11}... | collective-permute-start | bytes 196616 | tf_op jit(solution)/shard_map/ppermute | solution.py:176
  42.0 4.5 %collective-permute-start.21 = (bf16[128,256]{1,0:T(8,128)(2,1)S(1)}, bf16[128,256]{1,0:T(8,128)(2,1)S(1)}, u32[]{:S(2)}, u32[]{:S(2)}) collective-permute-start(bf16[128,256]{1,0:T(8,128)(2,1)S(1)} %get-tuple-element.50), channel_id=1, source_target_pairs={{0,12},{2,14},{4,0},{6,2},{8,4},{10,6},{12,8},{14,10},{1,13},{3,15... | collective-permute-start | bytes 196616 | tf_op jit(solution)/shard_map/ppermute | solution.py:176
  42.8 18.9 %collective-permute-start.11 = (bf16[128,1024]{1,0:T(8,128)(2,1)S(1)}, bf16[128,1024]{1,0:T(8,128)(2,1)S(1)}, u32[]{:S(2)}, u32[]{:S(2)}) collective-permute-start(bf16[128,1024]{1,0:T(8,128)(2,1)S(1)} %get-tuple-element.34), channel_id=1, source_target_pairs={{0,16},{16,0},{1,17},{17,1},{2,18},{18,2},{3,19},{19,3},{4,20},{20... | collective-permute-start | bytes 786440 | tf_op jit(solution)/shard_map/ppermute | solution.py:184
  43.9 2.6 %collective-permute-start.22 = (bf16[128,256]{1,0:T(8,128)(2,1)S(1)}, bf16[128,256]{1,0:T(8,128)(2,1)S(1)}, u32[]{:S(2)}, u32[]{:S(2)}) collective-permute-start(bf16[128,256]{1,0:T(8,128)(2,1)S(1)} %collective-permute-done.19.refs_0_), channel_id=1, source_target_pairs={{0,1},{1,0},{2,3},{3,2},{4,5},{5,4},{6,7},{7,6},{8,9},{9,8},{10,11... | collective-permute-start | bytes 196616 | tf_op jit(solution)/shard_map/ppermute | solution.py:187
  46.0 1.7 %collective-permute-start.23 = (bf16[128,256]{1,0:T(8,128)(2,1)S(1)}, bf16[128,256]{1,0:T(8,128)(2,1)S(1)}, u32[]{:S(2)}, u32[]{:S(2)}) collective-permute-start(bf16[128,256]{1,0:T(8,128)(2,1)S(1)} %collective-permute-done.20.refs_1_), channel_id=1, source_target_pairs={{0,1},{1,0},{2,3},{3,2},{4,5},{5,4},{6,7},{7,6},{8,9},{9,8},{10,11... | collective-permute-start | bytes 196616 | tf_op jit(solution)/shard_map/ppermute | solution.py:187
  46.5 4.5 %collective-permute-start.24 = (bf16[128,256]{1,0:T(8,128)(2,1)S(1)}, bf16[128,256]{1,0:T(8,128)(2,1)S(1)}, u32[]{:S(2)}, u32[]{:S(2)}) collective-permute-start(bf16[128,256]{1,0:T(8,128)(2,1)S(1)} %collective-permute-done.21.refs_2_), channel_id=1, source_target_pairs={{0,1},{1,0},{2,3},{3,2},{4,5},{5,4},{6,7},{7,6},{8,9},{9,8},{10,11... | collective-permute-start | bytes 196616 | tf_op jit(solution)/shard_map/ppermute | solution.py:187
  46.6 8.2 %collective-permute-start.25 = (bf16[128,512]{1,0:T(8,128)(2,1)S(1)}, bf16[128,512]{1,0:T(8,128)(2,1)S(1)}, u32[]{:S(2)}, u32[]{:S(2)}) collective-permute-start(bf16[128,512]{1,0:T(8,128)(2,1)S(1)} %get-tuple-element.31.n_ref), channel_id=1, source_target_pairs={{0,4},{2,6},{4,8},{6,10},{8,12},{10,14},{12,0},{14,2},{1,5},{3,7},... | collective-permute-start | bytes 393224 | tf_op jit(solution)/shard_map/ppermute | solution.py:176
  47.7 12.3 %collective-permute-start.26 = (bf16[128,512]{1,0:T(8,128)(2,1)S(1)}, bf16[128,512]{1,0:T(8,128)(2,1)S(1)}, u32[]{:S(2)}, u32[]{:S(2)}) collective-permute-start(bf16[128,512]{1,0:T(8,128)(2,1)S(1)} %get-tuple-element.31.n_ref), channel_id=1, source_target_pairs={{0,8},{2,10},{4,12},{6,14},{8,0},{10,2},{12,4},{14,6},{1,9},{3,11}... | collective-permute-start | bytes 393224 | tf_op jit(solution)/shard_map/ppermute | solution.py:176
  50.4 9.6 %collective-permute-start.27 = (bf16[128,512]{1,0:T(8,128)(2,1)S(1)}, bf16[128,512]{1,0:T(8,128)(2,1)S(1)}, u32[]{:S(2)}, u32[]{:S(2)}) collective-permute-start(bf16[128,512]{1,0:T(8,128)(2,1)S(1)} %get-tuple-element.31.n_ref), channel_id=1, source_target_pairs={{0,12},{2,14},{4,0},{6,2},{8,4},{10,6},{12,8},{14,10},{1,13},{3,15... | collective-permute-start | bytes 393224 | tf_op jit(solution)/shard_map/ppermute | solution.py:176
  51.1 11.1 %collective-permute-start.15 = (bf16[512,128]{1,0:T(8,128)(2,1)S(1)}, bf16[512,128]{1,0:T(8,128)(2,1)S(1)}, u32[]{:S(2)}, u32[]{:S(2)}) collective-permute-start(bf16[512,128]{1,0:T(8,128)(2,1)S(1)} %get-tuple-element.45), channel_id=1, source_target_pairs={{0,2},{2,0},{4,6},{6,4},{8,10},{10,8},{12,14},{14,12},{1,3},{3,1},... | collective-permute-start | bytes 393224 | tf_op jit(solution)/shard_map/ppermute | solution.py:181
  60.7 7.5 %collective-permute-start.28 = (bf16[256,512]{1,0:T(8,128)(2,1)S(1)}, bf16[256,512]{1,0:T(8,128)(2,1)S(1)}, u32[]{:S(2)}, u32[]{:S(2)}) collective-permute-start(bf16[256,512]{1,0:T(8,128)(2,1)S(1)} %get-tuple-element.52), channel_id=1, source_target_pairs={{0,2},{2,0},{4,6},{6,4},{8,10},{10,8},{12,14},{14,12},{1,3},{3,1},... | collective-permute-start | bytes 786440 | tf_op jit(solution)/shard_map/ppermute | solution.py:181
  61.6 11.7 %collective-permute-start.10 = (bf16[128,1024]{1,0:T(8,128)(2,1)S(1)}, bf16[128,1024]{1,0:T(8,128)(2,1)S(1)}, u32[]{:S(2)}, u32[]{:S(2)}) collective-permute-start(bf16[128,1024]{1,0:T(8,128)(2,1)S(1)} %get-tuple-element.33.a_ref), channel_id=1, source_target_pairs={{0,1},{1,0},{2,3},{3,2},{4,5},{5,4},{6,7},{7,6},{8,9},{9,8},{10,11... | collective-permute-start | bytes 786440 | tf_op jit(solution)/shard_map/ppermute | solution.py:187
  61.6 11.7 %collective-permute-start.12 = (bf16[128,1024]{1,0:T(8,128)(2,1)S(1)}, bf16[128,1024]{1,0:T(8,128)(2,1)S(1)}, u32[]{:S(2)}, u32[]{:S(2)}) collective-permute-start(bf16[128,1024]{1,0:T(8,128)(2,1)S(1)} %collective-permute-done.11.c_ref), channel_id=1, source_target_pairs={{0,1},{1,0},{2,3},{3,2},{4,5},{5,4},{6,7},{7,6},{8,9},{9,8},{10,11... | collective-permute-start | bytes 786440 | tf_op jit(solution)/shard_map/ppermute | solution.py:187
  62.2 12.1 %collective-permute-start.16 = (bf16[512,128]{1,0:T(8,128)(2,1)S(1)}, bf16[512,128]{1,0:T(8,128)(2,1)S(1)}, u32[]{:S(2)}, u32[]{:S(2)}) collective-permute-start(bf16[512,128]{1,0:T(8,128)(2,1)S(1)} %add_convert_fusion), channel_id=1, source_target_pairs={{0,4},{2,6},{4,8},{6,10},{8,12},{10,14},{12,0},{14,2},{1,5},{3,7},... | collective-permute-start | bytes 393224 | tf_op jit(solution)/shard_map/ppermute | solution.py:176
  65.5 9.7 %collective-permute-start.17 = (bf16[512,128]{1,0:T(8,128)(2,1)S(1)}, bf16[512,128]{1,0:T(8,128)(2,1)S(1)}, u32[]{:S(2)}, u32[]{:S(2)}) collective-permute-start(bf16[512,128]{1,0:T(8,128)(2,1)S(1)} %add_convert_fusion), channel_id=1, source_target_pairs={{0,8},{2,10},{4,12},{6,14},{8,0},{10,2},{12,4},{14,6},{1,9},{3,11}... | collective-permute-start | bytes 393224 | tf_op jit(solution)/shard_map/ppermute | solution.py:176
  68.2 8.5 %collective-permute-start.18 = (bf16[512,128]{1,0:T(8,128)(2,1)S(1)}, bf16[512,128]{1,0:T(8,128)(2,1)S(1)}, u32[]{:S(2)}, u32[]{:S(2)}) collective-permute-start(bf16[512,128]{1,0:T(8,128)(2,1)S(1)} %add_convert_fusion), channel_id=1, source_target_pairs={{0,12},{2,14},{4,0},{6,2},{8,4},{10,6},{12,8},{14,10},{1,13},{3,15... | collective-permute-start | bytes 393224 | tf_op jit(solution)/shard_map/ppermute | solution.py:176
  73.3 3.4 %copy-start.4 = (bf16[128,512]{1,0:T(8,128)(2,1)S(1)}, bf16[128,512]{1,0:T(8,128)(2,1)}, u32[]{:S(2)}) copy-start(bf16[128,512]{1,0:T(8,128)(2,1)} %k_ref.7) | copy-start | bytes 393220
  (5 other events, 4.7 us)

commit v2 on v1

--- a/solution.py
+++ b/solution.py
@@ -172,13 +172,14 @@
     outs = grad_y.shape[1]
     state = (heads * DH, DH)
 
+    def permute(array, pairs):
+        return lax.ppermute(array, "seq", pairs)
+
     def rotate(array, k):
-        return lax.ppermute(
-            array, "seq", [(i, (i + 2 * k) % seq) for i in range(seq)]
-        )
-
-    def swap_x(array):
-        return lax.ppermute(array, "seq", [(i, i ^ 1) for i in range(seq)])
+        return permute(array, [(i, (i + 2 * k) % seq) for i in range(seq)])
+
+    def swap(array, bit):
+        return permute(array, [(i, i ^ bit) for i in range(seq)])
 
     def swap_y(array):
         return lax.ppermute(array, "groups", [(0, 1), (1, 0)])
@@ -186,26 +187,58 @@
     def swap_core(array):
         return lax.ppermute(array, "head", [(0, 1), (1, 0)])
 
-    def first(k_ref, v_ref, w_ref, gy_ref, s_ref, wh_ref, ys_ref, *gz_refs):
-        g, z, x, h = place()
+    def side_by_side(*arrays):
+        return jnp.concatenate(arrays, axis=0)
+
+    g = lax.axis_index("groups")
+    my_weight = lax.dynamic_slice_in_dim(out_weight, g * half, half, 0)
+    z_weight = [rotate(my_weight, k) for k in turns]
+
+    def first(k_hbm, v_hbm, gy_hbm, s_ref, ys_ref, gz_ref, k_ref, v_ref, gy_ref, sems):
+        copies = [
+            pltpu.make_async_copy(src, dst, sems.at[i])
+            for i, (src, dst) in enumerate(
+                ((k_hbm, k_ref), (v_hbm, v_ref), (gy_hbm, gy_ref))
+            )
+        ]
+        for copy in copies:
+            copy.start()
+        g, z, x, h = place()
+        copies[0].wait()
+        copies[1].wait()
         for i in range(heads):
             s_ref[head_of(i), :] = dot(
                 k_ref[:, head_of(i)], v_ref[:, head_of(i)], ROWS_T
             ).astype(BF16)
-        wh_ref[...] = w_ref[pl.ds(pl.multiple_of(g * half, half), half), :]
+        copies[2].wait()
         for i in range(seq):
             ys_ref[:, i * half : (i + 1) * half] = gy_ref[:, lanes(2 * i + 1 - g, half)]
-        for k, gz_ref in zip(turns, gz_refs):
-            gz_ref[...] = gy_ref[:, lanes(lax.rem(z + k, line) * 2 + h, wrows)]
-
-    states, my_weight, y_send, *gz_send = call(
+        far = z // 2 * 2
+        far = 2 - far
+        for b in range(2):
+            gz_ref[b * rows : (b + 1) * rows, :] = gy_ref[
+                :, lanes((far + b) * 2 + h, wrows)
+            ]
+
+    states, y_send, far_send = pl.pallas_call(
         first,
-        [(state, BF16), ((half, feats), BF16), ((rows, seq * half), BF16)]
-        + [((rows, wrows), BF16) for _ in turns],
-        keys, values, out_weight, grad_y,
-    )
-    x_states = swap_x(states)
-    z_weight = [rotate(my_weight, k) for k in turns]
+        out_shape=[
+            jax.ShapeDtypeStruct(s, BF16)
+            for s in (state, (rows, seq * half), (2 * rows, wrows))
+        ],
+        in_specs=[pl.BlockSpec(memory_space=pltpu.HBM)] * 3,
+        out_specs=[pl.BlockSpec(memory_space=pltpu.VMEM)] * 3,
+        scratch_shapes=[
+            pltpu.VMEM(keys.shape, BF16),
+            pltpu.VMEM(values.shape, BF16),
+            pltpu.VMEM(grad_y.shape, BF16),
+            pltpu.SemaphoreType.DMA((3,)),
+        ],
+        cost_estimate=pl.CostEstimate(
+            flops=2**27, bytes_accessed=2**20, transcendentals=0
+        ),
+        compiler_params=pltpu.CompilerParams(vmem_limit_bytes=24 * 2**20),
+    )(keys, values, grad_y)
     y_cols = swap_y(y_send)
 
     def local(q_ref, k_ref, v_ref, sc_ref, att_ref):
@@ -220,11 +253,17 @@
         local, [((rows, feats), BF16), ((rows, feats), F32)], queries, keys, values
     )
 
-    pair_states = (states.astype(F32) + x_states.astype(F32)).astype(BF16)
-    z_states = [rotate(pair_states, k) for k in turns]
-
-    x_weight_a = swap_x(jnp.concatenate([my_weight, z_weight[0]], axis=0))
-    x_weight_b = swap_x(jnp.concatenate(z_weight[1:], axis=0))
+    def spread(own):
+        by_x = swap(own, 1)
+        total = own.astype(F32) + by_x.astype(F32)
+        by_near = swap(total.astype(BF16), 2)
+        total = total + by_near.astype(F32)
+        return by_x, by_near, swap(total.astype(BF16), 4)
+
+    got_states = spread(states)
+
+    x_weight_a = swap(side_by_side(my_weight, z_weight[0]), 1)
+    x_weight_b = swap(side_by_side(*z_weight[1:]), 1)
 
     def weight_blocks(refs):
         own, *others, xa_ref, xb_ref = refs
@@ -257,15 +296,32 @@
     )
     grad_other = swap_y(grad_send)
 
-    z_cols = [rotate(a, k) for a, k in zip(gz_send, turns)]
-    h_cols = [swap_core(a) for a in z_cols]
-
-    def forward(q_ref, local_ref, xs_ref, *refs):
-        *z_refs, att_ref, normed_ref, prefix_ref = refs
-        g, z, x, h = place()
-        total = jnp.where(x == 1, xs_ref[...].astype(F32), 0.0)
-        for k, z_ref in zip(turns, z_refs):
-            total += jnp.where(z >= k, z_ref[...].astype(F32), 0.0)
+    far_cols = swap(far_send, 4)
+
+    def relay(gy_ref, far_ref, near_ref):
+        g, z, x, h = place()
+        other = lax.rem(z + 1, 2)
+        near = z + 1 - 2 * lax.rem(z, 2)
+        near_ref[:rows, :] = gy_ref[:, lanes(near * 2 + h, wrows)]
+        near_ref[rows:, :] = far_ref[pl.ds(pl.multiple_of(other * rows, rows), rows), :]
+
+    (near_send,) = call(relay, [((2 * rows, wrows), BF16)], grad_y, far_cols)
+    near_cols = swap(near_send, 2)
+
+    def collect(far_ref, near_ref, out_ref):
+        g, z, x, h = place()
+        mine = lax.rem(z, 2)
+        out_ref[:rows, :] = far_ref[pl.ds(pl.multiple_of(mine * rows, rows), rows), :]
+        out_ref[rows:, :] = near_ref[...]
+
+    (my_cols,) = call(collect, [((3 * rows, wrows), BF16)], far_cols, near_cols)
+    core_cols = swap_core(my_cols)
+
+    def forward(q_ref, local_ref, x_ref, near_ref, far_ref, att_ref, normed_ref, prefix_ref):
+        g, z, x, h = place()
+        total = jnp.where(x == 1, x_ref[...].astype(F32), 0.0)
+        total += jnp.where(lax.rem(z, 2) == 1, near_ref[...].astype(F32), 0.0)
+        total += jnp.where(z >= 2, far_ref[...].astype(F32), 0.0)
         prefix = total.astype(BF16)
         prefix_ref[...] = prefix
         for i in range(heads):
@@ -279,10 +335,11 @@
     attended, normed, prefix = call(
         forward,
         [((rows, feats), F32), ((rows, feats), BF16), (state, BF16)],
-        queries, att_local, x_states, *z_states,
+        queries, att_local, *got_states,
     )
     y_normed = swap_y(normed)
-    z_normed = [rotate(normed, k) for k in turns]
+    far_normed = swap(normed, 4)
+    near_normed = swap(side_by_side(normed, far_normed), 2)
 
     def turn_back(att_ref, own_ref, other_ref, q_ref, go_ref, adj_ref):
         for i in range(heads):
@@ -299,7 +356,7 @@
         turn_back, [((rows, feats), BF16), (state, BF16)],
         attended, grad_own, grad_other, queries,
     )
-    x_adjoint = swap_x(adjoint)
+    got_adjoint = spread(adjoint)
 
     def local_grads(go_ref, q_ref, k_ref, v_ref, sc_ref, pre_ref, gq_ref, gk_ref, gv_ref):
         mask = causal_mask()
@@ -318,8 +375,6 @@
         [((rows, feats), BF16), ((rows, feats), F32), ((rows, feats), F32)],
         grad_out, queries, keys, values, scores, prefix,
     )
-    pair_adjoint = (adjoint.astype(F32) + x_adjoint.astype(F32)).astype(BF16)
-    z_adjoint = [rotate(pair_adjoint, k) for k in turns]
 
     def project(n_ref, yn_ref, *refs):
         *w_refs, own_ref, other_ref = refs
@@ -333,6 +388,23 @@
     out_other = swap_y(out_send)
     core_own = swap_core(out_own)
     core_other = swap_core(out_other)
+
+    def weight_grad(gy_ref, c_ref, o_ref, n_ref, far_ref, near_ref, keep_ref, send_ref):
+        g, z, x, h = place()
+        same = dot(gy_ref[:, lanes(z * 2 + h, wrows)], n_ref[...], ROWS_T)
+        other = dot(gy_ref[:, lanes(z * 2 + 1 - h, wrows)], n_ref[...], ROWS_T)
+        same += dot(c_ref[:rows, :], far_ref[...], ROWS_T)
+        other += dot(o_ref[:rows, :], far_ref[...], ROWS_T)
+        same += dot(c_ref[rows:, :], near_ref[...], ROWS_T)
+        other += dot(o_ref[rows:, :], near_ref[...], ROWS_T)
+        keep_ref[...] = jnp.where(x == h, same, other)
+        send_ref[...] = jnp.where(x == h, other, same).astype(BF16)
+
+    gw_keep, gw_send = call(
+        weight_grad, [((wrows, feats), F32), ((wrows, feats), BF16)],
+        grad_y, my_cols, core_cols, normed, far_normed, near_normed,
+    )
+    gw_other = swap(gw_send, 1)
 
     def join(a_ref, b_ref, c_ref, d_ref, y_ref):
         g = lax.axis_index("groups")
@@ -348,32 +420,13 @@
     (out_y,) = call(
         join, [((rows, outs), BF16)], out_own, core_own, out_other, core_other
     )
-
-    def weight_grad(gy_ref, n_ref, *refs):
-        *ins, keep_ref, send_ref = refs
-        count = line - 1
-        c_refs, o_refs, z_refs = ins[:count], ins[count : 2 * count], ins[2 * count :]
-        g, z, x, h = place()
-        same = dot(gy_ref[:, lanes(z * 2 + h, wrows)], n_ref[...], ROWS_T)
-        other = dot(gy_ref[:, lanes(z * 2 + 1 - h, wrows)], n_ref[...], ROWS_T)
-        for c_ref, o_ref, z_ref in zip(c_refs, o_refs, z_refs):
-            same += dot(c_ref[...], z_ref[...], ROWS_T)
-            other += dot(o_ref[...], z_ref[...], ROWS_T)
-        keep_ref[...] = jnp.where(x == h, same, other)
-        send_ref[...] = jnp.where(x == h, other, same).astype(BF16)
-
-    gw_keep, gw_send = call(
-        weight_grad, [((wrows, feats), F32), ((wrows, feats), BF16)],
-        grad_y, normed, *z_cols, *h_cols, *z_normed,
-    )
-    grad_weight = gw_keep + swap_x(gw_send).astype(F32)
-
-    def last(gk_ref, gv_ref, k_ref, v_ref, xa_ref, *refs):
-        *z_refs, ok_ref, ov_ref = refs
-        g, z, x, h = place()
-        total = jnp.where(x == 0, xa_ref[...].astype(F32), 0.0)
-        for k, z_ref in zip(turns, z_refs):
-            total += jnp.where(z < k, z_ref[...].astype(F32), 0.0)
+    grad_weight = gw_keep + gw_other.astype(F32)
+
+    def last(gk_ref, gv_ref, k_ref, v_ref, x_ref, near_ref, far_ref, ok_ref, ov_ref):
+        g, z, x, h = place()
+        total = jnp.where(x == 0, x_ref[...].astype(F32), 0.0)
+        total += jnp.where(lax.rem(z, 2) == 0, near_ref[...].astype(F32), 0.0)
+        total += jnp.where(z < 2, far_ref[...].astype(F32), 0.0)
         suffix = total.astype(BF16)
         for i in range(heads):
             at = head_of(i)
@@ -386,7 +439,7 @@
 
     grad_keys, grad_values = call(
         last, [((rows, feats), BF16)] * 2,
-        gk_local, gv_local, keys, values, x_adjoint, *z_adjoint,
+        gk_local, gv_local, keys, values, *got_adjoint,
     )
     return out_y, grad_queries, grad_keys, grad_values, grad_weight
 

time: 78 us -> 66.7 us (0.86)
  waiting for transfers between devices: 21.3 us -> 15.1 us
  starting transfers between devices: 43.6 us -> 40 us
  local copies, waits for them, and re-layouts: 3.85 us -> 2.02 us
    ppermute x20 -> x16, waiting for transfers between devices: 21.3 us -> 15.1 us  [permute(): return lax.ppermute(array, 'seq', pairs)]
    ppermute x20 -> x16, starting transfers between devices: 37.7 us -> 33.8 us  [permute(): return lax.ppermute(array, 'seq', pairs)]
    unnamed x16 -> x12, local copies, waits for them, and re-layouts: 3.85 us -> 2.01 us
    pallas_call x10 -> x11, Pallas kernels: 7.16 us -> 6.81 us  [call(): pl.pallas_call(body, out_shape=[jax.ShapeDtypeStruct(s, d) for s, d in sh...]
  transfers between devices with their start and end apart: 29 -> 23, of which waited for: 12 -> 9; matrix products, arithmetic and copies ran while one was open for 1% -> 2% of each run, Pallas kernels for 8% -> 10%
where the time goes in v2:
time: 66.7 us; the launch traced here: 66.5 us
  starting transfers between devices  40 us (60%)
  waiting for transfers between devices  15.1 us (23%)
  Pallas kernels  7.49 us (11%)
  local copies, waits for them, and re-layouts  2.02 us (3%)
  other arithmetic  1.11 us (2%)
  between operations  0.8 us (1%)
    ppermute x16, starting transfers between devices, permute(): return lax.ppermute(array, 'seq', pairs)  33.8 us
    ppermute x16, waiting for transfers between devices, permute(): return lax.ppermute(array, 'seq', pairs)  15.1 us
    pallas_call x11, Pallas kernels, call(): pl.pallas_call(body, out_shape=[jax.ShapeDtypeStruct(s, d) for s, d in sh...  6.81 us
    ppermute x4, starting transfers between devices, swap_y(): return lax.ppermute(array, 'groups', [(0, 1), (1, 0)])  5.54 us
    unnamed x12, local copies, waits for them, and re-layouts  2.01 us
  transfers between devices with their start and end apart: 23, of which 9 were waited for; matrix products, arithmetic and copies ran while one was open for 2% of the time, Pallas kernels for 10%

profile of v2, /device:TPU:0, one launch (start us, length us, event | category | flops | bytes accessed | tf_op | source)
XLA Modules:
  0.0 66.5 jit_solution(11237684770839743271)
XLA Ops:
  0.7 0.9 %copy-done = bf16[256,512]{1,0:T(8,128)(2,1)S(1)} copy-done((bf16[256,512]{1,0:T(8,128)(2,1)S(1)}, bf16[256,512]{1,0:T(8,128)(2,1)}, u32[]{:S(2)}) %copy-start) | copy-done | bytes 262168
  1.6 4.1 %collective-permute-start.5 = (bf16[128,512]{1,0:T(8,128)(2,1)S(1)}, bf16[128,512]{1,0:T(8,128)(2,1)S(1)}, u32[]{:S(2)}, u32[]{:S(2)}) collective-permute-start(bf16[128,512]{1,0:T(8,128)(2,1)S(1)} %constant_dynamic-slice_fusion.refs_0_), channel_id=1, source_target_pairs={{0,8},{2,10},{4,12},{6,14},{8,0},{10,2},{12,4},{14,6},{1,9},{3,11}... | collective-permute-start | bytes 393224 | tf_op jit(solution)/shard_map/ppermute | solution.py:176
  5.7 1.3 %collective-permute-start.6 = (bf16[128,512]{1,0:T(8,128)(2,1)S(1)}, bf16[128,512]{1,0:T(8,128)(2,1)S(1)}, u32[]{:S(2)}, u32[]{:S(2)}) collective-permute-start(bf16[128,512]{1,0:T(8,128)(2,1)S(1)} %constant_dynamic-slice_fusion.refs_0_), channel_id=1, source_target_pairs={{0,12},{2,14},{4,0},{6,2},{8,4},{10,6},{12,8},{14,10},{1,13},{3,15... | collective-permute-start | bytes 393224 | tf_op jit(solution)/shard_map/ppermute | solution.py:176
  7.7 1.0 %copy-done.1 = bf16[128,2048]{1,0:T(8,128)(2,1)S(1)} copy-done((bf16[128,2048]{1,0:T(8,128)(2,1)S(1)}, bf16[128,2048]{1,0:T(8,128)(2,1)}, u32[]{:S(2)}) %copy-start.1) | copy-done | bytes 524312
  9.5 1.6 %collective-permute-start = (bf16[512,128]{1,0:T(8,128)(2,1)S(1)}, bf16[512,128]{1,0:T(8,128)(2,1)S(1)}, u32[]{:S(2)}, u32[]{:S(2)}) collective-permute-start(bf16[512,128]{1,0:T(8,128)(2,1)S(1)} %get-tuple-element.27), channel_id=1, source_target_pairs={{0,2},{2,0},{4,6},{6,4},{8,10},{10,8},{12,14},{14,12},{1,3},{3,1},... | collective-permute-start | bytes 393224 | tf_op jit(solution)/shard_map/ppermute | solution.py:176
  11.0 1.5 %collective-permute-start.12 = (bf16[128,1024]{1,0:T(8,128)(2,1)S(1)}, bf16[128,1024]{1,0:T(8,128)(2,1)S(1)}, u32[]{:S(2)}, u32[]{:S(2)}) collective-permute-start(bf16[128,1024]{1,0:T(8,128)(2,1)S(1)} %get-tuple-element.32), channel_id=1, source_target_pairs={{0,16},{16,0},{1,17},{17,1},{2,18},{18,2},{3,19},{19,3},{4,20},{20... | collective-permute-start | bytes 786440 | tf_op jit(solution)/shard_map/ppermute | solution.py:185
  12.6 1.1 %collective-permute-done.5.refs_2_ = bf16[128,512]{1,0:T(8,128)(2,1)S(1)} collective-permute-done((bf16[128,512]{1,0:T(8,128)(2,1)S(1)}, bf16[128,512]{1,0:T(8,128)(2,1)S(1)}, u32[]{:S(2)}, u32[]{:S(2)}) %collective-permute-start.5) | collective-permute-done | bytes 131104 | tf_op jit(solution)/shard_map/ppermute | solution.py:176
  13.7 2.2 %collective-permute-start.8 = (bf16[256,512]{1,0:T(8,128)(2,1)S(1)}, bf16[256,512]{1,0:T(8,128)(2,1)S(1)}, u32[]{:S(2)}, u32[]{:S(2)}) collective-permute-start(bf16[256,512]{1,0:T(8,128)(2,1)S(1)} %pad_maximum_fusion.1), channel_id=1, source_target_pairs={{0,2},{2,0},{4,6},{6,4},{8,10},{10,8},{12,14},{14,12},{1,3},{3,1},... | collective-permute-start | bytes 786440 | tf_op jit(solution)/shard_map/ppermute | solution.py:176
  16.1 1.6 %collective-permute-start.7 = (bf16[256,512]{1,0:T(8,128)(2,1)S(1)}, bf16[256,512]{1,0:T(8,128)(2,1)S(1)}, u32[]{:S(2)}, u32[]{:S(2)}) collective-permute-start(bf16[256,512]{1,0:T(8,128)(2,1)S(1)} %pad_maximum_fusion), channel_id=1, source_target_pairs={{0,2},{2,0},{4,6},{6,4},{8,10},{10,8},{12,14},{14,12},{1,3},{3,1},... | collective-permute-start | bytes 786440 | tf_op jit(solution)/shard_map/ppermute | solution.py:176
  17.7 2.9 %collective-permute-start.1 = (bf16[512,128]{1,0:T(8,128)(2,1)S(1)}, bf16[512,128]{1,0:T(8,128)(2,1)S(1)}, u32[]{:S(2)}, u32[]{:S(2)}) collective-permute-start(bf16[512,128]{1,0:T(8,128)(2,1)S(1)} %fusion), channel_id=1, source_target_pairs={{0,4},{2,6},{4,0},{6,2},{8,12},{10,14},{12,8},{14,10},{1,5},{3,7},... | collective-permute-start | bytes 393224 | tf_op jit(solution)/shard_map/ppermute | solution.py:176
  20.5 1.6 %collective-permute-start.17 = (bf16[256,256]{1,0:T(8,128)(2,1)S(1)}, bf16[256,256]{1,0:T(8,128)(2,1)S(1)}, u32[]{:S(2)}, u32[]{:S(2)}) collective-permute-start(bf16[256,256]{1,0:T(8,128)(2,1)S(1)} %get-tuple-element.44), channel_id=1, source_target_pairs={{0,8},{2,10},{4,12},{6,14},{8,0},{10,2},{12,4},{14,6},{1,9},{3,11}... | collective-permute-start | bytes 393224 | tf_op jit(solution)/shard_map/ppermute | solution.py:176
  22.1 0.8 %collective-permute-done.8.refs_5_ = bf16[256,512]{1,0:T(8,128)(2,1)S(1)} collective-permute-done((bf16[256,512]{1,0:T(8,128)(2,1)S(1)}, bf16[256,512]{1,0:T(8,128)(2,1)S(1)}, u32[]{:S(2)}, u32[]{:S(2)}) %collective-permute-start.8) | collective-permute-done | bytes 262176 | tf_op jit(solution)/shard_map/ppermute | solution.py:176
  22.9 3.0 %collective-permute-done.7.refs_4_ = bf16[256,512]{1,0:T(8,128)(2,1)S(1)} collective-permute-done((bf16[256,512]{1,0:T(8,128)(2,1)S(1)}, bf16[256,512]{1,0:T(8,128)(2,1)S(1)}, u32[]{:S(2)}, u32[]{:S(2)}) %collective-permute-start.7) | collective-permute-done | bytes 262176 | tf_op jit(solution)/shard_map/ppermute | solution.py:176
  26.6 1.8 %collective-permute-start.13 = (f32[128,512]{1,0:T(8,128)S(1)}, f32[128,512]{1,0:T(8,128)S(1)}, u32[]{:S(2)}, u32[]{:S(2)}) collective-permute-start(f32[128,512]{1,0:T(8,128)S(1)} %get-tuple-element.34), channel_id=1, source_target_pairs={{0,16},{16,0},{1,17},{17,1},{2,18},{18,2},{3,19},{19,3},{4,20},{20... | collective-permute-start | bytes 786440 | tf_op jit(solution)/shard_map/ppermute | solution.py:185
  28.4 4.0 %collective-permute-start.2 = (bf16[512,128]{1,0:T(8,128)(2,1)S(1)}, bf16[512,128]{1,0:T(8,128)(2,1)S(1)}, u32[]{:S(2)}, u32[]{:S(2)}) collective-permute-start(bf16[512,128]{1,0:T(8,128)(2,1)S(1)} %add_convert_fusion.1), channel_id=1, source_target_pairs={{0,8},{2,10},{4,12},{6,14},{8,0},{10,2},{12,4},{14,6},{1,9},{3,11}... | collective-permute-start | bytes 393224 | tf_op jit(solution)/shard_map/ppermute | solution.py:176
  32.4 3.0 %collective-permute-start.18 = (bf16[256,256]{1,0:T(8,128)(2,1)S(1)}, bf16[256,256]{1,0:T(8,128)(2,1)S(1)}, u32[]{:S(2)}, u32[]{:S(2)}) collective-permute-start(bf16[256,256]{1,0:T(8,128)(2,1)S(1)} %shard_map.101), channel_id=1, source_target_pairs={{0,4},{2,6},{4,0},{6,2},{8,12},{10,14},{12,8},{14,10},{1,5},{3,7},... | collective-permute-start | bytes 393224 | tf_op jit(solution)/shard_map/ppermute | solution.py:176
  35.4 0.7 %shard_map.92 = (bf16[128,512]{1,0:T(8,128)(2,1)S(1)}, f32[128,512]{1,0:T(8,128)S(1)}) custom-call(bf16[128,512]{1,0:T(8,128)(2,1)S(1)} %copy-done.3, bf16[128,512]{1,0:T(8,128)(2,1)S(1)} %copy-done.4, bf16[128,512]{1,0:T(8,128)(2,1)S(1)} %copy-done.5), custom_call_target="tpu_custom_call" | custom-call | flops 134217728 | bytes 1048576 | tf_op jit(solution)/shard_map/pallas_call | solution.py:135
  37.2 2.4 %collective-permute-start.20 = (bf16[128,512]{1,0:T(8,128)(2,1)S(1)}, bf16[128,512]{1,0:T(8,128)(2,1)S(1)}, u32[]{:S(2)}, u32[]{:S(2)}) collective-permute-start(bf16[128,512]{1,0:T(8,128)(2,1)S(1)} %get-tuple-element.28.n_ref), channel_id=1, source_target_pairs={{0,8},{2,10},{4,12},{6,14},{8,0},{10,2},{12,4},{14,6},{1,9},{3,11}... | collective-permute-start | bytes 393224 | tf_op jit(solution)/shard_map/ppermute | solution.py:176
  39.7 1.0 %collective-permute-start.3 = (bf16[128,512]{1,0:T(8,128)(2,1)S(1)}, bf16[128,512]{1,0:T(8,128)(2,1)S(1)}, u32[]{:S(2)}, u32[]{:S(2)}) collective-permute-start(bf16[128,512]{1,0:T(8,128)(2,1)S(1)} %get-tuple-element.28.n_ref), channel_id=1, source_target_pairs={{0,16},{16,0},{1,17},{17,1},{2,18},{18,2},{3,19},{19,3},{4,20},{20... | collective-permute-start | bytes 393224 | tf_op jit(solution)/shard_map/ppermute | solution.py:185
  41.1 1.1 %collective-permute-start.14 = (bf16[512,128]{1,0:T(8,128)(2,1)S(1)}, bf16[512,128]{1,0:T(8,128)(2,1)S(1)}, u32[]{:S(2)}, u32[]{:S(2)}) collective-permute-start(bf16[512,128]{1,0:T(8,128)(2,1)S(1)} %get-tuple-element.41), channel_id=1, source_target_pairs={{0,2},{2,0},{4,6},{6,4},{8,10},{10,8},{12,14},{14,12},{1,3},{3,1},... | collective-permute-start | bytes 393224 | tf_op jit(solution)/shard_map/ppermute | solution.py:176
  42.3 1.7 %collective-permute-done.20.far_ref = bf16[128,512]{1,0:T(8,128)(2,1)S(1)} collective-permute-done((bf16[128,512]{1,0:T(8,128)(2,1)S(1)}, bf16[128,512]{1,0:T(8,128)(2,1)S(1)}, u32[]{:S(2)}, u32[]{:S(2)}) %collective-permute-start.20) | collective-permute-done | bytes 131104 | tf_op jit(solution)/shard_map/ppermute | solution.py:176
  44.0 2.2 %collective-permute-start.21 = (bf16[256,512]{1,0:T(8,128)(2,1)S(1)}, bf16[256,512]{1,0:T(8,128)(2,1)S(1)}, u32[]{:S(2)}, u32[]{:S(2)}) collective-permute-start(bf16[256,512]{1,0:T(8,128)(2,1)S(1)} %pad_maximum_fusion.2), channel_id=1, source_target_pairs={{0,4},{2,6},{4,0},{6,2},{8,12},{10,14},{12,8},{14,10},{1,5},{3,7},... | collective-permute-start | bytes 786440 | tf_op jit(solution)/shard_map/ppermute | solution.py:176
  46.9 1.3 %collective-permute-start.10 = (bf16[128,1024]{1,0:T(8,128)(2,1)S(1)}, bf16[128,1024]{1,0:T(8,128)(2,1)S(1)}, u32[]{:S(2)}, u32[]{:S(2)}) collective-permute-start(bf16[128,1024]{1,0:T(8,128)(2,1)S(1)} %get-tuple-element.30), channel_id=1, source_target_pairs={{0,16},{16,0},{1,17},{17,1},{2,18},{18,2},{3,19},{19,3},{4,20},{20... | collective-permute-start | bytes 786440 | tf_op jit(solution)/shard_map/ppermute | solution.py:185
  48.2 2.1 %collective-permute-start.15 = (bf16[512,128]{1,0:T(8,128)(2,1)S(1)}, bf16[512,128]{1,0:T(8,128)(2,1)S(1)}, u32[]{:S(2)}, u32[]{:S(2)}) collective-permute-start(bf16[512,128]{1,0:T(8,128)(2,1)S(1)} %fusion.1), channel_id=1, source_target_pairs={{0,4},{2,6},{4,0},{6,2},{8,12},{10,14},{12,8},{14,10},{1,5},{3,7},... | collective-permute-start | bytes 393224 | tf_op jit(solution)/shard_map/ppermute | solution.py:176
  50.3 3.0 %collective-permute-done.21.near_ref = bf16[256,512]{1,0:T(8,128)(2,1)S(1)} collective-permute-done((bf16[256,512]{1,0:T(8,128)(2,1)S(1)}, bf16[256,512]{1,0:T(8,128)(2,1)S(1)}, u32[]{:S(2)}, u32[]{:S(2)}) %collective-permute-start.21) | collective-permute-done | bytes 262176 | tf_op jit(solution)/shard_map/ppermute | solution.py:176
  54.1 1.4 %shard_map.99 = (bf16[128,512]{1,0:T(8,128)(2,1)}, f32[128,512]{1,0:T(8,128)S(1)}, f32[128,512]{1,0:T(8,128)S(1)}) custom-call(bf16[128,512]{1,0:T(8,128)(2,1)S(1)} %get-tuple-element.35.go_ref, bf16[128,512]{1,0:T(8,128)(2,1)S(1)} %copy-done.3, bf16[128,512]{1,0:T(8,128)(2,1)S(1)} %copy-done.4, bf16[128,512]{1,0:T(8,128)(2,1)S(1)} %copy-done.5, ...), custom_call_target="tpu_custom_call" | custom-call | flops 134217728 | bytes 1048576 | tf_op jit(solution)/shard_map/pallas_call | solution.py:135
  56.1 3.0 %collective-permute-start.16 = (bf16[512,128]{1,0:T(8,128)(2,1)S(1)}, bf16[512,128]{1,0:T(8,128)(2,1)S(1)}, u32[]{:S(2)}, u32[]{:S(2)}) collective-permute-start(bf16[512,128]{1,0:T(8,128)(2,1)S(1)} %add_convert_fusion), channel_id=1, source_target_pairs={{0,8},{2,10},{4,12},{6,14},{8,0},{10,2},{12,4},{14,6},{1,9},{3,11}... | collective-permute-start | bytes 393224 | tf_op jit(solution)/shard_map/ppermute | solution.py:176
  59.1 1.3 %collective-permute-done.22 = bf16[256,512]{1,0:T(8,128)(2,1)S(1)} collective-permute-done((bf16[256,512]{1,0:T(8,128)(2,1)S(1)}, bf16[256,512]{1,0:T(8,128)(2,1)S(1)}, u32[]{:S(2)}, u32[]{:S(2)}) %collective-permute-start.22) | collective-permute-done | bytes 262176 | tf_op jit(solution)/shard_map/ppermute | solution.py:176
  60.4 0.9 %convert_add_fusion = f32[256,512]{1,0:T(8,128)} fusion(f32[256,512]{1,0:T(8,128)S(1)} %get-tuple-element.45, bf16[256,512]{1,0:T(8,128)(2,1)S(1)} %collective-permute-done.22), kind=kLoop, calls=%fused_computation | loop fusion | flops 262144 | bytes 1310720 | tf_op jit(solution)/shard_map/add | solution.py:423
  61.3 1.0 %shard_map.96 = bf16[128,2048]{1,0:T(8,128)(2,1)} custom-call(bf16[128,1024]{1,0:T(8,128)(2,1)S(1)} %get-tuple-element.29.a_ref, bf16[128,1024]{1,0:T(8,128)(2,1)S(1)} %collective-permute-done.9.b_ref, bf16[128,1024]{1,0:T(8,128)(2,1)S(1)} %collective-permute-done.10.c_ref, bf16[128,1024]{1,0:T(8,128)(2,1)S(1)} %collective-permute-done.11.d_ref), custom_call_target="tpu_custom_call" | custom-call | flops 134217728 | bytes 1048576 | tf_op jit(solution)/shard_map/pallas_call | solution.py:135
  62.3 3.3 %collective-permute-done.16.far_ref = bf16[512,128]{1,0:T(8,128)(2,1)S(1)} collective-permute-done((bf16[512,128]{1,0:T(8,128)(2,1)S(1)}, bf16[512,128]{1,0:T(8,128)(2,1)S(1)}, u32[]{:S(2)}, u32[]{:S(2)}) %collective-permute-start.16) | collective-permute-done | bytes 131104 | tf_op jit(solution)/shard_map/ppermute | solution.py:176
  65.6 1.0 %shard_map.100 = (bf16[128,512]{1,0:T(8,128)(2,1)}, bf16[128,512]{1,0:T(8,128)(2,1)}) custom-call(f32[128,512]{1,0:T(8,128)S(1)} %get-tuple-element.39.gk_ref, f32[128,512]{1,0:T(8,128)S(1)} %get-tuple-element.40.gv_ref, bf16[128,512]{1,0:T(8,128)(2,1)S(1)} %copy-done.4, bf16[128,512]{1,0:T(8,128)(2,1)S(1)} %copy-done.5, ...), custom_call_target="tpu_custom_call" | custom-call | flops 134217728 | bytes 1048576 | tf_op jit(solution)/shard_map/pallas_call | solution.py:135
  (47 shorter events, 6.0 us)
Async XLA Ops:
  0.6 1.0 %copy-start = (bf16[256,512]{1,0:T(8,128)(2,1)S(1)}, bf16[256,512]{1,0:T(8,128)(2,1)}, u32[]{:S(2)}) copy-start(bf16[256,512]{1,0:T(8,128)(2,1)} %param.8) | copy-start | bytes 786436
  1.6 6.1 %copy-start.4 = (bf16[128,512]{1,0:T(8,128)(2,1)S(1)}, bf16[128,512]{1,0:T(8,128)(2,1)}, u32[]{:S(2)}) copy-start(bf16[128,512]{1,0:T(8,128)(2,1)} %k_ref.5) | copy-start | bytes 393220
  1.6 6.1 %copy-start.5 = (bf16[128,512]{1,0:T(8,128)(2,1)S(1)}, bf16[128,512]{1,0:T(8,128)(2,1)}, u32[]{:S(2)}) copy-start(bf16[128,512]{1,0:T(8,128)(2,1)} %v_ref.5) | copy-start | bytes 393220
  1.6 12.1 %collective-permute-start.5 = (bf16[128,512]{1,0:T(8,128)(2,1)S(1)}, bf16[128,512]{1,0:T(8,128)(2,1)S(1)}, u32[]{:S(2)}, u32[]{:S(2)}) collective-permute-start(bf16[128,512]{1,0:T(8,128)(2,1)S(1)} %constant_dynamic-slice_fusion.refs_0_), channel_id=1, source_target_pairs={{0,8},{2,10},{4,12},{6,14},{8,0},{10,2},{12,4},{14,6},{1,9},{3,11}... | collective-permute-start | bytes 393224 | tf_op jit(solution)/shard_map/ppermute | solution.py:176
  5.7 8.0 %collective-permute-start.6 = (bf16[128,512]{1,0:T(8,128)(2,1)S(1)}, bf16[128,512]{1,0:T(8,128)(2,1)S(1)}, u32[]{:S(2)}, u32[]{:S(2)}) collective-permute-start(bf16[128,512]{1,0:T(8,128)(2,1)S(1)} %constant_dynamic-slice_fusion.refs_0_), channel_id=1, source_target_pairs={{0,12},{2,14},{4,0},{6,2},{8,4},{10,6},{12,8},{14,10},{1,13},{3,15... | collective-permute-start | bytes 393224 | tf_op jit(solution)/shard_map/ppermute | solution.py:176
  7.1 9.0 %collective-permute-start.4 = (bf16[128,512]{1,0:T(8,128)(2,1)S(1)}, bf16[128,512]{1,0:T(8,128)(2,1)S(1)}, u32[]{:S(2)}, u32[]{:S(2)}) collective-permute-start(bf16[128,512]{1,0:T(8,128)(2,1)S(1)} %constant_dynamic-slice_fusion.refs_0_), channel_id=1, source_target_pairs={{0,4},{2,6},{4,8},{6,10},{8,12},{10,14},{12,0},{14,2},{1,5},{3,7},... | collective-permute-start | bytes 393224 | tf_op jit(solution)/shard_map/ppermute | solution.py:176
  7.7 1.0 %copy-start.1 = (bf16[128,2048]{1,0:T(8,128)(2,1)S(1)}, bf16[128,2048]{1,0:T(8,128)(2,1)}, u32[]{:S(2)}) copy-start(bf16[128,2048]{1,0:T(8,128)(2,1)} %gy_ref.5) | copy-start | bytes 1572868
  9.5 8.1 %collective-permute-start = (bf16[512,128]{1,0:T(8,128)(2,1)S(1)}, bf16[512,128]{1,0:T(8,128)(2,1)S(1)}, u32[]{:S(2)}, u32[]{:S(2)}) collective-permute-start(bf16[512,128]{1,0:T(8,128)(2,1)S(1)} %get-tuple-element.27), channel_id=1, source_target_pairs={{0,2},{2,0},{4,6},{6,4},{8,10},{10,8},{12,14},{14,12},{1,3},{3,1},... | collective-permute-start | bytes 393224 | tf_op jit(solution)/shard_map/ppermute | solution.py:176
  11.0 11.0 %collective-permute-start.12 = (bf16[128,1024]{1,0:T(8,128)(2,1)S(1)}, bf16[128,1024]{1,0:T(8,128)(2,1)S(1)}, u32[]{:S(2)}, u32[]{:S(2)}) collective-permute-start(bf16[128,1024]{1,0:T(8,128)(2,1)S(1)} %get-tuple-element.32), channel_id=1, source_target_pairs={{0,16},{16,0},{1,17},{17,1},{2,18},{18,2},{3,19},{19,3},{4,20},{20... | collective-permute-start | bytes 786440 | tf_op jit(solution)/shard_map/ppermute | solution.py:185
  13.7 12.2 %copy-start.2 = (bf16[128,2048]{1,0:T(8,128)(2,1)S(1)}, bf16[128,2048]{1,0:T(8,128)(2,1)}, u32[]{:S(2)}) copy-start(bf16[128,2048]{1,0:T(8,128)(2,1)} %gy_ref.5) | copy-start | bytes 1572868
  13.7 9.2 %collective-permute-start.8 = (bf16[256,512]{1,0:T(8,128)(2,1)S(1)}, bf16[256,512]{1,0:T(8,128)(2,1)S(1)}, u32[]{:S(2)}, u32[]{:S(2)}) collective-permute-start(bf16[256,512]{1,0:T(8,128)(2,1)S(1)} %pad_maximum_fusion.1), channel_id=1, source_target_pairs={{0,2},{2,0},{4,6},{6,4},{8,10},{10,8},{12,14},{14,12},{1,3},{3,1},... | collective-permute-start | bytes 786440 | tf_op jit(solution)/shard_map/ppermute | solution.py:176
  16.1 9.8 %collective-permute-start.7 = (bf16[256,512]{1,0:T(8,128)(2,1)S(1)}, bf16[256,512]{1,0:T(8,128)(2,1)S(1)}, u32[]{:S(2)}, u32[]{:S(2)}) collective-permute-start(bf16[256,512]{1,0:T(8,128)(2,1)S(1)} %pad_maximum_fusion), channel_id=1, source_target_pairs={{0,2},{2,0},{4,6},{6,4},{8,10},{10,8},{12,14},{14,12},{1,3},{3,1},... | collective-permute-start | bytes 786440 | tf_op jit(solution)/shard_map/ppermute | solution.py:176
  17.7 10.7 %collective-permute-start.1 = (bf16[512,128]{1,0:T(8,128)(2,1)S(1)}, bf16[512,128]{1,0:T(8,128)(2,1)S(1)}, u32[]{:S(2)}, u32[]{:S(2)}) collective-permute-start(bf16[512,128]{1,0:T(8,128)(2,1)S(1)} %fusion), channel_id=1, source_target_pairs={{0,4},{2,6},{4,0},{6,2},{8,12},{10,14},{12,8},{14,10},{1,5},{3,7},... | collective-permute-start | bytes 393224 | tf_op jit(solution)/shard_map/ppermute | solution.py:176
  20.5 11.9 %collective-permute-start.17 = (bf16[256,256]{1,0:T(8,128)(2,1)S(1)}, bf16[256,256]{1,0:T(8,128)(2,1)S(1)}, u32[]{:S(2)}, u32[]{:S(2)}) collective-permute-start(bf16[256,256]{1,0:T(8,128)(2,1)S(1)} %get-tuple-element.44), channel_id=1, source_target_pairs={{0,8},{2,10},{4,12},{6,14},{8,0},{10,2},{12,4},{14,6},{1,9},{3,11}... | collective-permute-start | bytes 393224 | tf_op jit(solution)/shard_map/ppermute | solution.py:176
  26.6 14.2 %collective-permute-start.13 = (f32[128,512]{1,0:T(8,128)S(1)}, f32[128,512]{1,0:T(8,128)S(1)}, u32[]{:S(2)}, u32[]{:S(2)}) collective-permute-start(f32[128,512]{1,0:T(8,128)S(1)} %get-tuple-element.34), channel_id=1, source_target_pairs={{0,16},{16,0},{1,17},{17,1},{2,18},{18,2},{3,19},{19,3},{4,20},{20... | collective-permute-start | bytes 786440 | tf_op jit(solution)/shard_map/ppermute | solution.py:185
  28.4 7.0 %copy-start.3 = (bf16[128,512]{1,0:T(8,128)(2,1)S(1)}, bf16[128,512]{1,0:T(8,128)(2,1)}, u32[]{:S(2)}) copy-start(bf16[128,512]{1,0:T(8,128)(2,1)} %q_ref.7) | copy-start | bytes 393220
  28.4 8.5 %collective-permute-start.2 = (bf16[512,128]{1,0:T(8,128)(2,1)S(1)}, bf16[512,128]{1,0:T(8,128)(2,1)S(1)}, u32[]{:S(2)}, u32[]{:S(2)}) collective-permute-start(bf16[512,128]{1,0:T(8,128)(2,1)S(1)} %add_convert_fusion.1), channel_id=1, source_target_pairs={{0,8},{2,10},{4,12},{6,14},{8,0},{10,2},{12,4},{14,6},{1,9},{3,11}... | collective-permute-start | bytes 393224 | tf_op jit(solution)/shard_map/ppermute | solution.py:176
  32.4 7.2 %collective-permute-start.18 = (bf16[256,256]{1,0:T(8,128)(2,1)S(1)}, bf16[256,256]{1,0:T(8,128)(2,1)S(1)}, u32[]{:S(2)}, u32[]{:S(2)}) collective-permute-start(bf16[256,256]{1,0:T(8,128)(2,1)S(1)} %shard_map.101), channel_id=1, source_target_pairs={{0,4},{2,6},{4,0},{6,2},{8,12},{10,14},{12,8},{14,10},{1,5},{3,7},... | collective-permute-start | bytes 393224 | tf_op jit(solution)/shard_map/ppermute | solution.py:176
  37.2 6.7 %collective-permute-start.20 = (bf16[128,512]{1,0:T(8,128)(2,1)S(1)}, bf16[128,512]{1,0:T(8,128)(2,1)S(1)}, u32[]{:S(2)}, u32[]{:S(2)}) collective-permute-start(bf16[128,512]{1,0:T(8,128)(2,1)S(1)} %get-tuple-element.28.n_ref), channel_id=1, source_target_pairs={{0,8},{2,10},{4,12},{6,14},{8,0},{10,2},{12,4},{14,6},{1,9},{3,11}... | collective-permute-start | bytes 393224 | tf_op jit(solution)/shard_map/ppermute | solution.py:176
  39.7 10.7 %collective-permute-start.19 = (bf16[384,256]{1,0:T(8,128)(2,1)S(1)}, bf16[384,256]{1,0:T(8,128)(2,1)S(1)}, u32[]{:S(2)}, u32[]{:S(2)}) collective-permute-start(bf16[384,256]{1,0:T(8,128)(2,1)S(1)} %shard_map.102.c_ref), channel_id=1, source_target_pairs={{0,1},{1,0},{2,3},{3,2},{4,5},{5,4},{6,7},{7,6},{8,9},{9,8},{10,11... | collective-permute-start | bytes 589832 | tf_op jit(solution)/shard_map/ppermute | solution.py:188
  39.7 6.4 %collective-permute-start.3 = (bf16[128,512]{1,0:T(8,128)(2,1)S(1)}, bf16[128,512]{1,0:T(8,128)(2,1)S(1)}, u32[]{:S(2)}, u32[]{:S(2)}) collective-permute-start(bf16[128,512]{1,0:T(8,128)(2,1)S(1)} %get-tuple-element.28.n_ref), channel_id=1, source_target_pairs={{0,16},{16,0},{1,17},{17,1},{2,18},{18,2},{3,19},{19,3},{4,20},{20... | collective-permute-start | bytes 393224 | tf_op jit(solution)/shard_map/ppermute | solution.py:185
  41.1 7.0 %collective-permute-start.14 = (bf16[512,128]{1,0:T(8,128)(2,1)S(1)}, bf16[512,128]{1,0:T(8,128)(2,1)S(1)}, u32[]{:S(2)}, u32[]{:S(2)}) collective-permute-start(bf16[512,128]{1,0:T(8,128)(2,1)S(1)} %get-tuple-element.41), channel_id=1, source_target_pairs={{0,2},{2,0},{4,6},{6,4},{8,10},{10,8},{12,14},{14,12},{1,3},{3,1},... | collective-permute-start | bytes 393224 | tf_op jit(solution)/shard_map/ppermute | solution.py:176
  44.0 9.4 %collective-permute-start.21 = (bf16[256,512]{1,0:T(8,128)(2,1)S(1)}, bf16[256,512]{1,0:T(8,128)(2,1)S(1)}, u32[]{:S(2)}, u32[]{:S(2)}) collective-permute-start(bf16[256,512]{1,0:T(8,128)(2,1)S(1)} %pad_maximum_fusion.2), channel_id=1, source_target_pairs={{0,4},{2,6},{4,0},{6,2},{8,12},{10,14},{12,8},{14,10},{1,5},{3,7},... | collective-permute-start | bytes 786440 | tf_op jit(solution)/shard_map/ppermute | solution.py:176
  46.9 8.6 %collective-permute-start.10 = (bf16[128,1024]{1,0:T(8,128)(2,1)S(1)}, bf16[128,1024]{1,0:T(8,128)(2,1)S(1)}, u32[]{:S(2)}, u32[]{:S(2)}) collective-permute-start(bf16[128,1024]{1,0:T(8,128)(2,1)S(1)} %get-tuple-element.30), channel_id=1, source_target_pairs={{0,16},{16,0},{1,17},{17,1},{2,18},{18,2},{3,19},{19,3},{4,20},{20... | collective-permute-start | bytes 786440 | tf_op jit(solution)/shard_map/ppermute | solution.py:185
  48.2 7.8 %collective-permute-start.15 = (bf16[512,128]{1,0:T(8,128)(2,1)S(1)}, bf16[512,128]{1,0:T(8,128)(2,1)S(1)}, u32[]{:S(2)}, u32[]{:S(2)}) collective-permute-start(bf16[512,128]{1,0:T(8,128)(2,1)S(1)} %fusion.1), channel_id=1, source_target_pairs={{0,4},{2,6},{4,0},{6,2},{8,12},{10,14},{12,8},{14,10},{1,5},{3,7},... | collective-permute-start | bytes 393224 | tf_op jit(solution)/shard_map/ppermute | solution.py:176
  54.0 6.4 %collective-permute-start.22 = (bf16[256,512]{1,0:T(8,128)(2,1)S(1)}, bf16[256,512]{1,0:T(8,128)(2,1)S(1)}, u32[]{:S(2)}, u32[]{:S(2)}) collective-permute-start(bf16[256,512]{1,0:T(8,128)(2,1)S(1)} %get-tuple-element.46), channel_id=1, source_target_pairs={{0,2},{2,0},{4,6},{6,4},{8,10},{10,8},{12,14},{14,12},{1,3},{3,1},... | collective-permute-start | bytes 786440 | tf_op jit(solution)/shard_map/ppermute | solution.py:176
  54.0 7.2 %collective-permute-start.9 = (bf16[128,1024]{1,0:T(8,128)(2,1)S(1)}, bf16[128,1024]{1,0:T(8,128)(2,1)S(1)}, u32[]{:S(2)}, u32[]{:S(2)}) collective-permute-start(bf16[128,1024]{1,0:T(8,128)(2,1)S(1)} %get-tuple-element.29.a_ref), channel_id=1, source_target_pairs={{0,1},{1,0},{2,3},{3,2},{4,5},{5,4},{6,7},{7,6},{8,9},{9,8},{10,11... | collective-permute-start | bytes 786440 | tf_op jit(solution)/shard_map/ppermute | solution.py:188
  55.5 5.8 %collective-permute-start.11 = (bf16[128,1024]{1,0:T(8,128)(2,1)S(1)}, bf16[128,1024]{1,0:T(8,128)(2,1)S(1)}, u32[]{:S(2)}, u32[]{:S(2)}) collective-permute-start(bf16[128,1024]{1,0:T(8,128)(2,1)S(1)} %collective-permute-done.10.c_ref), channel_id=1, source_target_pairs={{0,1},{1,0},{2,3},{3,2},{4,5},{5,4},{6,7},{7,6},{8,9},{9,8},{10,11... | collective-permute-start | bytes 786440 | tf_op jit(solution)/shard_map/ppermute | solution.py:188
  56.1 9.5 %collective-permute-start.16 = (bf16[512,128]{1,0:T(8,128)(2,1)S(1)}, bf16[512,128]{1,0:T(8,128)(2,1)S(1)}, u32[]{:S(2)}, u32[]{:S(2)}) collective-permute-start(bf16[512,128]{1,0:T(8,128)(2,1)S(1)} %add_convert_fusion), channel_id=1, source_target_pairs={{0,8},{2,10},{4,12},{6,14},{8,0},{10,2},{12,4},{14,6},{1,9},{3,11}... | collective-permute-start | bytes 393224 | tf_op jit(solution)/shard_map/ppermute | solution.py:176

commit v3 on v2

--- a/solution.py
+++ b/solution.py
@@ -131,7 +131,7 @@
     return lax.dot_general(a, b, dims, preferred_element_type=F32)
 
 
-def call(body, shapes, *args, flops=2**27, moved=2**20):
+def call(body, shapes, *args, flops=500000000, moved=2**20):
     return pl.pallas_call(
         body,
         out_shape=[jax.ShapeDtypeStruct(s, d) for s, d in shapes],
@@ -190,55 +190,35 @@
     def side_by_side(*arrays):
         return jnp.concatenate(arrays, axis=0)
 
+    def after(array, *others):
+        return lax.optimization_barrier((array, *others))[0]
+
     g = lax.axis_index("groups")
     my_weight = lax.dynamic_slice_in_dim(out_weight, g * half, half, 0)
     z_weight = [rotate(my_weight, k) for k in turns]
 
-    def first(k_hbm, v_hbm, gy_hbm, s_ref, ys_ref, gz_ref, k_ref, v_ref, gy_ref, sems):
-        copies = [
-            pltpu.make_async_copy(src, dst, sems.at[i])
-            for i, (src, dst) in enumerate(
-                ((k_hbm, k_ref), (v_hbm, v_ref), (gy_hbm, gy_ref))
-            )
-        ]
-        for copy in copies:
-            copy.start()
-        g, z, x, h = place()
-        copies[0].wait()
-        copies[1].wait()
+    def own_state(k_ref, v_ref, s_ref):
         for i in range(heads):
             s_ref[head_of(i), :] = dot(
                 k_ref[:, head_of(i)], v_ref[:, head_of(i)], ROWS_T
             ).astype(BF16)
-        copies[2].wait()
+
+    (states,) = call(own_state, [(state, BF16)], keys, values)
+    x_weight_own = swap(my_weight, 1)
+
+    def pack(gy_ref, ys_ref, gz_ref):
+        g, z, x, h = place()
         for i in range(seq):
             ys_ref[:, i * half : (i + 1) * half] = gy_ref[:, lanes(2 * i + 1 - g, half)]
-        far = z // 2 * 2
-        far = 2 - far
+        far = 2 - z // 2 * 2
         for b in range(2):
             gz_ref[b * rows : (b + 1) * rows, :] = gy_ref[
                 :, lanes((far + b) * 2 + h, wrows)
             ]
 
-    states, y_send, far_send = pl.pallas_call(
-        first,
-        out_shape=[
-            jax.ShapeDtypeStruct(s, BF16)
-            for s in (state, (rows, seq * half), (2 * rows, wrows))
-        ],
-        in_specs=[pl.BlockSpec(memory_space=pltpu.HBM)] * 3,
-        out_specs=[pl.BlockSpec(memory_space=pltpu.VMEM)] * 3,
-        scratch_shapes=[
-            pltpu.VMEM(keys.shape, BF16),
-            pltpu.VMEM(values.shape, BF16),
-            pltpu.VMEM(grad_y.shape, BF16),
-            pltpu.SemaphoreType.DMA((3,)),
-        ],
-        cost_estimate=pl.CostEstimate(
-            flops=2**27, bytes_accessed=2**20, transcendentals=0
-        ),
-        compiler_params=pltpu.CompilerParams(vmem_limit_bytes=24 * 2**20),
-    )(keys, values, grad_y)
+    y_send, far_send = call(
+        pack, [((rows, seq * half), BF16), ((2 * rows, wrows), BF16)], grad_y
+    )
     y_cols = swap_y(y_send)
 
     def local(q_ref, k_ref, v_ref, sc_ref, att_ref):
@@ -253,50 +233,58 @@
         local, [((rows, feats), BF16), ((rows, feats), F32)], queries, keys, values
     )
 
-    def spread(own):
-        by_x = swap(own, 1)
-        total = own.astype(F32) + by_x.astype(F32)
-        by_near = swap(total.astype(BF16), 2)
-        total = total + by_near.astype(F32)
-        return by_x, by_near, swap(total.astype(BF16), 4)
-
-    got_states = spread(states)
-
-    x_weight_a = swap(side_by_side(my_weight, z_weight[0]), 1)
-    x_weight_b = swap(side_by_side(*z_weight[1:]), 1)
+    def add(a, b):
+        return (a.astype(F32) + b.astype(F32)).astype(BF16)
+
+    x_states = swap(states, 1)
+    pair_states = add(states, x_states)
+    near_states = swap(pair_states, 2)
+    quad_states = add(pair_states, near_states)
+    got_states = x_states, near_states, swap(quad_states, 4)
+
+    x_weight_far = swap(side_by_side(*z_weight[1:]), 1)
+    x_weight_near = swap(after(z_weight[0], pair_states), 1)
 
     def weight_blocks(refs):
-        own, *others, xa_ref, xb_ref = refs
+        own, *others, x_own, x_near, x_far = refs
         g, z, x, h = place()
         blocks = []
         for k in range(line):
             zk = lax.rem(z - k + line, line)
             blocks.append((zk * 2 + x, (own, *others)[k][...]))
-            far = xa_ref if k < 2 else xb_ref
-            at = k if k < 2 else k - 2
-            blocks.append((zk * 2 + 1 - x, far[at * half : (at + 1) * half, :]))
+            if k < 2:
+                block = (x_own, x_near)[k][...]
+            else:
+                block = x_far[(k - 2) * half : (k - 1) * half, :]
+            blocks.append((zk * 2 + 1 - x, block))
         return blocks
 
-    weight_args = (my_weight, *z_weight, x_weight_a, x_weight_b)
-
-    def back(gy_ref, yc_ref, *refs):
-        *w_refs, own_ref, send_ref = refs
+    weight_args = (my_weight, *z_weight, x_weight_own, x_weight_near, x_weight_far)
+
+    def back_other(yc_ref, *refs):
+        *w_refs, out_ref = refs
+        total = jnp.zeros((rows, feats), F32)
+        for s, block in weight_blocks(w_refs):
+            total += dot(yc_ref[:, lanes(s, half)], block, PLAIN)
+        out_ref[...] = total
+
+    def back_own(gy_ref, *refs):
+        *w_refs, out_ref = refs
         g = lax.axis_index("groups")
-        own = jnp.zeros((rows, feats), F32)
-        other = jnp.zeros((rows, feats), F32)
+        total = jnp.zeros((rows, feats), F32)
         for s, block in weight_blocks(w_refs):
-            own += dot(gy_ref[:, lanes(2 * s + g, half)], block, PLAIN)
-            other += dot(yc_ref[:, lanes(s, half)], block, PLAIN)
-        own_ref[...] = own
-        send_ref[...] = other
-
-    grad_own, grad_send = call(
-        back, [((rows, feats), F32), ((rows, feats), F32)],
-        grad_y, y_cols, *weight_args,
+            total += dot(gy_ref[:, lanes(2 * s + g, half)], block, PLAIN)
+        out_ref[...] = total
+
+    (grad_send,) = call(
+        back_other, [((rows, feats), F32)], after(y_cols, quad_states), *weight_args
     )
     grad_other = swap_y(grad_send)
-
-    far_cols = swap(far_send, 4)
+    (grad_own,) = call(
+        back_own, [((rows, feats), F32)], after(grad_y, grad_send), *weight_args
+    )
+
+    far_cols = swap(after(far_send, grad_send), 4)
 
     def relay(gy_ref, far_ref, near_ref):
         g, z, x, h = place()
@@ -339,7 +327,8 @@
     )
     y_normed = swap_y(normed)
     far_normed = swap(normed, 4)
-    near_normed = swap(side_by_side(normed, far_normed), 2)
+    near_normed = swap(normed, 2)
+    last_normed = swap(far_normed, 2)
 
     def turn_back(att_ref, own_ref, other_ref, q_ref, go_ref, adj_ref):
         for i in range(heads):
@@ -356,7 +345,11 @@
         turn_back, [((rows, feats), BF16), (state, BF16)],
         attended, grad_own, grad_other, queries,
     )
-    got_adjoint = spread(adjoint)
+    x_adjoint = swap(adjoint, 1)
+    pair_adjoint = add(adjoint, x_adjoint)
+    near_adjoint = swap(pair_adjoint, 2)
+    quad_adjoint = add(pair_adjoint, near_adjoint)
+    got_adjoint = x_adjoint, near_adjoint, swap(quad_adjoint, 4)
 
     def local_grads(go_ref, q_ref, k_ref, v_ref, sc_ref, pre_ref, gq_ref, gk_ref, gv_ref):
         mask = causal_mask()
@@ -389,20 +382,21 @@
     core_own = swap_core(out_own)
     core_other = swap_core(out_other)
 
-    def weight_grad(gy_ref, c_ref, o_ref, n_ref, far_ref, near_ref, keep_ref, send_ref):
+    def weight_grad(gy_ref, c_ref, o_ref, n_ref, *refs):
+        *n_refs, keep_ref, send_ref = refs
         g, z, x, h = place()
         same = dot(gy_ref[:, lanes(z * 2 + h, wrows)], n_ref[...], ROWS_T)
         other = dot(gy_ref[:, lanes(z * 2 + 1 - h, wrows)], n_ref[...], ROWS_T)
-        same += dot(c_ref[:rows, :], far_ref[...], ROWS_T)
-        other += dot(o_ref[:rows, :], far_ref[...], ROWS_T)
-        same += dot(c_ref[rows:, :], near_ref[...], ROWS_T)
-        other += dot(o_ref[rows:, :], near_ref[...], ROWS_T)
+        for i, there_ref in enumerate(n_refs):
+            at = slice(i * rows, (i + 1) * rows)
+            same += dot(c_ref[at, :], there_ref[...], ROWS_T)
+            other += dot(o_ref[at, :], there_ref[...], ROWS_T)
         keep_ref[...] = jnp.where(x == h, same, other)
         send_ref[...] = jnp.where(x == h, other, same).astype(BF16)
 
     gw_keep, gw_send = call(
         weight_grad, [((wrows, feats), F32), ((wrows, feats), BF16)],
-        grad_y, my_cols, core_cols, normed, far_normed, near_normed,
+        grad_y, my_cols, core_cols, normed, far_normed, near_normed, last_normed,
     )
     gw_other = swap(gw_send, 1)
 

time: 66.7 us -> 70.3 us (1.054)
  waiting for transfers between devices: 15.1 us -> 33.2 us
  starting transfers between devices: 40 us -> 25.7 us
    ppermute x16 -> x18, waiting for transfers between devices: 15.1 us -> 32.2 us  [permute(): return lax.ppermute(array, 'seq', pairs)]
    ppermute x16 -> x18, starting transfers between devices: 33.8 us -> 21.5 us  [permute(): return lax.ppermute(array, 'seq', pairs)]
    ppermute x4, starting transfers between devices: 5.54 us -> 4.13 us  [swap_y(): return lax.ppermute(array, 'groups', [(0, 1), (1, 0)])]
    ppermute x4, waiting for transfers between devices: 0.01 us -> 1 us  [swap_y(): return lax.ppermute(array, 'groups', [(0, 1), (1, 0)])]
    pallas_call x11 -> x14, Pallas kernels: 6.81 us -> 7.38 us  [call(): pl.pallas_call(body, out_shape=[jax.ShapeDtypeStruct(s, d) for s, d in sh...]
    unnamed x12 -> x14, local copies, waits for them, and re-layouts: 2.01 us -> 1.91 us
  transfers between devices with their start and end apart: 23 -> 25, of which waited for: 9 -> 11; matrix products, arithmetic and copies ran while one was open for 2% -> 0% of each run, Pallas kernels for 10% -> 10%
where the time goes in v3:
time: 70.3 us; the launch traced here: 70.1 us
  waiting for transfers between devices  33.2 us (47%)
  starting transfers between devices  25.7 us (37%)
  Pallas kernels  7.38 us (10%)
  local copies, waits for them, and re-layouts  1.92 us (3%)
  other arithmetic  1.04 us (1%)
  between operations  0.85 us (1%)
    ppermute x18, waiting for transfers between devices, permute(): return lax.ppermute(array, 'seq', pairs)  32.2 us
    ppermute x18, starting transfers between devices, permute(): return lax.ppermute(array, 'seq', pairs)  21.5 us
    pallas_call x14, Pallas kernels, call(): pl.pallas_call(body, out_shape=[jax.ShapeDtypeStruct(s, d) for s, d in sh...  7.38 us
    ppermute x4, starting transfers between devices, swap_y(): return lax.ppermute(array, 'groups', [(0, 1), (1, 0)])  4.13 us
    unnamed x14, local copies, waits for them, and re-layouts  1.91 us
  transfers between devices with their start and end apart: 25, of which 11 were waited for; matrix products, arithmetic and copies ran while one was open for 0% of the time, Pallas kernels for 10%

profile of v3, /device:TPU:0, one launch (start us, length us, event | category | flops | bytes accessed | tf_op | source)
XLA Modules:
  0.0 70.1 jit_solution(18422735233926813362)
XLA Ops:
  0.7 1.0 %copy-done.3 = bf16[128,512]{1,0:T(8,128)(2,1)S(1)} copy-done((bf16[128,512]{1,0:T(8,128)(2,1)S(1)}, bf16[128,512]{1,0:T(8,128)(2,1)}, u32[]{:S(2)}) %copy-start.3) | copy-done | bytes 131096
  1.6 0.9 %copy-done.5 = bf16[128,512]{1,0:T(8,128)(2,1)S(1)} copy-done((bf16[128,512]{1,0:T(8,128)(2,1)S(1)}, bf16[128,512]{1,0:T(8,128)(2,1)}, u32[]{:S(2)}) %copy-start.5) | copy-done | bytes 131096
  2.8 3.0 %collective-permute-start = (bf16[512,128]{1,0:T(8,128)(2,1)S(1)}, bf16[512,128]{1,0:T(8,128)(2,1)S(1)}, u32[]{:S(2)}, u32[]{:S(2)}) collective-permute-start(bf16[512,128]{1,0:T(8,128)(2,1)S(1)} %shard_map.93), channel_id=1, source_target_pairs={{0,2},{2,0},{4,6},{6,4},{8,10},{10,8},{12,14},{14,12},{1,3},{3,1},... | collective-permute-start | bytes 393224 | tf_op jit(solution)/shard_map/ppermute | solution.py:176
  5.8 1.6 %collective-permute-start.4 = (bf16[128,512]{1,0:T(8,128)(2,1)S(1)}, bf16[128,512]{1,0:T(8,128)(2,1)S(1)}, u32[]{:S(2)}, u32[]{:S(2)}) collective-permute-start(bf16[128,512]{1,0:T(8,128)(2,1)S(1)} %constant_dynamic-slice_fusion.refs_0_), channel_id=1, source_target_pairs={{0,4},{2,6},{4,8},{6,10},{8,12},{10,14},{12,0},{14,2},{1,5},{3,7},... | collective-permute-start | bytes 393224 | tf_op jit(solution)/shard_map/ppermute | solution.py:176
  7.4 2.6 %collective-permute-start.5 = (bf16[128,512]{1,0:T(8,128)(2,1)S(1)}, bf16[128,512]{1,0:T(8,128)(2,1)S(1)}, u32[]{:S(2)}, u32[]{:S(2)}) collective-permute-start(bf16[128,512]{1,0:T(8,128)(2,1)S(1)} %constant_dynamic-slice_fusion.refs_0_), channel_id=1, source_target_pairs={{0,8},{2,10},{4,12},{6,14},{8,0},{10,2},{12,4},{14,6},{1,9},{3,11}... | collective-permute-start | bytes 393224 | tf_op jit(solution)/shard_map/ppermute | solution.py:176
  10.0 1.3 %collective-permute-start.6 = (bf16[128,512]{1,0:T(8,128)(2,1)S(1)}, bf16[128,512]{1,0:T(8,128)(2,1)S(1)}, u32[]{:S(2)}, u32[]{:S(2)}) collective-permute-start(bf16[128,512]{1,0:T(8,128)(2,1)S(1)} %constant_dynamic-slice_fusion.refs_0_), channel_id=1, source_target_pairs={{0,12},{2,14},{4,0},{6,2},{8,4},{10,6},{12,8},{14,10},{1,13},{3,15... | collective-permute-start | bytes 393224 | tf_op jit(solution)/shard_map/ppermute | solution.py:176
  11.4 1.6 %collective-permute-start.13 = (bf16[128,1024]{1,0:T(8,128)(2,1)S(1)}, bf16[128,1024]{1,0:T(8,128)(2,1)S(1)}, u32[]{:S(2)}, u32[]{:S(2)}) collective-permute-start(bf16[128,1024]{1,0:T(8,128)(2,1)S(1)} %get-tuple-element.33), channel_id=1, source_target_pairs={{0,16},{16,0},{1,17},{17,1},{2,18},{18,2},{3,19},{19,3},{4,20},{20... | collective-permute-start | bytes 786440 | tf_op jit(solution)/shard_map/ppermute | solution.py:185
  13.1 0.7 %collective-permute-start.1 = (bf16[512,128]{1,0:T(8,128)(2,1)S(1)}, bf16[512,128]{1,0:T(8,128)(2,1)S(1)}, u32[]{:S(2)}, u32[]{:S(2)}) collective-permute-start(bf16[512,128]{1,0:T(8,128)(2,1)S(1)} %add_convert_fusion.3), channel_id=1, source_target_pairs={{0,4},{2,6},{4,0},{6,2},{8,12},{10,14},{12,8},{14,10},{1,5},{3,7},... | collective-permute-start | bytes 393224 | tf_op jit(solution)/shard_map/ppermute | solution.py:176
  13.8 4.6 %collective-permute-done.5.refs_2_ = bf16[128,512]{1,0:T(8,128)(2,1)S(1)} collective-permute-done((bf16[128,512]{1,0:T(8,128)(2,1)S(1)}, bf16[128,512]{1,0:T(8,128)(2,1)S(1)}, u32[]{:S(2)}, u32[]{:S(2)}) %collective-permute-start.5) | collective-permute-done | bytes 131104 | tf_op jit(solution)/shard_map/ppermute | solution.py:176
  18.4 1.0 %collective-permute-done.6.refs_3_ = bf16[128,512]{1,0:T(8,128)(2,1)S(1)} collective-permute-done((bf16[128,512]{1,0:T(8,128)(2,1)S(1)}, bf16[128,512]{1,0:T(8,128)(2,1)S(1)}, u32[]{:S(2)}, u32[]{:S(2)}) %collective-permute-start.6) | collective-permute-done | bytes 131104 | tf_op jit(solution)/shard_map/ppermute | solution.py:176
  19.9 1.6 %collective-permute-start.7 = (bf16[128,512]{1,0:T(8,128)(2,1)S(1)}, bf16[128,512]{1,0:T(8,128)(2,1)S(1)}, u32[]{:S(2)}, u32[]{:S(2)}) collective-permute-start(bf16[128,512]{1,0:T(8,128)(2,1)S(1)} %constant_dynamic-slice_fusion.refs_0_), channel_id=1, source_target_pairs={{0,2},{2,0},{4,6},{6,4},{8,10},{10,8},{12,14},{14,12},{1,3},{3,1},... | collective-permute-start | bytes 393224 | tf_op jit(solution)/shard_map/ppermute | solution.py:176
  22.0 1.4 %collective-permute-start.2 = (bf16[512,128]{1,0:T(8,128)(2,1)S(1)}, bf16[512,128]{1,0:T(8,128)(2,1)S(1)}, u32[]{:S(2)}, u32[]{:S(2)}) collective-permute-start(bf16[512,128]{1,0:T(8,128)(2,1)S(1)} %add_convert_fusion.2), channel_id=1, source_target_pairs={{0,8},{2,10},{4,12},{6,14},{8,0},{10,2},{12,4},{14,6},{1,9},{3,11}... | collective-permute-start | bytes 393224 | tf_op jit(solution)/shard_map/ppermute | solution.py:176
  23.5 7.4 %collective-permute-done.7.refs_4_ = bf16[128,512]{1,0:T(8,128)(2,1)S(1)} collective-permute-done((bf16[128,512]{1,0:T(8,128)(2,1)S(1)}, bf16[128,512]{1,0:T(8,128)(2,1)S(1)}, u32[]{:S(2)}, u32[]{:S(2)}) %collective-permute-start.7) | collective-permute-done | bytes 131104 | tf_op jit(solution)/shard_map/ppermute | solution.py:176
  30.8 1.4 %collective-permute-done.8.refs_5_ = bf16[128,512]{1,0:T(8,128)(2,1)S(1)} collective-permute-done((bf16[128,512]{1,0:T(8,128)(2,1)S(1)}, bf16[128,512]{1,0:T(8,128)(2,1)S(1)}, u32[]{:S(2)}, u32[]{:S(2)}) %collective-permute-start.8) | collective-permute-done | bytes 131104 | tf_op jit(solution)/shard_map/ppermute | solution.py:176
  32.7 1.6 %collective-permute-start.14 = (f32[128,512]{1,0:T(8,128)S(1)}, f32[128,512]{1,0:T(8,128)S(1)}, u32[]{:S(2)}, u32[]{:S(2)}) collective-permute-start(f32[128,512]{1,0:T(8,128)S(1)} %shard_map.98), channel_id=1, source_target_pairs={{0,16},{16,0},{1,17},{17,1},{2,18},{18,2},{3,19},{19,3},{4,20},{20... | collective-permute-start | bytes 786440 | tf_op jit(solution)/shard_map/ppermute | solution.py:185
  34.3 2.4 %collective-permute-start.18 = (bf16[256,256]{1,0:T(8,128)(2,1)S(1)}, bf16[256,256]{1,0:T(8,128)(2,1)S(1)}, u32[]{:S(2)}, u32[]{:S(2)}) collective-permute-start(bf16[256,256]{1,0:T(8,128)(2,1)S(1)} %get-tuple-element.46), channel_id=1, source_target_pairs={{0,8},{2,10},{4,12},{6,14},{8,0},{10,2},{12,4},{14,6},{1,9},{3,11}... | collective-permute-start | bytes 393224 | tf_op jit(solution)/shard_map/ppermute | solution.py:176
  36.6 0.7 %shard_map.92 = (bf16[128,512]{1,0:T(8,128)(2,1)S(1)}, f32[128,512]{1,0:T(8,128)S(1)}) custom-call(bf16[128,512]{1,0:T(8,128)(2,1)S(1)} %copy-done.2, bf16[128,512]{1,0:T(8,128)(2,1)S(1)} %copy-done.4, bf16[128,512]{1,0:T(8,128)(2,1)S(1)} %copy-done.6), custom_call_target="tpu_custom_call" | custom-call | flops 500000000 | bytes 1048576 | tf_op jit(solution)/shard_map/pallas_call | solution.py:135
  39.3 7.0 %collective-permute-done.18.far_ref = bf16[256,256]{1,0:T(8,128)(2,1)S(1)} collective-permute-done((bf16[256,256]{1,0:T(8,128)(2,1)S(1)}, bf16[256,256]{1,0:T(8,128)(2,1)S(1)}, u32[]{:S(2)}, u32[]{:S(2)}) %collective-permute-start.18) | collective-permute-done | bytes 131104 | tf_op jit(solution)/shard_map/ppermute | solution.py:176
  47.4 2.0 %collective-permute-start.22 = (bf16[128,512]{1,0:T(8,128)(2,1)S(1)}, bf16[128,512]{1,0:T(8,128)(2,1)S(1)}, u32[]{:S(2)}, u32[]{:S(2)}) collective-permute-start(bf16[128,512]{1,0:T(8,128)(2,1)S(1)} %get-tuple-element.28.n_ref), channel_id=1, source_target_pairs={{0,4},{2,6},{4,0},{6,2},{8,12},{10,14},{12,8},{14,10},{1,5},{3,7},... | collective-permute-start | bytes 393224 | tf_op jit(solution)/shard_map/ppermute | solution.py:176
  49.4 0.7 shard_map.95
  50.6 2.2 %collective-permute-done.19.near_ref = bf16[256,256]{1,0:T(8,128)(2,1)S(1)} collective-permute-done((bf16[256,256]{1,0:T(8,128)(2,1)S(1)}, bf16[256,256]{1,0:T(8,128)(2,1)S(1)}, u32[]{:S(2)}, u32[]{:S(2)}) %collective-permute-start.19) | collective-permute-done | bytes 131104 | tf_op jit(solution)/shard_map/ppermute | solution.py:176
  52.9 1.0 %collective-permute-start.16 = (bf16[512,128]{1,0:T(8,128)(2,1)S(1)}, bf16[512,128]{1,0:T(8,128)(2,1)S(1)}, u32[]{:S(2)}, u32[]{:S(2)}) collective-permute-start(bf16[512,128]{1,0:T(8,128)(2,1)S(1)} %add_convert_fusion.1), channel_id=1, source_target_pairs={{0,4},{2,6},{4,0},{6,2},{8,12},{10,14},{12,8},{14,10},{1,5},{3,7},... | collective-permute-start | bytes 393224 | tf_op jit(solution)/shard_map/ppermute | solution.py:176
  53.9 1.7 %collective-permute-done.22.refs_1_ = bf16[128,512]{1,0:T(8,128)(2,1)S(1)} collective-permute-done((bf16[128,512]{1,0:T(8,128)(2,1)S(1)}, bf16[128,512]{1,0:T(8,128)(2,1)S(1)}, u32[]{:S(2)}, u32[]{:S(2)}) %collective-permute-start.22) | collective-permute-done | bytes 131104 | tf_op jit(solution)/shard_map/ppermute | solution.py:176
  55.6 1.0 %collective-permute-done.11.c_ref = bf16[128,1024]{1,0:T(8,128)(2,1)S(1)} collective-permute-done((bf16[128,1024]{1,0:T(8,128)(2,1)S(1)}, bf16[128,1024]{1,0:T(8,128)(2,1)S(1)}, u32[]{:S(2)}, u32[]{:S(2)}) %collective-permute-start.11) | collective-permute-done | bytes 262176 | tf_op jit(solution)/shard_map/ppermute | solution.py:185
  56.6 1.2 %collective-permute-done.23.refs_2_ = bf16[128,512]{1,0:T(8,128)(2,1)S(1)} collective-permute-done((bf16[128,512]{1,0:T(8,128)(2,1)S(1)}, bf16[128,512]{1,0:T(8,128)(2,1)S(1)}, u32[]{:S(2)}, u32[]{:S(2)}) %collective-permute-start.23) | collective-permute-done | bytes 131104 | tf_op jit(solution)/shard_map/ppermute | solution.py:176
  57.8 0.7 %shard_map.105 = (f32[256,512]{1,0:T(8,128)S(1)}, bf16[256,512]{1,0:T(8,128)(2,1)S(1)}) custom-call(bf16[128,2048]{1,0:T(8,128)(2,1)S(1)} %copy-done.1, bf16[384,256]{1,0:T(8,128)(2,1)S(1)} %shard_map.104.c_ref, bf16[384,256]{1,0:T(8,128)(2,1)S(1)} %collective-permute-done.20.o_ref, bf16[128,512]{1,0:T(8,128)(2,1)S(1)} %get-tuple-element.28.n_ref, ...), custom_call_target="tpu_custom_call" | custom-call | flops 500000000 | bytes 1048576 | tf_op jit(solution)/shard_map/pallas_call | solution.py:135
  59.8 1.0 %collective-permute-start.17 = (bf16[512,128]{1,0:T(8,128)(2,1)S(1)}, bf16[512,128]{1,0:T(8,128)(2,1)S(1)}, u32[]{:S(2)}, u32[]{:S(2)}) collective-permute-start(bf16[512,128]{1,0:T(8,128)(2,1)S(1)} %add_convert_fusion), channel_id=1, source_target_pairs={{0,8},{2,10},{4,12},{6,14},{8,0},{10,2},{12,4},{14,6},{1,9},{3,11}... | collective-permute-start | bytes 393224 | tf_op jit(solution)/shard_map/ppermute | solution.py:176
  60.9 1.4 %shard_map.101 = (bf16[128,512]{1,0:T(8,128)(2,1)}, f32[128,512]{1,0:T(8,128)S(1)}, f32[128,512]{1,0:T(8,128)S(1)}) custom-call(bf16[128,512]{1,0:T(8,128)(2,1)S(1)} %get-tuple-element.36.go_ref, bf16[128,512]{1,0:T(8,128)(2,1)S(1)} %copy-done.2, bf16[128,512]{1,0:T(8,128)(2,1)S(1)} %copy-done.4, bf16[128,512]{1,0:T(8,128)(2,1)S(1)} %copy-done.6, ...), custom_call_target="tpu_custom_call" | custom-call | flops 500000000 | bytes 1048576 | tf_op jit(solution)/shard_map/pallas_call | solution.py:135
  62.3 1.0 %shard_map.96 = bf16[128,2048]{1,0:T(8,128)(2,1)} custom-call(bf16[128,1024]{1,0:T(8,128)(2,1)S(1)} %get-tuple-element.30.a_ref, bf16[128,1024]{1,0:T(8,128)(2,1)S(1)} %collective-permute-done.10.b_ref, bf16[128,1024]{1,0:T(8,128)(2,1)S(1)} %collective-permute-done.11.c_ref, bf16[128,1024]{1,0:T(8,128)(2,1)S(1)} %collective-permute-done.12.d_ref), custom_call_target="tpu_custom_call" | custom-call | flops 500000000 | bytes 1048576 | tf_op jit(solution)/shard_map/pallas_call | solution.py:135
  63.2 5.1 %collective-permute-done.17.far_ref = bf16[512,128]{1,0:T(8,128)(2,1)S(1)} collective-permute-done((bf16[512,128]{1,0:T(8,128)(2,1)S(1)}, bf16[512,128]{1,0:T(8,128)(2,1)S(1)}, u32[]{:S(2)}, u32[]{:S(2)}) %collective-permute-start.17) | collective-permute-done | bytes 131104 | tf_op jit(solution)/shard_map/ppermute | solution.py:176
  68.3 1.0 %shard_map.102 = (bf16[128,512]{1,0:T(8,128)(2,1)}, bf16[128,512]{1,0:T(8,128)(2,1)}) custom-call(f32[128,512]{1,0:T(8,128)S(1)} %get-tuple-element.40.gk_ref, f32[128,512]{1,0:T(8,128)S(1)} %get-tuple-element.41.gv_ref, bf16[128,512]{1,0:T(8,128)(2,1)S(1)} %copy-done.4, bf16[128,512]{1,0:T(8,128)(2,1)S(1)} %copy-done.6, ...), custom_call_target="tpu_custom_call" | custom-call | flops 500000000 | bytes 1048576 | tf_op jit(solution)/shard_map/pallas_call | solution.py:135
  69.3 0.9 %convert_add_fusion = f32[256,512]{1,0:T(8,128)} fusion(f32[256,512]{1,0:T(8,128)S(1)} %get-tuple-element.47, bf16[256,512]{1,0:T(8,128)(2,1)S(1)} %collective-permute-done.24), kind=kLoop, calls=%fused_computation | loop fusion | flops 262144 | bytes 1310720 | tf_op jit(solution)/shard_map/add | solution.py:417
  (53 shorter events, 6.6 us)
Async XLA Ops:
  0.6 5.1 %copy-start = (bf16[256,512]{1,0:T(8,128)(2,1)S(1)}, bf16[256,512]{1,0:T(8,128)(2,1)}, u32[]{:S(2)}) copy-start(bf16[256,512]{1,0:T(8,128)(2,1)} %param.8) | copy-start | bytes 786436
  0.6 10.7 %copy-start.1 = (bf16[128,2048]{1,0:T(8,128)(2,1)S(1)}, bf16[128,2048]{1,0:T(8,128)(2,1)}, u32[]{:S(2)}) copy-start(bf16[128,2048]{1,0:T(8,128)(2,1)} %gy_ref.6) | copy-start | bytes 1572868
  0.7 1.0 %copy-start.3 = (bf16[128,512]{1,0:T(8,128)(2,1)S(1)}, bf16[128,512]{1,0:T(8,128)(2,1)}, u32[]{:S(2)}) copy-start(bf16[128,512]{1,0:T(8,128)(2,1)} %k_ref.7) | copy-start | bytes 393220
  1.6 0.9 %copy-start.5 = (bf16[128,512]{1,0:T(8,128)(2,1)S(1)}, bf16[128,512]{1,0:T(8,128)(2,1)}, u32[]{:S(2)}) copy-start(bf16[128,512]{1,0:T(8,128)(2,1)} %v_ref.7) | copy-start | bytes 393220
  2.8 10.3 %collective-permute-start = (bf16[512,128]{1,0:T(8,128)(2,1)S(1)}, bf16[512,128]{1,0:T(8,128)(2,1)S(1)}, u32[]{:S(2)}, u32[]{:S(2)}) collective-permute-start(bf16[512,128]{1,0:T(8,128)(2,1)S(1)} %shard_map.93), channel_id=1, source_target_pairs={{0,2},{2,0},{4,6},{6,4},{8,10},{10,8},{12,14},{14,12},{1,3},{3,1},... | collective-permute-start | bytes 393224 | tf_op jit(solution)/shard_map/ppermute | solution.py:176
  5.8 15.8 %collective-permute-start.4 = (bf16[128,512]{1,0:T(8,128)(2,1)S(1)}, bf16[128,512]{1,0:T(8,128)(2,1)S(1)}, u32[]{:S(2)}, u32[]{:S(2)}) collective-permute-start(bf16[128,512]{1,0:T(8,128)(2,1)S(1)} %constant_dynamic-slice_fusion.refs_0_), channel_id=1, source_target_pairs={{0,4},{2,6},{4,8},{6,10},{8,12},{10,14},{12,0},{14,2},{1,5},{3,7},... | collective-permute-start | bytes 393224 | tf_op jit(solution)/shard_map/ppermute | solution.py:176
  7.4 11.0 %collective-permute-start.5 = (bf16[128,512]{1,0:T(8,128)(2,1)S(1)}, bf16[128,512]{1,0:T(8,128)(2,1)S(1)}, u32[]{:S(2)}, u32[]{:S(2)}) collective-permute-start(bf16[128,512]{1,0:T(8,128)(2,1)S(1)} %constant_dynamic-slice_fusion.refs_0_), channel_id=1, source_target_pairs={{0,8},{2,10},{4,12},{6,14},{8,0},{10,2},{12,4},{14,6},{1,9},{3,11}... | collective-permute-start | bytes 393224 | tf_op jit(solution)/shard_map/ppermute | solution.py:176
  10.0 9.4 %collective-permute-start.6 = (bf16[128,512]{1,0:T(8,128)(2,1)S(1)}, bf16[128,512]{1,0:T(8,128)(2,1)S(1)}, u32[]{:S(2)}, u32[]{:S(2)}) collective-permute-start(bf16[128,512]{1,0:T(8,128)(2,1)S(1)} %constant_dynamic-slice_fusion.refs_0_), channel_id=1, source_target_pairs={{0,12},{2,14},{4,0},{6,2},{8,4},{10,6},{12,8},{14,10},{1,13},{3,15... | collective-permute-start | bytes 393224 | tf_op jit(solution)/shard_map/ppermute | solution.py:176
  11.4 12.0 %collective-permute-start.13 = (bf16[128,1024]{1,0:T(8,128)(2,1)S(1)}, bf16[128,1024]{1,0:T(8,128)(2,1)S(1)}, u32[]{:S(2)}, u32[]{:S(2)}) collective-permute-start(bf16[128,1024]{1,0:T(8,128)(2,1)S(1)} %get-tuple-element.33), channel_id=1, source_target_pairs={{0,16},{16,0},{1,17},{17,1},{2,18},{18,2},{3,19},{19,3},{4,20},{20... | collective-permute-start | bytes 786440 | tf_op jit(solution)/shard_map/ppermute | solution.py:185
  13.1 8.9 %collective-permute-start.1 = (bf16[512,128]{1,0:T(8,128)(2,1)S(1)}, bf16[512,128]{1,0:T(8,128)(2,1)S(1)}, u32[]{:S(2)}, u32[]{:S(2)}) collective-permute-start(bf16[512,128]{1,0:T(8,128)(2,1)S(1)} %add_convert_fusion.3), channel_id=1, source_target_pairs={{0,4},{2,6},{4,0},{6,2},{8,12},{10,14},{12,8},{14,10},{1,5},{3,7},... | collective-permute-start | bytes 393224 | tf_op jit(solution)/shard_map/ppermute | solution.py:176
  19.5 12.8 %collective-permute-start.9 = (bf16[256,512]{1,0:T(8,128)(2,1)S(1)}, bf16[256,512]{1,0:T(8,128)(2,1)S(1)}, u32[]{:S(2)}, u32[]{:S(2)}) collective-permute-start(bf16[256,512]{1,0:T(8,128)(2,1)S(1)} %pad_maximum_fusion), channel_id=1, source_target_pairs={{0,2},{2,0},{4,6},{6,4},{8,10},{10,8},{12,14},{14,12},{1,3},{3,1},... | collective-permute-start | bytes 786440 | tf_op jit(solution)/shard_map/ppermute | solution.py:176
  19.9 10.9 %collective-permute-start.7 = (bf16[128,512]{1,0:T(8,128)(2,1)S(1)}, bf16[128,512]{1,0:T(8,128)(2,1)S(1)}, u32[]{:S(2)}, u32[]{:S(2)}) collective-permute-start(bf16[128,512]{1,0:T(8,128)(2,1)S(1)} %constant_dynamic-slice_fusion.refs_0_), channel_id=1, source_target_pairs={{0,2},{2,0},{4,6},{6,4},{8,10},{10,8},{12,14},{14,12},{1,3},{3,1},... | collective-permute-start | bytes 393224 | tf_op jit(solution)/shard_map/ppermute | solution.py:176
  21.6 10.7 %collective-permute-start.8 = (bf16[128,512]{1,0:T(8,128)(2,1)S(1)}, bf16[128,512]{1,0:T(8,128)(2,1)S(1)}, u32[]{:S(2)}, u32[]{:S(2)}) collective-permute-start(bf16[128,512]{1,0:T(8,128)(2,1)S(1)} %collective-permute-done.4.refs_1_), channel_id=1, source_target_pairs={{0,2},{2,0},{4,6},{6,4},{8,10},{10,8},{12,14},{14,12},{1,3},{3,1},... | collective-permute-start | bytes 393224 | tf_op jit(solution)/shard_map/ppermute | solution.py:176
  22.0 14.6 %copy-start.2 = (bf16[128,512]{1,0:T(8,128)(2,1)S(1)}, bf16[128,512]{1,0:T(8,128)(2,1)}, u32[]{:S(2)}) copy-start(bf16[128,512]{1,0:T(8,128)(2,1)} %q_ref.7) | copy-start | bytes 393220
  22.0 14.6 %copy-start.4 = (bf16[128,512]{1,0:T(8,128)(2,1)S(1)}, bf16[128,512]{1,0:T(8,128)(2,1)}, u32[]{:S(2)}) copy-start(bf16[128,512]{1,0:T(8,128)(2,1)} %k_ref.7) | copy-start | bytes 393220
  22.0 14.6 %copy-start.6 = (bf16[128,512]{1,0:T(8,128)(2,1)S(1)}, bf16[128,512]{1,0:T(8,128)(2,1)}, u32[]{:S(2)}) copy-start(bf16[128,512]{1,0:T(8,128)(2,1)} %v_ref.7) | copy-start | bytes 393220
  22.0 15.3 %collective-permute-start.2 = (bf16[512,128]{1,0:T(8,128)(2,1)S(1)}, bf16[512,128]{1,0:T(8,128)(2,1)S(1)}, u32[]{:S(2)}, u32[]{:S(2)}) collective-permute-start(bf16[512,128]{1,0:T(8,128)(2,1)S(1)} %add_convert_fusion.2), channel_id=1, source_target_pairs={{0,8},{2,10},{4,12},{6,14},{8,0},{10,2},{12,4},{14,6},{1,9},{3,11}... | collective-permute-start | bytes 393224 | tf_op jit(solution)/shard_map/ppermute | solution.py:176
  32.7 13.7 %collective-permute-start.14 = (f32[128,512]{1,0:T(8,128)S(1)}, f32[128,512]{1,0:T(8,128)S(1)}, u32[]{:S(2)}, u32[]{:S(2)}) collective-permute-start(f32[128,512]{1,0:T(8,128)S(1)} %shard_map.98), channel_id=1, source_target_pairs={{0,16},{16,0},{1,17},{17,1},{2,18},{18,2},{3,19},{19,3},{4,20},{20... | collective-permute-start | bytes 786440 | tf_op jit(solution)/shard_map/ppermute | solution.py:185
  34.3 12.0 %collective-permute-start.18 = (bf16[256,256]{1,0:T(8,128)(2,1)S(1)}, bf16[256,256]{1,0:T(8,128)(2,1)S(1)}, u32[]{:S(2)}, u32[]{:S(2)}) collective-permute-start(bf16[256,256]{1,0:T(8,128)(2,1)S(1)} %get-tuple-element.46), channel_id=1, source_target_pairs={{0,8},{2,10},{4,12},{6,14},{8,0},{10,2},{12,4},{14,6},{1,9},{3,11}... | collective-permute-start | bytes 393224 | tf_op jit(solution)/shard_map/ppermute | solution.py:176
  37.7 11.7 %collective-permute-start.3 = (bf16[128,512]{1,0:T(8,128)(2,1)S(1)}, bf16[128,512]{1,0:T(8,128)(2,1)S(1)}, u32[]{:S(2)}, u32[]{:S(2)}) collective-permute-start(bf16[128,512]{1,0:T(8,128)(2,1)S(1)} %get-tuple-element.28.n_ref), channel_id=1, source_target_pairs={{0,16},{16,0},{1,17},{17,1},{2,18},{18,2},{3,19},{19,3},{4,20},{20... | collective-permute-start | bytes 393224 | tf_op jit(solution)/shard_map/ppermute | solution.py:185
  38.3 12.2 %collective-permute-start.21 = (bf16[128,512]{1,0:T(8,128)(2,1)S(1)}, bf16[128,512]{1,0:T(8,128)(2,1)S(1)}, u32[]{:S(2)}, u32[]{:S(2)}) collective-permute-start(bf16[128,512]{1,0:T(8,128)(2,1)S(1)} %get-tuple-element.28.n_ref), channel_id=1, source_target_pairs={{0,8},{2,10},{4,12},{6,14},{8,0},{10,2},{12,4},{14,6},{1,9},{3,11}... | collective-permute-start | bytes 393224 | tf_op jit(solution)/shard_map/ppermute | solution.py:176
  46.3 6.5 %collective-permute-start.19 = (bf16[256,256]{1,0:T(8,128)(2,1)S(1)}, bf16[256,256]{1,0:T(8,128)(2,1)S(1)}, u32[]{:S(2)}, u32[]{:S(2)}) collective-permute-start(bf16[256,256]{1,0:T(8,128)(2,1)S(1)} %shard_map.103), channel_id=1, source_target_pairs={{0,4},{2,6},{4,0},{6,2},{8,12},{10,14},{12,8},{14,10},{1,5},{3,7},... | collective-permute-start | bytes 393224 | tf_op jit(solution)/shard_map/ppermute | solution.py:176
  46.8 6.1 %collective-permute-start.15 = (bf16[512,128]{1,0:T(8,128)(2,1)S(1)}, bf16[512,128]{1,0:T(8,128)(2,1)S(1)}, u32[]{:S(2)}, u32[]{:S(2)}) collective-permute-start(bf16[512,128]{1,0:T(8,128)(2,1)S(1)} %get-tuple-element.42), channel_id=1, source_target_pairs={{0,2},{2,0},{4,6},{6,4},{8,10},{10,8},{12,14},{14,12},{1,3},{3,1},... | collective-permute-start | bytes 393224 | tf_op jit(solution)/shard_map/ppermute | solution.py:176
  47.4 8.2 %collective-permute-start.22 = (bf16[128,512]{1,0:T(8,128)(2,1)S(1)}, bf16[128,512]{1,0:T(8,128)(2,1)S(1)}, u32[]{:S(2)}, u32[]{:S(2)}) collective-permute-start(bf16[128,512]{1,0:T(8,128)(2,1)S(1)} %get-tuple-element.28.n_ref), channel_id=1, source_target_pairs={{0,4},{2,6},{4,0},{6,2},{8,12},{10,14},{12,8},{14,10},{1,5},{3,7},... | collective-permute-start | bytes 393224 | tf_op jit(solution)/shard_map/ppermute | solution.py:176
  50.1 6.4 %collective-permute-start.11 = (bf16[128,1024]{1,0:T(8,128)(2,1)S(1)}, bf16[128,1024]{1,0:T(8,128)(2,1)S(1)}, u32[]{:S(2)}, u32[]{:S(2)}) collective-permute-start(bf16[128,1024]{1,0:T(8,128)(2,1)S(1)} %get-tuple-element.31), channel_id=1, source_target_pairs={{0,16},{16,0},{1,17},{17,1},{2,18},{18,2},{3,19},{19,3},{4,20},{20... | collective-permute-start | bytes 786440 | tf_op jit(solution)/shard_map/ppermute | solution.py:185
  50.5 7.3 %collective-permute-start.23 = (bf16[128,512]{1,0:T(8,128)(2,1)S(1)}, bf16[128,512]{1,0:T(8,128)(2,1)S(1)}, u32[]{:S(2)}, u32[]{:S(2)}) collective-permute-start(bf16[128,512]{1,0:T(8,128)(2,1)S(1)} %collective-permute-done.21.refs_0_), channel_id=1, source_target_pairs={{0,4},{2,6},{4,0},{6,2},{8,12},{10,14},{12,8},{14,10},{1,5},{3,7},... | collective-permute-start | bytes 393224 | tf_op jit(solution)/shard_map/ppermute | solution.py:176
  52.8 5.0 %collective-permute-start.20 = (bf16[384,256]{1,0:T(8,128)(2,1)S(1)}, bf16[384,256]{1,0:T(8,128)(2,1)S(1)}, u32[]{:S(2)}, u32[]{:S(2)}) collective-permute-start(bf16[384,256]{1,0:T(8,128)(2,1)S(1)} %shard_map.104.c_ref), channel_id=1, source_target_pairs={{0,1},{1,0},{2,3},{3,2},{4,5},{5,4},{6,7},{7,6},{8,9},{9,8},{10,11... | collective-permute-start | bytes 589832 | tf_op jit(solution)/shard_map/ppermute | solution.py:188
  52.9 6.8 %collective-permute-start.16 = (bf16[512,128]{1,0:T(8,128)(2,1)S(1)}, bf16[512,128]{1,0:T(8,128)(2,1)S(1)}, u32[]{:S(2)}, u32[]{:S(2)}) collective-permute-start(bf16[512,128]{1,0:T(8,128)(2,1)S(1)} %add_convert_fusion.1), channel_id=1, source_target_pairs={{0,4},{2,6},{4,0},{6,2},{8,12},{10,14},{12,8},{14,10},{1,5},{3,7},... | collective-permute-start | bytes 393224 | tf_op jit(solution)/shard_map/ppermute | solution.py:176
  55.6 6.7 %collective-permute-start.10 = (bf16[128,1024]{1,0:T(8,128)(2,1)S(1)}, bf16[128,1024]{1,0:T(8,128)(2,1)S(1)}, u32[]{:S(2)}, u32[]{:S(2)}) collective-permute-start(bf16[128,1024]{1,0:T(8,128)(2,1)S(1)} %get-tuple-element.30.a_ref), channel_id=1, source_target_pairs={{0,1},{1,0},{2,3},{3,2},{4,5},{5,4},{6,7},{7,6},{8,9},{9,8},{10,11... | collective-permute-start | bytes 786440 | tf_op jit(solution)/shard_map/ppermute | solution.py:188
  56.6 5.7 %collective-permute-start.12 = (bf16[128,1024]{1,0:T(8,128)(2,1)S(1)}, bf16[128,1024]{1,0:T(8,128)(2,1)S(1)}, u32[]{:S(2)}, u32[]{:S(2)}) collective-permute-start(bf16[128,1024]{1,0:T(8,128)(2,1)S(1)} %collective-permute-done.11.c_ref), channel_id=1, source_target_pairs={{0,1},{1,0},{2,3},{3,2},{4,5},{5,4},{6,7},{7,6},{8,9},{9,8},{10,11... | collective-permute-start | bytes 786440 | tf_op jit(solution)/shard_map/ppermute | solution.py:188
  58.5 10.7 %collective-permute-start.24 = (bf16[256,512]{1,0:T(8,128)(2,1)S(1)}, bf16[256,512]{1,0:T(8,128)(2,1)S(1)}, u32[]{:S(2)}, u32[]{:S(2)}) collective-permute-start(bf16[256,512]{1,0:T(8,128)(2,1)S(1)} %get-tuple-element.48), channel_id=1, source_target_pairs={{0,2},{2,0},{4,6},{6,4},{8,10},{10,8},{12,14},{14,12},{1,3},{3,1},... | collective-permute-start | bytes 786440 | tf_op jit(solution)/shard_map/ppermute | solution.py:176
  59.8 8.5 %collective-permute-start.17 = (bf16[512,128]{1,0:T(8,128)(2,1)S(1)}, bf16[512,128]{1,0:T(8,128)(2,1)S(1)}, u32[]{:S(2)}, u32[]{:S(2)}) collective-permute-start(bf16[512,128]{1,0:T(8,128)(2,1)S(1)} %add_convert_fusion), channel_id=1, source_target_pairs={{0,8},{2,10},{4,12},{6,14},{8,0},{10,2},{12,4},{14,6},{1,9},{3,11}... | collective-permute-start | bytes 393224 | tf_op jit(solution)/shard_map/ppermute | solution.py:176

commit v4 on v3

--- a/solution.py
+++ b/solution.py
@@ -131,7 +131,7 @@
     return lax.dot_general(a, b, dims, preferred_element_type=F32)
 
 
-def call(body, shapes, *args, flops=500000000, moved=2**20):
+def call(body, shapes, *args, flops=1000000000, moved=2**20):
     return pl.pallas_call(
         body,
         out_shape=[jax.ShapeDtypeStruct(s, d) for s, d in shapes],
@@ -170,7 +170,7 @@
     line = seq // 2
     turns = range(1, line)
     outs = grad_y.shape[1]
-    state = (heads * DH, DH)
+    state = (DH, heads * DH)
 
     def permute(array, pairs):
         return lax.ppermute(array, "seq", pairs)
@@ -190,35 +190,41 @@
     def side_by_side(*arrays):
         return jnp.concatenate(arrays, axis=0)
 
-    def after(array, *others):
-        return lax.optimization_barrier((array, *others))[0]
+    def tie(*arrays):
+        return lax.optimization_barrier(arrays)
 
     g = lax.axis_index("groups")
     my_weight = lax.dynamic_slice_in_dim(out_weight, g * half, half, 0)
     z_weight = [rotate(my_weight, k) for k in turns]
 
-    def own_state(k_ref, v_ref, s_ref):
-        for i in range(heads):
-            s_ref[head_of(i), :] = dot(
+    def own_state(k_ref, v_ref, w_ref, out_ref):
+        out_ref[:half, :] = w_ref[...]
+        for i in range(heads):
+            out_ref[half:, head_of(i)] = dot(
                 k_ref[:, head_of(i)], v_ref[:, head_of(i)], ROWS_T
             ).astype(BF16)
 
-    (states,) = call(own_state, [(state, BF16)], keys, values)
-    x_weight_own = swap(my_weight, 1)
-
-    def pack(gy_ref, ys_ref, gz_ref):
+    (weight_states,) = call(
+        own_state, [((half + DH, feats), BF16)], keys, values, my_weight
+    )
+    x_weight_states = swap(weight_states, 1)
+    states, x_states = weight_states[half:], x_weight_states[half:]
+
+    def columns(gy_ref, z, h):
+        return gy_ref[:, lanes(z * 2 + h, wrows)]
+
+    def pack(gy_ref, ys_ref, near_ref):
         g, z, x, h = place()
         for i in range(seq):
             ys_ref[:, i * half : (i + 1) * half] = gy_ref[:, lanes(2 * i + 1 - g, half)]
-        far = 2 - z // 2 * 2
-        for b in range(2):
-            gz_ref[b * rows : (b + 1) * rows, :] = gy_ref[
-                :, lanes((far + b) * 2 + h, wrows)
-            ]
-
-    y_send, far_send = call(
+        near = z + 1 - 2 * lax.rem(z, 2)
+        near_ref[:rows, :] = columns(gy_ref, near, h)
+        near_ref[rows:, :] = columns(gy_ref, lax.rem(near + 2, line), h)
+
+    y_send, near_send = call(
         pack, [((rows, seq * half), BF16), ((2 * rows, wrows), BF16)], grad_y
     )
+    near_cols = swap(near_send, 2)
     y_cols = swap_y(y_send)
 
     def local(q_ref, k_ref, v_ref, sc_ref, att_ref):
@@ -236,17 +242,29 @@
     def add(a, b):
         return (a.astype(F32) + b.astype(F32)).astype(BF16)
 
-    x_states = swap(states, 1)
+    x_weight_far = swap(side_by_side(*z_weight[1:]), 1)
+    x_states, *z_weight[1:] = tie(x_states, *z_weight[1:])
     pair_states = add(states, x_states)
     near_states = swap(pair_states, 2)
+    pair_states, z_weight[0] = tie(pair_states, z_weight[0])
     quad_states = add(pair_states, near_states)
     got_states = x_states, near_states, swap(quad_states, 4)
 
-    x_weight_far = swap(side_by_side(*z_weight[1:]), 1)
-    x_weight_near = swap(after(z_weight[0], pair_states), 1)
+    x_weight_near = swap(z_weight[0], 1)
+    near_cols, z_weight[0] = tie(near_cols, z_weight[0])
+
+    def relay(gy_ref, near_ref, far_ref):
+        g, z, x, h = place()
+        far_ref[:rows, :] = columns(gy_ref, lax.rem(z + 2, line), h)
+        far_ref[rows:, :] = near_ref[rows:, :]
+
+    (far_send,) = call(relay, [((2 * rows, wrows), BF16)], grad_y, near_cols)
+
+    far_cols = swap(far_send, 4)
 
     def weight_blocks(refs):
         own, *others, x_own, x_near, x_far = refs
+        x_own = x_own.at[:half, :]
         g, z, x, h = place()
         blocks = []
         for k in range(line):
@@ -259,7 +277,7 @@
             blocks.append((zk * 2 + 1 - x, block))
         return blocks
 
-    weight_args = (my_weight, *z_weight, x_weight_own, x_weight_near, x_weight_far)
+    weight_args = (my_weight, *z_weight, x_weight_states, x_weight_near, x_weight_far)
 
     def back_other(yc_ref, *refs):
         *w_refs, out_ref = refs
@@ -277,32 +295,14 @@
         out_ref[...] = total
 
     (grad_send,) = call(
-        back_other, [((rows, feats), F32)], after(y_cols, quad_states), *weight_args
+        back_other, [((rows, feats), F32)], y_cols, *weight_args
     )
     grad_other = swap_y(grad_send)
     (grad_own,) = call(
-        back_own, [((rows, feats), F32)], after(grad_y, grad_send), *weight_args
-    )
-
-    far_cols = swap(after(far_send, grad_send), 4)
-
-    def relay(gy_ref, far_ref, near_ref):
-        g, z, x, h = place()
-        other = lax.rem(z + 1, 2)
-        near = z + 1 - 2 * lax.rem(z, 2)
-        near_ref[:rows, :] = gy_ref[:, lanes(near * 2 + h, wrows)]
-        near_ref[rows:, :] = far_ref[pl.ds(pl.multiple_of(other * rows, rows), rows), :]
-
-    (near_send,) = call(relay, [((2 * rows, wrows), BF16)], grad_y, far_cols)
-    near_cols = swap(near_send, 2)
-
-    def collect(far_ref, near_ref, out_ref):
-        g, z, x, h = place()
-        mine = lax.rem(z, 2)
-        out_ref[:rows, :] = far_ref[pl.ds(pl.multiple_of(mine * rows, rows), rows), :]
-        out_ref[rows:, :] = near_ref[...]
-
-    (my_cols,) = call(collect, [((3 * rows, wrows), BF16)], far_cols, near_cols)
+        back_own, [((rows, feats), F32)], grad_y, *weight_args
+    )
+
+    my_cols = side_by_side(near_cols[:rows], far_cols)
     core_cols = swap_core(my_cols)
 
     def forward(q_ref, local_ref, x_ref, near_ref, far_ref, att_ref, normed_ref, prefix_ref):
@@ -314,7 +314,7 @@
         prefix_ref[...] = prefix
         for i in range(heads):
             att = local_ref[:, head_of(i)] + dot(
-                q_ref[:, head_of(i)], prefix[head_of(i), :], PLAIN
+                q_ref[:, head_of(i)], prefix[:, head_of(i)], PLAIN
             )
             att_ref[:, head_of(i)] = att
             inv = lax.rsqrt(jnp.mean(att * att, axis=-1, keepdims=True) + epsilon)
@@ -339,7 +339,7 @@
             along = jnp.mean(grad * exact, axis=-1, keepdims=True)
             go = (inv * (grad - exact * along)).astype(BF16)
             go_ref[:, head_of(i)] = go
-            adj_ref[head_of(i), :] = dot(q_ref[:, head_of(i)], go, ROWS_T).astype(BF16)
+            adj_ref[:, head_of(i)] = dot(q_ref[:, head_of(i)], go, ROWS_T).astype(BF16)
 
     grad_out, adjoint = call(
         turn_back, [((rows, feats), BF16), (state, BF16)],
@@ -358,7 +358,7 @@
             go = go_ref[:, at]
             gs = dot(go, v_ref[:, at], LAST_T)
             gs = jnp.where(mask, gs, 0.0).astype(BF16)
-            gq = dot(gs, k_ref[:, at], PLAIN) + dot(go, pre_ref[at, :], LAST_T)
+            gq = dot(gs, k_ref[:, at], PLAIN) + dot(go, pre_ref[:, at], LAST_T)
             gq_ref[:, at] = gq.astype(BF16)
             gk_ref[:, at] = dot(gs, q_ref[:, at], ROWS_T)
             gv_ref[:, at] = dot(sc_ref[:, at], go, ROWS_T)
@@ -385,8 +385,8 @@
     def weight_grad(gy_ref, c_ref, o_ref, n_ref, *refs):
         *n_refs, keep_ref, send_ref = refs
         g, z, x, h = place()
-        same = dot(gy_ref[:, lanes(z * 2 + h, wrows)], n_ref[...], ROWS_T)
-        other = dot(gy_ref[:, lanes(z * 2 + 1 - h, wrows)], n_ref[...], ROWS_T)
+        same = dot(columns(gy_ref, z, h), n_ref[...], ROWS_T)
+        other = dot(columns(gy_ref, z, 1 - h), n_ref[...], ROWS_T)
         for i, there_ref in enumerate(n_refs):
             at = slice(i * rows, (i + 1) * rows)
             same += dot(c_ref[at, :], there_ref[...], ROWS_T)
@@ -396,7 +396,7 @@
 
     gw_keep, gw_send = call(
         weight_grad, [((wrows, feats), F32), ((wrows, feats), BF16)],
-        grad_y, my_cols, core_cols, normed, far_normed, near_normed, last_normed,
+        grad_y, my_cols, core_cols, normed, near_normed, far_normed, last_normed,
     )
     gw_other = swap(gw_send, 1)
 
@@ -425,10 +425,10 @@
         for i in range(heads):
             at = head_of(i)
             ok_ref[:, at] = (
-                gk_ref[:, at] + dot(v_ref[:, at], suffix[at, :], LAST_T)
+                gk_ref[:, at] + dot(v_ref[:, at], suffix[:, at], LAST_T)
             ).astype(BF16)
             ov_ref[:, at] = (
-                gv_ref[:, at] + dot(k_ref[:, at], suffix[at, :], PLAIN)
+                gv_ref[:, at] + dot(k_ref[:, at], suffix[:, at], PLAIN)
             ).astype(BF16)
 
     grad_keys, grad_values = call(

time: 70.3 us -> 66.6 us (0.947)
  waiting for transfers between devices: 33.2 us -> 27 us
  starting transfers between devices: 25.7 us -> 28.3 us
    ppermute x18 -> x17, waiting for transfers between devices: 32.2 us -> 23.7 us  [permute(): return lax.ppermute(array, 'seq', pairs)]
    ppermute x4, waiting for transfers between devices: 1 us -> 3.33 us  [swap_y(): return lax.ppermute(array, 'groups', [(0, 1), (1, 0)])]
    ppermute x18 -> x17, starting transfers between devices: 21.5 us -> 23.3 us  [permute(): return lax.ppermute(array, 'seq', pairs)]
    pallas_call x14 -> x13, Pallas kernels: 7.38 us -> 7.38 us  [call(): pl.pallas_call(body, out_shape=[jax.ShapeDtypeStruct(s, d) for s, d in sh...]
    unnamed x14 -> x10, local copies, waits for them, and re-layouts: 1.91 us -> 1.91 us
  transfers between devices with their start and end apart: 25 -> 24, of which waited for: 11 -> 10; matrix products, arithmetic and copies ran while one was open for 0% -> 2% of each run, Pallas kernels for 10% -> 9%
where the time goes in v4:
time: 66.6 us; the launch traced here: 66.5 us
  starting transfers between devices  28.3 us (42%)
  waiting for transfers between devices  27 us (41%)
  Pallas kernels  7.38 us (11%)
  local copies, waits for them, and re-layouts  1.93 us (3%)
  other arithmetic  1.03 us (2%)
  between operations  0.81 us (1%)
    ppermute x17, waiting for transfers between devices, permute(): return lax.ppermute(array, 'seq', pairs)  23.7 us
    ppermute x17, starting transfers between devices, permute(): return lax.ppermute(array, 'seq', pairs)  23.3 us
    pallas_call x13, Pallas kernels, call(): pl.pallas_call(body, out_shape=[jax.ShapeDtypeStruct(s, d) for s, d in sh...  7.38 us
    ppermute x4, starting transfers between devices, swap_y(): return lax.ppermute(array, 'groups', [(0, 1), (1, 0)])  4.43 us
    ppermute x4, waiting for transfers between devices, swap_y(): return lax.ppermute(array, 'groups', [(0, 1), (1, 0)])  3.33 us
    unnamed x10, local copies, waits for them, and re-layouts  1.91 us
  transfers between devices with their start and end apart: 24, of which 10 were waited for; matrix products, arithmetic and copies ran while one was open for 2% of the time, Pallas kernels for 9%

profile of v4, /device:TPU:0, one launch (start us, length us, event | category | flops | bytes accessed | tf_op | source)
XLA Modules:
  0.0 66.5 jit_solution(1533181858166822480)
XLA Ops:
  0.7 0.9 %copy-done = bf16[256,512]{1,0:T(8,128)(2,1)S(1)} copy-done((bf16[256,512]{1,0:T(8,128)(2,1)S(1)}, bf16[256,512]{1,0:T(8,128)(2,1)}, u32[]{:S(2)}) %copy-start) | copy-done | bytes 262168
  1.6 0.9 %copy-done.3 = bf16[128,512]{1,0:T(8,128)(2,1)S(1)} copy-done((bf16[128,512]{1,0:T(8,128)(2,1)S(1)}, bf16[128,512]{1,0:T(8,128)(2,1)}, u32[]{:S(2)}) %copy-start.3) | copy-done | bytes 131096
  2.8 3.0 %collective-permute-start = (bf16[256,512]{1,0:T(8,128)(2,1)S(1)}, bf16[256,512]{1,0:T(8,128)(2,1)S(1)}, u32[]{:S(2)}, u32[]{:S(2)}) collective-permute-start(bf16[256,512]{1,0:T(8,128)(2,1)S(1)} %shard_map.93), channel_id=1, source_target_pairs={{0,2},{2,0},{4,6},{6,4},{8,10},{10,8},{12,14},{14,12},{1,3},{3,1},... | collective-permute-start | bytes 786440 | tf_op jit(solution)/shard_map/ppermute | solution.py:176
  5.8 2.6 %collective-permute-start.1 = (bf16[128,512]{1,0:T(8,128)(2,1)S(1)}, bf16[128,512]{1,0:T(8,128)(2,1)S(1)}, u32[]{:S(2)}, u32[]{:S(2)}) collective-permute-start(bf16[128,512]{1,0:T(8,128)(2,1)S(1)} %constant_dynamic-slice_fusion.w_ref.refs_0_), channel_id=1, source_target_pairs={{0,8},{2,10},{4,12},{6,14},{8,0},{10,2},{12,4},{14,6},{1,9},{3,11}... | collective-permute-start | bytes 393224 | tf_op jit(solution)/shard_map/ppermute | solution.py:176
  8.4 1.3 %collective-permute-start.2 = (bf16[128,512]{1,0:T(8,128)(2,1)S(1)}, bf16[128,512]{1,0:T(8,128)(2,1)S(1)}, u32[]{:S(2)}, u32[]{:S(2)}) collective-permute-start(bf16[128,512]{1,0:T(8,128)(2,1)S(1)} %constant_dynamic-slice_fusion.w_ref.refs_0_), channel_id=1, source_target_pairs={{0,12},{2,14},{4,0},{6,2},{8,4},{10,6},{12,8},{14,10},{1,13},{3,15... | collective-permute-start | bytes 393224 | tf_op jit(solution)/shard_map/ppermute | solution.py:176
  10.5 1.6 %collective-permute-start.7 = (bf16[256,256]{1,0:T(8,128)(2,1)S(1)}, bf16[256,256]{1,0:T(8,128)(2,1)S(1)}, u32[]{:S(2)}, u32[]{:S(2)}) collective-permute-start(bf16[256,256]{1,0:T(8,128)(2,1)S(1)} %get-tuple-element.34), channel_id=1, source_target_pairs={{0,4},{2,6},{4,0},{6,2},{8,12},{10,14},{12,8},{14,10},{1,5},{3,7},... | collective-permute-start | bytes 393224 | tf_op jit(solution)/shard_map/ppermute | solution.py:176
  12.1 1.7 %collective-permute-start.13 = (bf16[128,1024]{1,0:T(8,128)(2,1)S(1)}, bf16[128,1024]{1,0:T(8,128)(2,1)S(1)}, u32[]{:S(2)}, u32[]{:S(2)}) collective-permute-start(bf16[128,1024]{1,0:T(8,128)(2,1)S(1)} %get-tuple-element.42), channel_id=1, source_target_pairs={{0,16},{16,0},{1,17},{17,1},{2,18},{18,2},{3,19},{19,3},{4,20},{20... | collective-permute-start | bytes 786440 | tf_op jit(solution)/shard_map/ppermute | solution.py:185
  13.9 3.2 %collective-permute-done.1.refs_2_ = bf16[128,512]{1,0:T(8,128)(2,1)S(1)} collective-permute-done((bf16[128,512]{1,0:T(8,128)(2,1)S(1)}, bf16[128,512]{1,0:T(8,128)(2,1)S(1)}, u32[]{:S(2)}, u32[]{:S(2)}) %collective-permute-start.1) | collective-permute-done | bytes 131104 | tf_op jit(solution)/shard_map/ppermute | solution.py:176
  17.1 1.1 %collective-permute-done.2.refs_3_ = bf16[128,512]{1,0:T(8,128)(2,1)S(1)} collective-permute-done((bf16[128,512]{1,0:T(8,128)(2,1)S(1)}, bf16[128,512]{1,0:T(8,128)(2,1)S(1)}, u32[]{:S(2)}, u32[]{:S(2)}) %collective-permute-start.2) | collective-permute-done | bytes 131104 | tf_op jit(solution)/shard_map/ppermute | solution.py:176
  18.2 2.5 %collective-permute-start.3 = (bf16[128,512]{1,0:T(8,128)(2,1)S(1)}, bf16[128,512]{1,0:T(8,128)(2,1)S(1)}, u32[]{:S(2)}, u32[]{:S(2)}) collective-permute-start(bf16[128,512]{1,0:T(8,128)(2,1)S(1)} %add_convert_fusion.3), channel_id=1, source_target_pairs={{0,4},{2,6},{4,0},{6,2},{8,12},{10,14},{12,8},{14,10},{1,5},{3,7},... | collective-permute-start | bytes 393224 | tf_op jit(solution)/shard_map/ppermute | solution.py:176
  21.3 0.7 %shard_map.92 = (bf16[128,512]{1,0:T(8,128)(2,1)S(1)}, f32[128,512]{1,0:T(8,128)S(1)}) custom-call(bf16[128,512]{1,0:T(8,128)(2,1)S(1)} %copy-done.2, bf16[128,512]{1,0:T(8,128)(2,1)S(1)} %copy-done.3, bf16[128,512]{1,0:T(8,128)(2,1)S(1)} %copy-done.4), custom_call_target="tpu_custom_call" | custom-call | flops 1000000000 | bytes 1048576 | tf_op jit(solution)/shard_map/pallas_call | solution.py:135
  22.1 1.6 %collective-permute-start.8 = (bf16[128,512]{1,0:T(8,128)(2,1)S(1)}, bf16[128,512]{1,0:T(8,128)(2,1)S(1)}, u32[]{:S(2)}, u32[]{:S(2)}) collective-permute-start(bf16[128,512]{1,0:T(8,128)(2,1)S(1)} %collective-permute-done.4.refs_1_), channel_id=1, source_target_pairs={{0,2},{2,0},{4,6},{6,4},{8,10},{10,8},{12,14},{14,12},{1,3},{3,1},... | collective-permute-start | bytes 393224 | tf_op jit(solution)/shard_map/ppermute | solution.py:176
  23.7 1.5 %collective-permute-start.5 = (bf16[128,512]{1,0:T(8,128)(2,1)S(1)}, bf16[128,512]{1,0:T(8,128)(2,1)S(1)}, u32[]{:S(2)}, u32[]{:S(2)}) collective-permute-start(bf16[128,512]{1,0:T(8,128)(2,1)S(1)} %add_convert_fusion.2), channel_id=1, source_target_pairs={{0,8},{2,10},{4,12},{6,14},{8,0},{10,2},{12,4},{14,6},{1,9},{3,11}... | collective-permute-start | bytes 393224 | tf_op jit(solution)/shard_map/ppermute | solution.py:176
  25.2 4.5 %collective-permute-done.8.refs_5_ = bf16[128,512]{1,0:T(8,128)(2,1)S(1)} collective-permute-done((bf16[128,512]{1,0:T(8,128)(2,1)S(1)}, bf16[128,512]{1,0:T(8,128)(2,1)S(1)}, u32[]{:S(2)}, u32[]{:S(2)}) %collective-permute-start.8) | collective-permute-done | bytes 131104 | tf_op jit(solution)/shard_map/ppermute | solution.py:176
  30.1 1.6 %collective-permute-start.14 = (f32[128,512]{1,0:T(8,128)S(1)}, f32[128,512]{1,0:T(8,128)S(1)}, u32[]{:S(2)}, u32[]{:S(2)}) collective-permute-start(f32[128,512]{1,0:T(8,128)S(1)} %shard_map.99), channel_id=1, source_target_pairs={{0,16},{16,0},{1,17},{17,1},{2,18},{18,2},{3,19},{19,3},{4,20},{20... | collective-permute-start | bytes 786440 | tf_op jit(solution)/shard_map/ppermute | solution.py:185
  31.7 2.7 %collective-permute-start.18 = (bf16[256,256]{1,0:T(8,128)(2,1)S(1)}, bf16[256,256]{1,0:T(8,128)(2,1)S(1)}, u32[]{:S(2)}, u32[]{:S(2)}) collective-permute-start(bf16[256,256]{1,0:T(8,128)(2,1)S(1)} %shard_map.103), channel_id=1, source_target_pairs={{0,8},{2,10},{4,12},{6,14},{8,0},{10,2},{12,4},{14,6},{1,9},{3,11}... | collective-permute-start | bytes 393224 | tf_op jit(solution)/shard_map/ppermute | solution.py:176
  35.5 1.0 %collective-permute-done.14.other_ref = f32[128,512]{1,0:T(8,128)S(1)} collective-permute-done((f32[128,512]{1,0:T(8,128)S(1)}, f32[128,512]{1,0:T(8,128)S(1)}, u32[]{:S(2)}, u32[]{:S(2)}) %collective-permute-start.14) | collective-permute-done | bytes 262176 | tf_op jit(solution)/shard_map/ppermute | solution.py:185
  37.5 5.7 %collective-permute-done.18 = bf16[256,256]{1,0:T(8,128)(2,1)S(1)} collective-permute-done((bf16[256,256]{1,0:T(8,128)(2,1)S(1)}, bf16[256,256]{1,0:T(8,128)(2,1)S(1)}, u32[]{:S(2)}, u32[]{:S(2)}) %collective-permute-start.18) | collective-permute-done | bytes 131104 | tf_op jit(solution)/shard_map/ppermute | solution.py:176
  43.9 0.8 %collective-permute-done.21.refs_1_ = bf16[128,512]{1,0:T(8,128)(2,1)S(1)} collective-permute-done((bf16[128,512]{1,0:T(8,128)(2,1)S(1)}, bf16[128,512]{1,0:T(8,128)(2,1)S(1)}, u32[]{:S(2)}, u32[]{:S(2)}) %collective-permute-start.21) | collective-permute-done | bytes 131104 | tf_op jit(solution)/shard_map/ppermute | solution.py:176
  44.7 1.2 %collective-permute-start.22 = (bf16[128,512]{1,0:T(8,128)(2,1)S(1)}, bf16[128,512]{1,0:T(8,128)(2,1)S(1)}, u32[]{:S(2)}, u32[]{:S(2)}) collective-permute-start(bf16[128,512]{1,0:T(8,128)(2,1)S(1)} %collective-permute-done.21.refs_1_), channel_id=1, source_target_pairs={{0,4},{2,6},{4,0},{6,2},{8,12},{10,14},{12,8},{14,10},{1,5},{3,7},... | collective-permute-start | bytes 393224 | tf_op jit(solution)/shard_map/ppermute | solution.py:176
  45.9 0.9 %collective-permute-start.16 = (bf16[128,512]{1,0:T(8,128)(2,1)S(1)}, bf16[128,512]{1,0:T(8,128)(2,1)S(1)}, u32[]{:S(2)}, u32[]{:S(2)}) collective-permute-start(bf16[128,512]{1,0:T(8,128)(2,1)S(1)} %add_convert_fusion.1), channel_id=1, source_target_pairs={{0,4},{2,6},{4,0},{6,2},{8,12},{10,14},{12,8},{14,10},{1,5},{3,7},... | collective-permute-start | bytes 393224 | tf_op jit(solution)/shard_map/ppermute | solution.py:176
  46.8 2.3 %collective-permute-done.6.yn_ref = bf16[128,512]{1,0:T(8,128)(2,1)S(1)} collective-permute-done((bf16[128,512]{1,0:T(8,128)(2,1)S(1)}, bf16[128,512]{1,0:T(8,128)(2,1)S(1)}, u32[]{:S(2)}, u32[]{:S(2)}) %collective-permute-start.6) | collective-permute-done | bytes 131104 | tf_op jit(solution)/shard_map/ppermute | solution.py:185
  49.1 0.7 %shard_map.96 = (bf16[128,1024]{1,0:T(8,128)(2,1)S(1)}, bf16[128,1024]{1,0:T(8,128)(2,1)S(1)}) custom-call(bf16[128,512]{1,0:T(8,128)(2,1)S(1)} %get-tuple-element.33.n_ref, bf16[128,512]{1,0:T(8,128)(2,1)S(1)} %collective-permute-done.6.yn_ref, bf16[128,512]{1,0:T(8,128)(2,1)S(1)} %constant_dynamic-slice_fusion.w_ref.refs_0_, ...), custom_call_target="tpu_custom_call" | custom-call | flops 1000000000 | bytes 1048576 | tf_op jit(solution)/shard_map/pallas_call | solution.py:135
  50.4 2.0 %collective-permute-done.22.refs_2_ = bf16[128,512]{1,0:T(8,128)(2,1)S(1)} collective-permute-done((bf16[128,512]{1,0:T(8,128)(2,1)S(1)}, bf16[128,512]{1,0:T(8,128)(2,1)S(1)}, u32[]{:S(2)}, u32[]{:S(2)}) %collective-permute-start.22) | collective-permute-done | bytes 131104 | tf_op jit(solution)/shard_map/ppermute | solution.py:176
  52.4 0.7 %shard_map.104 = (f32[256,512]{1,0:T(8,128)S(1)}, bf16[256,512]{1,0:T(8,128)(2,1)S(1)}) custom-call(bf16[128,2048]{1,0:T(8,128)(2,1)S(1)} %copy-done.1, bf16[384,256]{1,0:T(8,128)(2,1)S(1)} %pad_maximum_fusion.1.c_ref, bf16[384,256]{1,0:T(8,128)(2,1)S(1)} %collective-permute-done.19.o_ref, bf16[128,512]{1,0:T(8,128)(2,1)S(1)} %get-tuple-element.33.n_ref, ...), custom_call_target="tpu_custom_call" | custom-call | flops 1000000000 | bytes 1048576 | tf_op jit(solution)/shard_map/pallas_call | solution.py:135
  53.7 1.0 %collective-permute-done.16.near_ref = bf16[128,512]{1,0:T(8,128)(2,1)S(1)} collective-permute-done((bf16[128,512]{1,0:T(8,128)(2,1)S(1)}, bf16[128,512]{1,0:T(8,128)(2,1)S(1)}, u32[]{:S(2)}, u32[]{:S(2)}) %collective-permute-start.16) | collective-permute-done | bytes 131104 | tf_op jit(solution)/shard_map/ppermute | solution.py:176
  54.8 1.5 %collective-permute-start.17 = (bf16[128,512]{1,0:T(8,128)(2,1)S(1)}, bf16[128,512]{1,0:T(8,128)(2,1)S(1)}, u32[]{:S(2)}, u32[]{:S(2)}) collective-permute-start(bf16[128,512]{1,0:T(8,128)(2,1)S(1)} %add_convert_fusion), channel_id=1, source_target_pairs={{0,8},{2,10},{4,12},{6,14},{8,0},{10,2},{12,4},{14,6},{1,9},{3,11}... | collective-permute-start | bytes 393224 | tf_op jit(solution)/shard_map/ppermute | solution.py:176
  56.3 1.4 %shard_map.101 = (bf16[128,512]{1,0:T(8,128)(2,1)}, f32[128,512]{1,0:T(8,128)S(1)}, f32[128,512]{1,0:T(8,128)S(1)}) custom-call(bf16[128,512]{1,0:T(8,128)(2,1)S(1)} %get-tuple-element.43.go_ref, bf16[128,512]{1,0:T(8,128)(2,1)S(1)} %copy-done.2, bf16[128,512]{1,0:T(8,128)(2,1)S(1)} %copy-done.3, bf16[128,512]{1,0:T(8,128)(2,1)S(1)} %copy-done.4, ...), custom_call_target="tpu_custom_call" | custom-call | flops 1000000000 | bytes 1048576 | tf_op jit(solution)/shard_map/pallas_call | solution.py:135
  58.2 5.4 %collective-permute-done.17.far_ref = bf16[128,512]{1,0:T(8,128)(2,1)S(1)} collective-permute-done((bf16[128,512]{1,0:T(8,128)(2,1)S(1)}, bf16[128,512]{1,0:T(8,128)(2,1)S(1)}, u32[]{:S(2)}, u32[]{:S(2)}) %collective-permute-start.17) | collective-permute-done | bytes 131104 | tf_op jit(solution)/shard_map/ppermute | solution.py:176
  63.6 1.0 %shard_map.102 = (bf16[128,512]{1,0:T(8,128)(2,1)}, bf16[128,512]{1,0:T(8,128)(2,1)}) custom-call(f32[128,512]{1,0:T(8,128)S(1)} %get-tuple-element.47.gk_ref, f32[128,512]{1,0:T(8,128)S(1)} %get-tuple-element.48.gv_ref, bf16[128,512]{1,0:T(8,128)(2,1)S(1)} %copy-done.3, bf16[128,512]{1,0:T(8,128)(2,1)S(1)} %copy-done.4, ...), custom_call_target="tpu_custom_call" | custom-call | flops 1000000000 | bytes 1048576 | tf_op jit(solution)/shard_map/pallas_call | solution.py:135
  64.6 0.9 %convert_add_fusion = f32[256,512]{1,0:T(8,128)} fusion(f32[256,512]{1,0:T(8,128)S(1)} %get-tuple-element.53, bf16[256,512]{1,0:T(8,128)(2,1)S(1)} %collective-permute-done.23), kind=kLoop, calls=%fused_computation | loop fusion | flops 262144 | bytes 1310720 | tf_op jit(solution)/shard_map/add | solution.py:417
  65.5 1.0 %shard_map.97 = bf16[128,2048]{1,0:T(8,128)(2,1)} custom-call(bf16[128,1024]{1,0:T(8,128)(2,1)S(1)} %get-tuple-element.39.a_ref, bf16[128,1024]{1,0:T(8,128)(2,1)S(1)} %collective-permute-done.10.b_ref, bf16[128,1024]{1,0:T(8,128)(2,1)S(1)} %collective-permute-done.11.c_ref, bf16[128,1024]{1,0:T(8,128)(2,1)S(1)} %collective-permute-done.12.d_ref), custom_call_target="tpu_custom_call" | custom-call | flops 1000000000 | bytes 1048576 | tf_op jit(solution)/shard_map/pallas_call | solution.py:135
  (49 shorter events, 6.7 us)
Async XLA Ops:
  0.6 1.0 %copy-start = (bf16[256,512]{1,0:T(8,128)(2,1)S(1)}, bf16[256,512]{1,0:T(8,128)(2,1)}, u32[]{:S(2)}) copy-start(bf16[256,512]{1,0:T(8,128)(2,1)} %param.8) | copy-start | bytes 786436
  1.6 0.9 %copy-start.3 = (bf16[128,512]{1,0:T(8,128)(2,1)S(1)}, bf16[128,512]{1,0:T(8,128)(2,1)}, u32[]{:S(2)}) copy-start(bf16[128,512]{1,0:T(8,128)(2,1)} %k_ref.7) | copy-start | bytes 393220
  1.6 1.0 %copy-start.4 = (bf16[128,512]{1,0:T(8,128)(2,1)S(1)}, bf16[128,512]{1,0:T(8,128)(2,1)}, u32[]{:S(2)}) copy-start(bf16[128,512]{1,0:T(8,128)(2,1)} %v_ref.7) | copy-start | bytes 393220
  2.6 7.8 %copy-start.1 = (bf16[128,2048]{1,0:T(8,128)(2,1)S(1)}, bf16[128,2048]{1,0:T(8,128)(2,1)}, u32[]{:S(2)}) copy-start(bf16[128,2048]{1,0:T(8,128)(2,1)} %gy_ref.7) | copy-start | bytes 1572868
  2.8 9.4 %collective-permute-start = (bf16[256,512]{1,0:T(8,128)(2,1)S(1)}, bf16[256,512]{1,0:T(8,128)(2,1)S(1)}, u32[]{:S(2)}, u32[]{:S(2)}) collective-permute-start(bf16[256,512]{1,0:T(8,128)(2,1)S(1)} %shard_map.93), channel_id=1, source_target_pairs={{0,2},{2,0},{4,6},{6,4},{8,10},{10,8},{12,14},{14,12},{1,3},{3,1},... | collective-permute-start | bytes 786440 | tf_op jit(solution)/shard_map/ppermute | solution.py:176
  5.8 11.3 %collective-permute-start.1 = (bf16[128,512]{1,0:T(8,128)(2,1)S(1)}, bf16[128,512]{1,0:T(8,128)(2,1)S(1)}, u32[]{:S(2)}, u32[]{:S(2)}) collective-permute-start(bf16[128,512]{1,0:T(8,128)(2,1)S(1)} %constant_dynamic-slice_fusion.w_ref.refs_0_), channel_id=1, source_target_pairs={{0,8},{2,10},{4,12},{6,14},{8,0},{10,2},{12,4},{14,6},{1,9},{3,11}... | collective-permute-start | bytes 393224 | tf_op jit(solution)/shard_map/ppermute | solution.py:176
  8.4 9.8 %collective-permute-start.2 = (bf16[128,512]{1,0:T(8,128)(2,1)S(1)}, bf16[128,512]{1,0:T(8,128)(2,1)S(1)}, u32[]{:S(2)}, u32[]{:S(2)}) collective-permute-start(bf16[128,512]{1,0:T(8,128)(2,1)S(1)} %constant_dynamic-slice_fusion.w_ref.refs_0_), channel_id=1, source_target_pairs={{0,12},{2,14},{4,0},{6,2},{8,4},{10,6},{12,8},{14,10},{1,13},{3,15... | collective-permute-start | bytes 393224 | tf_op jit(solution)/shard_map/ppermute | solution.py:176
  9.7 12.3 %collective-permute-start.4 = (bf16[128,512]{1,0:T(8,128)(2,1)S(1)}, bf16[128,512]{1,0:T(8,128)(2,1)S(1)}, u32[]{:S(2)}, u32[]{:S(2)}) collective-permute-start(bf16[128,512]{1,0:T(8,128)(2,1)S(1)} %constant_dynamic-slice_fusion.w_ref.refs_0_), channel_id=1, source_target_pairs={{0,4},{2,6},{4,8},{6,10},{8,12},{10,14},{12,0},{14,2},{1,5},{3,7},... | collective-permute-start | bytes 393224 | tf_op jit(solution)/shard_map/ppermute | solution.py:176
  10.5 13.2 %collective-permute-start.7 = (bf16[256,256]{1,0:T(8,128)(2,1)S(1)}, bf16[256,256]{1,0:T(8,128)(2,1)S(1)}, u32[]{:S(2)}, u32[]{:S(2)}) collective-permute-start(bf16[256,256]{1,0:T(8,128)(2,1)S(1)} %get-tuple-element.34), channel_id=1, source_target_pairs={{0,4},{2,6},{4,0},{6,2},{8,12},{10,14},{12,8},{14,10},{1,5},{3,7},... | collective-permute-start | bytes 393224 | tf_op jit(solution)/shard_map/ppermute | solution.py:176
  12.1 13.1 %collective-permute-start.13 = (bf16[128,1024]{1,0:T(8,128)(2,1)S(1)}, bf16[128,1024]{1,0:T(8,128)(2,1)S(1)}, u32[]{:S(2)}, u32[]{:S(2)}) collective-permute-start(bf16[128,1024]{1,0:T(8,128)(2,1)S(1)} %get-tuple-element.42), channel_id=1, source_target_pairs={{0,16},{16,0},{1,17},{17,1},{2,18},{18,2},{3,19},{19,3},{4,20},{20... | collective-permute-start | bytes 786440 | tf_op jit(solution)/shard_map/ppermute | solution.py:185
  18.2 3.1 %copy-start.2 = (bf16[128,512]{1,0:T(8,128)(2,1)S(1)}, bf16[128,512]{1,0:T(8,128)(2,1)}, u32[]{:S(2)}) copy-start(bf16[128,512]{1,0:T(8,128)(2,1)} %q_ref.7) | copy-start | bytes 393220
  18.2 5.5 %collective-permute-start.3 = (bf16[128,512]{1,0:T(8,128)(2,1)S(1)}, bf16[128,512]{1,0:T(8,128)(2,1)S(1)}, u32[]{:S(2)}, u32[]{:S(2)}) collective-permute-start(bf16[128,512]{1,0:T(8,128)(2,1)S(1)} %add_convert_fusion.3), channel_id=1, source_target_pairs={{0,4},{2,6},{4,0},{6,2},{8,12},{10,14},{12,8},{14,10},{1,5},{3,7},... | collective-permute-start | bytes 393224 | tf_op jit(solution)/shard_map/ppermute | solution.py:176
  20.8 8.9 %collective-permute-start.9 = (bf16[256,512]{1,0:T(8,128)(2,1)S(1)}, bf16[256,512]{1,0:T(8,128)(2,1)S(1)}, u32[]{:S(2)}, u32[]{:S(2)}) collective-permute-start(bf16[256,512]{1,0:T(8,128)(2,1)S(1)} %pad_maximum_fusion), channel_id=1, source_target_pairs={{0,2},{2,0},{4,6},{6,4},{8,10},{10,8},{12,14},{14,12},{1,3},{3,1},... | collective-permute-start | bytes 786440 | tf_op jit(solution)/shard_map/ppermute | solution.py:176
  22.1 7.6 %collective-permute-start.8 = (bf16[128,512]{1,0:T(8,128)(2,1)S(1)}, bf16[128,512]{1,0:T(8,128)(2,1)S(1)}, u32[]{:S(2)}, u32[]{:S(2)}) collective-permute-start(bf16[128,512]{1,0:T(8,128)(2,1)S(1)} %collective-permute-done.4.refs_1_), channel_id=1, source_target_pairs={{0,2},{2,0},{4,6},{6,4},{8,10},{10,8},{12,14},{14,12},{1,3},{3,1},... | collective-permute-start | bytes 393224 | tf_op jit(solution)/shard_map/ppermute | solution.py:176
  23.7 11.1 %collective-permute-start.5 = (bf16[128,512]{1,0:T(8,128)(2,1)S(1)}, bf16[128,512]{1,0:T(8,128)(2,1)S(1)}, u32[]{:S(2)}, u32[]{:S(2)}) collective-permute-start(bf16[128,512]{1,0:T(8,128)(2,1)S(1)} %add_convert_fusion.2), channel_id=1, source_target_pairs={{0,8},{2,10},{4,12},{6,14},{8,0},{10,2},{12,4},{14,6},{1,9},{3,11}... | collective-permute-start | bytes 393224 | tf_op jit(solution)/shard_map/ppermute | solution.py:176
  30.1 6.4 %collective-permute-start.14 = (f32[128,512]{1,0:T(8,128)S(1)}, f32[128,512]{1,0:T(8,128)S(1)}, u32[]{:S(2)}, u32[]{:S(2)}) collective-permute-start(f32[128,512]{1,0:T(8,128)S(1)} %shard_map.99), channel_id=1, source_target_pairs={{0,16},{16,0},{1,17},{17,1},{2,18},{18,2},{3,19},{19,3},{4,20},{20... | collective-permute-start | bytes 786440 | tf_op jit(solution)/shard_map/ppermute | solution.py:185
  31.7 11.5 %collective-permute-start.18 = (bf16[256,256]{1,0:T(8,128)(2,1)S(1)}, bf16[256,256]{1,0:T(8,128)(2,1)S(1)}, u32[]{:S(2)}, u32[]{:S(2)}) collective-permute-start(bf16[256,256]{1,0:T(8,128)(2,1)S(1)} %shard_map.103), channel_id=1, source_target_pairs={{0,8},{2,10},{4,12},{6,14},{8,0},{10,2},{12,4},{14,6},{1,9},{3,11}... | collective-permute-start | bytes 393224 | tf_op jit(solution)/shard_map/ppermute | solution.py:176
  35.1 9.6 %collective-permute-start.21 = (bf16[128,512]{1,0:T(8,128)(2,1)S(1)}, bf16[128,512]{1,0:T(8,128)(2,1)S(1)}, u32[]{:S(2)}, u32[]{:S(2)}) collective-permute-start(bf16[128,512]{1,0:T(8,128)(2,1)S(1)} %get-tuple-element.33.n_ref), channel_id=1, source_target_pairs={{0,8},{2,10},{4,12},{6,14},{8,0},{10,2},{12,4},{14,6},{1,9},{3,11}... | collective-permute-start | bytes 393224 | tf_op jit(solution)/shard_map/ppermute | solution.py:176
  36.9 8.9 %collective-permute-start.15 = (bf16[128,512]{1,0:T(8,128)(2,1)S(1)}, bf16[128,512]{1,0:T(8,128)(2,1)S(1)}, u32[]{:S(2)}, u32[]{:S(2)}) collective-permute-start(bf16[128,512]{1,0:T(8,128)(2,1)S(1)} %get-tuple-element.49), channel_id=1, source_target_pairs={{0,2},{2,0},{4,6},{6,4},{8,10},{10,8},{12,14},{14,12},{1,3},{3,1},... | collective-permute-start | bytes 393224 | tf_op jit(solution)/shard_map/ppermute | solution.py:176
  43.2 7.3 %collective-permute-start.19 = (bf16[384,256]{1,0:T(8,128)(2,1)S(1)}, bf16[384,256]{1,0:T(8,128)(2,1)S(1)}, u32[]{:S(2)}, u32[]{:S(2)}) collective-permute-start(bf16[384,256]{1,0:T(8,128)(2,1)S(1)} %pad_maximum_fusion.1.c_ref), channel_id=1, source_target_pairs={{0,1},{1,0},{2,3},{3,2},{4,5},{5,4},{6,7},{7,6},{8,9},{9,8},{10,11... | collective-permute-start | bytes 589832 | tf_op jit(solution)/shard_map/ppermute | solution.py:188
  43.2 7.2 %collective-permute-start.20 = (bf16[128,512]{1,0:T(8,128)(2,1)S(1)}, bf16[128,512]{1,0:T(8,128)(2,1)S(1)}, u32[]{:S(2)}, u32[]{:S(2)}) collective-permute-start(bf16[128,512]{1,0:T(8,128)(2,1)S(1)} %get-tuple-element.33.n_ref), channel_id=1, source_target_pairs={{0,4},{2,6},{4,0},{6,2},{8,12},{10,14},{12,8},{14,10},{1,5},{3,7},... | collective-permute-start | bytes 393224 | tf_op jit(solution)/shard_map/ppermute | solution.py:176
  43.3 5.8 %collective-permute-start.6 = (bf16[128,512]{1,0:T(8,128)(2,1)S(1)}, bf16[128,512]{1,0:T(8,128)(2,1)S(1)}, u32[]{:S(2)}, u32[]{:S(2)}) collective-permute-start(bf16[128,512]{1,0:T(8,128)(2,1)S(1)} %get-tuple-element.33.n_ref), channel_id=1, source_target_pairs={{0,16},{16,0},{1,17},{17,1},{2,18},{18,2},{3,19},{19,3},{4,20},{20... | collective-permute-start | bytes 393224 | tf_op jit(solution)/shard_map/ppermute | solution.py:185
  44.7 7.7 %collective-permute-start.22 = (bf16[128,512]{1,0:T(8,128)(2,1)S(1)}, bf16[128,512]{1,0:T(8,128)(2,1)S(1)}, u32[]{:S(2)}, u32[]{:S(2)}) collective-permute-start(bf16[128,512]{1,0:T(8,128)(2,1)S(1)} %collective-permute-done.21.refs_1_), channel_id=1, source_target_pairs={{0,4},{2,6},{4,0},{6,2},{8,12},{10,14},{12,8},{14,10},{1,5},{3,7},... | collective-permute-start | bytes 393224 | tf_op jit(solution)/shard_map/ppermute | solution.py:176
  45.9 8.9 %collective-permute-start.16 = (bf16[128,512]{1,0:T(8,128)(2,1)S(1)}, bf16[128,512]{1,0:T(8,128)(2,1)S(1)}, u32[]{:S(2)}, u32[]{:S(2)}) collective-permute-start(bf16[128,512]{1,0:T(8,128)(2,1)S(1)} %add_convert_fusion.1), channel_id=1, source_target_pairs={{0,4},{2,6},{4,0},{6,2},{8,12},{10,14},{12,8},{14,10},{1,5},{3,7},... | collective-permute-start | bytes 393224 | tf_op jit(solution)/shard_map/ppermute | solution.py:176
  49.9 7.9 %collective-permute-start.11 = (bf16[128,1024]{1,0:T(8,128)(2,1)S(1)}, bf16[128,1024]{1,0:T(8,128)(2,1)S(1)}, u32[]{:S(2)}, u32[]{:S(2)}) collective-permute-start(bf16[128,1024]{1,0:T(8,128)(2,1)S(1)} %get-tuple-element.40), channel_id=1, source_target_pairs={{0,16},{16,0},{1,17},{17,1},{2,18},{18,2},{3,19},{19,3},{4,20},{20... | collective-permute-start | bytes 786440 | tf_op jit(solution)/shard_map/ppermute | solution.py:185
  53.2 11.5 %collective-permute-start.23 = (bf16[256,512]{1,0:T(8,128)(2,1)S(1)}, bf16[256,512]{1,0:T(8,128)(2,1)S(1)}, u32[]{:S(2)}, u32[]{:S(2)}) collective-permute-start(bf16[256,512]{1,0:T(8,128)(2,1)S(1)} %get-tuple-element.54), channel_id=1, source_target_pairs={{0,2},{2,0},{4,6},{6,4},{8,10},{10,8},{12,14},{14,12},{1,3},{3,1},... | collective-permute-start | bytes 786440 | tf_op jit(solution)/shard_map/ppermute | solution.py:176
  54.8 8.8 %collective-permute-start.17 = (bf16[128,512]{1,0:T(8,128)(2,1)S(1)}, bf16[128,512]{1,0:T(8,128)(2,1)S(1)}, u32[]{:S(2)}, u32[]{:S(2)}) collective-permute-start(bf16[128,512]{1,0:T(8,128)(2,1)S(1)} %add_convert_fusion), channel_id=1, source_target_pairs={{0,8},{2,10},{4,12},{6,14},{8,0},{10,2},{12,4},{14,6},{1,9},{3,11}... | collective-permute-start | bytes 393224 | tf_op jit(solution)/shard_map/ppermute | solution.py:176
  56.3 9.1 %collective-permute-start.10 = (bf16[128,1024]{1,0:T(8,128)(2,1)S(1)}, bf16[128,1024]{1,0:T(8,128)(2,1)S(1)}, u32[]{:S(2)}, u32[]{:S(2)}) collective-permute-start(bf16[128,1024]{1,0:T(8,128)(2,1)S(1)} %get-tuple-element.39.a_ref), channel_id=1, source_target_pairs={{0,1},{1,0},{2,3},{3,2},{4,5},{5,4},{6,7},{7,6},{8,9},{9,8},{10,11... | collective-permute-start | bytes 786440 | tf_op jit(solution)/shard_map/ppermute | solution.py:188
  57.7 7.8 %collective-permute-start.12 = (bf16[128,1024]{1,0:T(8,128)(2,1)S(1)}, bf16[128,1024]{1,0:T(8,128)(2,1)S(1)}, u32[]{:S(2)}, u32[]{:S(2)}) collective-permute-start(bf16[128,1024]{1,0:T(8,128)(2,1)S(1)} %collective-permute-done.11.c_ref), channel_id=1, source_target_pairs={{0,1},{1,0},{2,3},{3,2},{4,5},{5,4},{6,7},{7,6},{8,9},{9,8},{10,11... | collective-permute-start | bytes 786440 | tf_op jit(solution)/shard_map/ppermute | solution.py:188

commit v5 on v4

--- a/solution.py
+++ b/solution.py
@@ -14,6 +14,7 @@
 BF16 = jnp.bfloat16
 ROWS_T = (((0,), (0,)), ((), ()))
 LAST_T = (((1,), (1,)), ((), ()))
+LIGHT = 2**20
 PLAIN = (((1,), (0,)), ((), ()))
 
 
@@ -242,16 +243,15 @@
     def add(a, b):
         return (a.astype(F32) + b.astype(F32)).astype(BF16)
 
-    x_weight_far = swap(side_by_side(*z_weight[1:]), 1)
-    x_states, *z_weight[1:] = tie(x_states, *z_weight[1:])
     pair_states = add(states, x_states)
     near_states = swap(pair_states, 2)
-    pair_states, z_weight[0] = tie(pair_states, z_weight[0])
+    pair_states, *z_weight = tie(pair_states, *z_weight)
+    near_states, near_cols, y_cols = tie(near_states, near_cols, y_cols)
     quad_states = add(pair_states, near_states)
     got_states = x_states, near_states, swap(quad_states, 4)
 
-    x_weight_near = swap(z_weight[0], 1)
-    near_cols, z_weight[0] = tie(near_cols, z_weight[0])
+    x_weight = swap(side_by_side(*z_weight), 1)
+    near_cols, quad_states = tie(near_cols, quad_states)
 
     def relay(gy_ref, near_ref, far_ref):
         g, z, x, h = place()
@@ -263,21 +263,20 @@
     far_cols = swap(far_send, 4)
 
     def weight_blocks(refs):
-        own, *others, x_own, x_near, x_far = refs
-        x_own = x_own.at[:half, :]
+        own, *others, x_own, x_others = refs
         g, z, x, h = place()
         blocks = []
         for k in range(line):
             zk = lax.rem(z - k + line, line)
             blocks.append((zk * 2 + x, (own, *others)[k][...]))
-            if k < 2:
-                block = (x_own, x_near)[k][...]
+            if k == 0:
+                block = x_own[:half, :]
             else:
-                block = x_far[(k - 2) * half : (k - 1) * half, :]
+                block = x_others[(k - 1) * half : k * half, :]
             blocks.append((zk * 2 + 1 - x, block))
         return blocks
 
-    weight_args = (my_weight, *z_weight, x_weight_states, x_weight_near, x_weight_far)
+    weight_args = (my_weight, *z_weight, x_weight_states, x_weight)
 
     def back_other(yc_ref, *refs):
         *w_refs, out_ref = refs
@@ -302,9 +301,6 @@
         back_own, [((rows, feats), F32)], grad_y, *weight_args
     )
 
-    my_cols = side_by_side(near_cols[:rows], far_cols)
-    core_cols = swap_core(my_cols)
-
     def forward(q_ref, local_ref, x_ref, near_ref, far_ref, att_ref, normed_ref, prefix_ref):
         g, z, x, h = place()
         total = jnp.where(x == 1, x_ref[...].astype(F32), 0.0)
@@ -325,10 +321,9 @@
         [((rows, feats), F32), ((rows, feats), BF16), (state, BF16)],
         queries, att_local, *got_states,
     )
+    far_cols, normed = tie(far_cols, normed)
     y_normed = swap_y(normed)
     far_normed = swap(normed, 4)
-    near_normed = swap(normed, 2)
-    last_normed = swap(far_normed, 2)
 
     def turn_back(att_ref, own_ref, other_ref, q_ref, go_ref, adj_ref):
         for i in range(heads):
@@ -345,12 +340,26 @@
         turn_back, [((rows, feats), BF16), (state, BF16)],
         attended, grad_own, grad_other, queries,
     )
-    x_adjoint = swap(adjoint, 1)
+    my_cols = side_by_side(near_cols[:rows], far_cols)
+    core_cols = swap_core(my_cols)
+
+    near_normed = swap(normed, 2)
+    x_adjoint, near_normed, far_normed, core_cols = tie(
+        swap(adjoint, 1), near_normed, far_normed, core_cols
+    )
+    def project(n_ref, yn_ref, *refs):
+        *w_refs, own_ref, other_ref = refs
+        for s, block in weight_blocks(w_refs):
+            own_ref[:, lanes(s, half)] = dot(n_ref[...], block, LAST_T).astype(BF16)
+            other_ref[:, lanes(s, half)] = dot(yn_ref[...], block, LAST_T).astype(BF16)
+
+    out_own, out_send = call(
+        project, [((rows, seq * half), BF16)] * 2, normed, y_normed, *weight_args
+    )
+    out_other = swap_y(out_send)
+    last_normed = swap(far_normed, 2)
     pair_adjoint = add(adjoint, x_adjoint)
     near_adjoint = swap(pair_adjoint, 2)
-    quad_adjoint = add(pair_adjoint, near_adjoint)
-    got_adjoint = x_adjoint, near_adjoint, swap(quad_adjoint, 4)
-
     def local_grads(go_ref, q_ref, k_ref, v_ref, sc_ref, pre_ref, gq_ref, gk_ref, gv_ref):
         mask = causal_mask()
         for i in range(heads):
@@ -367,18 +376,16 @@
         local_grads,
         [((rows, feats), BF16), ((rows, feats), F32), ((rows, feats), F32)],
         grad_out, queries, keys, values, scores, prefix,
-    )
-
-    def project(n_ref, yn_ref, *refs):
-        *w_refs, own_ref, other_ref = refs
-        for s, block in weight_blocks(w_refs):
-            own_ref[:, lanes(s, half)] = dot(n_ref[...], block, LAST_T).astype(BF16)
-            other_ref[:, lanes(s, half)] = dot(yn_ref[...], block, LAST_T).astype(BF16)
-
-    out_own, out_send = call(
-        project, [((rows, seq * half), BF16)] * 2, normed, y_normed, *weight_args
-    )
-    out_other = swap_y(out_send)
+        flops=LIGHT,
+    )
+
+    near_adjoint, last_normed, out_other, gk_local = tie(
+        near_adjoint, last_normed, out_other, gk_local
+    )
+    quad_adjoint = add(pair_adjoint, near_adjoint)
+    far_adjoint = swap(quad_adjoint, 4)
+    quad_adjoint, last_normed = tie(quad_adjoint, last_normed)
+
     core_own = swap_core(out_own)
     core_other = swap_core(out_other)
 
@@ -397,6 +404,7 @@
     gw_keep, gw_send = call(
         weight_grad, [((wrows, feats), F32), ((wrows, feats), BF16)],
         grad_y, my_cols, core_cols, normed, near_normed, far_normed, last_normed,
+        flops=LIGHT,
     )
     gw_other = swap(gw_send, 1)
 
@@ -412,9 +420,12 @@
             ).astype(BF16)
 
     (out_y,) = call(
-        join, [((rows, outs), BF16)], out_own, core_own, out_other, core_other
+        join, [((rows, outs), BF16)], out_own, core_own, out_other, core_other,
+        flops=LIGHT,
     )
     grad_weight = gw_keep + gw_other.astype(F32)
+
+    far_adjoint, out_y, grad_weight = tie(far_adjoint, out_y, grad_weight)
 
     def last(gk_ref, gv_ref, k_ref, v_ref, x_ref, near_ref, far_ref, ok_ref, ov_ref):
         g, z, x, h = place()
@@ -433,7 +444,7 @@
 
     grad_keys, grad_values = call(
         last, [((rows, feats), BF16)] * 2,
-        gk_local, gv_local, keys, values, *got_adjoint,
+        gk_local, gv_local, keys, values, x_adjoint, near_adjoint, far_adjoint,
     )
     return out_y, grad_queries, grad_keys, grad_values, grad_weight
 

time: 66.6 us -> 69.5 us (1.044)
  starting transfers between devices: 28.3 us -> 29.9 us
  waiting for transfers between devices: 27 us -> 28.3 us
    ppermute x17 -> x16, waiting for transfers between devices: 23.7 us -> 27.5 us  [permute(): return lax.ppermute(array, 'seq', pairs)]
    ppermute x4, waiting for transfers between devices: 3.33 us -> 0.79 us  [swap_y(): return lax.ppermute(array, 'groups', [(0, 1), (1, 0)])]
    ppermute x17 -> x16, starting transfers between devices: 23.3 us -> 24.5 us  [permute(): return lax.ppermute(array, 'seq', pairs)]
    ppermute x4, starting transfers between devices: 4.43 us -> 5.25 us  [swap_y(): return lax.ppermute(array, 'groups', [(0, 1), (1, 0)])]
    unnamed x10 -> x12, local copies, waits for them, and re-layouts: 1.91 us -> 1.91 us
  transfers between devices with their start and end apart: 24 -> 23, of which waited for: 10 -> 15; matrix products, arithmetic and copies ran while one was open for 2% -> 2% of each run, Pallas kernels for 9% -> 9%
where the time goes in v5:
time: 69.5 us; the launch traced here: 69.3 us
  starting transfers between devices  29.9 us (43%)
  waiting for transfers between devices  28.3 us (41%)
  Pallas kernels  7.39 us (11%)
  local copies, waits for them, and re-layouts  1.93 us (3%)
  other arithmetic  1.04 us (1%)
  between operations  0.82 us (1%)
    ppermute x16, waiting for transfers between devices, permute(): return lax.ppermute(array, 'seq', pairs)  27.5 us
    ppermute x16, starting transfers between devices, permute(): return lax.ppermute(array, 'seq', pairs)  24.5 us
    pallas_call x13, Pallas kernels, call(): pl.pallas_call(body, out_shape=[jax.ShapeDtypeStruct(s, d) for s, d in sh...  7.39 us
    ppermute x4, starting transfers between devices, swap_y(): return lax.ppermute(array, 'groups', [(0, 1), (1, 0)])  5.25 us
    unnamed x12, local copies, waits for them, and re-layouts  1.91 us
  transfers between devices with their start and end apart: 23, of which 15 were waited for; matrix products, arithmetic and copies ran while one was open for 2% of the time, Pallas kernels for 9%

profile of v5, /device:TPU:0, one launch (start us, length us, event | category | flops | bytes accessed | tf_op | source)
XLA Modules:
  0.0 69.3 jit_solution(14739375185869891337)
XLA Ops:
  0.7 0.9 %copy-done = bf16[256,512]{1,0:T(8,128)(2,1)S(1)} copy-done((bf16[256,512]{1,0:T(8,128)(2,1)S(1)}, bf16[256,512]{1,0:T(8,128)(2,1)}, u32[]{:S(2)}) %copy-start) | copy-done | bytes 262168
  1.6 0.9 %copy-done.3 = bf16[128,512]{1,0:T(8,128)(2,1)S(1)} copy-done((bf16[128,512]{1,0:T(8,128)(2,1)S(1)}, bf16[128,512]{1,0:T(8,128)(2,1)}, u32[]{:S(2)}) %copy-start.3) | copy-done | bytes 131096
  2.8 3.0 %collective-permute-start = (bf16[256,512]{1,0:T(8,128)(2,1)S(1)}, bf16[256,512]{1,0:T(8,128)(2,1)S(1)}, u32[]{:S(2)}, u32[]{:S(2)}) collective-permute-start(bf16[256,512]{1,0:T(8,128)(2,1)S(1)} %shard_map.93), channel_id=1, source_target_pairs={{0,2},{2,0},{4,6},{6,4},{8,10},{10,8},{12,14},{14,12},{1,3},{3,1},... | collective-permute-start | bytes 786440 | tf_op jit(solution)/shard_map/ppermute | solution.py:177
  5.8 1.6 %collective-permute-start.4 = (bf16[128,512]{1,0:T(8,128)(2,1)S(1)}, bf16[128,512]{1,0:T(8,128)(2,1)S(1)}, u32[]{:S(2)}, u32[]{:S(2)}) collective-permute-start(bf16[128,512]{1,0:T(8,128)(2,1)S(1)} %constant_dynamic-slice_fusion.w_ref.refs_0_), channel_id=1, source_target_pairs={{0,4},{2,6},{4,8},{6,10},{8,12},{10,14},{12,0},{14,2},{1,5},{3,7},... | collective-permute-start | bytes 393224 | tf_op jit(solution)/shard_map/ppermute | solution.py:177
  7.4 2.6 %collective-permute-start.5 = (bf16[128,512]{1,0:T(8,128)(2,1)S(1)}, bf16[128,512]{1,0:T(8,128)(2,1)S(1)}, u32[]{:S(2)}, u32[]{:S(2)}) collective-permute-start(bf16[128,512]{1,0:T(8,128)(2,1)S(1)} %constant_dynamic-slice_fusion.w_ref.refs_0_), channel_id=1, source_target_pairs={{0,8},{2,10},{4,12},{6,14},{8,0},{10,2},{12,4},{14,6},{1,9},{3,11}... | collective-permute-start | bytes 393224 | tf_op jit(solution)/shard_map/ppermute | solution.py:177
  9.9 1.3 %collective-permute-start.6 = (bf16[128,512]{1,0:T(8,128)(2,1)S(1)}, bf16[128,512]{1,0:T(8,128)(2,1)S(1)}, u32[]{:S(2)}, u32[]{:S(2)}) collective-permute-start(bf16[128,512]{1,0:T(8,128)(2,1)S(1)} %constant_dynamic-slice_fusion.w_ref.refs_0_), channel_id=1, source_target_pairs={{0,12},{2,14},{4,0},{6,2},{8,4},{10,6},{12,8},{14,10},{1,13},{3,15... | collective-permute-start | bytes 393224 | tf_op jit(solution)/shard_map/ppermute | solution.py:177
  11.4 1.6 %collective-permute-start.3 = (bf16[128,1024]{1,0:T(8,128)(2,1)S(1)}, bf16[128,1024]{1,0:T(8,128)(2,1)S(1)}, u32[]{:S(2)}, u32[]{:S(2)}) collective-permute-start(bf16[128,1024]{1,0:T(8,128)(2,1)S(1)} %get-tuple-element.47), channel_id=1, source_target_pairs={{0,16},{16,0},{1,17},{17,1},{2,18},{18,2},{3,19},{19,3},{4,20},{20... | collective-permute-start | bytes 786440 | tf_op jit(solution)/shard_map/ppermute | solution.py:186
  13.0 0.9 %collective-permute-start.2 = (bf16[256,256]{1,0:T(8,128)(2,1)S(1)}, bf16[256,256]{1,0:T(8,128)(2,1)S(1)}, u32[]{:S(2)}, u32[]{:S(2)}) collective-permute-start(bf16[256,256]{1,0:T(8,128)(2,1)S(1)} %get-tuple-element.46), channel_id=1, source_target_pairs={{0,4},{2,6},{4,0},{6,2},{8,12},{10,14},{12,8},{14,10},{1,5},{3,7},... | collective-permute-start | bytes 393224 | tf_op jit(solution)/shard_map/ppermute | solution.py:177
  14.1 4.4 %collective-permute-start.1 = (bf16[128,512]{1,0:T(8,128)(2,1)S(1)}, bf16[128,512]{1,0:T(8,128)(2,1)S(1)}, u32[]{:S(2)}, u32[]{:S(2)}) collective-permute-start(bf16[128,512]{1,0:T(8,128)(2,1)S(1)} %add_convert_fusion.3), channel_id=1, source_target_pairs={{0,4},{2,6},{4,0},{6,2},{8,12},{10,14},{12,8},{14,10},{1,5},{3,7},... | collective-permute-start | bytes 393224 | tf_op jit(solution)/shard_map/ppermute | solution.py:177
  18.5 0.9 %collective-permute-done.6.refs_3_ = bf16[128,512]{1,0:T(8,128)(2,1)S(1)} collective-permute-done((bf16[128,512]{1,0:T(8,128)(2,1)S(1)}, bf16[128,512]{1,0:T(8,128)(2,1)S(1)}, u32[]{:S(2)}, u32[]{:S(2)}) %collective-permute-start.6) | collective-permute-done | bytes 131104 | tf_op jit(solution)/shard_map/ppermute | solution.py:177
  20.4 1.8 %collective-permute-done.2.near_ref = bf16[256,256]{1,0:T(8,128)(2,1)S(1)} collective-permute-done((bf16[256,256]{1,0:T(8,128)(2,1)S(1)}, bf16[256,256]{1,0:T(8,128)(2,1)S(1)}, u32[]{:S(2)}, u32[]{:S(2)}) %collective-permute-start.2) | collective-permute-done | bytes 131104 | tf_op jit(solution)/shard_map/ppermute | solution.py:177
  22.2 1.8 %collective-permute-done.1.near_ref = bf16[128,512]{1,0:T(8,128)(2,1)S(1)} collective-permute-done((bf16[128,512]{1,0:T(8,128)(2,1)S(1)}, bf16[128,512]{1,0:T(8,128)(2,1)S(1)}, u32[]{:S(2)}, u32[]{:S(2)}) %collective-permute-start.1) | collective-permute-done | bytes 131104 | tf_op jit(solution)/shard_map/ppermute | solution.py:177
  24.0 1.4 %collective-permute-start.7 = (bf16[128,512]{1,0:T(8,128)(2,1)S(1)}, bf16[128,512]{1,0:T(8,128)(2,1)S(1)}, u32[]{:S(2)}, u32[]{:S(2)}) collective-permute-start(bf16[128,512]{1,0:T(8,128)(2,1)S(1)} %add_convert_fusion.2), channel_id=1, source_target_pairs={{0,8},{2,10},{4,12},{6,14},{8,0},{10,2},{12,4},{14,6},{1,9},{3,11}... | collective-permute-start | bytes 393224 | tf_op jit(solution)/shard_map/ppermute | solution.py:177
  25.4 1.6 %collective-permute-start.11 = (bf16[256,256]{1,0:T(8,128)(2,1)S(1)}, bf16[256,256]{1,0:T(8,128)(2,1)S(1)}, u32[]{:S(2)}, u32[]{:S(2)}) collective-permute-start(bf16[256,256]{1,0:T(8,128)(2,1)S(1)} %shard_map.99), channel_id=1, source_target_pairs={{0,8},{2,10},{4,12},{6,14},{8,0},{10,2},{12,4},{14,6},{1,9},{3,11}... | collective-permute-start | bytes 393224 | tf_op jit(solution)/shard_map/ppermute | solution.py:177
  27.1 2.3 %collective-permute-done.8.refs_5_ = bf16[384,512]{1,0:T(8,128)(2,1)S(1)} collective-permute-done((bf16[384,512]{1,0:T(8,128)(2,1)S(1)}, bf16[384,512]{1,0:T(8,128)(2,1)S(1)}, u32[]{:S(2)}, u32[]{:S(2)}) %collective-permute-start.8) | collective-permute-done | bytes 393248 | tf_op jit(solution)/shard_map/ppermute | solution.py:177
  29.8 1.6 %collective-permute-start.9 = (f32[128,512]{1,0:T(8,128)S(1)}, f32[128,512]{1,0:T(8,128)S(1)}, u32[]{:S(2)}, u32[]{:S(2)}) collective-permute-start(f32[128,512]{1,0:T(8,128)S(1)} %shard_map.97), channel_id=1, source_target_pairs={{0,16},{16,0},{1,17},{17,1},{2,18},{18,2},{3,19},{19,3},{4,20},{20... | collective-permute-start | bytes 786440 | tf_op jit(solution)/shard_map/ppermute | solution.py:186
  31.4 4.7 %collective-permute-done.7.far_ref = bf16[128,512]{1,0:T(8,128)(2,1)S(1)} collective-permute-done((bf16[128,512]{1,0:T(8,128)(2,1)S(1)}, bf16[128,512]{1,0:T(8,128)(2,1)S(1)}, u32[]{:S(2)}, u32[]{:S(2)}) %collective-permute-start.7) | collective-permute-done | bytes 131104 | tf_op jit(solution)/shard_map/ppermute | solution.py:177
  36.5 1.4 %collective-permute-done.11 = bf16[256,256]{1,0:T(8,128)(2,1)S(1)} collective-permute-done((bf16[256,256]{1,0:T(8,128)(2,1)S(1)}, bf16[256,256]{1,0:T(8,128)(2,1)S(1)}, u32[]{:S(2)}, u32[]{:S(2)}) %collective-permute-start.11) | collective-permute-done | bytes 131104 | tf_op jit(solution)/shard_map/ppermute | solution.py:177
  37.8 1.5 %collective-permute-start.17 = (bf16[128,512]{1,0:T(8,128)(2,1)S(1)}, bf16[128,512]{1,0:T(8,128)(2,1)S(1)}, u32[]{:S(2)}, u32[]{:S(2)}) collective-permute-start(bf16[128,512]{1,0:T(8,128)(2,1)S(1)} %get-tuple-element.59.n_ref), channel_id=1, source_target_pairs={{0,16},{16,0},{1,17},{17,1},{2,18},{18,2},{3,19},{19,3},{4,20},{20... | collective-permute-start | bytes 393224 | tf_op jit(solution)/shard_map/ppermute | solution.py:186
  39.4 3.1 %collective-permute-start.13 = (bf16[128,512]{1,0:T(8,128)(2,1)S(1)}, bf16[128,512]{1,0:T(8,128)(2,1)S(1)}, u32[]{:S(2)}, u32[]{:S(2)}) collective-permute-start(bf16[128,512]{1,0:T(8,128)(2,1)S(1)} %get-tuple-element.59.n_ref), channel_id=1, source_target_pairs={{0,8},{2,10},{4,12},{6,14},{8,0},{10,2},{12,4},{14,6},{1,9},{3,11}... | collective-permute-start | bytes 393224 | tf_op jit(solution)/shard_map/ppermute | solution.py:177
  43.4 1.1 %collective-permute-start.10 = (bf16[128,512]{1,0:T(8,128)(2,1)S(1)}, bf16[128,512]{1,0:T(8,128)(2,1)S(1)}, u32[]{:S(2)}, u32[]{:S(2)}) collective-permute-start(bf16[128,512]{1,0:T(8,128)(2,1)S(1)} %get-tuple-element.55), channel_id=1, source_target_pairs={{0,2},{2,0},{4,6},{6,4},{8,10},{10,8},{12,14},{14,12},{1,3},{3,1},... | collective-permute-start | bytes 393224 | tf_op jit(solution)/shard_map/ppermute | solution.py:177
  45.8 1.0 %collective-permute-done.12.refs_0_ = bf16[128,512]{1,0:T(8,128)(2,1)S(1)} collective-permute-done((bf16[128,512]{1,0:T(8,128)(2,1)S(1)}, bf16[128,512]{1,0:T(8,128)(2,1)S(1)}, u32[]{:S(2)}, u32[]{:S(2)}) %collective-permute-start.12) | collective-permute-done | bytes 131104 | tf_op jit(solution)/shard_map/ppermute | solution.py:177
  46.8 1.6 %collective-permute-done.13.refs_1_ = bf16[128,512]{1,0:T(8,128)(2,1)S(1)} collective-permute-done((bf16[128,512]{1,0:T(8,128)(2,1)S(1)}, bf16[128,512]{1,0:T(8,128)(2,1)S(1)}, u32[]{:S(2)}, u32[]{:S(2)}) %collective-permute-start.13) | collective-permute-done | bytes 131104 | tf_op jit(solution)/shard_map/ppermute | solution.py:177
  48.4 1.0 %collective-permute-done.10.x_ref = bf16[128,512]{1,0:T(8,128)(2,1)S(1)} collective-permute-done((bf16[128,512]{1,0:T(8,128)(2,1)S(1)}, bf16[128,512]{1,0:T(8,128)(2,1)S(1)}, u32[]{:S(2)}, u32[]{:S(2)}) %collective-permute-start.10) | collective-permute-done | bytes 131104 | tf_op jit(solution)/shard_map/ppermute | solution.py:177
  49.5 2.0 %collective-permute-start.16 = (bf16[128,512]{1,0:T(8,128)(2,1)S(1)}, bf16[128,512]{1,0:T(8,128)(2,1)S(1)}, u32[]{:S(2)}, u32[]{:S(2)}) collective-permute-start(bf16[128,512]{1,0:T(8,128)(2,1)S(1)} %collective-permute-done.13.refs_1_), channel_id=1, source_target_pairs={{0,4},{2,6},{4,0},{6,2},{8,12},{10,14},{12,8},{14,10},{1,5},{3,7},... | collective-permute-start | bytes 393224 | tf_op jit(solution)/shard_map/ppermute | solution.py:177
  51.5 1.4 %shard_map.101 = (bf16[128,512]{1,0:T(8,128)(2,1)}, f32[128,512]{1,0:T(8,128)S(1)}, f32[128,512]{1,0:T(8,128)S(1)}) custom-call(bf16[128,512]{1,0:T(8,128)(2,1)S(1)} %get-tuple-element.64.go_ref, bf16[128,512]{1,0:T(8,128)(2,1)S(1)} %copy-done.2, bf16[128,512]{1,0:T(8,128)(2,1)S(1)} %copy-done.3, bf16[128,512]{1,0:T(8,128)(2,1)S(1)} %copy-done.4, ...), custom_call_target="tpu_custom_call" | custom-call | flops 1048576 | bytes 1048576 | tf_op jit(solution)/shard_map/pallas_call | solution.py:136
  53.7 2.2 %collective-permute-done.15.near_ref = bf16[128,512]{1,0:T(8,128)(2,1)S(1)} collective-permute-done((bf16[128,512]{1,0:T(8,128)(2,1)S(1)}, bf16[128,512]{1,0:T(8,128)(2,1)S(1)}, u32[]{:S(2)}, u32[]{:S(2)}) %collective-permute-start.15) | collective-permute-done | bytes 131104 | tf_op jit(solution)/shard_map/ppermute | solution.py:177
  55.9 1.5 %collective-permute-done.16.refs_2_ = bf16[128,512]{1,0:T(8,128)(2,1)S(1)} collective-permute-done((bf16[128,512]{1,0:T(8,128)(2,1)S(1)}, bf16[128,512]{1,0:T(8,128)(2,1)S(1)}, u32[]{:S(2)}, u32[]{:S(2)}) %collective-permute-start.16) | collective-permute-done | bytes 131104 | tf_op jit(solution)/shard_map/ppermute | solution.py:177
  58.2 1.1 %collective-permute-start.22 = (bf16[256,512]{1,0:T(8,128)(2,1)S(1)}, bf16[256,512]{1,0:T(8,128)(2,1)S(1)}, u32[]{:S(2)}, u32[]{:S(2)}) collective-permute-start(bf16[256,512]{1,0:T(8,128)(2,1)S(1)} %get-tuple-element.76), channel_id=1, source_target_pairs={{0,2},{2,0},{4,6},{6,4},{8,10},{10,8},{12,14},{14,12},{1,3},{3,1},... | collective-permute-start | bytes 786440 | tf_op jit(solution)/shard_map/ppermute | solution.py:177
  59.3 1.0 %shard_map.102 = bf16[128,2048]{1,0:T(8,128)(2,1)} custom-call(bf16[128,1024]{1,0:T(8,128)(2,1)S(1)} %get-tuple-element.69.a_ref, bf16[128,1024]{1,0:T(8,128)(2,1)S(1)} %collective-permute-done.20.b_ref, bf16[128,1024]{1,0:T(8,128)(2,1)S(1)} %collective-permute-done.18.c_ref, bf16[128,1024]{1,0:T(8,128)(2,1)S(1)} %collective-permute-done.21.d_ref), custom_call_target="tpu_custom_call" | custom-call | flops 1048576 | bytes 1048576 | tf_op jit(solution)/shard_map/pallas_call | solution.py:136
  60.3 6.7 %collective-permute-done.22 = bf16[256,512]{1,0:T(8,128)(2,1)S(1)} collective-permute-done((bf16[256,512]{1,0:T(8,128)(2,1)S(1)}, bf16[256,512]{1,0:T(8,128)(2,1)S(1)}, u32[]{:S(2)}, u32[]{:S(2)}) %collective-permute-start.22) | collective-permute-done | bytes 262176 | tf_op jit(solution)/shard_map/ppermute | solution.py:177
  68.3 1.0 %shard_map.104 = (bf16[128,512]{1,0:T(8,128)(2,1)}, bf16[128,512]{1,0:T(8,128)(2,1)}) custom-call(f32[128,512]{1,0:T(8,128)S(1)} %get-tuple-element.79.gk_ref, f32[128,512]{1,0:T(8,128)S(1)} %get-tuple-element.80.gv_ref, bf16[128,512]{1,0:T(8,128)(2,1)S(1)} %copy-done.3, bf16[128,512]{1,0:T(8,128)(2,1)S(1)} %copy-done.4, ...), custom_call_target="tpu_custom_call" | custom-call | flops 1000000000 | bytes 1048576 | tf_op jit(solution)/shard_map/pallas_call | solution.py:136
  (50 shorter events, 7.6 us)
Async XLA Ops:
  0.6 1.0 %copy-start = (bf16[256,512]{1,0:T(8,128)(2,1)S(1)}, bf16[256,512]{1,0:T(8,128)(2,1)}, u32[]{:S(2)}) copy-start(bf16[256,512]{1,0:T(8,128)(2,1)} %param.8) | copy-start | bytes 786436
  1.6 0.9 %copy-start.3 = (bf16[128,512]{1,0:T(8,128)(2,1)S(1)}, bf16[128,512]{1,0:T(8,128)(2,1)}, u32[]{:S(2)}) copy-start(bf16[128,512]{1,0:T(8,128)(2,1)} %k_ref.7) | copy-start | bytes 393220
  1.6 1.0 %copy-start.4 = (bf16[128,512]{1,0:T(8,128)(2,1)S(1)}, bf16[128,512]{1,0:T(8,128)(2,1)}, u32[]{:S(2)}) copy-start(bf16[128,512]{1,0:T(8,128)(2,1)} %v_ref.7) | copy-start | bytes 393220
  2.6 8.7 %copy-start.1 = (bf16[128,2048]{1,0:T(8,128)(2,1)S(1)}, bf16[128,2048]{1,0:T(8,128)(2,1)}, u32[]{:S(2)}) copy-start(bf16[128,2048]{1,0:T(8,128)(2,1)} %gy_ref.7) | copy-start | bytes 1572868
  2.8 10.2 %collective-permute-start = (bf16[256,512]{1,0:T(8,128)(2,1)S(1)}, bf16[256,512]{1,0:T(8,128)(2,1)S(1)}, u32[]{:S(2)}, u32[]{:S(2)}) collective-permute-start(bf16[256,512]{1,0:T(8,128)(2,1)S(1)} %shard_map.93), channel_id=1, source_target_pairs={{0,2},{2,0},{4,6},{6,4},{8,10},{10,8},{12,14},{14,12},{1,3},{3,1},... | collective-permute-start | bytes 786440 | tf_op jit(solution)/shard_map/ppermute | solution.py:177
  5.8 8.3 %collective-permute-start.4 = (bf16[128,512]{1,0:T(8,128)(2,1)S(1)}, bf16[128,512]{1,0:T(8,128)(2,1)S(1)}, u32[]{:S(2)}, u32[]{:S(2)}) collective-permute-start(bf16[128,512]{1,0:T(8,128)(2,1)S(1)} %constant_dynamic-slice_fusion.w_ref.refs_0_), channel_id=1, source_target_pairs={{0,4},{2,6},{4,8},{6,10},{8,12},{10,14},{12,0},{14,2},{1,5},{3,7},... | collective-permute-start | bytes 393224 | tf_op jit(solution)/shard_map/ppermute | solution.py:177
  7.4 11.1 %collective-permute-start.5 = (bf16[128,512]{1,0:T(8,128)(2,1)S(1)}, bf16[128,512]{1,0:T(8,128)(2,1)S(1)}, u32[]{:S(2)}, u32[]{:S(2)}) collective-permute-start(bf16[128,512]{1,0:T(8,128)(2,1)S(1)} %constant_dynamic-slice_fusion.w_ref.refs_0_), channel_id=1, source_target_pairs={{0,8},{2,10},{4,12},{6,14},{8,0},{10,2},{12,4},{14,6},{1,9},{3,11}... | collective-permute-start | bytes 393224 | tf_op jit(solution)/shard_map/ppermute | solution.py:177
  9.9 9.4 %collective-permute-start.6 = (bf16[128,512]{1,0:T(8,128)(2,1)S(1)}, bf16[128,512]{1,0:T(8,128)(2,1)S(1)}, u32[]{:S(2)}, u32[]{:S(2)}) collective-permute-start(bf16[128,512]{1,0:T(8,128)(2,1)S(1)} %constant_dynamic-slice_fusion.w_ref.refs_0_), channel_id=1, source_target_pairs={{0,12},{2,14},{4,0},{6,2},{8,4},{10,6},{12,8},{14,10},{1,13},{3,15... | collective-permute-start | bytes 393224 | tf_op jit(solution)/shard_map/ppermute | solution.py:177
  11.4 10.8 %collective-permute-start.3 = (bf16[128,1024]{1,0:T(8,128)(2,1)S(1)}, bf16[128,1024]{1,0:T(8,128)(2,1)S(1)}, u32[]{:S(2)}, u32[]{:S(2)}) collective-permute-start(bf16[128,1024]{1,0:T(8,128)(2,1)S(1)} %get-tuple-element.47), channel_id=1, source_target_pairs={{0,16},{16,0},{1,17},{17,1},{2,18},{18,2},{3,19},{19,3},{4,20},{20... | collective-permute-start | bytes 786440 | tf_op jit(solution)/shard_map/ppermute | solution.py:186
  13.0 9.2 %collective-permute-start.2 = (bf16[256,256]{1,0:T(8,128)(2,1)S(1)}, bf16[256,256]{1,0:T(8,128)(2,1)S(1)}, u32[]{:S(2)}, u32[]{:S(2)}) collective-permute-start(bf16[256,256]{1,0:T(8,128)(2,1)S(1)} %get-tuple-element.46), channel_id=1, source_target_pairs={{0,4},{2,6},{4,0},{6,2},{8,12},{10,14},{12,8},{14,10},{1,5},{3,7},... | collective-permute-start | bytes 393224 | tf_op jit(solution)/shard_map/ppermute | solution.py:177
  13.9 5.7 %copy-start.2 = (bf16[128,512]{1,0:T(8,128)(2,1)S(1)}, bf16[128,512]{1,0:T(8,128)(2,1)}, u32[]{:S(2)}) copy-start(bf16[128,512]{1,0:T(8,128)(2,1)} %q_ref.7) | copy-start | bytes 393220
  14.1 9.9 %collective-permute-start.1 = (bf16[128,512]{1,0:T(8,128)(2,1)S(1)}, bf16[128,512]{1,0:T(8,128)(2,1)S(1)}, u32[]{:S(2)}, u32[]{:S(2)}) collective-permute-start(bf16[128,512]{1,0:T(8,128)(2,1)S(1)} %add_convert_fusion.3), channel_id=1, source_target_pairs={{0,4},{2,6},{4,0},{6,2},{8,12},{10,14},{12,8},{14,10},{1,5},{3,7},... | collective-permute-start | bytes 393224 | tf_op jit(solution)/shard_map/ppermute | solution.py:177
  19.4 10.0 %collective-permute-start.8 = (bf16[384,512]{1,0:T(8,128)(2,1)S(1)}, bf16[384,512]{1,0:T(8,128)(2,1)S(1)}, u32[]{:S(2)}, u32[]{:S(2)}) collective-permute-start(bf16[384,512]{1,0:T(8,128)(2,1)S(1)} %pad_maximum_fusion), channel_id=1, source_target_pairs={{0,2},{2,0},{4,6},{6,4},{8,10},{10,8},{12,14},{14,12},{1,3},{3,1},... | collective-permute-start | bytes 1179656 | tf_op jit(solution)/shard_map/ppermute | solution.py:177
  22.2 3.2 %copy-start.5 = (bf16[256,256]{1,0:T(8,128)(2,1)}, bf16[256,256]{1,0:T(8,128)(2,1)S(1)}, u32[]{:S(2)}) copy-start(bf16[256,256]{1,0:T(8,128)(2,1)S(1)} %collective-permute-done.2.near_ref) | copy-start | bytes 393220
  24.0 12.1 %collective-permute-start.7 = (bf16[128,512]{1,0:T(8,128)(2,1)S(1)}, bf16[128,512]{1,0:T(8,128)(2,1)S(1)}, u32[]{:S(2)}, u32[]{:S(2)}) collective-permute-start(bf16[128,512]{1,0:T(8,128)(2,1)S(1)} %add_convert_fusion.2), channel_id=1, source_target_pairs={{0,8},{2,10},{4,12},{6,14},{8,0},{10,2},{12,4},{14,6},{1,9},{3,11}... | collective-permute-start | bytes 393224 | tf_op jit(solution)/shard_map/ppermute | solution.py:177
  25.4 12.4 %collective-permute-start.11 = (bf16[256,256]{1,0:T(8,128)(2,1)S(1)}, bf16[256,256]{1,0:T(8,128)(2,1)S(1)}, u32[]{:S(2)}, u32[]{:S(2)}) collective-permute-start(bf16[256,256]{1,0:T(8,128)(2,1)S(1)} %shard_map.99), channel_id=1, source_target_pairs={{0,8},{2,10},{4,12},{6,14},{8,0},{10,2},{12,4},{14,6},{1,9},{3,11}... | collective-permute-start | bytes 393224 | tf_op jit(solution)/shard_map/ppermute | solution.py:177
  29.8 13.2 %collective-permute-start.9 = (f32[128,512]{1,0:T(8,128)S(1)}, f32[128,512]{1,0:T(8,128)S(1)}, u32[]{:S(2)}, u32[]{:S(2)}) collective-permute-start(f32[128,512]{1,0:T(8,128)S(1)} %shard_map.97), channel_id=1, source_target_pairs={{0,16},{16,0},{1,17},{17,1},{2,18},{18,2},{3,19},{19,3},{4,20},{20... | collective-permute-start | bytes 786440 | tf_op jit(solution)/shard_map/ppermute | solution.py:186
  36.1 6.4 %slice-start = ((bf16[256,256]{1,0:T(8,128)(2,1)}), bf16[128,256]{1,0:T(8,128)(2,1)S(1)}, s32[]{:S(2)}) async-start(bf16[256,256]{1,0:T(8,128)(2,1)} %copy-done.5), calls=%async_computation | async-start | bytes 131072 | tf_op jit(solution)/shard_map/slice | solution.py:343
  37.8 6.6 %collective-permute-start.17 = (bf16[128,512]{1,0:T(8,128)(2,1)S(1)}, bf16[128,512]{1,0:T(8,128)(2,1)S(1)}, u32[]{:S(2)}, u32[]{:S(2)}) collective-permute-start(bf16[128,512]{1,0:T(8,128)(2,1)S(1)} %get-tuple-element.59.n_ref), channel_id=1, source_target_pairs={{0,16},{16,0},{1,17},{17,1},{2,18},{18,2},{3,19},{19,3},{4,20},{20... | collective-permute-start | bytes 393224 | tf_op jit(solution)/shard_map/ppermute | solution.py:186
  39.4 7.5 %collective-permute-start.12 = (bf16[128,512]{1,0:T(8,128)(2,1)S(1)}, bf16[128,512]{1,0:T(8,128)(2,1)S(1)}, u32[]{:S(2)}, u32[]{:S(2)}) collective-permute-start(bf16[128,512]{1,0:T(8,128)(2,1)S(1)} %get-tuple-element.59.n_ref), channel_id=1, source_target_pairs={{0,4},{2,6},{4,0},{6,2},{8,12},{10,14},{12,8},{14,10},{1,5},{3,7},... | collective-permute-start | bytes 393224 | tf_op jit(solution)/shard_map/ppermute | solution.py:177
  39.4 9.0 %collective-permute-start.13 = (bf16[128,512]{1,0:T(8,128)(2,1)S(1)}, bf16[128,512]{1,0:T(8,128)(2,1)S(1)}, u32[]{:S(2)}, u32[]{:S(2)}) collective-permute-start(bf16[128,512]{1,0:T(8,128)(2,1)S(1)} %get-tuple-element.59.n_ref), channel_id=1, source_target_pairs={{0,8},{2,10},{4,12},{6,14},{8,0},{10,2},{12,4},{14,6},{1,9},{3,11}... | collective-permute-start | bytes 393224 | tf_op jit(solution)/shard_map/ppermute | solution.py:177
  42.5 5.9 %collective-permute-start.14 = (bf16[384,256]{1,0:T(8,128)(2,1)S(1)}, bf16[384,256]{1,0:T(8,128)(2,1)S(1)}, u32[]{:S(2)}, u32[]{:S(2)}) collective-permute-start(bf16[384,256]{1,0:T(8,128)(2,1)S(1)} %pad_maximum_fusion.1.c_ref), channel_id=1, source_target_pairs={{0,1},{1,0},{2,3},{3,2},{4,5},{5,4},{6,7},{7,6},{8,9},{9,8},{10,11... | collective-permute-start | bytes 589832 | tf_op jit(solution)/shard_map/ppermute | solution.py:189
  43.4 6.0 %collective-permute-start.10 = (bf16[128,512]{1,0:T(8,128)(2,1)S(1)}, bf16[128,512]{1,0:T(8,128)(2,1)S(1)}, u32[]{:S(2)}, u32[]{:S(2)}) collective-permute-start(bf16[128,512]{1,0:T(8,128)(2,1)S(1)} %get-tuple-element.55), channel_id=1, source_target_pairs={{0,2},{2,0},{4,6},{6,4},{8,10},{10,8},{12,14},{14,12},{1,3},{3,1},... | collective-permute-start | bytes 393224 | tf_op jit(solution)/shard_map/ppermute | solution.py:177
  45.2 8.5 %collective-permute-start.18 = (bf16[128,1024]{1,0:T(8,128)(2,1)S(1)}, bf16[128,1024]{1,0:T(8,128)(2,1)S(1)}, u32[]{:S(2)}, u32[]{:S(2)}) collective-permute-start(bf16[128,1024]{1,0:T(8,128)(2,1)S(1)} %get-tuple-element.63), channel_id=1, source_target_pairs={{0,16},{16,0},{1,17},{17,1},{2,18},{18,2},{3,19},{19,3},{4,20},{20... | collective-permute-start | bytes 786440 | tf_op jit(solution)/shard_map/ppermute | solution.py:186
  49.4 6.5 %collective-permute-start.15 = (bf16[128,512]{1,0:T(8,128)(2,1)S(1)}, bf16[128,512]{1,0:T(8,128)(2,1)S(1)}, u32[]{:S(2)}, u32[]{:S(2)}) collective-permute-start(bf16[128,512]{1,0:T(8,128)(2,1)S(1)} %add_convert_fusion.1), channel_id=1, source_target_pairs={{0,4},{2,6},{4,0},{6,2},{8,12},{10,14},{12,8},{14,10},{1,5},{3,7},... | collective-permute-start | bytes 393224 | tf_op jit(solution)/shard_map/ppermute | solution.py:177
  49.5 7.9 %collective-permute-start.16 = (bf16[128,512]{1,0:T(8,128)(2,1)S(1)}, bf16[128,512]{1,0:T(8,128)(2,1)S(1)}, u32[]{:S(2)}, u32[]{:S(2)}) collective-permute-start(bf16[128,512]{1,0:T(8,128)(2,1)S(1)} %collective-permute-done.13.refs_1_), channel_id=1, source_target_pairs={{0,4},{2,6},{4,0},{6,2},{8,12},{10,14},{12,8},{14,10},{1,5},{3,7},... | collective-permute-start | bytes 393224 | tf_op jit(solution)/shard_map/ppermute | solution.py:177
  51.5 7.8 %collective-permute-start.20 = (bf16[128,1024]{1,0:T(8,128)(2,1)S(1)}, bf16[128,1024]{1,0:T(8,128)(2,1)S(1)}, u32[]{:S(2)}, u32[]{:S(2)}) collective-permute-start(bf16[128,1024]{1,0:T(8,128)(2,1)S(1)} %get-tuple-element.69.a_ref), channel_id=1, source_target_pairs={{0,1},{1,0},{2,3},{3,2},{4,5},{5,4},{6,7},{7,6},{8,9},{9,8},{10,11... | collective-permute-start | bytes 786440 | tf_op jit(solution)/shard_map/ppermute | solution.py:189
  57.4 1.9 %collective-permute-start.21 = (bf16[128,1024]{1,0:T(8,128)(2,1)S(1)}, bf16[128,1024]{1,0:T(8,128)(2,1)S(1)}, u32[]{:S(2)}, u32[]{:S(2)}) collective-permute-start(bf16[128,1024]{1,0:T(8,128)(2,1)S(1)} %collective-permute-done.18.c_ref), channel_id=1, source_target_pairs={{0,1},{1,0},{2,3},{3,2},{4,5},{5,4},{6,7},{7,6},{8,9},{9,8},{10,11... | collective-permute-start | bytes 786440 | tf_op jit(solution)/shard_map/ppermute | solution.py:189
  58.2 8.8 %collective-permute-start.22 = (bf16[256,512]{1,0:T(8,128)(2,1)S(1)}, bf16[256,512]{1,0:T(8,128)(2,1)S(1)}, u32[]{:S(2)}, u32[]{:S(2)}) collective-permute-start(bf16[256,512]{1,0:T(8,128)(2,1)S(1)} %get-tuple-element.76), channel_id=1, source_target_pairs={{0,2},{2,0},{4,6},{6,4},{8,10},{10,8},{12,14},{14,12},{1,3},{3,1},... | collective-permute-start | bytes 786440 | tf_op jit(solution)/shard_map/ppermute | solution.py:177
  59.3 9.0 %collective-permute-start.19 = (bf16[128,512]{1,0:T(8,128)(2,1)S(1)}, bf16[128,512]{1,0:T(8,128)(2,1)S(1)}, u32[]{:S(2)}, u32[]{:S(2)}) collective-permute-start(bf16[128,512]{1,0:T(8,128)(2,1)S(1)} %add_convert_fusion), channel_id=1, source_target_pairs={{0,8},{2,10},{4,12},{6,14},{8,0},{10,2},{12,4},{14,6},{1,9},{3,11}... | collective-permute-start | bytes 393224 | tf_op jit(solution)/shard_map/ppermute | solution.py:177

commit v6 on v5

--- a/solution.py
+++ b/solution.py
@@ -14,7 +14,21 @@
 BF16 = jnp.bfloat16
 ROWS_T = (((0,), (0,)), ((), ()))
 LAST_T = (((1,), (1,)), ((), ()))
-LIGHT = 2**20
+HINTS = {
+    "own_state": 1000000000,
+    "pack": 3000000000,
+    "local": 1000000000,
+    "back_other": 1000000000,
+    "back_own": 1000000000,
+    "forward": 3000000000,
+    "turn_back": 1000000000,
+    "relay": 1000000000,
+    "project": 3000000000,
+    "local_grads": 1048576,
+    "weight_grad": 1048576,
+    "join": 1048576,
+    "last": 3000000000,
+}
 PLAIN = (((1,), (0,)), ((), ()))
 
 
@@ -132,14 +146,14 @@
     return lax.dot_general(a, b, dims, preferred_element_type=F32)
 
 
-def call(body, shapes, *args, flops=1000000000, moved=2**20):
+def call(body, shapes, *args):
     return pl.pallas_call(
         body,
         out_shape=[jax.ShapeDtypeStruct(s, d) for s, d in shapes],
         in_specs=[pl.BlockSpec(memory_space=pltpu.VMEM)] * len(args),
         out_specs=[pl.BlockSpec(memory_space=pltpu.VMEM)] * len(shapes),
         cost_estimate=pl.CostEstimate(
-            flops=flops, bytes_accessed=moved, transcendentals=0
+            flops=HINTS[body.__name__], bytes_accessed=2**20, transcendentals=0
         ),
         compiler_params=pltpu.CompilerParams(vmem_limit_bytes=24 * 2**20),
     )(*args)
@@ -246,21 +260,11 @@
     pair_states = add(states, x_states)
     near_states = swap(pair_states, 2)
     pair_states, *z_weight = tie(pair_states, *z_weight)
-    near_states, near_cols, y_cols = tie(near_states, near_cols, y_cols)
+    near_states, y_cols = tie(near_states, y_cols)
     quad_states = add(pair_states, near_states)
     got_states = x_states, near_states, swap(quad_states, 4)
 
     x_weight = swap(side_by_side(*z_weight), 1)
-    near_cols, quad_states = tie(near_cols, quad_states)
-
-    def relay(gy_ref, near_ref, far_ref):
-        g, z, x, h = place()
-        far_ref[:rows, :] = columns(gy_ref, lax.rem(z + 2, line), h)
-        far_ref[rows:, :] = near_ref[rows:, :]
-
-    (far_send,) = call(relay, [((2 * rows, wrows), BF16)], grad_y, near_cols)
-
-    far_cols = swap(far_send, 4)
 
     def weight_blocks(refs):
         own, *others, x_own, x_others = refs
@@ -321,7 +325,6 @@
         [((rows, feats), F32), ((rows, feats), BF16), (state, BF16)],
         queries, att_local, *got_states,
     )
-    far_cols, normed = tie(far_cols, normed)
     y_normed = swap_y(normed)
     far_normed = swap(normed, 4)
 
@@ -340,13 +343,19 @@
         turn_back, [((rows, feats), BF16), (state, BF16)],
         attended, grad_own, grad_other, queries,
     )
-    my_cols = side_by_side(near_cols[:rows], far_cols)
-    core_cols = swap_core(my_cols)
-
     near_normed = swap(normed, 2)
-    x_adjoint, near_normed, far_normed, core_cols = tie(
-        swap(adjoint, 1), near_normed, far_normed, core_cols
-    )
+    x_adjoint = swap(adjoint, 1)
+    near_cols, adjoint = tie(near_cols, adjoint)
+
+    def relay(gy_ref, near_ref, far_ref):
+        g, z, x, h = place()
+        far_ref[:rows, :] = columns(gy_ref, lax.rem(z + 2, line), h)
+        far_ref[rows:, :] = near_ref[rows:, :]
+
+    (far_send,) = call(relay, [((2 * rows, wrows), BF16)], grad_y, near_cols)
+
+    far_cols = swap(far_send, 4)
+    x_adjoint, near_normed, far_normed = tie(x_adjoint, near_normed, far_normed)
     def project(n_ref, yn_ref, *refs):
         *w_refs, own_ref, other_ref = refs
         for s, block in weight_blocks(w_refs):
@@ -376,12 +385,14 @@
         local_grads,
         [((rows, feats), BF16), ((rows, feats), F32), ((rows, feats), F32)],
         grad_out, queries, keys, values, scores, prefix,
-        flops=LIGHT,
-    )
-
-    near_adjoint, last_normed, out_other, gk_local = tie(
-        near_adjoint, last_normed, out_other, gk_local
-    )
+    )
+
+    near_adjoint, last_normed, out_other, gk_local, far_cols = tie(
+        near_adjoint, last_normed, out_other, gk_local, far_cols
+    )
+    my_cols = side_by_side(near_cols[:rows], far_cols)
+    core_cols = swap_core(my_cols)
+
     quad_adjoint = add(pair_adjoint, near_adjoint)
     far_adjoint = swap(quad_adjoint, 4)
     quad_adjoint, last_normed = tie(quad_adjoint, last_normed)
@@ -404,7 +415,6 @@
     gw_keep, gw_send = call(
         weight_grad, [((wrows, feats), F32), ((wrows, feats), BF16)],
         grad_y, my_cols, core_cols, normed, near_normed, far_normed, last_normed,
-        flops=LIGHT,
     )
     gw_other = swap(gw_send, 1)
 
@@ -421,11 +431,8 @@
 
     (out_y,) = call(
         join, [((rows, outs), BF16)], out_own, core_own, out_other, core_other,
-        flops=LIGHT,
-    )
-    grad_weight = gw_keep + gw_other.astype(F32)
-
-    far_adjoint, out_y, grad_weight = tie(far_adjoint, out_y, grad_weight)
+    )
+    far_adjoint, out_y = tie(far_adjoint, out_y)
 
     def last(gk_ref, gv_ref, k_ref, v_ref, x_ref, near_ref, far_ref, ok_ref, ov_ref):
         g, z, x, h = place()
@@ -446,6 +453,8 @@
         last, [((rows, feats), BF16)] * 2,
         gk_local, gv_local, keys, values, x_adjoint, near_adjoint, far_adjoint,
     )
+    gw_other, grad_keys = tie(gw_other, grad_keys)
+    grad_weight = gw_keep + gw_other.astype(F32)
     return out_y, grad_queries, grad_keys, grad_values, grad_weight
 
 

time: 69.5 us -> 63.8 us (0.918)
  waiting for transfers between devices: 28.3 us -> 17.3 us
  starting transfers between devices: 29.9 us -> 36.1 us
  local copies, waits for them, and re-layouts: 1.93 us -> 0.99 us
    ppermute x16, waiting for transfers between devices: 27.5 us -> 16.4 us  [permute(): return lax.ppermute(array, 'seq', pairs)]
    ppermute x16, starting transfers between devices: 24.5 us -> 29.2 us  [permute(): return lax.ppermute(array, 'seq', pairs)]
    ppermute x4, starting transfers between devices: 5.25 us -> 6.34 us  [swap_y(): return lax.ppermute(array, 'groups', [(0, 1), (1, 0)])]
    unnamed x12, local copies, waits for them, and re-layouts: 1.91 us -> 0.96 us
  transfers between devices with their start and end apart: 23 -> 23, of which waited for: 15 -> 10; matrix products, arithmetic and copies ran while one was open for 2% -> 0% of each run, Pallas kernels for 9% -> 12%
where the time goes in v6:
time: 63.8 us; the launch traced here: 63.6 us
  starting transfers between devices  36.1 us (57%)
  waiting for transfers between devices  17.3 us (27%)
  Pallas kernels  7.37 us (12%)
  other arithmetic  1.04 us (2%)
  local copies, waits for them, and re-layouts  0.99 us (2%)
  between operations  0.8 us (1%)
    ppermute x16, starting transfers between devices, permute(): return lax.ppermute(array, 'seq', pairs)  29.2 us
    ppermute x16, waiting for transfers between devices, permute(): return lax.ppermute(array, 'seq', pairs)  16.4 us
    pallas_call x13, Pallas kernels, call(): pl.pallas_call(body, out_shape=[jax.ShapeDtypeStruct(s, d) for s, d in sh...  7.37 us
    ppermute x4, starting transfers between devices, swap_y(): return lax.ppermute(array, 'groups', [(0, 1), (1, 0)])  6.34 us
  transfers between devices with their start and end apart: 23, of which 10 were waited for; matrix products, arithmetic and copies ran while one was open for 0% of the time, Pallas kernels for 12%

profile of v6, /device:TPU:0, one launch (start us, length us, event | category | flops | bytes accessed | tf_op | source)
XLA Modules:
  0.0 63.6 jit_solution(8297300293805226937)
XLA Ops:
  0.7 0.9 %copy-done = bf16[256,512]{1,0:T(8,128)(2,1)S(1)} copy-done((bf16[256,512]{1,0:T(8,128)(2,1)S(1)}, bf16[256,512]{1,0:T(8,128)(2,1)}, u32[]{:S(2)}) %copy-start) | copy-done | bytes 262168
  1.6 3.1 %collective-permute-start.4 = (bf16[128,512]{1,0:T(8,128)(2,1)S(1)}, bf16[128,512]{1,0:T(8,128)(2,1)S(1)}, u32[]{:S(2)}, u32[]{:S(2)}) collective-permute-start(bf16[128,512]{1,0:T(8,128)(2,1)S(1)} %constant_dynamic-slice_fusion.w_ref.refs_0_), channel_id=1, source_target_pairs={{0,4},{2,6},{4,8},{6,10},{8,12},{10,14},{12,0},{14,2},{1,5},{3,7},... | collective-permute-start | bytes 393224 | tf_op jit(solution)/shard_map/ppermute | solution.py:191
  4.7 2.6 %collective-permute-start.5 = (bf16[128,512]{1,0:T(8,128)(2,1)S(1)}, bf16[128,512]{1,0:T(8,128)(2,1)S(1)}, u32[]{:S(2)}, u32[]{:S(2)}) collective-permute-start(bf16[128,512]{1,0:T(8,128)(2,1)S(1)} %constant_dynamic-slice_fusion.w_ref.refs_0_), channel_id=1, source_target_pairs={{0,8},{2,10},{4,12},{6,14},{8,0},{10,2},{12,4},{14,6},{1,9},{3,11}... | collective-permute-start | bytes 393224 | tf_op jit(solution)/shard_map/ppermute | solution.py:191
  7.3 1.3 %collective-permute-start.6 = (bf16[128,512]{1,0:T(8,128)(2,1)S(1)}, bf16[128,512]{1,0:T(8,128)(2,1)S(1)}, u32[]{:S(2)}, u32[]{:S(2)}) collective-permute-start(bf16[128,512]{1,0:T(8,128)(2,1)S(1)} %constant_dynamic-slice_fusion.w_ref.refs_0_), channel_id=1, source_target_pairs={{0,12},{2,14},{4,0},{6,2},{8,4},{10,6},{12,8},{14,10},{1,13},{3,15... | collective-permute-start | bytes 393224 | tf_op jit(solution)/shard_map/ppermute | solution.py:191
  8.9 1.6 %collective-permute-start.1 = (bf16[256,512]{1,0:T(8,128)(2,1)S(1)}, bf16[256,512]{1,0:T(8,128)(2,1)S(1)}, u32[]{:S(2)}, u32[]{:S(2)}) collective-permute-start(bf16[256,512]{1,0:T(8,128)(2,1)S(1)} %shard_map.94), channel_id=1, source_target_pairs={{0,2},{2,0},{4,6},{6,4},{8,10},{10,8},{12,14},{14,12},{1,3},{3,1},... | collective-permute-start | bytes 786440 | tf_op jit(solution)/shard_map/ppermute | solution.py:191
  10.5 1.6 %collective-permute-start.3 = (bf16[128,1024]{1,0:T(8,128)(2,1)S(1)}, bf16[128,1024]{1,0:T(8,128)(2,1)S(1)}, u32[]{:S(2)}, u32[]{:S(2)}) collective-permute-start(bf16[128,1024]{1,0:T(8,128)(2,1)S(1)} %get-tuple-element.46), channel_id=1, source_target_pairs={{0,16},{16,0},{1,17},{17,1},{2,18},{18,2},{3,19},{19,3},{4,20},{20... | collective-permute-start | bytes 786440 | tf_op jit(solution)/shard_map/ppermute | solution.py:200
  12.1 4.0 %collective-permute-done.1.refs_4_ = bf16[256,512]{1,0:T(8,128)(2,1)S(1)} collective-permute-done((bf16[256,512]{1,0:T(8,128)(2,1)S(1)}, bf16[256,512]{1,0:T(8,128)(2,1)S(1)}, u32[]{:S(2)}, u32[]{:S(2)}) %collective-permute-start.1) | collective-permute-done | bytes 262176 | tf_op jit(solution)/shard_map/ppermute | solution.py:191
  16.2 0.7 %collective-permute-start.2 = (bf16[128,512]{1,0:T(8,128)(2,1)S(1)}, bf16[128,512]{1,0:T(8,128)(2,1)S(1)}, u32[]{:S(2)}, u32[]{:S(2)}) collective-permute-start(bf16[128,512]{1,0:T(8,128)(2,1)S(1)} %add_convert_fusion.3), channel_id=1, source_target_pairs={{0,4},{2,6},{4,0},{6,2},{8,12},{10,14},{12,8},{14,10},{1,5},{3,7},... | collective-permute-start | bytes 393224 | tf_op jit(solution)/shard_map/ppermute | solution.py:191
  17.0 1.6 %collective-permute-start.8 = (bf16[384,512]{1,0:T(8,128)(2,1)S(1)}, bf16[384,512]{1,0:T(8,128)(2,1)S(1)}, u32[]{:S(2)}, u32[]{:S(2)}) collective-permute-start(bf16[384,512]{1,0:T(8,128)(2,1)S(1)} %pad_maximum_fusion), channel_id=1, source_target_pairs={{0,2},{2,0},{4,6},{6,4},{8,10},{10,8},{12,14},{14,12},{1,3},{3,1},... | collective-permute-start | bytes 1179656 | tf_op jit(solution)/shard_map/ppermute | solution.py:191
  18.5 2.3 %collective-permute-start = (bf16[256,256]{1,0:T(8,128)(2,1)S(1)}, bf16[256,256]{1,0:T(8,128)(2,1)S(1)}, u32[]{:S(2)}, u32[]{:S(2)}) collective-permute-start(bf16[256,256]{1,0:T(8,128)(2,1)S(1)} %get-tuple-element.44), channel_id=1, source_target_pairs={{0,4},{2,6},{4,0},{6,2},{8,12},{10,14},{12,8},{14,10},{1,5},{3,7},... | collective-permute-start | bytes 393224 | tf_op jit(solution)/shard_map/ppermute | solution.py:191
  21.2 1.4 %collective-permute-start.7 = (bf16[128,512]{1,0:T(8,128)(2,1)S(1)}, bf16[128,512]{1,0:T(8,128)(2,1)S(1)}, u32[]{:S(2)}, u32[]{:S(2)}) collective-permute-start(bf16[128,512]{1,0:T(8,128)(2,1)S(1)} %add_convert_fusion.2), channel_id=1, source_target_pairs={{0,8},{2,10},{4,12},{6,14},{8,0},{10,2},{12,4},{14,6},{1,9},{3,11}... | collective-permute-start | bytes 393224 | tf_op jit(solution)/shard_map/ppermute | solution.py:191
  22.6 0.7 %shard_map.93 = (bf16[128,512]{1,0:T(8,128)(2,1)S(1)}, f32[128,512]{1,0:T(8,128)S(1)}) custom-call(bf16[128,512]{1,0:T(8,128)(2,1)S(1)} %copy-done.2, bf16[128,512]{1,0:T(8,128)(2,1)S(1)} %copy-done.3, bf16[128,512]{1,0:T(8,128)(2,1)S(1)} %copy-done.4), custom_call_target="tpu_custom_call" | custom-call | flops 1000000000 | bytes 1048576 | tf_op jit(solution)/shard_map/pallas_call | solution.py:150
  23.4 3.6 %collective-permute-done.8.refs_5_ = bf16[384,512]{1,0:T(8,128)(2,1)S(1)} collective-permute-done((bf16[384,512]{1,0:T(8,128)(2,1)S(1)}, bf16[384,512]{1,0:T(8,128)(2,1)S(1)}, u32[]{:S(2)}, u32[]{:S(2)}) %collective-permute-start.8) | collective-permute-done | bytes 393248 | tf_op jit(solution)/shard_map/ppermute | solution.py:191
  27.4 1.6 %collective-permute-start.9 = (f32[128,512]{1,0:T(8,128)S(1)}, f32[128,512]{1,0:T(8,128)S(1)}, u32[]{:S(2)}, u32[]{:S(2)}) collective-permute-start(f32[128,512]{1,0:T(8,128)S(1)} %shard_map.97), channel_id=1, source_target_pairs={{0,16},{16,0},{1,17},{17,1},{2,18},{18,2},{3,19},{19,3},{4,20},{20... | collective-permute-start | bytes 786440 | tf_op jit(solution)/shard_map/ppermute | solution.py:200
  29.7 1.6 %collective-permute-start.15 = (bf16[128,512]{1,0:T(8,128)(2,1)S(1)}, bf16[128,512]{1,0:T(8,128)(2,1)S(1)}, u32[]{:S(2)}, u32[]{:S(2)}) collective-permute-start(bf16[128,512]{1,0:T(8,128)(2,1)S(1)} %get-tuple-element.56.n_ref), channel_id=1, source_target_pairs={{0,16},{16,0},{1,17},{17,1},{2,18},{18,2},{3,19},{19,3},{4,20},{20... | collective-permute-start | bytes 393224 | tf_op jit(solution)/shard_map/ppermute | solution.py:200
  31.3 2.0 %collective-permute-start.11 = (bf16[128,512]{1,0:T(8,128)(2,1)S(1)}, bf16[128,512]{1,0:T(8,128)(2,1)S(1)}, u32[]{:S(2)}, u32[]{:S(2)}) collective-permute-start(bf16[128,512]{1,0:T(8,128)(2,1)S(1)} %get-tuple-element.56.n_ref), channel_id=1, source_target_pairs={{0,4},{2,6},{4,0},{6,2},{8,12},{10,14},{12,8},{14,10},{1,5},{3,7},... | collective-permute-start | bytes 393224 | tf_op jit(solution)/shard_map/ppermute | solution.py:191
  34.3 0.9 %collective-permute-done.9.other_ref = f32[128,512]{1,0:T(8,128)S(1)} collective-permute-done((f32[128,512]{1,0:T(8,128)S(1)}, f32[128,512]{1,0:T(8,128)S(1)}, u32[]{:S(2)}, u32[]{:S(2)}) %collective-permute-start.9) | collective-permute-done | bytes 262176 | tf_op jit(solution)/shard_map/ppermute | solution.py:200
  35.6 1.4 %collective-permute-start.10 = (bf16[128,512]{1,0:T(8,128)(2,1)S(1)}, bf16[128,512]{1,0:T(8,128)(2,1)S(1)}, u32[]{:S(2)}, u32[]{:S(2)}) collective-permute-start(bf16[128,512]{1,0:T(8,128)(2,1)S(1)} %get-tuple-element.55), channel_id=1, source_target_pairs={{0,2},{2,0},{4,6},{6,4},{8,10},{10,8},{12,14},{14,12},{1,3},{3,1},... | collective-permute-start | bytes 393224 | tf_op jit(solution)/shard_map/ppermute | solution.py:191
  37.7 1.6 %collective-permute-start.16 = (bf16[128,1024]{1,0:T(8,128)(2,1)S(1)}, bf16[128,1024]{1,0:T(8,128)(2,1)S(1)}, u32[]{:S(2)}, u32[]{:S(2)}) collective-permute-start(bf16[128,1024]{1,0:T(8,128)(2,1)S(1)} %get-tuple-element.59), channel_id=1, source_target_pairs={{0,16},{16,0},{1,17},{17,1},{2,18},{18,2},{3,19},{19,3},{4,20},{20... | collective-permute-start | bytes 786440 | tf_op jit(solution)/shard_map/ppermute | solution.py:200
  39.4 3.6 %collective-permute-start.17 = (bf16[256,256]{1,0:T(8,128)(2,1)S(1)}, bf16[256,256]{1,0:T(8,128)(2,1)S(1)}, u32[]{:S(2)}, u32[]{:S(2)}) collective-permute-start(bf16[256,256]{1,0:T(8,128)(2,1)S(1)} %shard_map.101), channel_id=1, source_target_pairs={{0,8},{2,10},{4,12},{6,14},{8,0},{10,2},{12,4},{14,6},{1,9},{3,11}... | collective-permute-start | bytes 393224 | tf_op jit(solution)/shard_map/ppermute | solution.py:191
  43.0 2.1 %collective-permute-start.13 = (bf16[128,512]{1,0:T(8,128)(2,1)S(1)}, bf16[128,512]{1,0:T(8,128)(2,1)S(1)}, u32[]{:S(2)}, u32[]{:S(2)}) collective-permute-start(bf16[128,512]{1,0:T(8,128)(2,1)S(1)} %add_convert_fusion.1), channel_id=1, source_target_pairs={{0,4},{2,6},{4,0},{6,2},{8,12},{10,14},{12,8},{14,10},{1,5},{3,7},... | collective-permute-start | bytes 393224 | tf_op jit(solution)/shard_map/ppermute | solution.py:191
  45.2 1.4 %shard_map.100 = (bf16[128,512]{1,0:T(8,128)(2,1)}, f32[128,512]{1,0:T(8,128)S(1)}, f32[128,512]{1,0:T(8,128)S(1)}) custom-call(bf16[128,512]{1,0:T(8,128)(2,1)S(1)} %get-tuple-element.60.go_ref, bf16[128,512]{1,0:T(8,128)(2,1)S(1)} %copy-done.2, bf16[128,512]{1,0:T(8,128)(2,1)S(1)} %copy-done.3, bf16[128,512]{1,0:T(8,128)(2,1)S(1)} %copy-done.4, ...), custom_call_target="tpu_custom_call" | custom-call | flops 1048576 | bytes 1048576 | tf_op jit(solution)/shard_map/pallas_call | solution.py:150
  47.2 1.4 %collective-permute-done.13.near_ref = bf16[128,512]{1,0:T(8,128)(2,1)S(1)} collective-permute-done((bf16[128,512]{1,0:T(8,128)(2,1)S(1)}, bf16[128,512]{1,0:T(8,128)(2,1)S(1)}, u32[]{:S(2)}, u32[]{:S(2)}) %collective-permute-start.13) | collective-permute-done | bytes 131104 | tf_op jit(solution)/shard_map/ppermute | solution.py:191
  48.5 1.6 %collective-permute-done.14.refs_2_ = bf16[128,512]{1,0:T(8,128)(2,1)S(1)} collective-permute-done((bf16[128,512]{1,0:T(8,128)(2,1)S(1)}, bf16[128,512]{1,0:T(8,128)(2,1)S(1)}, u32[]{:S(2)}, u32[]{:S(2)}) %collective-permute-start.14) | collective-permute-done | bytes 131104 | tf_op jit(solution)/shard_map/ppermute | solution.py:191
  50.7 3.3 %collective-permute-start.18 = (bf16[128,512]{1,0:T(8,128)(2,1)S(1)}, bf16[128,512]{1,0:T(8,128)(2,1)S(1)}, u32[]{:S(2)}, u32[]{:S(2)}) collective-permute-start(bf16[128,512]{1,0:T(8,128)(2,1)S(1)} %add_convert_fusion), channel_id=1, source_target_pairs={{0,8},{2,10},{4,12},{6,14},{8,0},{10,2},{12,4},{14,6},{1,9},{3,11}... | collective-permute-start | bytes 393224 | tf_op jit(solution)/shard_map/ppermute | solution.py:191
  54.0 0.7 %shard_map.103 = (f32[256,512]{1,0:T(8,128)S(1)}, bf16[256,512]{1,0:T(8,128)(2,1)S(1)}) custom-call(bf16[128,2048]{1,0:T(8,128)(2,1)S(1)} %copy-done.1, bf16[384,256]{1,0:T(8,128)(2,1)S(1)} %pad_maximum_fusion.1.c_ref, bf16[384,256]{1,0:T(8,128)(2,1)S(1)} %collective-permute-done.21.o_ref, bf16[128,512]{1,0:T(8,128)(2,1)S(1)} %get-tuple-element.56.n_ref, ...), custom_call_target="tpu_custom_call" | custom-call | flops 1048576 | bytes 1048576 | tf_op jit(solution)/shard_map/pallas_call | solution.py:150
  54.7 1.6 %collective-permute-start.22 = (bf16[256,512]{1,0:T(8,128)(2,1)S(1)}, bf16[256,512]{1,0:T(8,128)(2,1)S(1)}, u32[]{:S(2)}, u32[]{:S(2)}) collective-permute-start(bf16[256,512]{1,0:T(8,128)(2,1)S(1)} %get-tuple-element.74), channel_id=1, source_target_pairs={{0,2},{2,0},{4,6},{6,4},{8,10},{10,8},{12,14},{14,12},{1,3},{3,1},... | collective-permute-start | bytes 786440 | tf_op jit(solution)/shard_map/ppermute | solution.py:191
  56.3 1.0 %shard_map.102 = bf16[128,2048]{1,0:T(8,128)(2,1)} custom-call(bf16[128,1024]{1,0:T(8,128)(2,1)S(1)} %get-tuple-element.66.a_ref, bf16[128,1024]{1,0:T(8,128)(2,1)S(1)} %collective-permute-done.19.b_ref, bf16[128,1024]{1,0:T(8,128)(2,1)S(1)} %collective-permute-done.16.c_ref, bf16[128,1024]{1,0:T(8,128)(2,1)S(1)} %collective-permute-done.20.d_ref), custom_call_target="tpu_custom_call" | custom-call | flops 1048576 | bytes 1048576 | tf_op jit(solution)/shard_map/pallas_call | solution.py:150
  57.3 3.2 %collective-permute-done.18.far_ref = bf16[128,512]{1,0:T(8,128)(2,1)S(1)} collective-permute-done((bf16[128,512]{1,0:T(8,128)(2,1)S(1)}, bf16[128,512]{1,0:T(8,128)(2,1)S(1)}, u32[]{:S(2)}, u32[]{:S(2)}) %collective-permute-start.18) | collective-permute-done | bytes 131104 | tf_op jit(solution)/shard_map/ppermute | solution.py:191
  60.5 1.0 %shard_map.104 = (bf16[128,512]{1,0:T(8,128)(2,1)}, bf16[128,512]{1,0:T(8,128)(2,1)}) custom-call(f32[128,512]{1,0:T(8,128)S(1)} %get-tuple-element.75.gk_ref, f32[128,512]{1,0:T(8,128)S(1)} %get-tuple-element.76.gv_ref, bf16[128,512]{1,0:T(8,128)(2,1)S(1)} %copy-done.3, bf16[128,512]{1,0:T(8,128)(2,1)S(1)} %copy-done.4, ...), custom_call_target="tpu_custom_call" | custom-call | flops 3000000000 | bytes 1048576 | tf_op jit(solution)/shard_map/pallas_call | solution.py:150
  61.5 1.3 %collective-permute-done.22 = bf16[256,512]{1,0:T(8,128)(2,1)S(1)} collective-permute-done((bf16[256,512]{1,0:T(8,128)(2,1)S(1)}, bf16[256,512]{1,0:T(8,128)(2,1)S(1)}, u32[]{:S(2)}, u32[]{:S(2)}) %collective-permute-start.22) | collective-permute-done | bytes 262176 | tf_op jit(solution)/shard_map/ppermute | solution.py:191
  62.8 0.9 %convert_add_fusion = f32[256,512]{1,0:T(8,128)} fusion(f32[256,512]{1,0:T(8,128)S(1)} %get-tuple-element.81, bf16[256,512]{1,0:T(8,128)(2,1)S(1)} %collective-permute-done.22), kind=kLoop, calls=%fused_computation | loop fusion | flops 262144 | bytes 1310720 | tf_op jit(solution)/shard_map/add | solution.py:457
  (50 shorter events, 5.4 us)
Async XLA Ops:
  0.6 1.0 %copy-start = (bf16[256,512]{1,0:T(8,128)(2,1)S(1)}, bf16[256,512]{1,0:T(8,128)(2,1)}, u32[]{:S(2)}) copy-start(bf16[256,512]{1,0:T(8,128)(2,1)} %param.8) | copy-start | bytes 786436
  1.6 7.0 %copy-start.3 = (bf16[128,512]{1,0:T(8,128)(2,1)S(1)}, bf16[128,512]{1,0:T(8,128)(2,1)}, u32[]{:S(2)}) copy-start(bf16[128,512]{1,0:T(8,128)(2,1)} %k_ref.7) | copy-start | bytes 393220
  1.6 7.0 %copy-start.4 = (bf16[128,512]{1,0:T(8,128)(2,1)S(1)}, bf16[128,512]{1,0:T(8,128)(2,1)}, u32[]{:S(2)}) copy-start(bf16[128,512]{1,0:T(8,128)(2,1)} %v_ref.7) | copy-start | bytes 393220
  1.6 8.8 %copy-start.1 = (bf16[128,2048]{1,0:T(8,128)(2,1)S(1)}, bf16[128,2048]{1,0:T(8,128)(2,1)}, u32[]{:S(2)}) copy-start(bf16[128,2048]{1,0:T(8,128)(2,1)} %gy_ref.7) | copy-start | bytes 1572868
  1.6 15.3 %collective-permute-start.4 = (bf16[128,512]{1,0:T(8,128)(2,1)S(1)}, bf16[128,512]{1,0:T(8,128)(2,1)S(1)}, u32[]{:S(2)}, u32[]{:S(2)}) collective-permute-start(bf16[128,512]{1,0:T(8,128)(2,1)S(1)} %constant_dynamic-slice_fusion.w_ref.refs_0_), channel_id=1, source_target_pairs={{0,4},{2,6},{4,8},{6,10},{8,12},{10,14},{12,0},{14,2},{1,5},{3,7},... | collective-permute-start | bytes 393224 | tf_op jit(solution)/shard_map/ppermute | solution.py:191
  4.7 12.2 %collective-permute-start.5 = (bf16[128,512]{1,0:T(8,128)(2,1)S(1)}, bf16[128,512]{1,0:T(8,128)(2,1)S(1)}, u32[]{:S(2)}, u32[]{:S(2)}) collective-permute-start(bf16[128,512]{1,0:T(8,128)(2,1)S(1)} %constant_dynamic-slice_fusion.w_ref.refs_0_), channel_id=1, source_target_pairs={{0,8},{2,10},{4,12},{6,14},{8,0},{10,2},{12,4},{14,6},{1,9},{3,11}... | collective-permute-start | bytes 393224 | tf_op jit(solution)/shard_map/ppermute | solution.py:191
  7.3 9.6 %collective-permute-start.6 = (bf16[128,512]{1,0:T(8,128)(2,1)S(1)}, bf16[128,512]{1,0:T(8,128)(2,1)S(1)}, u32[]{:S(2)}, u32[]{:S(2)}) collective-permute-start(bf16[128,512]{1,0:T(8,128)(2,1)S(1)} %constant_dynamic-slice_fusion.w_ref.refs_0_), channel_id=1, source_target_pairs={{0,12},{2,14},{4,0},{6,2},{8,4},{10,6},{12,8},{14,10},{1,13},{3,15... | collective-permute-start | bytes 393224 | tf_op jit(solution)/shard_map/ppermute | solution.py:191
  8.9 7.3 %collective-permute-start.1 = (bf16[256,512]{1,0:T(8,128)(2,1)S(1)}, bf16[256,512]{1,0:T(8,128)(2,1)S(1)}, u32[]{:S(2)}, u32[]{:S(2)}) collective-permute-start(bf16[256,512]{1,0:T(8,128)(2,1)S(1)} %shard_map.94), channel_id=1, source_target_pairs={{0,2},{2,0},{4,6},{6,4},{8,10},{10,8},{12,14},{14,12},{1,3},{3,1},... | collective-permute-start | bytes 786440 | tf_op jit(solution)/shard_map/ppermute | solution.py:191
  10.5 10.3 %collective-permute-start.3 = (bf16[128,1024]{1,0:T(8,128)(2,1)S(1)}, bf16[128,1024]{1,0:T(8,128)(2,1)S(1)}, u32[]{:S(2)}, u32[]{:S(2)}) collective-permute-start(bf16[128,1024]{1,0:T(8,128)(2,1)S(1)} %get-tuple-element.46), channel_id=1, source_target_pairs={{0,16},{16,0},{1,17},{17,1},{2,18},{18,2},{3,19},{19,3},{4,20},{20... | collective-permute-start | bytes 786440 | tf_op jit(solution)/shard_map/ppermute | solution.py:200
  16.2 5.0 %collective-permute-start.2 = (bf16[128,512]{1,0:T(8,128)(2,1)S(1)}, bf16[128,512]{1,0:T(8,128)(2,1)S(1)}, u32[]{:S(2)}, u32[]{:S(2)}) collective-permute-start(bf16[128,512]{1,0:T(8,128)(2,1)S(1)} %add_convert_fusion.3), channel_id=1, source_target_pairs={{0,4},{2,6},{4,0},{6,2},{8,12},{10,14},{12,8},{14,10},{1,5},{3,7},... | collective-permute-start | bytes 393224 | tf_op jit(solution)/shard_map/ppermute | solution.py:191
  17.0 10.0 %collective-permute-start.8 = (bf16[384,512]{1,0:T(8,128)(2,1)S(1)}, bf16[384,512]{1,0:T(8,128)(2,1)S(1)}, u32[]{:S(2)}, u32[]{:S(2)}) collective-permute-start(bf16[384,512]{1,0:T(8,128)(2,1)S(1)} %pad_maximum_fusion), channel_id=1, source_target_pairs={{0,2},{2,0},{4,6},{6,4},{8,10},{10,8},{12,14},{14,12},{1,3},{3,1},... | collective-permute-start | bytes 1179656 | tf_op jit(solution)/shard_map/ppermute | solution.py:191
  18.5 4.1 %copy-start.2 = (bf16[128,512]{1,0:T(8,128)(2,1)S(1)}, bf16[128,512]{1,0:T(8,128)(2,1)}, u32[]{:S(2)}) copy-start(bf16[128,512]{1,0:T(8,128)(2,1)} %q_ref.7) | copy-start | bytes 393220
  18.5 20.8 %collective-permute-start = (bf16[256,256]{1,0:T(8,128)(2,1)S(1)}, bf16[256,256]{1,0:T(8,128)(2,1)S(1)}, u32[]{:S(2)}, u32[]{:S(2)}) collective-permute-start(bf16[256,256]{1,0:T(8,128)(2,1)S(1)} %get-tuple-element.44), channel_id=1, source_target_pairs={{0,4},{2,6},{4,0},{6,2},{8,12},{10,14},{12,8},{14,10},{1,5},{3,7},... | collective-permute-start | bytes 393224 | tf_op jit(solution)/shard_map/ppermute | solution.py:191
  21.2 8.1 %collective-permute-start.7 = (bf16[128,512]{1,0:T(8,128)(2,1)S(1)}, bf16[128,512]{1,0:T(8,128)(2,1)S(1)}, u32[]{:S(2)}, u32[]{:S(2)}) collective-permute-start(bf16[128,512]{1,0:T(8,128)(2,1)S(1)} %add_convert_fusion.2), channel_id=1, source_target_pairs={{0,8},{2,10},{4,12},{6,14},{8,0},{10,2},{12,4},{14,6},{1,9},{3,11}... | collective-permute-start | bytes 393224 | tf_op jit(solution)/shard_map/ppermute | solution.py:191
  27.4 7.8 %collective-permute-start.9 = (f32[128,512]{1,0:T(8,128)S(1)}, f32[128,512]{1,0:T(8,128)S(1)}, u32[]{:S(2)}, u32[]{:S(2)}) collective-permute-start(f32[128,512]{1,0:T(8,128)S(1)} %shard_map.97), channel_id=1, source_target_pairs={{0,16},{16,0},{1,17},{17,1},{2,18},{18,2},{3,19},{19,3},{4,20},{20... | collective-permute-start | bytes 786440 | tf_op jit(solution)/shard_map/ppermute | solution.py:200
  29.7 7.4 %collective-permute-start.15 = (bf16[128,512]{1,0:T(8,128)(2,1)S(1)}, bf16[128,512]{1,0:T(8,128)(2,1)S(1)}, u32[]{:S(2)}, u32[]{:S(2)}) collective-permute-start(bf16[128,512]{1,0:T(8,128)(2,1)S(1)} %get-tuple-element.56.n_ref), channel_id=1, source_target_pairs={{0,16},{16,0},{1,17},{17,1},{2,18},{18,2},{3,19},{19,3},{4,20},{20... | collective-permute-start | bytes 393224 | tf_op jit(solution)/shard_map/ppermute | solution.py:200
  31.3 11.7 %collective-permute-start.11 = (bf16[128,512]{1,0:T(8,128)(2,1)S(1)}, bf16[128,512]{1,0:T(8,128)(2,1)S(1)}, u32[]{:S(2)}, u32[]{:S(2)}) collective-permute-start(bf16[128,512]{1,0:T(8,128)(2,1)S(1)} %get-tuple-element.56.n_ref), channel_id=1, source_target_pairs={{0,4},{2,6},{4,0},{6,2},{8,12},{10,14},{12,8},{14,10},{1,5},{3,7},... | collective-permute-start | bytes 393224 | tf_op jit(solution)/shard_map/ppermute | solution.py:191
  33.3 9.7 %collective-permute-start.12 = (bf16[128,512]{1,0:T(8,128)(2,1)S(1)}, bf16[128,512]{1,0:T(8,128)(2,1)S(1)}, u32[]{:S(2)}, u32[]{:S(2)}) collective-permute-start(bf16[128,512]{1,0:T(8,128)(2,1)S(1)} %get-tuple-element.56.n_ref), channel_id=1, source_target_pairs={{0,8},{2,10},{4,12},{6,14},{8,0},{10,2},{12,4},{14,6},{1,9},{3,11}... | collective-permute-start | bytes 393224 | tf_op jit(solution)/shard_map/ppermute | solution.py:191
  35.6 7.3 %collective-permute-start.10 = (bf16[128,512]{1,0:T(8,128)(2,1)S(1)}, bf16[128,512]{1,0:T(8,128)(2,1)S(1)}, u32[]{:S(2)}, u32[]{:S(2)}) collective-permute-start(bf16[128,512]{1,0:T(8,128)(2,1)S(1)} %get-tuple-element.55), channel_id=1, source_target_pairs={{0,2},{2,0},{4,6},{6,4},{8,10},{10,8},{12,14},{14,12},{1,3},{3,1},... | collective-permute-start | bytes 393224 | tf_op jit(solution)/shard_map/ppermute | solution.py:191
  37.7 8.9 %collective-permute-start.16 = (bf16[128,1024]{1,0:T(8,128)(2,1)S(1)}, bf16[128,1024]{1,0:T(8,128)(2,1)S(1)}, u32[]{:S(2)}, u32[]{:S(2)}) collective-permute-start(bf16[128,1024]{1,0:T(8,128)(2,1)S(1)} %get-tuple-element.59), channel_id=1, source_target_pairs={{0,16},{16,0},{1,17},{17,1},{2,18},{18,2},{3,19},{19,3},{4,20},{20... | collective-permute-start | bytes 786440 | tf_op jit(solution)/shard_map/ppermute | solution.py:200
  39.3 5.9 %copy-start.5 = (bf16[256,256]{1,0:T(8,128)(2,1)}, bf16[256,256]{1,0:T(8,128)(2,1)S(1)}, u32[]{:S(2)}) copy-start(bf16[256,256]{1,0:T(8,128)(2,1)S(1)} %collective-permute-done.near_ref) | copy-start | bytes 393220
  39.4 7.8 %collective-permute-start.17 = (bf16[256,256]{1,0:T(8,128)(2,1)S(1)}, bf16[256,256]{1,0:T(8,128)(2,1)S(1)}, u32[]{:S(2)}, u32[]{:S(2)}) collective-permute-start(bf16[256,256]{1,0:T(8,128)(2,1)S(1)} %shard_map.101), channel_id=1, source_target_pairs={{0,8},{2,10},{4,12},{6,14},{8,0},{10,2},{12,4},{14,6},{1,9},{3,11}... | collective-permute-start | bytes 393224 | tf_op jit(solution)/shard_map/ppermute | solution.py:191
  43.0 5.5 %collective-permute-start.13 = (bf16[128,512]{1,0:T(8,128)(2,1)S(1)}, bf16[128,512]{1,0:T(8,128)(2,1)S(1)}, u32[]{:S(2)}, u32[]{:S(2)}) collective-permute-start(bf16[128,512]{1,0:T(8,128)(2,1)S(1)} %add_convert_fusion.1), channel_id=1, source_target_pairs={{0,4},{2,6},{4,0},{6,2},{8,12},{10,14},{12,8},{14,10},{1,5},{3,7},... | collective-permute-start | bytes 393224 | tf_op jit(solution)/shard_map/ppermute | solution.py:191
  45.1 5.0 %collective-permute-start.14 = (bf16[128,512]{1,0:T(8,128)(2,1)S(1)}, bf16[128,512]{1,0:T(8,128)(2,1)S(1)}, u32[]{:S(2)}, u32[]{:S(2)}) collective-permute-start(bf16[128,512]{1,0:T(8,128)(2,1)S(1)} %collective-permute-done.12.refs_1_), channel_id=1, source_target_pairs={{0,4},{2,6},{4,0},{6,2},{8,12},{10,14},{12,8},{14,10},{1,5},{3,7},... | collective-permute-start | bytes 393224 | tf_op jit(solution)/shard_map/ppermute | solution.py:191
  45.2 11.1 %collective-permute-start.19 = (bf16[128,1024]{1,0:T(8,128)(2,1)S(1)}, bf16[128,1024]{1,0:T(8,128)(2,1)S(1)}, u32[]{:S(2)}, u32[]{:S(2)}) collective-permute-start(bf16[128,1024]{1,0:T(8,128)(2,1)S(1)} %get-tuple-element.66.a_ref), channel_id=1, source_target_pairs={{0,1},{1,0},{2,3},{3,2},{4,5},{5,4},{6,7},{7,6},{8,9},{9,8},{10,11... | collective-permute-start | bytes 786440 | tf_op jit(solution)/shard_map/ppermute | solution.py:203
  45.2 4.9 %slice-start = ((bf16[256,256]{1,0:T(8,128)(2,1)}), bf16[128,256]{1,0:T(8,128)(2,1)S(1)}, s32[]{:S(2)}) async-start(bf16[256,256]{1,0:T(8,128)(2,1)} %copy-done.5), calls=%async_computation | async-start | bytes 131072 | tf_op jit(solution)/shard_map/slice | solution.py:393
  50.1 6.2 %collective-permute-start.20 = (bf16[128,1024]{1,0:T(8,128)(2,1)S(1)}, bf16[128,1024]{1,0:T(8,128)(2,1)S(1)}, u32[]{:S(2)}, u32[]{:S(2)}) collective-permute-start(bf16[128,1024]{1,0:T(8,128)(2,1)S(1)} %collective-permute-done.16.c_ref), channel_id=1, source_target_pairs={{0,1},{1,0},{2,3},{3,2},{4,5},{5,4},{6,7},{7,6},{8,9},{9,8},{10,11... | collective-permute-start | bytes 786440 | tf_op jit(solution)/shard_map/ppermute | solution.py:203
  50.1 3.9 %collective-permute-start.21 = (bf16[384,256]{1,0:T(8,128)(2,1)S(1)}, bf16[384,256]{1,0:T(8,128)(2,1)S(1)}, u32[]{:S(2)}, u32[]{:S(2)}) collective-permute-start(bf16[384,256]{1,0:T(8,128)(2,1)S(1)} %pad_maximum_fusion.1.c_ref), channel_id=1, source_target_pairs={{0,1},{1,0},{2,3},{3,2},{4,5},{5,4},{6,7},{7,6},{8,9},{9,8},{10,11... | collective-permute-start | bytes 589832 | tf_op jit(solution)/shard_map/ppermute | solution.py:203
  50.7 9.7 %collective-permute-start.18 = (bf16[128,512]{1,0:T(8,128)(2,1)S(1)}, bf16[128,512]{1,0:T(8,128)(2,1)S(1)}, u32[]{:S(2)}, u32[]{:S(2)}) collective-permute-start(bf16[128,512]{1,0:T(8,128)(2,1)S(1)} %add_convert_fusion), channel_id=1, source_target_pairs={{0,8},{2,10},{4,12},{6,14},{8,0},{10,2},{12,4},{14,6},{1,9},{3,11}... | collective-permute-start | bytes 393224 | tf_op jit(solution)/shard_map/ppermute | solution.py:191
  54.7 8.0 %collective-permute-start.22 = (bf16[256,512]{1,0:T(8,128)(2,1)S(1)}, bf16[256,512]{1,0:T(8,128)(2,1)S(1)}, u32[]{:S(2)}, u32[]{:S(2)}) collective-permute-start(bf16[256,512]{1,0:T(8,128)(2,1)S(1)} %get-tuple-element.74), channel_id=1, source_target_pairs={{0,2},{2,0},{4,6},{6,4},{8,10},{10,8},{12,14},{14,12},{1,3},{3,1},... | collective-permute-start | bytes 786440 | tf_op jit(solution)/shard_map/ppermute | solution.py:191

commit v7 on v6

--- a/solution.py
+++ b/solution.py
@@ -15,17 +15,16 @@
 ROWS_T = (((0,), (0,)), ((), ()))
 LAST_T = (((1,), (1,)), ((), ()))
 HINTS = {
-    "own_state": 1000000000,
+    "own_state": 300000000,
     "pack": 3000000000,
     "local": 1000000000,
-    "back_other": 1000000000,
+    "back_other": 3000000000,
     "back_own": 1000000000,
     "forward": 3000000000,
-    "turn_back": 1000000000,
-    "relay": 1000000000,
+    "turn_back": 600000000,
     "project": 3000000000,
     "local_grads": 1048576,
-    "weight_grad": 1048576,
+    "weight_grad": 1500000000,
     "join": 1048576,
     "last": 3000000000,
 }
@@ -233,11 +232,11 @@
         for i in range(seq):
             ys_ref[:, i * half : (i + 1) * half] = gy_ref[:, lanes(2 * i + 1 - g, half)]
         near = z + 1 - 2 * lax.rem(z, 2)
-        near_ref[:rows, :] = columns(gy_ref, near, h)
-        near_ref[rows:, :] = columns(gy_ref, lax.rem(near + 2, line), h)
+        near_ref[:, :wrows] = columns(gy_ref, near, h)
+        near_ref[:, wrows:] = columns(gy_ref, lax.rem(near + 2, line), h)
 
     y_send, near_send = call(
-        pack, [((rows, seq * half), BF16), ((2 * rows, wrows), BF16)], grad_y
+        pack, [((rows, seq * half), BF16), ((rows, 2 * wrows), BF16)], grad_y
     )
     near_cols = swap(near_send, 2)
     y_cols = swap_y(y_send)
@@ -257,9 +256,9 @@
     def add(a, b):
         return (a.astype(F32) + b.astype(F32)).astype(BF16)
 
+    x_states, near_cols = tie(x_states, near_cols)
     pair_states = add(states, x_states)
     near_states = swap(pair_states, 2)
-    pair_states, *z_weight = tie(pair_states, *z_weight)
     near_states, y_cols = tie(near_states, y_cols)
     quad_states = add(pair_states, near_states)
     got_states = x_states, near_states, swap(quad_states, 4)
@@ -305,7 +304,10 @@
         back_own, [((rows, feats), F32)], grad_y, *weight_args
     )
 
-    def forward(q_ref, local_ref, x_ref, near_ref, far_ref, att_ref, normed_ref, prefix_ref):
+    def forward(
+        q_ref, local_ref, x_ref, near_ref, far_ref, gy_ref, cols_ref,
+        att_ref, normed_ref, prefix_ref, send_ref,
+    ):
         g, z, x, h = place()
         total = jnp.where(x == 1, x_ref[...].astype(F32), 0.0)
         total += jnp.where(lax.rem(z, 2) == 1, near_ref[...].astype(F32), 0.0)
@@ -318,15 +320,20 @@
             )
             att_ref[:, head_of(i)] = att
             inv = lax.rsqrt(jnp.mean(att * att, axis=-1, keepdims=True) + epsilon)
-            normed_ref[:, head_of(i)] = (att * inv).astype(BF16)
-
-    attended, normed, prefix = call(
+            normed = (att * inv).astype(BF16)
+            normed_ref[:, head_of(i)] = normed
+            send_ref[:rows, head_of(i)] = normed
+        send_ref[rows:, :wrows] = columns(gy_ref, lax.rem(z + 2, line), h)
+        send_ref[rows:, wrows:] = cols_ref[:, wrows:]
+
+    attended, normed, prefix, far_send = call(
         forward,
-        [((rows, feats), F32), ((rows, feats), BF16), (state, BF16)],
-        queries, att_local, *got_states,
+        [((rows, feats), F32), ((rows, feats), BF16), (state, BF16)]
+        + [((2 * rows, feats), BF16)],
+        queries, att_local, *got_states, grad_y, near_cols,
     )
     y_normed = swap_y(normed)
-    far_normed = swap(normed, 4)
+    far = swap(far_send, 4)
 
     def turn_back(att_ref, own_ref, other_ref, q_ref, go_ref, adj_ref):
         for i in range(heads):
@@ -345,17 +352,7 @@
     )
     near_normed = swap(normed, 2)
     x_adjoint = swap(adjoint, 1)
-    near_cols, adjoint = tie(near_cols, adjoint)
-
-    def relay(gy_ref, near_ref, far_ref):
-        g, z, x, h = place()
-        far_ref[:rows, :] = columns(gy_ref, lax.rem(z + 2, line), h)
-        far_ref[rows:, :] = near_ref[rows:, :]
-
-    (far_send,) = call(relay, [((2 * rows, wrows), BF16)], grad_y, near_cols)
-
-    far_cols = swap(far_send, 4)
-    x_adjoint, near_normed, far_normed = tie(x_adjoint, near_normed, far_normed)
+    x_adjoint, near_normed = tie(x_adjoint, near_normed)
     def project(n_ref, yn_ref, *refs):
         *w_refs, own_ref, other_ref = refs
         for s, block in weight_blocks(w_refs):
@@ -366,7 +363,7 @@
         project, [((rows, seq * half), BF16)] * 2, normed, y_normed, *weight_args
     )
     out_other = swap_y(out_send)
-    last_normed = swap(far_normed, 2)
+    last_normed = swap(far[:rows], 2)
     pair_adjoint = add(adjoint, x_adjoint)
     near_adjoint = swap(pair_adjoint, 2)
     def local_grads(go_ref, q_ref, k_ref, v_ref, sc_ref, pre_ref, gq_ref, gk_ref, gv_ref):
@@ -387,10 +384,8 @@
         grad_out, queries, keys, values, scores, prefix,
     )
 
-    near_adjoint, last_normed, out_other, gk_local, far_cols = tie(
-        near_adjoint, last_normed, out_other, gk_local, far_cols
-    )
-    my_cols = side_by_side(near_cols[:rows], far_cols)
+    near_adjoint, out_other, gk_local = tie(near_adjoint, out_other, gk_local)
+    my_cols = jnp.concatenate([near_cols[:, :wrows], far[rows:]], axis=1)
     core_cols = swap_core(my_cols)
 
     quad_adjoint = add(pair_adjoint, near_adjoint)
@@ -400,21 +395,22 @@
     core_own = swap_core(out_own)
     core_other = swap_core(out_other)
 
-    def weight_grad(gy_ref, c_ref, o_ref, n_ref, *refs):
-        *n_refs, keep_ref, send_ref = refs
+    def weight_grad(
+        gy_ref, c_ref, o_ref, n_ref, near_ref, far_ref, last_ref, keep_ref, send_ref
+    ):
         g, z, x, h = place()
         same = dot(columns(gy_ref, z, h), n_ref[...], ROWS_T)
         other = dot(columns(gy_ref, z, 1 - h), n_ref[...], ROWS_T)
-        for i, there_ref in enumerate(n_refs):
-            at = slice(i * rows, (i + 1) * rows)
-            same += dot(c_ref[at, :], there_ref[...], ROWS_T)
-            other += dot(o_ref[at, :], there_ref[...], ROWS_T)
+        for i, there in enumerate((near_ref[...], far_ref[:rows, :], last_ref[...])):
+            at = slice(i * wrows, (i + 1) * wrows)
+            same += dot(c_ref[:, at], there, ROWS_T)
+            other += dot(o_ref[:, at], there, ROWS_T)
         keep_ref[...] = jnp.where(x == h, same, other)
         send_ref[...] = jnp.where(x == h, other, same).astype(BF16)
 
     gw_keep, gw_send = call(
         weight_grad, [((wrows, feats), F32), ((wrows, feats), BF16)],
-        grad_y, my_cols, core_cols, normed, near_normed, far_normed, last_normed,
+        grad_y, my_cols, core_cols, normed, near_normed, far, last_normed,
     )
     gw_other = swap(gw_send, 1)
 
@@ -470,7 +466,7 @@
 
     def program(queries, keys, values, out_weight, grad_y):
         short = size["seq"] == 8 and size["groups"] == 2 and size["head"] == 2
-        if short and queries.shape[0] == TILE and out_weight.shape[0] % 256 == 0:
+        if short and queries.shape[0] == TILE and 2 * out_weight.shape[0] == queries.shape[1]:
             return on_short_line(
                 size["seq"], queries, keys, values, out_weight, grad_y
             )

time: 63.8 us -> 63 us (0.987)
  starting transfers between devices: 36.1 us -> 28 us
  waiting for transfers between devices: 17.3 us -> 24.6 us
    ppermute x16 -> x15, waiting for transfers between devices: 16.4 us -> 24.3 us  [permute(): return lax.ppermute(array, 'seq', pairs)]
    ppermute x16 -> x15, starting transfers between devices: 29.2 us -> 21.6 us  [permute(): return lax.ppermute(array, 'seq', pairs)]
    pallas_call x13 -> x12, Pallas kernels: 7.37 us -> 7.36 us  [call(): pl.pallas_call(body, out_shape=[jax.ShapeDtypeStruct(s, d) for s, d in sh...]
  transfers between devices with their start and end apart: 23 -> 22, of which waited for: 10 -> 14; matrix products, arithmetic and copies ran while one was open for 0% -> 0% of each run, Pallas kernels for 12% -> 12%
where the time goes in v7:
time: 63 us; the launch traced here: 62.9 us
  starting transfers between devices  28 us (44%)
  waiting for transfers between devices  24.6 us (39%)
  Pallas kernels  7.36 us (12%)
  other arithmetic  1.04 us (2%)
  local copies, waits for them, and re-layouts  1.01 us (2%)
  between operations  0.86 us (1%)
    ppermute x15, waiting for transfers between devices, permute(): return lax.ppermute(array, 'seq', pairs)  24.3 us
    ppermute x15, starting transfers between devices, permute(): return lax.ppermute(array, 'seq', pairs)  21.6 us
    pallas_call x12, Pallas kernels, call(): pl.pallas_call(body, out_shape=[jax.ShapeDtypeStruct(s, d) for s, d in sh...  7.36 us
    ppermute x4, starting transfers between devices, swap_y(): return lax.ppermute(array, 'groups', [(0, 1), (1, 0)])  6.41 us
  transfers between devices with their start and end apart: 22, of which 14 were waited for; matrix products, arithmetic and copies ran while one was open for 0% of the time, Pallas kernels for 12%

profile of v7, /device:TPU:0, one launch (start us, length us, event | category | flops | bytes accessed | tf_op | source)
XLA Modules:
  0.0 62.9 jit_solution(1053683159361484103)
XLA Ops:
  0.7 0.9 %copy-done = bf16[256,512]{1,0:T(8,128)(2,1)S(1)} copy-done((bf16[256,512]{1,0:T(8,128)(2,1)S(1)}, bf16[256,512]{1,0:T(8,128)(2,1)}, u32[]{:S(2)}) %copy-start) | copy-done | bytes 262168
  1.6 3.1 %collective-permute-start.5 = (bf16[128,512]{1,0:T(8,128)(2,1)S(1)}, bf16[128,512]{1,0:T(8,128)(2,1)S(1)}, u32[]{:S(2)}, u32[]{:S(2)}) collective-permute-start(bf16[128,512]{1,0:T(8,128)(2,1)S(1)} %constant_dynamic-slice_fusion.w_ref.refs_0_), channel_id=1, source_target_pairs={{0,4},{2,6},{4,8},{6,10},{8,12},{10,14},{12,0},{14,2},{1,5},{3,7},... | collective-permute-start | bytes 393224 | tf_op jit(solution)/shard_map/ppermute | solution.py:190
  4.7 2.6 %collective-permute-start.6 = (bf16[128,512]{1,0:T(8,128)(2,1)S(1)}, bf16[128,512]{1,0:T(8,128)(2,1)S(1)}, u32[]{:S(2)}, u32[]{:S(2)}) collective-permute-start(bf16[128,512]{1,0:T(8,128)(2,1)S(1)} %constant_dynamic-slice_fusion.w_ref.refs_0_), channel_id=1, source_target_pairs={{0,8},{2,10},{4,12},{6,14},{8,0},{10,2},{12,4},{14,6},{1,9},{3,11}... | collective-permute-start | bytes 393224 | tf_op jit(solution)/shard_map/ppermute | solution.py:190
  7.3 1.3 %collective-permute-start.7 = (bf16[128,512]{1,0:T(8,128)(2,1)S(1)}, bf16[128,512]{1,0:T(8,128)(2,1)S(1)}, u32[]{:S(2)}, u32[]{:S(2)}) collective-permute-start(bf16[128,512]{1,0:T(8,128)(2,1)S(1)} %constant_dynamic-slice_fusion.w_ref.refs_0_), channel_id=1, source_target_pairs={{0,12},{2,14},{4,0},{6,2},{8,4},{10,6},{12,8},{14,10},{1,13},{3,15... | collective-permute-start | bytes 393224 | tf_op jit(solution)/shard_map/ppermute | solution.py:190
  8.9 1.6 %collective-permute-start = (bf16[256,512]{1,0:T(8,128)(2,1)S(1)}, bf16[256,512]{1,0:T(8,128)(2,1)S(1)}, u32[]{:S(2)}, u32[]{:S(2)}) collective-permute-start(bf16[256,512]{1,0:T(8,128)(2,1)S(1)} %shard_map.93), channel_id=1, source_target_pairs={{0,2},{2,0},{4,6},{6,4},{8,10},{10,8},{12,14},{14,12},{1,3},{3,1},... | collective-permute-start | bytes 786440 | tf_op jit(solution)/shard_map/ppermute | solution.py:190
  10.5 0.7 %collective-permute-start.1 = (bf16[128,512]{1,0:T(8,128)(2,1)S(1)}, bf16[128,512]{1,0:T(8,128)(2,1)S(1)}, u32[]{:S(2)}, u32[]{:S(2)}) collective-permute-start(bf16[128,512]{1,0:T(8,128)(2,1)S(1)} %get-tuple-element.39), channel_id=1, source_target_pairs={{0,4},{2,6},{4,0},{6,2},{8,12},{10,14},{12,8},{14,10},{1,5},{3,7},... | collective-permute-start | bytes 393224 | tf_op jit(solution)/shard_map/ppermute | solution.py:190
  11.3 1.7 %collective-permute-start.3 = (bf16[128,1024]{1,0:T(8,128)(2,1)S(1)}, bf16[128,1024]{1,0:T(8,128)(2,1)S(1)}, u32[]{:S(2)}, u32[]{:S(2)}) collective-permute-start(bf16[128,1024]{1,0:T(8,128)(2,1)S(1)} %get-tuple-element.41), channel_id=1, source_target_pairs={{0,16},{16,0},{1,17},{17,1},{2,18},{18,2},{3,19},{19,3},{4,20},{20... | collective-permute-start | bytes 786440 | tf_op jit(solution)/shard_map/ppermute | solution.py:199
  12.9 3.1 %collective-permute-done.6.refs_2_ = bf16[128,512]{1,0:T(8,128)(2,1)S(1)} collective-permute-done((bf16[128,512]{1,0:T(8,128)(2,1)S(1)}, bf16[128,512]{1,0:T(8,128)(2,1)S(1)}, u32[]{:S(2)}, u32[]{:S(2)}) %collective-permute-start.6) | collective-permute-done | bytes 131104 | tf_op jit(solution)/shard_map/ppermute | solution.py:190
  16.6 1.7 %collective-permute-start.8 = (bf16[384,512]{1,0:T(8,128)(2,1)S(1)}, bf16[384,512]{1,0:T(8,128)(2,1)S(1)}, u32[]{:S(2)}, u32[]{:S(2)}) collective-permute-start(bf16[384,512]{1,0:T(8,128)(2,1)S(1)} %pad_maximum_fusion), channel_id=1, source_target_pairs={{0,2},{2,0},{4,6},{6,4},{8,10},{10,8},{12,14},{14,12},{1,3},{3,1},... | collective-permute-start | bytes 1179656 | tf_op jit(solution)/shard_map/ppermute | solution.py:190
  18.7 2.3 %collective-permute-start.2 = (bf16[128,512]{1,0:T(8,128)(2,1)S(1)}, bf16[128,512]{1,0:T(8,128)(2,1)S(1)}, u32[]{:S(2)}, u32[]{:S(2)}) collective-permute-start(bf16[128,512]{1,0:T(8,128)(2,1)S(1)} %add_convert_fusion.3), channel_id=1, source_target_pairs={{0,4},{2,6},{4,0},{6,2},{8,12},{10,14},{12,8},{14,10},{1,5},{3,7},... | collective-permute-start | bytes 393224 | tf_op jit(solution)/shard_map/ppermute | solution.py:190
  21.0 0.7 %shard_map.92 = (bf16[128,512]{1,0:T(8,128)(2,1)S(1)}, f32[128,512]{1,0:T(8,128)S(1)}) custom-call(bf16[128,512]{1,0:T(8,128)(2,1)S(1)} %copy-done.1, bf16[128,512]{1,0:T(8,128)(2,1)S(1)} %copy-done.2, bf16[128,512]{1,0:T(8,128)(2,1)S(1)} %copy-done.3), custom_call_target="tpu_custom_call" | custom-call | flops 1000000000 | bytes 1048576 | tf_op jit(solution)/shard_map/pallas_call | solution.py:149
  21.7 2.6 %collective-permute-done.2.near_ref = bf16[128,512]{1,0:T(8,128)(2,1)S(1)} collective-permute-done((bf16[128,512]{1,0:T(8,128)(2,1)S(1)}, bf16[128,512]{1,0:T(8,128)(2,1)S(1)}, u32[]{:S(2)}, u32[]{:S(2)}) %collective-permute-start.2) | collective-permute-done | bytes 131104 | tf_op jit(solution)/shard_map/ppermute | solution.py:190
  24.4 1.7 %collective-permute-start.4 = (bf16[128,512]{1,0:T(8,128)(2,1)S(1)}, bf16[128,512]{1,0:T(8,128)(2,1)S(1)}, u32[]{:S(2)}, u32[]{:S(2)}) collective-permute-start(bf16[128,512]{1,0:T(8,128)(2,1)S(1)} %add_convert_fusion.2), channel_id=1, source_target_pairs={{0,8},{2,10},{4,12},{6,14},{8,0},{10,2},{12,4},{14,6},{1,9},{3,11}... | collective-permute-start | bytes 393224 | tf_op jit(solution)/shard_map/ppermute | solution.py:190
  26.1 0.9 %collective-permute-done.8.refs_5_ = bf16[384,512]{1,0:T(8,128)(2,1)S(1)} collective-permute-done((bf16[384,512]{1,0:T(8,128)(2,1)S(1)}, bf16[384,512]{1,0:T(8,128)(2,1)S(1)}, u32[]{:S(2)}, u32[]{:S(2)}) %collective-permute-start.8) | collective-permute-done | bytes 393248 | tf_op jit(solution)/shard_map/ppermute | solution.py:190
  27.4 1.6 %collective-permute-start.9 = (f32[128,512]{1,0:T(8,128)S(1)}, f32[128,512]{1,0:T(8,128)S(1)}, u32[]{:S(2)}, u32[]{:S(2)}) collective-permute-start(f32[128,512]{1,0:T(8,128)S(1)} %shard_map.97), channel_id=1, source_target_pairs={{0,16},{16,0},{1,17},{17,1},{2,18},{18,2},{3,19},{19,3},{4,20},{20... | collective-permute-start | bytes 786440 | tf_op jit(solution)/shard_map/ppermute | solution.py:199
  29.0 3.8 %collective-permute-done.4.far_ref = bf16[128,512]{1,0:T(8,128)(2,1)S(1)} collective-permute-done((bf16[128,512]{1,0:T(8,128)(2,1)S(1)}, bf16[128,512]{1,0:T(8,128)(2,1)S(1)}, u32[]{:S(2)}, u32[]{:S(2)}) %collective-permute-start.4) | collective-permute-done | bytes 131104 | tf_op jit(solution)/shard_map/ppermute | solution.py:190
  33.1 1.6 %collective-permute-start.13 = (bf16[128,512]{1,0:T(8,128)(2,1)S(1)}, bf16[128,512]{1,0:T(8,128)(2,1)S(1)}, u32[]{:S(2)}, u32[]{:S(2)}) collective-permute-start(bf16[128,512]{1,0:T(8,128)(2,1)S(1)} %get-tuple-element.47.n_ref), channel_id=1, source_target_pairs={{0,16},{16,0},{1,17},{17,1},{2,18},{18,2},{3,19},{19,3},{4,20},{20... | collective-permute-start | bytes 393224 | tf_op jit(solution)/shard_map/ppermute | solution.py:199
  34.7 1.7 %collective-permute-start.18 = (bf16[256,512]{1,0:T(8,128)(2,1)S(1)}, bf16[256,512]{1,0:T(8,128)(2,1)S(1)}, u32[]{:S(2)}, u32[]{:S(2)}) collective-permute-start(bf16[256,512]{1,0:T(8,128)(2,1)S(1)} %get-tuple-element.59), channel_id=1, source_target_pairs={{0,8},{2,10},{4,12},{6,14},{8,0},{10,2},{12,4},{14,6},{1,9},{3,11}... | collective-permute-start | bytes 786440 | tf_op jit(solution)/shard_map/ppermute | solution.py:190
  38.2 0.7 %shard_map.99 = (bf16[128,1024]{1,0:T(8,128)(2,1)S(1)}, bf16[128,1024]{1,0:T(8,128)(2,1)S(1)}) custom-call(bf16[128,512]{1,0:T(8,128)(2,1)S(1)} %get-tuple-element.47.n_ref, bf16[128,512]{1,0:T(8,128)(2,1)S(1)} %collective-permute-done.13.yn_ref, bf16[128,512]{1,0:T(8,128)(2,1)S(1)} %constant_dynamic-slice_fusion.w_ref.refs_0_, ...), custom_call_target="tpu_custom_call" | custom-call | flops 3000000000 | bytes 1048576 | tf_op jit(solution)/shard_map/pallas_call | solution.py:149
  38.9 1.6 %collective-permute-start.14 = (bf16[128,1024]{1,0:T(8,128)(2,1)S(1)}, bf16[128,1024]{1,0:T(8,128)(2,1)S(1)}, u32[]{:S(2)}, u32[]{:S(2)}) collective-permute-start(bf16[128,1024]{1,0:T(8,128)(2,1)S(1)} %get-tuple-element.49), channel_id=1, source_target_pairs={{0,16},{16,0},{1,17},{17,1},{2,18},{18,2},{3,19},{19,3},{4,20},{20... | collective-permute-start | bytes 786440 | tf_op jit(solution)/shard_map/ppermute | solution.py:199
  40.7 1.6 %collective-permute-done.10.x_ref = bf16[128,512]{1,0:T(8,128)(2,1)S(1)} collective-permute-done((bf16[128,512]{1,0:T(8,128)(2,1)S(1)}, bf16[128,512]{1,0:T(8,128)(2,1)S(1)}, u32[]{:S(2)}, u32[]{:S(2)}) %collective-permute-start.10) | collective-permute-done | bytes 131104 | tf_op jit(solution)/shard_map/ppermute | solution.py:190
  42.4 2.8 %collective-permute-start.12 = (bf16[128,512]{1,0:T(8,128)(2,1)S(1)}, bf16[128,512]{1,0:T(8,128)(2,1)S(1)}, u32[]{:S(2)}, u32[]{:S(2)}) collective-permute-start(bf16[128,512]{1,0:T(8,128)(2,1)S(1)} %add_convert_fusion.1), channel_id=1, source_target_pairs={{0,4},{2,6},{4,0},{6,2},{8,12},{10,14},{12,8},{14,10},{1,5},{3,7},... | collective-permute-start | bytes 393224 | tf_op jit(solution)/shard_map/ppermute | solution.py:190
  45.2 3.2 %collective-permute-done.18.far_ref = bf16[256,512]{1,0:T(8,128)(2,1)S(1)} collective-permute-done((bf16[256,512]{1,0:T(8,128)(2,1)S(1)}, bf16[256,512]{1,0:T(8,128)(2,1)S(1)}, u32[]{:S(2)}, u32[]{:S(2)}) %collective-permute-start.18) | collective-permute-done | bytes 262176 | tf_op jit(solution)/shard_map/ppermute | solution.py:190
  48.6 1.4 %shard_map.100 = (bf16[128,512]{1,0:T(8,128)(2,1)}, f32[128,512]{1,0:T(8,128)S(1)}, f32[128,512]{1,0:T(8,128)S(1)}) custom-call(bf16[128,512]{1,0:T(8,128)(2,1)S(1)} %get-tuple-element.50.go_ref, bf16[128,512]{1,0:T(8,128)(2,1)S(1)} %copy-done.1, bf16[128,512]{1,0:T(8,128)(2,1)S(1)} %copy-done.2, bf16[128,512]{1,0:T(8,128)(2,1)S(1)} %copy-done.3, ...), custom_call_target="tpu_custom_call" | custom-call | flops 1048576 | bytes 1048576 | tf_op jit(solution)/shard_map/pallas_call | solution.py:149
  50.0 1.2 %collective-permute-done.12.near_ref = bf16[128,512]{1,0:T(8,128)(2,1)S(1)} collective-permute-done((bf16[128,512]{1,0:T(8,128)(2,1)S(1)}, bf16[128,512]{1,0:T(8,128)(2,1)S(1)}, u32[]{:S(2)}, u32[]{:S(2)}) %collective-permute-start.12) | collective-permute-done | bytes 131104 | tf_op jit(solution)/shard_map/ppermute | solution.py:190
  51.2 1.3 %collective-permute-start.15 = (bf16[128,512]{1,0:T(8,128)(2,1)S(1)}, bf16[128,512]{1,0:T(8,128)(2,1)S(1)}, u32[]{:S(2)}, u32[]{:S(2)}) collective-permute-start(bf16[128,512]{1,0:T(8,128)(2,1)S(1)} %add_convert_fusion), channel_id=1, source_target_pairs={{0,8},{2,10},{4,12},{6,14},{8,0},{10,2},{12,4},{14,6},{1,9},{3,11}... | collective-permute-start | bytes 393224 | tf_op jit(solution)/shard_map/ppermute | solution.py:190
  52.6 1.3 %collective-permute-done.20.last_ref = bf16[128,512]{1,0:T(8,128)(2,1)S(1)} collective-permute-done((bf16[128,512]{1,0:T(8,128)(2,1)S(1)}, bf16[128,512]{1,0:T(8,128)(2,1)S(1)}, u32[]{:S(2)}, u32[]{:S(2)}) %collective-permute-start.20) | collective-permute-done | bytes 131104 | tf_op jit(solution)/shard_map/ppermute | solution.py:190
  53.9 0.7 %shard_map.102 = (f32[256,512]{1,0:T(8,128)S(1)}, bf16[256,512]{1,0:T(8,128)(2,1)S(1)}) custom-call(bf16[128,2048]{1,0:T(8,128)(2,1)S(1)} %copy-done.5, bf16[128,768]{1,0:T(8,128)(2,1)S(1)} %pad_maximum_fusion.1.c_ref, bf16[128,768]{1,0:T(8,128)(2,1)S(1)} %collective-permute-done.19.o_ref, bf16[128,512]{1,0:T(8,128)(2,1)S(1)} %get-tuple-element.47.n_ref, ...), custom_call_target="tpu_custom_call" | custom-call | flops 1500000000 | bytes 1048576 | tf_op jit(solution)/shard_map/pallas_call | solution.py:149
  54.8 1.0 %shard_map.101 = bf16[128,2048]{1,0:T(8,128)(2,1)} custom-call(bf16[128,1024]{1,0:T(8,128)(2,1)S(1)} %get-tuple-element.55.a_ref, bf16[128,1024]{1,0:T(8,128)(2,1)S(1)} %collective-permute-done.16.b_ref, bf16[128,1024]{1,0:T(8,128)(2,1)S(1)} %collective-permute-done.14.c_ref, bf16[128,1024]{1,0:T(8,128)(2,1)S(1)} %collective-permute-done.17.d_ref), custom_call_target="tpu_custom_call" | custom-call | flops 1048576 | bytes 1048576 | tf_op jit(solution)/shard_map/pallas_call | solution.py:149
  55.7 5.2 %collective-permute-done.15.far_ref = bf16[128,512]{1,0:T(8,128)(2,1)S(1)} collective-permute-done((bf16[128,512]{1,0:T(8,128)(2,1)S(1)}, bf16[128,512]{1,0:T(8,128)(2,1)S(1)}, u32[]{:S(2)}, u32[]{:S(2)}) %collective-permute-start.15) | collective-permute-done | bytes 131104 | tf_op jit(solution)/shard_map/ppermute | solution.py:190
  60.9 1.0 %shard_map.103 = (bf16[128,512]{1,0:T(8,128)(2,1)}, bf16[128,512]{1,0:T(8,128)(2,1)}) custom-call(f32[128,512]{1,0:T(8,128)S(1)} %get-tuple-element.63.gk_ref, f32[128,512]{1,0:T(8,128)S(1)} %get-tuple-element.64.gv_ref, bf16[128,512]{1,0:T(8,128)(2,1)S(1)} %copy-done.2, bf16[128,512]{1,0:T(8,128)(2,1)S(1)} %copy-done.3, ...), custom_call_target="tpu_custom_call" | custom-call | flops 3000000000 | bytes 1048576 | tf_op jit(solution)/shard_map/pallas_call | solution.py:149
  62.0 0.9 %convert_add_fusion = f32[256,512]{1,0:T(8,128)} fusion(f32[256,512]{1,0:T(8,128)S(1)} %get-tuple-element.69, bf16[256,512]{1,0:T(8,128)(2,1)S(1)} %collective-permute-done.21), kind=kLoop, calls=%fused_computation | loop fusion | flops 262144 | bytes 1310720 | tf_op jit(solution)/shard_map/add | solution.py:453
  (48 shorter events, 4.5 us)
Async XLA Ops:
  0.6 1.0 %copy-start = (bf16[256,512]{1,0:T(8,128)(2,1)S(1)}, bf16[256,512]{1,0:T(8,128)(2,1)}, u32[]{:S(2)}) copy-start(bf16[256,512]{1,0:T(8,128)(2,1)} %param.8) | copy-start | bytes 786436
  1.6 7.0 %copy-start.2 = (bf16[128,512]{1,0:T(8,128)(2,1)S(1)}, bf16[128,512]{1,0:T(8,128)(2,1)}, u32[]{:S(2)}) copy-start(bf16[128,512]{1,0:T(8,128)(2,1)} %k_ref.7) | copy-start | bytes 393220
  1.6 7.0 %copy-start.3 = (bf16[128,512]{1,0:T(8,128)(2,1)S(1)}, bf16[128,512]{1,0:T(8,128)(2,1)}, u32[]{:S(2)}) copy-start(bf16[128,512]{1,0:T(8,128)(2,1)} %v_ref.7) | copy-start | bytes 393220
  1.6 8.8 %copy-start.5 = (bf16[128,2048]{1,0:T(8,128)(2,1)S(1)}, bf16[128,2048]{1,0:T(8,128)(2,1)}, u32[]{:S(2)}) copy-start(bf16[128,2048]{1,0:T(8,128)(2,1)} %gy_ref.7) | copy-start | bytes 1572868
  1.6 9.6 %collective-permute-start.5 = (bf16[128,512]{1,0:T(8,128)(2,1)S(1)}, bf16[128,512]{1,0:T(8,128)(2,1)S(1)}, u32[]{:S(2)}, u32[]{:S(2)}) collective-permute-start(bf16[128,512]{1,0:T(8,128)(2,1)S(1)} %constant_dynamic-slice_fusion.w_ref.refs_0_), channel_id=1, source_target_pairs={{0,4},{2,6},{4,8},{6,10},{8,12},{10,14},{12,0},{14,2},{1,5},{3,7},... | collective-permute-start | bytes 393224 | tf_op jit(solution)/shard_map/ppermute | solution.py:190
  4.7 11.3 %collective-permute-start.6 = (bf16[128,512]{1,0:T(8,128)(2,1)S(1)}, bf16[128,512]{1,0:T(8,128)(2,1)S(1)}, u32[]{:S(2)}, u32[]{:S(2)}) collective-permute-start(bf16[128,512]{1,0:T(8,128)(2,1)S(1)} %constant_dynamic-slice_fusion.w_ref.refs_0_), channel_id=1, source_target_pairs={{0,8},{2,10},{4,12},{6,14},{8,0},{10,2},{12,4},{14,6},{1,9},{3,11}... | collective-permute-start | bytes 393224 | tf_op jit(solution)/shard_map/ppermute | solution.py:190
  7.3 9.3 %collective-permute-start.7 = (bf16[128,512]{1,0:T(8,128)(2,1)S(1)}, bf16[128,512]{1,0:T(8,128)(2,1)S(1)}, u32[]{:S(2)}, u32[]{:S(2)}) collective-permute-start(bf16[128,512]{1,0:T(8,128)(2,1)S(1)} %constant_dynamic-slice_fusion.w_ref.refs_0_), channel_id=1, source_target_pairs={{0,12},{2,14},{4,0},{6,2},{8,4},{10,6},{12,8},{14,10},{1,13},{3,15... | collective-permute-start | bytes 393224 | tf_op jit(solution)/shard_map/ppermute | solution.py:190
  8.9 9.4 %collective-permute-start = (bf16[256,512]{1,0:T(8,128)(2,1)S(1)}, bf16[256,512]{1,0:T(8,128)(2,1)S(1)}, u32[]{:S(2)}, u32[]{:S(2)}) collective-permute-start(bf16[256,512]{1,0:T(8,128)(2,1)S(1)} %shard_map.93), channel_id=1, source_target_pairs={{0,2},{2,0},{4,6},{6,4},{8,10},{10,8},{12,14},{14,12},{1,3},{3,1},... | collective-permute-start | bytes 786440 | tf_op jit(solution)/shard_map/ppermute | solution.py:190
  10.5 8.1 %collective-permute-start.1 = (bf16[128,512]{1,0:T(8,128)(2,1)S(1)}, bf16[128,512]{1,0:T(8,128)(2,1)S(1)}, u32[]{:S(2)}, u32[]{:S(2)}) collective-permute-start(bf16[128,512]{1,0:T(8,128)(2,1)S(1)} %get-tuple-element.39), channel_id=1, source_target_pairs={{0,4},{2,6},{4,0},{6,2},{8,12},{10,14},{12,8},{14,10},{1,5},{3,7},... | collective-permute-start | bytes 393224 | tf_op jit(solution)/shard_map/ppermute | solution.py:190
  11.3 10.5 %collective-permute-start.3 = (bf16[128,1024]{1,0:T(8,128)(2,1)S(1)}, bf16[128,1024]{1,0:T(8,128)(2,1)S(1)}, u32[]{:S(2)}, u32[]{:S(2)}) collective-permute-start(bf16[128,1024]{1,0:T(8,128)(2,1)S(1)} %get-tuple-element.41), channel_id=1, source_target_pairs={{0,16},{16,0},{1,17},{17,1},{2,18},{18,2},{3,19},{19,3},{4,20},{20... | collective-permute-start | bytes 786440 | tf_op jit(solution)/shard_map/ppermute | solution.py:199
  16.6 10.4 %collective-permute-start.8 = (bf16[384,512]{1,0:T(8,128)(2,1)S(1)}, bf16[384,512]{1,0:T(8,128)(2,1)S(1)}, u32[]{:S(2)}, u32[]{:S(2)}) collective-permute-start(bf16[384,512]{1,0:T(8,128)(2,1)S(1)} %pad_maximum_fusion), channel_id=1, source_target_pairs={{0,2},{2,0},{4,6},{6,4},{8,10},{10,8},{12,14},{14,12},{1,3},{3,1},... | collective-permute-start | bytes 1179656 | tf_op jit(solution)/shard_map/ppermute | solution.py:190
  18.3 2.7 %copy-start.1 = (bf16[128,512]{1,0:T(8,128)(2,1)S(1)}, bf16[128,512]{1,0:T(8,128)(2,1)}, u32[]{:S(2)}) copy-start(bf16[128,512]{1,0:T(8,128)(2,1)} %q_ref.7) | copy-start | bytes 393220
  18.6 14.1 %copy-start.4 = (bf16[128,512]{1,0:T(8,128)(2,1)}, bf16[128,512]{1,0:T(8,128)(2,1)S(1)}, u32[]{:S(2)}) copy-start(bf16[128,512]{1,0:T(8,128)(2,1)S(1)} %collective-permute-done.1.cols_ref) | copy-start | bytes 393220
  18.7 5.7 %collective-permute-start.2 = (bf16[128,512]{1,0:T(8,128)(2,1)S(1)}, bf16[128,512]{1,0:T(8,128)(2,1)S(1)}, u32[]{:S(2)}, u32[]{:S(2)}) collective-permute-start(bf16[128,512]{1,0:T(8,128)(2,1)S(1)} %add_convert_fusion.3), channel_id=1, source_target_pairs={{0,4},{2,6},{4,0},{6,2},{8,12},{10,14},{12,8},{14,10},{1,5},{3,7},... | collective-permute-start | bytes 393224 | tf_op jit(solution)/shard_map/ppermute | solution.py:190
  24.4 8.3 %collective-permute-start.4 = (bf16[128,512]{1,0:T(8,128)(2,1)S(1)}, bf16[128,512]{1,0:T(8,128)(2,1)S(1)}, u32[]{:S(2)}, u32[]{:S(2)}) collective-permute-start(bf16[128,512]{1,0:T(8,128)(2,1)S(1)} %add_convert_fusion.2), channel_id=1, source_target_pairs={{0,8},{2,10},{4,12},{6,14},{8,0},{10,2},{12,4},{14,6},{1,9},{3,11}... | collective-permute-start | bytes 393224 | tf_op jit(solution)/shard_map/ppermute | solution.py:190
  27.4 9.4 %collective-permute-start.9 = (f32[128,512]{1,0:T(8,128)S(1)}, f32[128,512]{1,0:T(8,128)S(1)}, u32[]{:S(2)}, u32[]{:S(2)}) collective-permute-start(f32[128,512]{1,0:T(8,128)S(1)} %shard_map.97), channel_id=1, source_target_pairs={{0,16},{16,0},{1,17},{17,1},{2,18},{18,2},{3,19},{19,3},{4,20},{20... | collective-permute-start | bytes 786440 | tf_op jit(solution)/shard_map/ppermute | solution.py:199
  33.1 5.0 %collective-permute-start.13 = (bf16[128,512]{1,0:T(8,128)(2,1)S(1)}, bf16[128,512]{1,0:T(8,128)(2,1)S(1)}, u32[]{:S(2)}, u32[]{:S(2)}) collective-permute-start(bf16[128,512]{1,0:T(8,128)(2,1)S(1)} %get-tuple-element.47.n_ref), channel_id=1, source_target_pairs={{0,16},{16,0},{1,17},{17,1},{2,18},{18,2},{3,19},{19,3},{4,20},{20... | collective-permute-start | bytes 393224 | tf_op jit(solution)/shard_map/ppermute | solution.py:199
  34.7 6.0 %collective-permute-start.11 = (bf16[128,512]{1,0:T(8,128)(2,1)S(1)}, bf16[128,512]{1,0:T(8,128)(2,1)S(1)}, u32[]{:S(2)}, u32[]{:S(2)}) collective-permute-start(bf16[128,512]{1,0:T(8,128)(2,1)S(1)} %get-tuple-element.47.n_ref), channel_id=1, source_target_pairs={{0,4},{2,6},{4,0},{6,2},{8,12},{10,14},{12,8},{14,10},{1,5},{3,7},... | collective-permute-start | bytes 393224 | tf_op jit(solution)/shard_map/ppermute | solution.py:190
  34.7 13.7 %collective-permute-start.18 = (bf16[256,512]{1,0:T(8,128)(2,1)S(1)}, bf16[256,512]{1,0:T(8,128)(2,1)S(1)}, u32[]{:S(2)}, u32[]{:S(2)}) collective-permute-start(bf16[256,512]{1,0:T(8,128)(2,1)S(1)} %get-tuple-element.59), channel_id=1, source_target_pairs={{0,8},{2,10},{4,12},{6,14},{8,0},{10,2},{12,4},{14,6},{1,9},{3,11}... | collective-permute-start | bytes 786440 | tf_op jit(solution)/shard_map/ppermute | solution.py:190
  37.3 5.0 %collective-permute-start.10 = (bf16[128,512]{1,0:T(8,128)(2,1)S(1)}, bf16[128,512]{1,0:T(8,128)(2,1)S(1)}, u32[]{:S(2)}, u32[]{:S(2)}) collective-permute-start(bf16[128,512]{1,0:T(8,128)(2,1)S(1)} %get-tuple-element.46), channel_id=1, source_target_pairs={{0,2},{2,0},{4,6},{6,4},{8,10},{10,8},{12,14},{14,12},{1,3},{3,1},... | collective-permute-start | bytes 393224 | tf_op jit(solution)/shard_map/ppermute | solution.py:190
  38.9 11.2 %collective-permute-start.14 = (bf16[128,1024]{1,0:T(8,128)(2,1)S(1)}, bf16[128,1024]{1,0:T(8,128)(2,1)S(1)}, u32[]{:S(2)}, u32[]{:S(2)}) collective-permute-start(bf16[128,1024]{1,0:T(8,128)(2,1)S(1)} %get-tuple-element.49), channel_id=1, source_target_pairs={{0,16},{16,0},{1,17},{17,1},{2,18},{18,2},{3,19},{19,3},{4,20},{20... | collective-permute-start | bytes 786440 | tf_op jit(solution)/shard_map/ppermute | solution.py:199
  40.5 14.3 %collective-permute-start.16 = (bf16[128,1024]{1,0:T(8,128)(2,1)S(1)}, bf16[128,1024]{1,0:T(8,128)(2,1)S(1)}, u32[]{:S(2)}, u32[]{:S(2)}) collective-permute-start(bf16[128,1024]{1,0:T(8,128)(2,1)S(1)} %get-tuple-element.55.a_ref), channel_id=1, source_target_pairs={{0,1},{1,0},{2,3},{3,2},{4,5},{5,4},{6,7},{7,6},{8,9},{9,8},{10,11... | collective-permute-start | bytes 786440 | tf_op jit(solution)/shard_map/ppermute | solution.py:202
  42.4 6.2 %slice-start = ((bf16[128,512]{1,0:T(8,128)(2,1)}), bf16[128,256]{1,0:T(8,128)(2,1)S(1)}, s32[]{:S(2)}) async-start(bf16[128,512]{1,0:T(8,128)(2,1)} %copy-done.4), calls=%async_computation | async-start | bytes 131072 | tf_op jit(solution)/shard_map/slice | solution.py:388
  42.4 8.8 %collective-permute-start.12 = (bf16[128,512]{1,0:T(8,128)(2,1)S(1)}, bf16[128,512]{1,0:T(8,128)(2,1)S(1)}, u32[]{:S(2)}, u32[]{:S(2)}) collective-permute-start(bf16[128,512]{1,0:T(8,128)(2,1)S(1)} %add_convert_fusion.1), channel_id=1, source_target_pairs={{0,4},{2,6},{4,0},{6,2},{8,12},{10,14},{12,8},{14,10},{1,5},{3,7},... | collective-permute-start | bytes 393224 | tf_op jit(solution)/shard_map/ppermute | solution.py:190
  48.4 5.5 %collective-permute-start.20 = (bf16[128,512]{1,0:T(8,128)(2,1)S(1)}, bf16[128,512]{1,0:T(8,128)(2,1)S(1)}, u32[]{:S(2)}, u32[]{:S(2)}) collective-permute-start(bf16[128,512]{1,0:T(8,128)(2,1)S(1)} %get-tuple-element.71), channel_id=1, source_target_pairs={{0,4},{2,6},{4,0},{6,2},{8,12},{10,14},{12,8},{14,10},{1,5},{3,7},... | collective-permute-start | bytes 393224 | tf_op jit(solution)/shard_map/ppermute | solution.py:190
  48.5 5.4 %collective-permute-start.19 = (bf16[128,768]{1,0:T(8,128)(2,1)S(1)}, bf16[128,768]{1,0:T(8,128)(2,1)S(1)}, u32[]{:S(2)}, u32[]{:S(2)}) collective-permute-start(bf16[128,768]{1,0:T(8,128)(2,1)S(1)} %pad_maximum_fusion.1.c_ref), channel_id=1, source_target_pairs={{0,1},{1,0},{2,3},{3,2},{4,5},{5,4},{6,7},{7,6},{8,9},{9,8},{10,11... | collective-permute-start | bytes 589832 | tf_op jit(solution)/shard_map/ppermute | solution.py:202
  51.2 3.5 %collective-permute-start.17 = (bf16[128,1024]{1,0:T(8,128)(2,1)S(1)}, bf16[128,1024]{1,0:T(8,128)(2,1)S(1)}, u32[]{:S(2)}, u32[]{:S(2)}) collective-permute-start(bf16[128,1024]{1,0:T(8,128)(2,1)S(1)} %collective-permute-done.14.c_ref), channel_id=1, source_target_pairs={{0,1},{1,0},{2,3},{3,2},{4,5},{5,4},{6,7},{7,6},{8,9},{9,8},{10,11... | collective-permute-start | bytes 786440 | tf_op jit(solution)/shard_map/ppermute | solution.py:202
  51.2 9.7 %collective-permute-start.15 = (bf16[128,512]{1,0:T(8,128)(2,1)S(1)}, bf16[128,512]{1,0:T(8,128)(2,1)S(1)}, u32[]{:S(2)}, u32[]{:S(2)}) collective-permute-start(bf16[128,512]{1,0:T(8,128)(2,1)S(1)} %add_convert_fusion), channel_id=1, source_target_pairs={{0,8},{2,10},{4,12},{6,14},{8,0},{10,2},{12,4},{14,6},{1,9},{3,11}... | collective-permute-start | bytes 393224 | tf_op jit(solution)/shard_map/ppermute | solution.py:190
  54.7 7.4 %collective-permute-start.21 = (bf16[256,512]{1,0:T(8,128)(2,1)S(1)}, bf16[256,512]{1,0:T(8,128)(2,1)S(1)}, u32[]{:S(2)}, u32[]{:S(2)}) collective-permute-start(bf16[256,512]{1,0:T(8,128)(2,1)S(1)} %get-tuple-element.62), channel_id=1, source_target_pairs={{0,2},{2,0},{4,6},{6,4},{8,10},{10,8},{12,14},{14,12},{1,3},{3,1},... | collective-permute-start | bytes 786440 | tf_op jit(solution)/shard_map/ppermute | solution.py:190

commit v8 on v7

--- a/solution.py
+++ b/solution.py
@@ -18,10 +18,10 @@
     "own_state": 300000000,
     "pack": 3000000000,
     "local": 1000000000,
-    "back_other": 3000000000,
+    "back_other": 1000000000,
     "back_own": 1000000000,
     "forward": 3000000000,
-    "turn_back": 600000000,
+    "turn_back": 1048576,
     "project": 3000000000,
     "local_grads": 1048576,
     "weight_grad": 1500000000,
@@ -211,18 +211,16 @@
     my_weight = lax.dynamic_slice_in_dim(out_weight, g * half, half, 0)
     z_weight = [rotate(my_weight, k) for k in turns]
 
-    def own_state(k_ref, v_ref, w_ref, out_ref):
-        out_ref[:half, :] = w_ref[...]
-        for i in range(heads):
-            out_ref[half:, head_of(i)] = dot(
+    def own_state(k_ref, v_ref, out_ref):
+        for i in range(heads):
+            out_ref[:, head_of(i)] = dot(
                 k_ref[:, head_of(i)], v_ref[:, head_of(i)], ROWS_T
             ).astype(BF16)
 
-    (weight_states,) = call(
-        own_state, [((half + DH, feats), BF16)], keys, values, my_weight
-    )
-    x_weight_states = swap(weight_states, 1)
-    states, x_states = weight_states[half:], x_weight_states[half:]
+    (states,) = call(own_state, [(state, BF16)], keys, values)
+    x_states = swap(states, 1)
+    states, own_weight = tie(states, my_weight)
+    x_weight_own = swap(own_weight, 1)
 
     def columns(gy_ref, z, h):
         return gy_ref[:, lanes(z * 2 + h, wrows)]
@@ -256,9 +254,11 @@
     def add(a, b):
         return (a.astype(F32) + b.astype(F32)).astype(BF16)
 
-    x_states, near_cols = tie(x_states, near_cols)
     pair_states = add(states, x_states)
     near_states = swap(pair_states, 2)
+    pair_states, x_weight_own, near_cols, *z_weight = tie(
+        pair_states, x_weight_own, near_cols, *z_weight
+    )
     near_states, y_cols = tie(near_states, y_cols)
     quad_states = add(pair_states, near_states)
     got_states = x_states, near_states, swap(quad_states, 4)
@@ -273,13 +273,13 @@
             zk = lax.rem(z - k + line, line)
             blocks.append((zk * 2 + x, (own, *others)[k][...]))
             if k == 0:
-                block = x_own[:half, :]
+                block = x_own[...]
             else:
                 block = x_others[(k - 1) * half : k * half, :]
             blocks.append((zk * 2 + 1 - x, block))
         return blocks
 
-    weight_args = (my_weight, *z_weight, x_weight_states, x_weight)
+    weight_args = (my_weight, *z_weight, x_weight_own, x_weight)
 
     def back_other(yc_ref, *refs):
         *w_refs, out_ref = refs

time: 63 us -> 61.1 us (0.970)
  waiting for transfers between devices: 24.6 us -> 21.4 us
  starting transfers between devices: 28 us -> 29.3 us
    ppermute x15 -> x16, waiting for transfers between devices: 24.3 us -> 21.4 us  [permute(): return lax.ppermute(array, 'seq', pairs)]
    ppermute x15 -> x16, starting transfers between devices: 21.6 us -> 23.9 us  [permute(): return lax.ppermute(array, 'seq', pairs)]
    ppermute x4, starting transfers between devices: 6.41 us -> 5.3 us  [swap_y(): return lax.ppermute(array, 'groups', [(0, 1), (1, 0)])]
  transfers between devices with their start and end apart: 22 -> 23, of which waited for: 14 -> 11; matrix products, arithmetic and copies ran while one was open for 0% -> 0% of each run, Pallas kernels for 12% -> 12%
where the time goes in v8:
time: 61.1 us; the launch traced here: 60.9 us
  starting transfers between devices  29.3 us (48%)
  waiting for transfers between devices  21.4 us (35%)
  Pallas kernels  7.35 us (12%)
  other arithmetic  1.04 us (2%)
  local copies, waits for them, and re-layouts  1 us (2%)
  between operations  0.83 us (1%)
    ppermute x16, starting transfers between devices, permute(): return lax.ppermute(array, 'seq', pairs)  23.9 us
    ppermute x16, waiting for transfers between devices, permute(): return lax.ppermute(array, 'seq', pairs)  21.4 us
    pallas_call x12, Pallas kernels, call(): pl.pallas_call(body, out_shape=[jax.ShapeDtypeStruct(s, d) for s, d in sh...  7.35 us
    ppermute x4, starting transfers between devices, swap_y(): return lax.ppermute(array, 'groups', [(0, 1), (1, 0)])  5.3 us
  transfers between devices with their start and end apart: 23, of which 11 were waited for; matrix products, arithmetic and copies ran while one was open for 0% of the time, Pallas kernels for 12%

profile of v8, /device:TPU:0, one launch (start us, length us, event | category | flops | bytes accessed | tf_op | source)
XLA Modules:
  0.0 60.9 jit_solution(14781878499553993715)
XLA Ops:
  0.7 0.9 %copy-done = bf16[256,512]{1,0:T(8,128)(2,1)S(1)} copy-done((bf16[256,512]{1,0:T(8,128)(2,1)S(1)}, bf16[256,512]{1,0:T(8,128)(2,1)}, u32[]{:S(2)}) %copy-start) | copy-done | bytes 262168
  1.6 3.1 %collective-permute-start.5 = (bf16[128,512]{1,0:T(8,128)(2,1)S(1)}, bf16[128,512]{1,0:T(8,128)(2,1)S(1)}, u32[]{:S(2)}, u32[]{:S(2)}) collective-permute-start(bf16[128,512]{1,0:T(8,128)(2,1)S(1)} %constant_dynamic-slice_fusion.refs_0_), channel_id=1, source_target_pairs={{0,4},{2,6},{4,8},{6,10},{8,12},{10,14},{12,0},{14,2},{1,5},{3,7},... | collective-permute-start | bytes 393224 | tf_op jit(solution)/shard_map/ppermute | solution.py:190
  4.7 2.6 %collective-permute-start.6 = (bf16[128,512]{1,0:T(8,128)(2,1)S(1)}, bf16[128,512]{1,0:T(8,128)(2,1)S(1)}, u32[]{:S(2)}, u32[]{:S(2)}) collective-permute-start(bf16[128,512]{1,0:T(8,128)(2,1)S(1)} %constant_dynamic-slice_fusion.refs_0_), channel_id=1, source_target_pairs={{0,8},{2,10},{4,12},{6,14},{8,0},{10,2},{12,4},{14,6},{1,9},{3,11}... | collective-permute-start | bytes 393224 | tf_op jit(solution)/shard_map/ppermute | solution.py:190
  7.3 1.3 %collective-permute-start.7 = (bf16[128,512]{1,0:T(8,128)(2,1)S(1)}, bf16[128,512]{1,0:T(8,128)(2,1)S(1)}, u32[]{:S(2)}, u32[]{:S(2)}) collective-permute-start(bf16[128,512]{1,0:T(8,128)(2,1)S(1)} %constant_dynamic-slice_fusion.refs_0_), channel_id=1, source_target_pairs={{0,12},{2,14},{4,0},{6,2},{8,4},{10,6},{12,8},{14,10},{1,13},{3,15... | collective-permute-start | bytes 393224 | tf_op jit(solution)/shard_map/ppermute | solution.py:190
  8.9 1.6 %collective-permute-start = (bf16[128,512]{1,0:T(8,128)(2,1)S(1)}, bf16[128,512]{1,0:T(8,128)(2,1)S(1)}, u32[]{:S(2)}, u32[]{:S(2)}) collective-permute-start(bf16[128,512]{1,0:T(8,128)(2,1)S(1)} %shard_map.93), channel_id=1, source_target_pairs={{0,2},{2,0},{4,6},{6,4},{8,10},{10,8},{12,14},{14,12},{1,3},{3,1},... | collective-permute-start | bytes 393224 | tf_op jit(solution)/shard_map/ppermute | solution.py:190
  11.0 3.7 %collective-permute-done.x_ref = bf16[128,512]{1,0:T(8,128)(2,1)S(1)} collective-permute-done((bf16[128,512]{1,0:T(8,128)(2,1)S(1)}, bf16[128,512]{1,0:T(8,128)(2,1)S(1)}, u32[]{:S(2)}, u32[]{:S(2)}) %collective-permute-start) | collective-permute-done | bytes 131104 | tf_op jit(solution)/shard_map/ppermute | solution.py:190
  15.4 0.7 %collective-permute-done.3.refs_4_ = bf16[128,512]{1,0:T(8,128)(2,1)S(1)} collective-permute-done((bf16[128,512]{1,0:T(8,128)(2,1)S(1)}, bf16[128,512]{1,0:T(8,128)(2,1)S(1)}, u32[]{:S(2)}, u32[]{:S(2)}) %collective-permute-start.3) | collective-permute-done | bytes 131104 | tf_op jit(solution)/shard_map/ppermute | solution.py:190
  16.1 1.5 %collective-permute-start.2 = (bf16[128,1024]{1,0:T(8,128)(2,1)S(1)}, bf16[128,1024]{1,0:T(8,128)(2,1)S(1)}, u32[]{:S(2)}, u32[]{:S(2)}) collective-permute-start(bf16[128,1024]{1,0:T(8,128)(2,1)S(1)} %get-tuple-element.46), channel_id=1, source_target_pairs={{0,16},{16,0},{1,17},{17,1},{2,18},{18,2},{3,19},{19,3},{4,20},{20... | collective-permute-start | bytes 786440 | tf_op jit(solution)/shard_map/ppermute | solution.py:199
  17.7 0.7 %collective-permute-start.1 = (bf16[128,512]{1,0:T(8,128)(2,1)S(1)}, bf16[128,512]{1,0:T(8,128)(2,1)S(1)}, u32[]{:S(2)}, u32[]{:S(2)}) collective-permute-start(bf16[128,512]{1,0:T(8,128)(2,1)S(1)} %add_convert_fusion.3), channel_id=1, source_target_pairs={{0,4},{2,6},{4,0},{6,2},{8,12},{10,14},{12,8},{14,10},{1,5},{3,7},... | collective-permute-start | bytes 393224 | tf_op jit(solution)/shard_map/ppermute | solution.py:190
  18.4 2.5 %collective-permute-done.4.cols_ref = bf16[128,512]{1,0:T(8,128)(2,1)S(1)} collective-permute-done((bf16[128,512]{1,0:T(8,128)(2,1)S(1)}, bf16[128,512]{1,0:T(8,128)(2,1)S(1)}, u32[]{:S(2)}, u32[]{:S(2)}) %collective-permute-start.4) | collective-permute-done | bytes 131104 | tf_op jit(solution)/shard_map/ppermute | solution.py:190
  21.0 1.6 %collective-permute-start.9 = (bf16[384,512]{1,0:T(8,128)(2,1)S(1)}, bf16[384,512]{1,0:T(8,128)(2,1)S(1)}, u32[]{:S(2)}, u32[]{:S(2)}) collective-permute-start(bf16[384,512]{1,0:T(8,128)(2,1)S(1)} %pad_maximum_fusion), channel_id=1, source_target_pairs={{0,2},{2,0},{4,6},{6,4},{8,10},{10,8},{12,14},{14,12},{1,3},{3,1},... | collective-permute-start | bytes 1179656 | tf_op jit(solution)/shard_map/ppermute | solution.py:190
  23.3 0.7 %shard_map.92 = (bf16[128,512]{1,0:T(8,128)(2,1)S(1)}, f32[128,512]{1,0:T(8,128)S(1)}) custom-call(bf16[128,512]{1,0:T(8,128)(2,1)S(1)} %copy-done.1, bf16[128,512]{1,0:T(8,128)(2,1)S(1)} %copy-done.2, bf16[128,512]{1,0:T(8,128)(2,1)S(1)} %copy-done.3), custom_call_target="tpu_custom_call" | custom-call | flops 1000000000 | bytes 1048576 | tf_op jit(solution)/shard_map/pallas_call | solution.py:149
  24.0 4.8 %collective-permute-done.9.refs_5_ = bf16[384,512]{1,0:T(8,128)(2,1)S(1)} collective-permute-done((bf16[384,512]{1,0:T(8,128)(2,1)S(1)}, bf16[384,512]{1,0:T(8,128)(2,1)S(1)}, u32[]{:S(2)}, u32[]{:S(2)}) %collective-permute-start.9) | collective-permute-done | bytes 393248 | tf_op jit(solution)/shard_map/ppermute | solution.py:190
  29.3 0.9 %collective-permute-start.10 = (f32[128,512]{1,0:T(8,128)S(1)}, f32[128,512]{1,0:T(8,128)S(1)}, u32[]{:S(2)}, u32[]{:S(2)}) collective-permute-start(f32[128,512]{1,0:T(8,128)S(1)} %shard_map.97), channel_id=1, source_target_pairs={{0,16},{16,0},{1,17},{17,1},{2,18},{18,2},{3,19},{19,3},{4,20},{20... | collective-permute-start | bytes 786440 | tf_op jit(solution)/shard_map/ppermute | solution.py:199
  30.5 1.3 %collective-permute-start.14 = (bf16[128,512]{1,0:T(8,128)(2,1)S(1)}, bf16[128,512]{1,0:T(8,128)(2,1)S(1)}, u32[]{:S(2)}, u32[]{:S(2)}) collective-permute-start(bf16[128,512]{1,0:T(8,128)(2,1)S(1)} %get-tuple-element.59.n_ref), channel_id=1, source_target_pairs={{0,16},{16,0},{1,17},{17,1},{2,18},{18,2},{3,19},{19,3},{4,20},{20... | collective-permute-start | bytes 393224 | tf_op jit(solution)/shard_map/ppermute | solution.py:199
  31.8 1.5 %collective-permute-start.12 = (bf16[128,512]{1,0:T(8,128)(2,1)S(1)}, bf16[128,512]{1,0:T(8,128)(2,1)S(1)}, u32[]{:S(2)}, u32[]{:S(2)}) collective-permute-start(bf16[128,512]{1,0:T(8,128)(2,1)S(1)} %get-tuple-element.59.n_ref), channel_id=1, source_target_pairs={{0,4},{2,6},{4,0},{6,2},{8,12},{10,14},{12,8},{14,10},{1,5},{3,7},... | collective-permute-start | bytes 393224 | tf_op jit(solution)/shard_map/ppermute | solution.py:190
  33.3 2.7 %collective-permute-start.19 = (bf16[256,512]{1,0:T(8,128)(2,1)S(1)}, bf16[256,512]{1,0:T(8,128)(2,1)S(1)}, u32[]{:S(2)}, u32[]{:S(2)}) collective-permute-start(bf16[256,512]{1,0:T(8,128)(2,1)S(1)} %get-tuple-element.71), channel_id=1, source_target_pairs={{0,8},{2,10},{4,12},{6,14},{8,0},{10,2},{12,4},{14,6},{1,9},{3,11}... | collective-permute-start | bytes 786440 | tf_op jit(solution)/shard_map/ppermute | solution.py:190
  36.8 1.6 %collective-permute-start.11 = (bf16[128,512]{1,0:T(8,128)(2,1)S(1)}, bf16[128,512]{1,0:T(8,128)(2,1)S(1)}, u32[]{:S(2)}, u32[]{:S(2)}) collective-permute-start(bf16[128,512]{1,0:T(8,128)(2,1)S(1)} %get-tuple-element.58), channel_id=1, source_target_pairs={{0,2},{2,0},{4,6},{6,4},{8,10},{10,8},{12,14},{14,12},{1,3},{3,1},... | collective-permute-start | bytes 393224 | tf_op jit(solution)/shard_map/ppermute | solution.py:190
  38.4 0.7 %shard_map.99 = (bf16[128,1024]{1,0:T(8,128)(2,1)S(1)}, bf16[128,1024]{1,0:T(8,128)(2,1)S(1)}) custom-call(bf16[128,512]{1,0:T(8,128)(2,1)S(1)} %get-tuple-element.59.n_ref, bf16[128,512]{1,0:T(8,128)(2,1)S(1)} %collective-permute-done.14.yn_ref, bf16[128,512]{1,0:T(8,128)(2,1)S(1)} %constant_dynamic-slice_fusion.refs_0_, ...), custom_call_target="tpu_custom_call" | custom-call | flops 3000000000 | bytes 1048576 | tf_op jit(solution)/shard_map/pallas_call | solution.py:149
  39.1 1.6 %collective-permute-start.15 = (bf16[128,1024]{1,0:T(8,128)(2,1)S(1)}, bf16[128,1024]{1,0:T(8,128)(2,1)S(1)}, u32[]{:S(2)}, u32[]{:S(2)}) collective-permute-start(bf16[128,1024]{1,0:T(8,128)(2,1)S(1)} %get-tuple-element.61), channel_id=1, source_target_pairs={{0,16},{16,0},{1,17},{17,1},{2,18},{18,2},{3,19},{19,3},{4,20},{20... | collective-permute-start | bytes 786440 | tf_op jit(solution)/shard_map/ppermute | solution.py:199
  40.7 1.2 %collective-permute-done.11.x_ref = bf16[128,512]{1,0:T(8,128)(2,1)S(1)} collective-permute-done((bf16[128,512]{1,0:T(8,128)(2,1)S(1)}, bf16[128,512]{1,0:T(8,128)(2,1)S(1)}, u32[]{:S(2)}, u32[]{:S(2)}) %collective-permute-start.11) | collective-permute-done | bytes 131104 | tf_op jit(solution)/shard_map/ppermute | solution.py:190
  41.9 1.6 %collective-permute-start.13 = (bf16[128,512]{1,0:T(8,128)(2,1)S(1)}, bf16[128,512]{1,0:T(8,128)(2,1)S(1)}, u32[]{:S(2)}, u32[]{:S(2)}) collective-permute-start(bf16[128,512]{1,0:T(8,128)(2,1)S(1)} %add_convert_fusion.1), channel_id=1, source_target_pairs={{0,4},{2,6},{4,0},{6,2},{8,12},{10,14},{12,8},{14,10},{1,5},{3,7},... | collective-permute-start | bytes 393224 | tf_op jit(solution)/shard_map/ppermute | solution.py:190
  43.5 2.7 %collective-permute-done.19.far_ref = bf16[256,512]{1,0:T(8,128)(2,1)S(1)} collective-permute-done((bf16[256,512]{1,0:T(8,128)(2,1)S(1)}, bf16[256,512]{1,0:T(8,128)(2,1)S(1)}, u32[]{:S(2)}, u32[]{:S(2)}) %collective-permute-start.19) | collective-permute-done | bytes 262176 | tf_op jit(solution)/shard_map/ppermute | solution.py:190
  46.4 1.4 %shard_map.100 = (bf16[128,512]{1,0:T(8,128)(2,1)}, f32[128,512]{1,0:T(8,128)S(1)}, f32[128,512]{1,0:T(8,128)S(1)}) custom-call(bf16[128,512]{1,0:T(8,128)(2,1)S(1)} %get-tuple-element.62.go_ref, bf16[128,512]{1,0:T(8,128)(2,1)S(1)} %copy-done.1, bf16[128,512]{1,0:T(8,128)(2,1)S(1)} %copy-done.2, bf16[128,512]{1,0:T(8,128)(2,1)S(1)} %copy-done.3, ...), custom_call_target="tpu_custom_call" | custom-call | flops 1048576 | bytes 1048576 | tf_op jit(solution)/shard_map/pallas_call | solution.py:149
  47.8 1.2 %collective-permute-done.13.near_ref = bf16[128,512]{1,0:T(8,128)(2,1)S(1)} collective-permute-done((bf16[128,512]{1,0:T(8,128)(2,1)S(1)}, bf16[128,512]{1,0:T(8,128)(2,1)S(1)}, u32[]{:S(2)}, u32[]{:S(2)}) %collective-permute-start.13) | collective-permute-done | bytes 131104 | tf_op jit(solution)/shard_map/ppermute | solution.py:190
  49.0 2.3 %collective-permute-start.16 = (bf16[128,512]{1,0:T(8,128)(2,1)S(1)}, bf16[128,512]{1,0:T(8,128)(2,1)S(1)}, u32[]{:S(2)}, u32[]{:S(2)}) collective-permute-start(bf16[128,512]{1,0:T(8,128)(2,1)S(1)} %add_convert_fusion), channel_id=1, source_target_pairs={{0,8},{2,10},{4,12},{6,14},{8,0},{10,2},{12,4},{14,6},{1,9},{3,11}... | collective-permute-start | bytes 393224 | tf_op jit(solution)/shard_map/ppermute | solution.py:190
  51.7 0.7 %shard_map.102 = (f32[256,512]{1,0:T(8,128)S(1)}, bf16[256,512]{1,0:T(8,128)(2,1)S(1)}) custom-call(bf16[128,2048]{1,0:T(8,128)(2,1)S(1)} %copy-done.5, bf16[128,768]{1,0:T(8,128)(2,1)S(1)} %pad_maximum_fusion.1.c_ref, bf16[128,768]{1,0:T(8,128)(2,1)S(1)} %collective-permute-done.20.o_ref, bf16[128,512]{1,0:T(8,128)(2,1)S(1)} %get-tuple-element.59.n_ref, ...), custom_call_target="tpu_custom_call" | custom-call | flops 1500000000 | bytes 1048576 | tf_op jit(solution)/shard_map/pallas_call | solution.py:149
  52.4 1.6 %collective-permute-start.22 = (bf16[256,512]{1,0:T(8,128)(2,1)S(1)}, bf16[256,512]{1,0:T(8,128)(2,1)S(1)}, u32[]{:S(2)}, u32[]{:S(2)}) collective-permute-start(bf16[256,512]{1,0:T(8,128)(2,1)S(1)} %get-tuple-element.74), channel_id=1, source_target_pairs={{0,2},{2,0},{4,6},{6,4},{8,10},{10,8},{12,14},{14,12},{1,3},{3,1},... | collective-permute-start | bytes 786440 | tf_op jit(solution)/shard_map/ppermute | solution.py:190
  54.0 1.0 %shard_map.101 = bf16[128,2048]{1,0:T(8,128)(2,1)} custom-call(bf16[128,1024]{1,0:T(8,128)(2,1)S(1)} %get-tuple-element.67.a_ref, bf16[128,1024]{1,0:T(8,128)(2,1)S(1)} %collective-permute-done.17.b_ref, bf16[128,1024]{1,0:T(8,128)(2,1)S(1)} %collective-permute-done.15.c_ref, bf16[128,1024]{1,0:T(8,128)(2,1)S(1)} %collective-permute-done.18.d_ref), custom_call_target="tpu_custom_call" | custom-call | flops 1048576 | bytes 1048576 | tf_op jit(solution)/shard_map/pallas_call | solution.py:149
  54.9 3.7 %collective-permute-done.16.far_ref = bf16[128,512]{1,0:T(8,128)(2,1)S(1)} collective-permute-done((bf16[128,512]{1,0:T(8,128)(2,1)S(1)}, bf16[128,512]{1,0:T(8,128)(2,1)S(1)}, u32[]{:S(2)}, u32[]{:S(2)}) %collective-permute-start.16) | collective-permute-done | bytes 131104 | tf_op jit(solution)/shard_map/ppermute | solution.py:190
  58.7 1.0 %shard_map.103 = (bf16[128,512]{1,0:T(8,128)(2,1)}, bf16[128,512]{1,0:T(8,128)(2,1)}) custom-call(f32[128,512]{1,0:T(8,128)S(1)} %get-tuple-element.75.gk_ref, f32[128,512]{1,0:T(8,128)S(1)} %get-tuple-element.76.gv_ref, bf16[128,512]{1,0:T(8,128)(2,1)S(1)} %copy-done.2, bf16[128,512]{1,0:T(8,128)(2,1)S(1)} %copy-done.3, ...), custom_call_target="tpu_custom_call" | custom-call | flops 3000000000 | bytes 1048576 | tf_op jit(solution)/shard_map/pallas_call | solution.py:149
  60.1 0.9 %convert_add_fusion = f32[256,512]{1,0:T(8,128)} fusion(f32[256,512]{1,0:T(8,128)S(1)} %get-tuple-element.81, bf16[256,512]{1,0:T(8,128)(2,1)S(1)} %collective-permute-done.22), kind=kLoop, calls=%fused_computation | loop fusion | flops 262144 | bytes 1310720 | tf_op jit(solution)/shard_map/add | solution.py:453
  (49 shorter events, 5.0 us)
Async XLA Ops:
  0.6 1.0 %copy-start = (bf16[256,512]{1,0:T(8,128)(2,1)S(1)}, bf16[256,512]{1,0:T(8,128)(2,1)}, u32[]{:S(2)}) copy-start(bf16[256,512]{1,0:T(8,128)(2,1)} %param.8) | copy-start | bytes 786436
  1.6 7.0 %copy-start.2 = (bf16[128,512]{1,0:T(8,128)(2,1)S(1)}, bf16[128,512]{1,0:T(8,128)(2,1)}, u32[]{:S(2)}) copy-start(bf16[128,512]{1,0:T(8,128)(2,1)} %k_ref.7) | copy-start | bytes 393220
  1.6 7.0 %copy-start.3 = (bf16[128,512]{1,0:T(8,128)(2,1)S(1)}, bf16[128,512]{1,0:T(8,128)(2,1)}, u32[]{:S(2)}) copy-start(bf16[128,512]{1,0:T(8,128)(2,1)} %v_ref.7) | copy-start | bytes 393220
  1.6 9.3 %copy-start.5 = (bf16[128,2048]{1,0:T(8,128)(2,1)S(1)}, bf16[128,2048]{1,0:T(8,128)(2,1)}, u32[]{:S(2)}) copy-start(bf16[128,2048]{1,0:T(8,128)(2,1)} %gy_ref.7) | copy-start | bytes 1572868
  1.6 16.1 %collective-permute-start.5 = (bf16[128,512]{1,0:T(8,128)(2,1)S(1)}, bf16[128,512]{1,0:T(8,128)(2,1)S(1)}, u32[]{:S(2)}, u32[]{:S(2)}) collective-permute-start(bf16[128,512]{1,0:T(8,128)(2,1)S(1)} %constant_dynamic-slice_fusion.refs_0_), channel_id=1, source_target_pairs={{0,4},{2,6},{4,8},{6,10},{8,12},{10,14},{12,0},{14,2},{1,5},{3,7},... | collective-permute-start | bytes 393224 | tf_op jit(solution)/shard_map/ppermute | solution.py:190
  4.7 13.7 %collective-permute-start.6 = (bf16[128,512]{1,0:T(8,128)(2,1)S(1)}, bf16[128,512]{1,0:T(8,128)(2,1)S(1)}, u32[]{:S(2)}, u32[]{:S(2)}) collective-permute-start(bf16[128,512]{1,0:T(8,128)(2,1)S(1)} %constant_dynamic-slice_fusion.refs_0_), channel_id=1, source_target_pairs={{0,8},{2,10},{4,12},{6,14},{8,0},{10,2},{12,4},{14,6},{1,9},{3,11}... | collective-permute-start | bytes 393224 | tf_op jit(solution)/shard_map/ppermute | solution.py:190
  7.3 11.2 %collective-permute-start.7 = (bf16[128,512]{1,0:T(8,128)(2,1)S(1)}, bf16[128,512]{1,0:T(8,128)(2,1)S(1)}, u32[]{:S(2)}, u32[]{:S(2)}) collective-permute-start(bf16[128,512]{1,0:T(8,128)(2,1)S(1)} %constant_dynamic-slice_fusion.refs_0_), channel_id=1, source_target_pairs={{0,12},{2,14},{4,0},{6,2},{8,4},{10,6},{12,8},{14,10},{1,13},{3,15... | collective-permute-start | bytes 393224 | tf_op jit(solution)/shard_map/ppermute | solution.py:190
  8.9 5.9 %collective-permute-start = (bf16[128,512]{1,0:T(8,128)(2,1)S(1)}, bf16[128,512]{1,0:T(8,128)(2,1)S(1)}, u32[]{:S(2)}, u32[]{:S(2)}) collective-permute-start(bf16[128,512]{1,0:T(8,128)(2,1)S(1)} %shard_map.93), channel_id=1, source_target_pairs={{0,2},{2,0},{4,6},{6,4},{8,10},{10,8},{12,14},{14,12},{1,3},{3,1},... | collective-permute-start | bytes 393224 | tf_op jit(solution)/shard_map/ppermute | solution.py:190
  10.4 5.7 %collective-permute-start.3 = (bf16[128,512]{1,0:T(8,128)(2,1)S(1)}, bf16[128,512]{1,0:T(8,128)(2,1)S(1)}, u32[]{:S(2)}, u32[]{:S(2)}) collective-permute-start(bf16[128,512]{1,0:T(8,128)(2,1)S(1)} %constant_dynamic-slice_fusion.refs_0_), channel_id=1, source_target_pairs={{0,2},{2,0},{4,6},{6,4},{8,10},{10,8},{12,14},{14,12},{1,3},{3,1},... | collective-permute-start | bytes 393224 | tf_op jit(solution)/shard_map/ppermute | solution.py:190
  14.7 6.2 %collective-permute-start.4 = (bf16[128,512]{1,0:T(8,128)(2,1)S(1)}, bf16[128,512]{1,0:T(8,128)(2,1)S(1)}, u32[]{:S(2)}, u32[]{:S(2)}) collective-permute-start(bf16[128,512]{1,0:T(8,128)(2,1)S(1)} %get-tuple-element.49), channel_id=1, source_target_pairs={{0,4},{2,6},{4,0},{6,2},{8,12},{10,14},{12,8},{14,10},{1,5},{3,7},... | collective-permute-start | bytes 393224 | tf_op jit(solution)/shard_map/ppermute | solution.py:190
  16.1 6.6 %collective-permute-start.2 = (bf16[128,1024]{1,0:T(8,128)(2,1)S(1)}, bf16[128,1024]{1,0:T(8,128)(2,1)S(1)}, u32[]{:S(2)}, u32[]{:S(2)}) collective-permute-start(bf16[128,1024]{1,0:T(8,128)(2,1)S(1)} %get-tuple-element.46), channel_id=1, source_target_pairs={{0,16},{16,0},{1,17},{17,1},{2,18},{18,2},{3,19},{19,3},{4,20},{20... | collective-permute-start | bytes 786440 | tf_op jit(solution)/shard_map/ppermute | solution.py:199
  17.7 5.0 %collective-permute-start.1 = (bf16[128,512]{1,0:T(8,128)(2,1)S(1)}, bf16[128,512]{1,0:T(8,128)(2,1)S(1)}, u32[]{:S(2)}, u32[]{:S(2)}) collective-permute-start(bf16[128,512]{1,0:T(8,128)(2,1)S(1)} %add_convert_fusion.3), channel_id=1, source_target_pairs={{0,4},{2,6},{4,0},{6,2},{8,12},{10,14},{12,8},{14,10},{1,5},{3,7},... | collective-permute-start | bytes 393224 | tf_op jit(solution)/shard_map/ppermute | solution.py:190
  20.9 10.9 %copy-start.4 = (bf16[128,512]{1,0:T(8,128)(2,1)}, bf16[128,512]{1,0:T(8,128)(2,1)S(1)}, u32[]{:S(2)}) copy-start(bf16[128,512]{1,0:T(8,128)(2,1)S(1)} %collective-permute-done.4.cols_ref) | copy-start | bytes 393220
  21.0 2.3 %copy-start.1 = (bf16[128,512]{1,0:T(8,128)(2,1)S(1)}, bf16[128,512]{1,0:T(8,128)(2,1)}, u32[]{:S(2)}) copy-start(bf16[128,512]{1,0:T(8,128)(2,1)} %q_ref.7) | copy-start | bytes 393220
  21.0 7.8 %collective-permute-start.9 = (bf16[384,512]{1,0:T(8,128)(2,1)S(1)}, bf16[384,512]{1,0:T(8,128)(2,1)S(1)}, u32[]{:S(2)}, u32[]{:S(2)}) collective-permute-start(bf16[384,512]{1,0:T(8,128)(2,1)S(1)} %pad_maximum_fusion), channel_id=1, source_target_pairs={{0,2},{2,0},{4,6},{6,4},{8,10},{10,8},{12,14},{14,12},{1,3},{3,1},... | collective-permute-start | bytes 1179656 | tf_op jit(solution)/shard_map/ppermute | solution.py:190
  22.8 7.4 %collective-permute-start.8 = (bf16[128,512]{1,0:T(8,128)(2,1)S(1)}, bf16[128,512]{1,0:T(8,128)(2,1)S(1)}, u32[]{:S(2)}, u32[]{:S(2)}) collective-permute-start(bf16[128,512]{1,0:T(8,128)(2,1)S(1)} %add_convert_fusion.2), channel_id=1, source_target_pairs={{0,8},{2,10},{4,12},{6,14},{8,0},{10,2},{12,4},{14,6},{1,9},{3,11}... | collective-permute-start | bytes 393224 | tf_op jit(solution)/shard_map/ppermute | solution.py:190
  29.3 7.2 %collective-permute-start.10 = (f32[128,512]{1,0:T(8,128)S(1)}, f32[128,512]{1,0:T(8,128)S(1)}, u32[]{:S(2)}, u32[]{:S(2)}) collective-permute-start(f32[128,512]{1,0:T(8,128)S(1)} %shard_map.97), channel_id=1, source_target_pairs={{0,16},{16,0},{1,17},{17,1},{2,18},{18,2},{3,19},{19,3},{4,20},{20... | collective-permute-start | bytes 786440 | tf_op jit(solution)/shard_map/ppermute | solution.py:199
  30.5 7.9 %collective-permute-start.14 = (bf16[128,512]{1,0:T(8,128)(2,1)S(1)}, bf16[128,512]{1,0:T(8,128)(2,1)S(1)}, u32[]{:S(2)}, u32[]{:S(2)}) collective-permute-start(bf16[128,512]{1,0:T(8,128)(2,1)S(1)} %get-tuple-element.59.n_ref), channel_id=1, source_target_pairs={{0,16},{16,0},{1,17},{17,1},{2,18},{18,2},{3,19},{19,3},{4,20},{20... | collective-permute-start | bytes 393224 | tf_op jit(solution)/shard_map/ppermute | solution.py:199
  31.8 8.9 %collective-permute-start.12 = (bf16[128,512]{1,0:T(8,128)(2,1)S(1)}, bf16[128,512]{1,0:T(8,128)(2,1)S(1)}, u32[]{:S(2)}, u32[]{:S(2)}) collective-permute-start(bf16[128,512]{1,0:T(8,128)(2,1)S(1)} %get-tuple-element.59.n_ref), channel_id=1, source_target_pairs={{0,4},{2,6},{4,0},{6,2},{8,12},{10,14},{12,8},{14,10},{1,5},{3,7},... | collective-permute-start | bytes 393224 | tf_op jit(solution)/shard_map/ppermute | solution.py:190
  33.3 12.9 %collective-permute-start.19 = (bf16[256,512]{1,0:T(8,128)(2,1)S(1)}, bf16[256,512]{1,0:T(8,128)(2,1)S(1)}, u32[]{:S(2)}, u32[]{:S(2)}) collective-permute-start(bf16[256,512]{1,0:T(8,128)(2,1)S(1)} %get-tuple-element.71), channel_id=1, source_target_pairs={{0,8},{2,10},{4,12},{6,14},{8,0},{10,2},{12,4},{14,6},{1,9},{3,11}... | collective-permute-start | bytes 786440 | tf_op jit(solution)/shard_map/ppermute | solution.py:190
  36.8 5.0 %collective-permute-start.11 = (bf16[128,512]{1,0:T(8,128)(2,1)S(1)}, bf16[128,512]{1,0:T(8,128)(2,1)S(1)}, u32[]{:S(2)}, u32[]{:S(2)}) collective-permute-start(bf16[128,512]{1,0:T(8,128)(2,1)S(1)} %get-tuple-element.58), channel_id=1, source_target_pairs={{0,2},{2,0},{4,6},{6,4},{8,10},{10,8},{12,14},{14,12},{1,3},{3,1},... | collective-permute-start | bytes 393224 | tf_op jit(solution)/shard_map/ppermute | solution.py:190
  39.1 8.6 %collective-permute-start.15 = (bf16[128,1024]{1,0:T(8,128)(2,1)S(1)}, bf16[128,1024]{1,0:T(8,128)(2,1)S(1)}, u32[]{:S(2)}, u32[]{:S(2)}) collective-permute-start(bf16[128,1024]{1,0:T(8,128)(2,1)S(1)} %get-tuple-element.61), channel_id=1, source_target_pairs={{0,16},{16,0},{1,17},{17,1},{2,18},{18,2},{3,19},{19,3},{4,20},{20... | collective-permute-start | bytes 786440 | tf_op jit(solution)/shard_map/ppermute | solution.py:199
  40.7 13.3 %collective-permute-start.17 = (bf16[128,1024]{1,0:T(8,128)(2,1)S(1)}, bf16[128,1024]{1,0:T(8,128)(2,1)S(1)}, u32[]{:S(2)}, u32[]{:S(2)}) collective-permute-start(bf16[128,1024]{1,0:T(8,128)(2,1)S(1)} %get-tuple-element.67.a_ref), channel_id=1, source_target_pairs={{0,1},{1,0},{2,3},{3,2},{4,5},{5,4},{6,7},{7,6},{8,9},{9,8},{10,11... | collective-permute-start | bytes 786440 | tf_op jit(solution)/shard_map/ppermute | solution.py:202
  41.9 4.3 %slice-start = ((bf16[128,512]{1,0:T(8,128)(2,1)}), bf16[128,256]{1,0:T(8,128)(2,1)S(1)}, s32[]{:S(2)}) async-start(bf16[128,512]{1,0:T(8,128)(2,1)} %copy-done.4), calls=%async_computation | async-start | bytes 131072 | tf_op jit(solution)/shard_map/slice | solution.py:388
  41.9 7.0 %collective-permute-start.13 = (bf16[128,512]{1,0:T(8,128)(2,1)S(1)}, bf16[128,512]{1,0:T(8,128)(2,1)S(1)}, u32[]{:S(2)}, u32[]{:S(2)}) collective-permute-start(bf16[128,512]{1,0:T(8,128)(2,1)S(1)} %add_convert_fusion.1), channel_id=1, source_target_pairs={{0,4},{2,6},{4,0},{6,2},{8,12},{10,14},{12,8},{14,10},{1,5},{3,7},... | collective-permute-start | bytes 393224 | tf_op jit(solution)/shard_map/ppermute | solution.py:190
  46.2 5.5 %collective-permute-start.21 = (bf16[128,512]{1,0:T(8,128)(2,1)S(1)}, bf16[128,512]{1,0:T(8,128)(2,1)S(1)}, u32[]{:S(2)}, u32[]{:S(2)}) collective-permute-start(bf16[128,512]{1,0:T(8,128)(2,1)S(1)} %get-tuple-element.83), channel_id=1, source_target_pairs={{0,4},{2,6},{4,0},{6,2},{8,12},{10,14},{12,8},{14,10},{1,5},{3,7},... | collective-permute-start | bytes 393224 | tf_op jit(solution)/shard_map/ppermute | solution.py:190
  46.3 5.4 %collective-permute-start.20 = (bf16[128,768]{1,0:T(8,128)(2,1)S(1)}, bf16[128,768]{1,0:T(8,128)(2,1)S(1)}, u32[]{:S(2)}, u32[]{:S(2)}) collective-permute-start(bf16[128,768]{1,0:T(8,128)(2,1)S(1)} %pad_maximum_fusion.1.c_ref), channel_id=1, source_target_pairs={{0,1},{1,0},{2,3},{3,2},{4,5},{5,4},{6,7},{7,6},{8,9},{9,8},{10,11... | collective-permute-start | bytes 589832 | tf_op jit(solution)/shard_map/ppermute | solution.py:202
  49.0 5.0 %collective-permute-start.18 = (bf16[128,1024]{1,0:T(8,128)(2,1)S(1)}, bf16[128,1024]{1,0:T(8,128)(2,1)S(1)}, u32[]{:S(2)}, u32[]{:S(2)}) collective-permute-start(bf16[128,1024]{1,0:T(8,128)(2,1)S(1)} %collective-permute-done.15.c_ref), channel_id=1, source_target_pairs={{0,1},{1,0},{2,3},{3,2},{4,5},{5,4},{6,7},{7,6},{8,9},{9,8},{10,11... | collective-permute-start | bytes 786440 | tf_op jit(solution)/shard_map/ppermute | solution.py:202
  49.0 9.7 %collective-permute-start.16 = (bf16[128,512]{1,0:T(8,128)(2,1)S(1)}, bf16[128,512]{1,0:T(8,128)(2,1)S(1)}, u32[]{:S(2)}, u32[]{:S(2)}) collective-permute-start(bf16[128,512]{1,0:T(8,128)(2,1)S(1)} %add_convert_fusion), channel_id=1, source_target_pairs={{0,8},{2,10},{4,12},{6,14},{8,0},{10,2},{12,4},{14,6},{1,9},{3,11}... | collective-permute-start | bytes 393224 | tf_op jit(solution)/shard_map/ppermute | solution.py:190
  52.4 7.7 %collective-permute-start.22 = (bf16[256,512]{1,0:T(8,128)(2,1)S(1)}, bf16[256,512]{1,0:T(8,128)(2,1)S(1)}, u32[]{:S(2)}, u32[]{:S(2)}) collective-permute-start(bf16[256,512]{1,0:T(8,128)(2,1)S(1)} %get-tuple-element.74), channel_id=1, source_target_pairs={{0,2},{2,0},{4,6},{6,4},{8,10},{10,8},{12,14},{14,12},{1,3},{3,1},... | collective-permute-start | bytes 786440 | tf_op jit(solution)/shard_map/ppermute | solution.py:190

commit v9 on v8

--- a/solution.py
+++ b/solution.py
@@ -16,15 +16,15 @@
 LAST_T = (((1,), (1,)), ((), ()))
 HINTS = {
     "own_state": 300000000,
-    "pack": 3000000000,
-    "local": 1000000000,
-    "back_other": 1000000000,
+    "pack": 600000000,
+    "local": 3000000000,
+    "back_other": 1048576,
     "back_own": 1000000000,
     "forward": 3000000000,
-    "turn_back": 1048576,
+    "turn_back": 3000000000,
     "project": 3000000000,
     "local_grads": 1048576,
-    "weight_grad": 1500000000,
+    "weight_grad": 600000000,
     "join": 1048576,
     "last": 3000000000,
 }
@@ -219,7 +219,7 @@
 
     (states,) = call(own_state, [(state, BF16)], keys, values)
     x_states = swap(states, 1)
-    states, own_weight = tie(states, my_weight)
+    states, own_weight, packed = tie(states, my_weight, grad_y)
     x_weight_own = swap(own_weight, 1)
 
     def columns(gy_ref, z, h):
@@ -234,9 +234,10 @@
         near_ref[:, wrows:] = columns(gy_ref, lax.rem(near + 2, line), h)
 
     y_send, near_send = call(
-        pack, [((rows, seq * half), BF16), ((rows, 2 * wrows), BF16)], grad_y
+        pack, [((rows, seq * half), BF16), ((rows, 2 * wrows), BF16)], packed
     )
     near_cols = swap(near_send, 2)
+    y_send, later_values = tie(y_send, values)
     y_cols = swap_y(y_send)
 
     def local(q_ref, k_ref, v_ref, sc_ref, att_ref):
@@ -248,18 +249,17 @@
             att_ref[:, head_of(i)] = dot(sc, v_ref[:, head_of(i)], PLAIN)
 
     scores, att_local = call(
-        local, [((rows, feats), BF16), ((rows, feats), F32)], queries, keys, values
+        local, [((rows, feats), BF16), ((rows, feats), F32)], queries, keys, later_values
     )
 
     def add(a, b):
         return (a.astype(F32) + b.astype(F32)).astype(BF16)
 
+    x_states, x_weight_own, att_local = tie(x_states, x_weight_own, att_local)
     pair_states = add(states, x_states)
     near_states = swap(pair_states, 2)
-    pair_states, x_weight_own, near_cols, *z_weight = tie(
-        pair_states, x_weight_own, near_cols, *z_weight
-    )
-    near_states, y_cols = tie(near_states, y_cols)
+    pair_states, *z_weight = tie(pair_states, *z_weight)
+    near_states, y_cols, near_cols = tie(near_states, y_cols, near_cols)
     quad_states = add(pair_states, near_states)
     got_states = x_states, near_states, swap(quad_states, 4)
 
@@ -332,7 +332,8 @@
         + [((2 * rows, feats), BF16)],
         queries, att_local, *got_states, grad_y, near_cols,
     )
-    y_normed = swap_y(normed)
+    y_send, grad_own = tie(normed, grad_own)
+    y_normed = swap_y(y_send)
     far = swap(far_send, 4)
 
     def turn_back(att_ref, own_ref, other_ref, q_ref, go_ref, adj_ref):
@@ -350,9 +351,9 @@
         turn_back, [((rows, feats), BF16), (state, BF16)],
         attended, grad_own, grad_other, queries,
     )
-    near_normed = swap(normed, 2)
+    near_send, grad_out = tie(normed, grad_out)
+    near_normed = swap(near_send, 2)
     x_adjoint = swap(adjoint, 1)
-    x_adjoint, near_normed = tie(x_adjoint, near_normed)
     def project(n_ref, yn_ref, *refs):
         *w_refs, own_ref, other_ref = refs
         for s, block in weight_blocks(w_refs):
@@ -364,6 +365,7 @@
     )
     out_other = swap_y(out_send)
     last_normed = swap(far[:rows], 2)
+    x_adjoint, near_normed = tie(x_adjoint, near_normed)
     pair_adjoint = add(adjoint, x_adjoint)
     near_adjoint = swap(pair_adjoint, 2)
     def local_grads(go_ref, q_ref, k_ref, v_ref, sc_ref, pre_ref, gq_ref, gk_ref, gv_ref):

time: 61.1 us -> 62.3 us (1.020)
  waiting for transfers between devices: 21.4 us -> 26 us
  starting transfers between devices: 29.3 us -> 25.8 us
    ppermute x16, starting transfers between devices: 23.9 us -> 20.4 us  [permute(): return lax.ppermute(array, 'seq', pairs)]
    ppermute x4, waiting for transfers between devices: 0.01 us -> 2.47 us  [swap_y(): return lax.ppermute(array, 'groups', [(0, 1), (1, 0)])]
    ppermute x16, waiting for transfers between devices: 21.4 us -> 23.5 us  [permute(): return lax.ppermute(array, 'seq', pairs)]
where the time goes in v9:
time: 62.3 us; the launch traced here: 62.1 us
  waiting for transfers between devices  26 us (42%)
  starting transfers between devices  25.8 us (41%)
  Pallas kernels  7.39 us (12%)
  other arithmetic  1.04 us (2%)
  local copies, waits for them, and re-layouts  1 us (2%)
  between operations  0.83 us (1%)
    ppermute x16, waiting for transfers between devices, permute(): return lax.ppermute(array, 'seq', pairs)  23.5 us
    ppermute x16, starting transfers between devices, permute(): return lax.ppermute(array, 'seq', pairs)  20.4 us
    pallas_call x12, Pallas kernels, call(): pl.pallas_call(body, out_shape=[jax.ShapeDtypeStruct(s, d) for s, d in sh...  7.39 us
    ppermute x4, starting transfers between devices, swap_y(): return lax.ppermute(array, 'groups', [(0, 1), (1, 0)])  5.33 us
    ppermute x4, waiting for transfers between devices, swap_y(): return lax.ppermute(array, 'groups', [(0, 1), (1, 0)])  2.47 us
  transfers between devices with their start and end apart: 23, of which 11 were waited for; matrix products, arithmetic and copies ran while one was open for 0% of the time, Pallas kernels for 12%

profile of v9, /device:TPU:0, one launch (start us, length us, event | category | flops | bytes accessed | tf_op | source)
XLA Modules:
  0.0 62.1 jit_solution(6756190263565206083)
XLA Ops:
  0.7 0.9 %copy-done = bf16[256,512]{1,0:T(8,128)(2,1)S(1)} copy-done((bf16[256,512]{1,0:T(8,128)(2,1)S(1)}, bf16[256,512]{1,0:T(8,128)(2,1)}, u32[]{:S(2)}) %copy-start) | copy-done | bytes 262168
  1.6 3.1 %collective-permute-start.5 = (bf16[128,512]{1,0:T(8,128)(2,1)S(1)}, bf16[128,512]{1,0:T(8,128)(2,1)S(1)}, u32[]{:S(2)}, u32[]{:S(2)}) collective-permute-start(bf16[128,512]{1,0:T(8,128)(2,1)S(1)} %constant_dynamic-slice_fusion.refs_0_), channel_id=1, source_target_pairs={{0,4},{2,6},{4,8},{6,10},{8,12},{10,14},{12,0},{14,2},{1,5},{3,7},... | collective-permute-start | bytes 393224 | tf_op jit(solution)/shard_map/ppermute | solution.py:190
  4.7 2.6 %collective-permute-start.6 = (bf16[128,512]{1,0:T(8,128)(2,1)S(1)}, bf16[128,512]{1,0:T(8,128)(2,1)S(1)}, u32[]{:S(2)}, u32[]{:S(2)}) collective-permute-start(bf16[128,512]{1,0:T(8,128)(2,1)S(1)} %constant_dynamic-slice_fusion.refs_0_), channel_id=1, source_target_pairs={{0,8},{2,10},{4,12},{6,14},{8,0},{10,2},{12,4},{14,6},{1,9},{3,11}... | collective-permute-start | bytes 393224 | tf_op jit(solution)/shard_map/ppermute | solution.py:190
  7.3 1.3 %collective-permute-start.7 = (bf16[128,512]{1,0:T(8,128)(2,1)S(1)}, bf16[128,512]{1,0:T(8,128)(2,1)S(1)}, u32[]{:S(2)}, u32[]{:S(2)}) collective-permute-start(bf16[128,512]{1,0:T(8,128)(2,1)S(1)} %constant_dynamic-slice_fusion.refs_0_), channel_id=1, source_target_pairs={{0,12},{2,14},{4,0},{6,2},{8,4},{10,6},{12,8},{14,10},{1,13},{3,15... | collective-permute-start | bytes 393224 | tf_op jit(solution)/shard_map/ppermute | solution.py:190
  8.9 1.6 %collective-permute-start = (bf16[128,512]{1,0:T(8,128)(2,1)S(1)}, bf16[128,512]{1,0:T(8,128)(2,1)S(1)}, u32[]{:S(2)}, u32[]{:S(2)}) collective-permute-start(bf16[128,512]{1,0:T(8,128)(2,1)S(1)} %shard_map.92), channel_id=1, source_target_pairs={{0,2},{2,0},{4,6},{6,4},{8,10},{10,8},{12,14},{14,12},{1,3},{3,1},... | collective-permute-start | bytes 393224 | tf_op jit(solution)/shard_map/ppermute | solution.py:190
  11.1 0.7 %shard_map.94 = (bf16[128,512]{1,0:T(8,128)(2,1)S(1)}, f32[128,512]{1,0:T(8,128)S(1)}) custom-call(bf16[128,512]{1,0:T(8,128)(2,1)S(1)} %copy-done.1, bf16[128,512]{1,0:T(8,128)(2,1)S(1)} %copy-done.2, bf16[128,512]{1,0:T(8,128)(2,1)S(1)} %copy-done.3), custom_call_target="tpu_custom_call" | custom-call | flops 3000000000 | bytes 1048576 | tf_op jit(solution)/shard_map/pallas_call | solution.py:149
  11.8 4.3 %collective-permute-done.1.refs_4_ = bf16[128,512]{1,0:T(8,128)(2,1)S(1)} collective-permute-done((bf16[128,512]{1,0:T(8,128)(2,1)S(1)}, bf16[128,512]{1,0:T(8,128)(2,1)S(1)}, u32[]{:S(2)}, u32[]{:S(2)}) %collective-permute-start.1) | collective-permute-done | bytes 131104 | tf_op jit(solution)/shard_map/ppermute | solution.py:190
  16.1 1.5 %collective-permute-start.3 = (bf16[128,1024]{1,0:T(8,128)(2,1)S(1)}, bf16[128,1024]{1,0:T(8,128)(2,1)S(1)}, u32[]{:S(2)}, u32[]{:S(2)}) collective-permute-start(bf16[128,1024]{1,0:T(8,128)(2,1)S(1)} %get-tuple-element.61), channel_id=1, source_target_pairs={{0,16},{16,0},{1,17},{17,1},{2,18},{18,2},{3,19},{19,3},{4,20},{20... | collective-permute-start | bytes 786440 | tf_op jit(solution)/shard_map/ppermute | solution.py:199
  17.7 0.7 %collective-permute-start.4 = (bf16[128,512]{1,0:T(8,128)(2,1)S(1)}, bf16[128,512]{1,0:T(8,128)(2,1)S(1)}, u32[]{:S(2)}, u32[]{:S(2)}) collective-permute-start(bf16[128,512]{1,0:T(8,128)(2,1)S(1)} %get-tuple-element.62), channel_id=1, source_target_pairs={{0,4},{2,6},{4,0},{6,2},{8,12},{10,14},{12,8},{14,10},{1,5},{3,7},... | collective-permute-start | bytes 393224 | tf_op jit(solution)/shard_map/ppermute | solution.py:190
  18.4 1.4 %collective-permute-start.2 = (bf16[128,512]{1,0:T(8,128)(2,1)S(1)}, bf16[128,512]{1,0:T(8,128)(2,1)S(1)}, u32[]{:S(2)}, u32[]{:S(2)}) collective-permute-start(bf16[128,512]{1,0:T(8,128)(2,1)S(1)} %add_convert_fusion.3), channel_id=1, source_target_pairs={{0,4},{2,6},{4,0},{6,2},{8,12},{10,14},{12,8},{14,10},{1,5},{3,7},... | collective-permute-start | bytes 393224 | tf_op jit(solution)/shard_map/ppermute | solution.py:190
  19.8 1.6 %collective-permute-start.9 = (bf16[384,512]{1,0:T(8,128)(2,1)S(1)}, bf16[384,512]{1,0:T(8,128)(2,1)S(1)}, u32[]{:S(2)}, u32[]{:S(2)}) collective-permute-start(bf16[384,512]{1,0:T(8,128)(2,1)S(1)} %pad_maximum_fusion), channel_id=1, source_target_pairs={{0,2},{2,0},{4,6},{6,4},{8,10},{10,8},{12,14},{14,12},{1,3},{3,1},... | collective-permute-start | bytes 1179656 | tf_op jit(solution)/shard_map/ppermute | solution.py:190
  21.4 1.2 %collective-permute-done.4.cols_ref = bf16[128,512]{1,0:T(8,128)(2,1)S(1)} collective-permute-done((bf16[128,512]{1,0:T(8,128)(2,1)S(1)}, bf16[128,512]{1,0:T(8,128)(2,1)S(1)}, u32[]{:S(2)}, u32[]{:S(2)}) %collective-permute-start.4) | collective-permute-done | bytes 131104 | tf_op jit(solution)/shard_map/ppermute | solution.py:190
  22.6 1.4 %collective-permute-done.2.near_ref = bf16[128,512]{1,0:T(8,128)(2,1)S(1)} collective-permute-done((bf16[128,512]{1,0:T(8,128)(2,1)S(1)}, bf16[128,512]{1,0:T(8,128)(2,1)S(1)}, u32[]{:S(2)}, u32[]{:S(2)}) %collective-permute-start.2) | collective-permute-done | bytes 131104 | tf_op jit(solution)/shard_map/ppermute | solution.py:190
  24.6 3.5 %collective-permute-done.9.refs_5_ = bf16[384,512]{1,0:T(8,128)(2,1)S(1)} collective-permute-done((bf16[384,512]{1,0:T(8,128)(2,1)S(1)}, bf16[384,512]{1,0:T(8,128)(2,1)S(1)}, u32[]{:S(2)}, u32[]{:S(2)}) %collective-permute-start.9) | collective-permute-done | bytes 393248 | tf_op jit(solution)/shard_map/ppermute | solution.py:190
  29.1 2.5 %collective-permute-done.8.far_ref = bf16[128,512]{1,0:T(8,128)(2,1)S(1)} collective-permute-done((bf16[128,512]{1,0:T(8,128)(2,1)S(1)}, bf16[128,512]{1,0:T(8,128)(2,1)S(1)}, u32[]{:S(2)}, u32[]{:S(2)}) %collective-permute-start.8) | collective-permute-done | bytes 131104 | tf_op jit(solution)/shard_map/ppermute | solution.py:190
  32.5 1.4 %collective-permute-start.14 = (bf16[128,512]{1,0:T(8,128)(2,1)S(1)}, bf16[128,512]{1,0:T(8,128)(2,1)S(1)}, u32[]{:S(2)}, u32[]{:S(2)}) collective-permute-start(bf16[128,512]{1,0:T(8,128)(2,1)S(1)} %get-tuple-element.78.n_ref), channel_id=1, source_target_pairs={{0,16},{16,0},{1,17},{17,1},{2,18},{18,2},{3,19},{19,3},{4,20},{20... | collective-permute-start | bytes 393224 | tf_op jit(solution)/shard_map/ppermute | solution.py:199
  34.0 2.5 %collective-permute-done.10.other_ref = f32[128,512]{1,0:T(8,128)S(1)} collective-permute-done((f32[128,512]{1,0:T(8,128)S(1)}, f32[128,512]{1,0:T(8,128)S(1)}, u32[]{:S(2)}, u32[]{:S(2)}) %collective-permute-start.10) | collective-permute-done | bytes 262176 | tf_op jit(solution)/shard_map/ppermute | solution.py:199
  36.8 2.7 %collective-permute-start.12 = (bf16[128,512]{1,0:T(8,128)(2,1)S(1)}, bf16[128,512]{1,0:T(8,128)(2,1)S(1)}, u32[]{:S(2)}, u32[]{:S(2)}) collective-permute-start(bf16[128,512]{1,0:T(8,128)(2,1)S(1)} %get-tuple-element.78.n_ref), channel_id=1, source_target_pairs={{0,4},{2,6},{4,0},{6,2},{8,12},{10,14},{12,8},{14,10},{1,5},{3,7},... | collective-permute-start | bytes 393224 | tf_op jit(solution)/shard_map/ppermute | solution.py:190
  39.6 1.5 %collective-permute-start.11 = (bf16[128,512]{1,0:T(8,128)(2,1)S(1)}, bf16[128,512]{1,0:T(8,128)(2,1)S(1)}, u32[]{:S(2)}, u32[]{:S(2)}) collective-permute-start(bf16[128,512]{1,0:T(8,128)(2,1)S(1)} %get-tuple-element.74), channel_id=1, source_target_pairs={{0,2},{2,0},{4,6},{6,4},{8,10},{10,8},{12,14},{14,12},{1,3},{3,1},... | collective-permute-start | bytes 393224 | tf_op jit(solution)/shard_map/ppermute | solution.py:190
  41.0 0.7 %shard_map.99 = (bf16[128,1024]{1,0:T(8,128)(2,1)S(1)}, bf16[128,1024]{1,0:T(8,128)(2,1)S(1)}) custom-call(bf16[128,512]{1,0:T(8,128)(2,1)S(1)} %get-tuple-element.78.n_ref, bf16[128,512]{1,0:T(8,128)(2,1)S(1)} %collective-permute-done.14.yn_ref, bf16[128,512]{1,0:T(8,128)(2,1)S(1)} %constant_dynamic-slice_fusion.refs_0_, ...), custom_call_target="tpu_custom_call" | custom-call | flops 3000000000 | bytes 1048576 | tf_op jit(solution)/shard_map/pallas_call | solution.py:149
  41.7 1.8 %collective-permute-start.15 = (bf16[128,1024]{1,0:T(8,128)(2,1)S(1)}, bf16[128,1024]{1,0:T(8,128)(2,1)S(1)}, u32[]{:S(2)}, u32[]{:S(2)}) collective-permute-start(bf16[128,1024]{1,0:T(8,128)(2,1)S(1)} %get-tuple-element.79), channel_id=1, source_target_pairs={{0,16},{16,0},{1,17},{17,1},{2,18},{18,2},{3,19},{19,3},{4,20},{20... | collective-permute-start | bytes 786440 | tf_op jit(solution)/shard_map/ppermute | solution.py:199
  43.9 0.6 collective-permute-done.11.x_ref
  44.7 2.0 %collective-permute-start.21 = (bf16[128,512]{1,0:T(8,128)(2,1)S(1)}, bf16[128,512]{1,0:T(8,128)(2,1)S(1)}, u32[]{:S(2)}, u32[]{:S(2)}) collective-permute-start(bf16[128,512]{1,0:T(8,128)(2,1)S(1)} %get-tuple-element.101), channel_id=1, source_target_pairs={{0,4},{2,6},{4,0},{6,2},{8,12},{10,14},{12,8},{14,10},{1,5},{3,7},... | collective-permute-start | bytes 393224 | tf_op jit(solution)/shard_map/ppermute | solution.py:190
  46.9 1.4 %shard_map.100 = (bf16[128,512]{1,0:T(8,128)(2,1)}, f32[128,512]{1,0:T(8,128)S(1)}, f32[128,512]{1,0:T(8,128)S(1)}) custom-call(bf16[128,512]{1,0:T(8,128)(2,1)S(1)} %get-tuple-element.80.go_ref, bf16[128,512]{1,0:T(8,128)(2,1)S(1)} %copy-done.1, bf16[128,512]{1,0:T(8,128)(2,1)S(1)} %copy-done.2, bf16[128,512]{1,0:T(8,128)(2,1)S(1)} %copy-done.3, ...), custom_call_target="tpu_custom_call" | custom-call | flops 1048576 | bytes 1048576 | tf_op jit(solution)/shard_map/pallas_call | solution.py:149
  48.3 2.7 %collective-permute-done.13.near_ref = bf16[128,512]{1,0:T(8,128)(2,1)S(1)} collective-permute-done((bf16[128,512]{1,0:T(8,128)(2,1)S(1)}, bf16[128,512]{1,0:T(8,128)(2,1)S(1)}, u32[]{:S(2)}, u32[]{:S(2)}) %collective-permute-start.13) | collective-permute-done | bytes 131104 | tf_op jit(solution)/shard_map/ppermute | solution.py:190
  51.1 1.3 %collective-permute-done.21.last_ref = bf16[128,512]{1,0:T(8,128)(2,1)S(1)} collective-permute-done((bf16[128,512]{1,0:T(8,128)(2,1)S(1)}, bf16[128,512]{1,0:T(8,128)(2,1)S(1)}, u32[]{:S(2)}, u32[]{:S(2)}) %collective-permute-start.21) | collective-permute-done | bytes 131104 | tf_op jit(solution)/shard_map/ppermute | solution.py:190
  52.4 0.7 %shard_map.102 = (f32[256,512]{1,0:T(8,128)S(1)}, bf16[256,512]{1,0:T(8,128)(2,1)S(1)}) custom-call(bf16[128,2048]{1,0:T(8,128)(2,1)S(1)} %copy-done.5, bf16[128,768]{1,0:T(8,128)(2,1)S(1)} %pad_maximum_fusion.1.c_ref, bf16[128,768]{1,0:T(8,128)(2,1)S(1)} %collective-permute-done.20.o_ref, bf16[128,512]{1,0:T(8,128)(2,1)S(1)} %get-tuple-element.78.n_ref, ...), custom_call_target="tpu_custom_call" | custom-call | flops 600000000 | bytes 1048576 | tf_op jit(solution)/shard_map/pallas_call | solution.py:149
  53.1 0.6 collective-permute-start.22
  53.8 1.0 %shard_map.101 = bf16[128,2048]{1,0:T(8,128)(2,1)} custom-call(bf16[128,1024]{1,0:T(8,128)(2,1)S(1)} %get-tuple-element.85.a_ref, bf16[128,1024]{1,0:T(8,128)(2,1)S(1)} %collective-permute-done.17.b_ref, bf16[128,1024]{1,0:T(8,128)(2,1)S(1)} %collective-permute-done.15.c_ref, bf16[128,1024]{1,0:T(8,128)(2,1)S(1)} %collective-permute-done.18.d_ref), custom_call_target="tpu_custom_call" | custom-call | flops 1048576 | bytes 1048576 | tf_op jit(solution)/shard_map/pallas_call | solution.py:149
  54.7 5.5 %collective-permute-done.16.far_ref = bf16[128,512]{1,0:T(8,128)(2,1)S(1)} collective-permute-done((bf16[128,512]{1,0:T(8,128)(2,1)S(1)}, bf16[128,512]{1,0:T(8,128)(2,1)S(1)}, u32[]{:S(2)}, u32[]{:S(2)}) %collective-permute-start.16) | collective-permute-done | bytes 131104 | tf_op jit(solution)/shard_map/ppermute | solution.py:190
  60.3 1.0 %shard_map.103 = (bf16[128,512]{1,0:T(8,128)(2,1)}, bf16[128,512]{1,0:T(8,128)(2,1)}) custom-call(f32[128,512]{1,0:T(8,128)S(1)} %get-tuple-element.93.gk_ref, f32[128,512]{1,0:T(8,128)S(1)} %get-tuple-element.94.gv_ref, bf16[128,512]{1,0:T(8,128)(2,1)S(1)} %copy-done.2, bf16[128,512]{1,0:T(8,128)(2,1)S(1)} %copy-done.3, ...), custom_call_target="tpu_custom_call" | custom-call | flops 3000000000 | bytes 1048576 | tf_op jit(solution)/shard_map/pallas_call | solution.py:149
  61.2 0.9 %convert_add_fusion = f32[256,512]{1,0:T(8,128)} fusion(f32[256,512]{1,0:T(8,128)S(1)} %get-tuple-element.99, bf16[256,512]{1,0:T(8,128)(2,1)S(1)} %collective-permute-done.22), kind=kLoop, calls=%fused_computation | loop fusion | flops 262144 | bytes 1310720 | tf_op jit(solution)/shard_map/add | solution.py:455
  (49 shorter events, 4.5 us)
Async XLA Ops:
  0.6 1.0 %copy-start = (bf16[256,512]{1,0:T(8,128)(2,1)S(1)}, bf16[256,512]{1,0:T(8,128)(2,1)}, u32[]{:S(2)}) copy-start(bf16[256,512]{1,0:T(8,128)(2,1)} %param.8) | copy-start | bytes 786436
  1.6 7.0 %copy-start.2 = (bf16[128,512]{1,0:T(8,128)(2,1)S(1)}, bf16[128,512]{1,0:T(8,128)(2,1)}, u32[]{:S(2)}) copy-start(bf16[128,512]{1,0:T(8,128)(2,1)} %k_ref.7) | copy-start | bytes 393220
  1.6 7.0 %copy-start.3 = (bf16[128,512]{1,0:T(8,128)(2,1)S(1)}, bf16[128,512]{1,0:T(8,128)(2,1)}, u32[]{:S(2)}) copy-start(bf16[128,512]{1,0:T(8,128)(2,1)} %v_ref.6) | copy-start | bytes 393220
  1.6 9.4 %copy-start.5 = (bf16[128,2048]{1,0:T(8,128)(2,1)S(1)}, bf16[128,2048]{1,0:T(8,128)(2,1)}, u32[]{:S(2)}) copy-start(bf16[128,2048]{1,0:T(8,128)(2,1)} %gy_ref.6) | copy-start | bytes 1572868
  1.6 16.8 %collective-permute-start.5 = (bf16[128,512]{1,0:T(8,128)(2,1)S(1)}, bf16[128,512]{1,0:T(8,128)(2,1)S(1)}, u32[]{:S(2)}, u32[]{:S(2)}) collective-permute-start(bf16[128,512]{1,0:T(8,128)(2,1)S(1)} %constant_dynamic-slice_fusion.refs_0_), channel_id=1, source_target_pairs={{0,4},{2,6},{4,8},{6,10},{8,12},{10,14},{12,0},{14,2},{1,5},{3,7},... | collective-permute-start | bytes 393224 | tf_op jit(solution)/shard_map/ppermute | solution.py:190
  4.7 15.1 %collective-permute-start.6 = (bf16[128,512]{1,0:T(8,128)(2,1)S(1)}, bf16[128,512]{1,0:T(8,128)(2,1)S(1)}, u32[]{:S(2)}, u32[]{:S(2)}) collective-permute-start(bf16[128,512]{1,0:T(8,128)(2,1)S(1)} %constant_dynamic-slice_fusion.refs_0_), channel_id=1, source_target_pairs={{0,8},{2,10},{4,12},{6,14},{8,0},{10,2},{12,4},{14,6},{1,9},{3,11}... | collective-permute-start | bytes 393224 | tf_op jit(solution)/shard_map/ppermute | solution.py:190
  7.3 12.5 %collective-permute-start.7 = (bf16[128,512]{1,0:T(8,128)(2,1)S(1)}, bf16[128,512]{1,0:T(8,128)(2,1)S(1)}, u32[]{:S(2)}, u32[]{:S(2)}) collective-permute-start(bf16[128,512]{1,0:T(8,128)(2,1)S(1)} %constant_dynamic-slice_fusion.refs_0_), channel_id=1, source_target_pairs={{0,12},{2,14},{4,0},{6,2},{8,4},{10,6},{12,8},{14,10},{1,13},{3,15... | collective-permute-start | bytes 393224 | tf_op jit(solution)/shard_map/ppermute | solution.py:190
  8.9 2.2 %copy-start.1 = (bf16[128,512]{1,0:T(8,128)(2,1)S(1)}, bf16[128,512]{1,0:T(8,128)(2,1)}, u32[]{:S(2)}) copy-start(bf16[128,512]{1,0:T(8,128)(2,1)} %q_ref.7) | copy-start | bytes 393220
  8.9 8.8 %collective-permute-start = (bf16[128,512]{1,0:T(8,128)(2,1)S(1)}, bf16[128,512]{1,0:T(8,128)(2,1)S(1)}, u32[]{:S(2)}, u32[]{:S(2)}) collective-permute-start(bf16[128,512]{1,0:T(8,128)(2,1)S(1)} %shard_map.92), channel_id=1, source_target_pairs={{0,2},{2,0},{4,6},{6,4},{8,10},{10,8},{12,14},{14,12},{1,3},{3,1},... | collective-permute-start | bytes 393224 | tf_op jit(solution)/shard_map/ppermute | solution.py:190
  10.4 5.7 %collective-permute-start.1 = (bf16[128,512]{1,0:T(8,128)(2,1)S(1)}, bf16[128,512]{1,0:T(8,128)(2,1)S(1)}, u32[]{:S(2)}, u32[]{:S(2)}) collective-permute-start(bf16[128,512]{1,0:T(8,128)(2,1)S(1)} %constant_dynamic-slice_fusion.refs_0_), channel_id=1, source_target_pairs={{0,2},{2,0},{4,6},{6,4},{8,10},{10,8},{12,14},{14,12},{1,3},{3,1},... | collective-permute-start | bytes 393224 | tf_op jit(solution)/shard_map/ppermute | solution.py:190
  16.1 7.9 %collective-permute-start.3 = (bf16[128,1024]{1,0:T(8,128)(2,1)S(1)}, bf16[128,1024]{1,0:T(8,128)(2,1)S(1)}, u32[]{:S(2)}, u32[]{:S(2)}) collective-permute-start(bf16[128,1024]{1,0:T(8,128)(2,1)S(1)} %get-tuple-element.61), channel_id=1, source_target_pairs={{0,16},{16,0},{1,17},{17,1},{2,18},{18,2},{3,19},{19,3},{4,20},{20... | collective-permute-start | bytes 786440 | tf_op jit(solution)/shard_map/ppermute | solution.py:199
  17.7 5.0 %collective-permute-start.4 = (bf16[128,512]{1,0:T(8,128)(2,1)S(1)}, bf16[128,512]{1,0:T(8,128)(2,1)S(1)}, u32[]{:S(2)}, u32[]{:S(2)}) collective-permute-start(bf16[128,512]{1,0:T(8,128)(2,1)S(1)} %get-tuple-element.62), channel_id=1, source_target_pairs={{0,4},{2,6},{4,0},{6,2},{8,12},{10,14},{12,8},{14,10},{1,5},{3,7},... | collective-permute-start | bytes 393224 | tf_op jit(solution)/shard_map/ppermute | solution.py:190
  18.4 5.6 %collective-permute-start.2 = (bf16[128,512]{1,0:T(8,128)(2,1)S(1)}, bf16[128,512]{1,0:T(8,128)(2,1)S(1)}, u32[]{:S(2)}, u32[]{:S(2)}) collective-permute-start(bf16[128,512]{1,0:T(8,128)(2,1)S(1)} %add_convert_fusion.3), channel_id=1, source_target_pairs={{0,4},{2,6},{4,0},{6,2},{8,12},{10,14},{12,8},{14,10},{1,5},{3,7},... | collective-permute-start | bytes 393224 | tf_op jit(solution)/shard_map/ppermute | solution.py:190
  19.8 8.3 %collective-permute-start.9 = (bf16[384,512]{1,0:T(8,128)(2,1)S(1)}, bf16[384,512]{1,0:T(8,128)(2,1)S(1)}, u32[]{:S(2)}, u32[]{:S(2)}) collective-permute-start(bf16[384,512]{1,0:T(8,128)(2,1)S(1)} %pad_maximum_fusion), channel_id=1, source_target_pairs={{0,2},{2,0},{4,6},{6,4},{8,10},{10,8},{12,14},{14,12},{1,3},{3,1},... | collective-permute-start | bytes 1179656 | tf_op jit(solution)/shard_map/ppermute | solution.py:190
  22.6 9.0 %copy-start.4 = (bf16[128,512]{1,0:T(8,128)(2,1)}, bf16[128,512]{1,0:T(8,128)(2,1)S(1)}, u32[]{:S(2)}) copy-start(bf16[128,512]{1,0:T(8,128)(2,1)S(1)} %collective-permute-done.4.cols_ref) | copy-start | bytes 393220
  24.1 7.6 %collective-permute-start.8 = (bf16[128,512]{1,0:T(8,128)(2,1)S(1)}, bf16[128,512]{1,0:T(8,128)(2,1)S(1)}, u32[]{:S(2)}, u32[]{:S(2)}) collective-permute-start(bf16[128,512]{1,0:T(8,128)(2,1)S(1)} %add_convert_fusion.2), channel_id=1, source_target_pairs={{0,8},{2,10},{4,12},{6,14},{8,0},{10,2},{12,4},{14,6},{1,9},{3,11}... | collective-permute-start | bytes 393224 | tf_op jit(solution)/shard_map/ppermute | solution.py:190
  28.6 7.8 %collective-permute-start.10 = (f32[128,512]{1,0:T(8,128)S(1)}, f32[128,512]{1,0:T(8,128)S(1)}, u32[]{:S(2)}, u32[]{:S(2)}) collective-permute-start(f32[128,512]{1,0:T(8,128)S(1)} %shard_map.97), channel_id=1, source_target_pairs={{0,16},{16,0},{1,17},{17,1},{2,18},{18,2},{3,19},{19,3},{4,20},{20... | collective-permute-start | bytes 786440 | tf_op jit(solution)/shard_map/ppermute | solution.py:199
  32.0 12.7 %collective-permute-start.19 = (bf16[256,512]{1,0:T(8,128)(2,1)S(1)}, bf16[256,512]{1,0:T(8,128)(2,1)S(1)}, u32[]{:S(2)}, u32[]{:S(2)}) collective-permute-start(bf16[256,512]{1,0:T(8,128)(2,1)S(1)} %get-tuple-element.89), channel_id=1, source_target_pairs={{0,8},{2,10},{4,12},{6,14},{8,0},{10,2},{12,4},{14,6},{1,9},{3,11}... | collective-permute-start | bytes 786440 | tf_op jit(solution)/shard_map/ppermute | solution.py:190
  32.5 8.5 %collective-permute-start.14 = (bf16[128,512]{1,0:T(8,128)(2,1)S(1)}, bf16[128,512]{1,0:T(8,128)(2,1)S(1)}, u32[]{:S(2)}, u32[]{:S(2)}) collective-permute-start(bf16[128,512]{1,0:T(8,128)(2,1)S(1)} %get-tuple-element.78.n_ref), channel_id=1, source_target_pairs={{0,16},{16,0},{1,17},{17,1},{2,18},{18,2},{3,19},{19,3},{4,20},{20... | collective-permute-start | bytes 393224 | tf_op jit(solution)/shard_map/ppermute | solution.py:199
  36.8 7.1 %collective-permute-start.12 = (bf16[128,512]{1,0:T(8,128)(2,1)S(1)}, bf16[128,512]{1,0:T(8,128)(2,1)S(1)}, u32[]{:S(2)}, u32[]{:S(2)}) collective-permute-start(bf16[128,512]{1,0:T(8,128)(2,1)S(1)} %get-tuple-element.78.n_ref), channel_id=1, source_target_pairs={{0,4},{2,6},{4,0},{6,2},{8,12},{10,14},{12,8},{14,10},{1,5},{3,7},... | collective-permute-start | bytes 393224 | tf_op jit(solution)/shard_map/ppermute | solution.py:190
  39.6 5.0 %collective-permute-start.11 = (bf16[128,512]{1,0:T(8,128)(2,1)S(1)}, bf16[128,512]{1,0:T(8,128)(2,1)S(1)}, u32[]{:S(2)}, u32[]{:S(2)}) collective-permute-start(bf16[128,512]{1,0:T(8,128)(2,1)S(1)} %get-tuple-element.74), channel_id=1, source_target_pairs={{0,2},{2,0},{4,6},{6,4},{8,10},{10,8},{12,14},{14,12},{1,3},{3,1},... | collective-permute-start | bytes 393224 | tf_op jit(solution)/shard_map/ppermute | solution.py:190
  41.7 6.5 %collective-permute-start.15 = (bf16[128,1024]{1,0:T(8,128)(2,1)S(1)}, bf16[128,1024]{1,0:T(8,128)(2,1)S(1)}, u32[]{:S(2)}, u32[]{:S(2)}) collective-permute-start(bf16[128,1024]{1,0:T(8,128)(2,1)S(1)} %get-tuple-element.79), channel_id=1, source_target_pairs={{0,16},{16,0},{1,17},{17,1},{2,18},{18,2},{3,19},{19,3},{4,20},{20... | collective-permute-start | bytes 786440 | tf_op jit(solution)/shard_map/ppermute | solution.py:199
  43.6 10.2 %collective-permute-start.17 = (bf16[128,1024]{1,0:T(8,128)(2,1)S(1)}, bf16[128,1024]{1,0:T(8,128)(2,1)S(1)}, u32[]{:S(2)}, u32[]{:S(2)}) collective-permute-start(bf16[128,1024]{1,0:T(8,128)(2,1)S(1)} %get-tuple-element.85.a_ref), channel_id=1, source_target_pairs={{0,1},{1,0},{2,3},{3,2},{4,5},{5,4},{6,7},{7,6},{8,9},{9,8},{10,11... | collective-permute-start | bytes 786440 | tf_op jit(solution)/shard_map/ppermute | solution.py:202
  44.6 2.2 %slice-start = ((bf16[128,512]{1,0:T(8,128)(2,1)}), bf16[128,256]{1,0:T(8,128)(2,1)S(1)}, s32[]{:S(2)}) async-start(bf16[128,512]{1,0:T(8,128)(2,1)} %copy-done.4), calls=%async_computation | async-start | bytes 131072 | tf_op jit(solution)/shard_map/slice | solution.py:390
  44.6 6.4 %collective-permute-start.13 = (bf16[128,512]{1,0:T(8,128)(2,1)S(1)}, bf16[128,512]{1,0:T(8,128)(2,1)S(1)}, u32[]{:S(2)}, u32[]{:S(2)}) collective-permute-start(bf16[128,512]{1,0:T(8,128)(2,1)S(1)} %add_convert_fusion.1), channel_id=1, source_target_pairs={{0,4},{2,6},{4,0},{6,2},{8,12},{10,14},{12,8},{14,10},{1,5},{3,7},... | collective-permute-start | bytes 393224 | tf_op jit(solution)/shard_map/ppermute | solution.py:190
  44.7 7.7 %collective-permute-start.21 = (bf16[128,512]{1,0:T(8,128)(2,1)S(1)}, bf16[128,512]{1,0:T(8,128)(2,1)S(1)}, u32[]{:S(2)}, u32[]{:S(2)}) collective-permute-start(bf16[128,512]{1,0:T(8,128)(2,1)S(1)} %get-tuple-element.101), channel_id=1, source_target_pairs={{0,4},{2,6},{4,0},{6,2},{8,12},{10,14},{12,8},{14,10},{1,5},{3,7},... | collective-permute-start | bytes 393224 | tf_op jit(solution)/shard_map/ppermute | solution.py:190
  46.8 5.6 %collective-permute-start.20 = (bf16[128,768]{1,0:T(8,128)(2,1)S(1)}, bf16[128,768]{1,0:T(8,128)(2,1)S(1)}, u32[]{:S(2)}, u32[]{:S(2)}) collective-permute-start(bf16[128,768]{1,0:T(8,128)(2,1)S(1)} %pad_maximum_fusion.1.c_ref), channel_id=1, source_target_pairs={{0,1},{1,0},{2,3},{3,2},{4,5},{5,4},{6,7},{7,6},{8,9},{9,8},{10,11... | collective-permute-start | bytes 589832 | tf_op jit(solution)/shard_map/ppermute | solution.py:202
  51.0 2.8 %collective-permute-start.18 = (bf16[128,1024]{1,0:T(8,128)(2,1)S(1)}, bf16[128,1024]{1,0:T(8,128)(2,1)S(1)}, u32[]{:S(2)}, u32[]{:S(2)}) collective-permute-start(bf16[128,1024]{1,0:T(8,128)(2,1)S(1)} %collective-permute-done.15.c_ref), channel_id=1, source_target_pairs={{0,1},{1,0},{2,3},{3,2},{4,5},{5,4},{6,7},{7,6},{8,9},{9,8},{10,11... | collective-permute-start | bytes 786440 | tf_op jit(solution)/shard_map/ppermute | solution.py:202
  51.0 9.2 %collective-permute-start.16 = (bf16[128,512]{1,0:T(8,128)(2,1)S(1)}, bf16[128,512]{1,0:T(8,128)(2,1)S(1)}, u32[]{:S(2)}, u32[]{:S(2)}) collective-permute-start(bf16[128,512]{1,0:T(8,128)(2,1)S(1)} %add_convert_fusion), channel_id=1, source_target_pairs={{0,8},{2,10},{4,12},{6,14},{8,0},{10,2},{12,4},{14,6},{1,9},{3,11}... | collective-permute-start | bytes 393224 | tf_op jit(solution)/shard_map/ppermute | solution.py:190
  53.1 8.1 %collective-permute-start.22 = (bf16[256,512]{1,0:T(8,128)(2,1)S(1)}, bf16[256,512]{1,0:T(8,128)(2,1)S(1)}, u32[]{:S(2)}, u32[]{:S(2)}) collective-permute-start(bf16[256,512]{1,0:T(8,128)(2,1)S(1)} %get-tuple-element.92), channel_id=1, source_target_pairs={{0,2},{2,0},{4,6},{6,4},{8,10},{10,8},{12,14},{14,12},{1,3},{3,1},... | collective-permute-start | bytes 786440 | tf_op jit(solution)/shard_map/ppermute | solution.py:190

commit v10 on v9

--- a/solution.py
+++ b/solution.py
@@ -332,8 +332,9 @@
         + [((2 * rows, feats), BF16)],
         queries, att_local, *got_states, grad_y, near_cols,
     )
-    y_send, grad_own = tie(normed, grad_own)
-    y_normed = swap_y(y_send)
+    swap_send, grad_own = tie(normed, grad_own)
+    y_normed = swap_y(swap_send)
+    near_normed = swap(swap_send, 2)
     far = swap(far_send, 4)
 
     def turn_back(att_ref, own_ref, other_ref, q_ref, go_ref, adj_ref):
@@ -351,8 +352,6 @@
         turn_back, [((rows, feats), BF16), (state, BF16)],
         attended, grad_own, grad_other, queries,
     )
-    near_send, grad_out = tie(normed, grad_out)
-    near_normed = swap(near_send, 2)
     x_adjoint = swap(adjoint, 1)
     def project(n_ref, yn_ref, *refs):
         *w_refs, own_ref, other_ref = refs

time: 62.3 us -> 61 us (0.979)
  waiting for transfers between devices: 26 us -> 23.8 us
  starting transfers between devices: 25.8 us -> 26.9 us
    ppermute x16, starting transfers between devices: 20.4 us -> 22.7 us  [permute(): return lax.ppermute(array, 'seq', pairs)]
    ppermute x4, waiting for transfers between devices: 2.47 us -> 0.8 us  [swap_y(): return lax.ppermute(array, 'groups', [(0, 1), (1, 0)])]
    ppermute x4, starting transfers between devices: 5.33 us -> 4.15 us  [swap_y(): return lax.ppermute(array, 'groups', [(0, 1), (1, 0)])]
where the time goes in v10:
time: 61 us; the launch traced here: 60.9 us
  starting transfers between devices  26.9 us (44%)
  waiting for transfers between devices  23.8 us (39%)
  Pallas kernels  7.39 us (12%)
  other arithmetic  1.04 us (2%)
  local copies, waits for them, and re-layouts  1 us (2%)
  between operations  0.82 us (1%)
    ppermute x16, waiting for transfers between devices, permute(): return lax.ppermute(array, 'seq', pairs)  23 us
    ppermute x16, starting transfers between devices, permute(): return lax.ppermute(array, 'seq', pairs)  22.7 us
    pallas_call x12, Pallas kernels, call(): pl.pallas_call(body, out_shape=[jax.ShapeDtypeStruct(s, d) for s, d in sh...  7.39 us
    ppermute x4, starting transfers between devices, swap_y(): return lax.ppermute(array, 'groups', [(0, 1), (1, 0)])  4.15 us
  transfers between devices with their start and end apart: 23, of which 11 were waited for; matrix products, arithmetic and copies ran while one was open for 0% of the time, Pallas kernels for 12%

profile of v10, /device:TPU:0, one launch (start us, length us, event | category | flops | bytes accessed | tf_op | source)
XLA Modules:
  0.0 60.9 jit_solution(18205107971069593264)
XLA Ops:
  0.7 0.9 %copy-done = bf16[256,512]{1,0:T(8,128)(2,1)S(1)} copy-done((bf16[256,512]{1,0:T(8,128)(2,1)S(1)}, bf16[256,512]{1,0:T(8,128)(2,1)}, u32[]{:S(2)}) %copy-start) | copy-done | bytes 262168
  1.6 3.1 %collective-permute-start.5 = (bf16[128,512]{1,0:T(8,128)(2,1)S(1)}, bf16[128,512]{1,0:T(8,128)(2,1)S(1)}, u32[]{:S(2)}, u32[]{:S(2)}) collective-permute-start(bf16[128,512]{1,0:T(8,128)(2,1)S(1)} %constant_dynamic-slice_fusion.refs_0_), channel_id=1, source_target_pairs={{0,4},{2,6},{4,8},{6,10},{8,12},{10,14},{12,0},{14,2},{1,5},{3,7},... | collective-permute-start | bytes 393224 | tf_op jit(solution)/shard_map/ppermute | solution.py:190
  4.7 2.6 %collective-permute-start.6 = (bf16[128,512]{1,0:T(8,128)(2,1)S(1)}, bf16[128,512]{1,0:T(8,128)(2,1)S(1)}, u32[]{:S(2)}, u32[]{:S(2)}) collective-permute-start(bf16[128,512]{1,0:T(8,128)(2,1)S(1)} %constant_dynamic-slice_fusion.refs_0_), channel_id=1, source_target_pairs={{0,8},{2,10},{4,12},{6,14},{8,0},{10,2},{12,4},{14,6},{1,9},{3,11}... | collective-permute-start | bytes 393224 | tf_op jit(solution)/shard_map/ppermute | solution.py:190
  7.3 1.3 %collective-permute-start.7 = (bf16[128,512]{1,0:T(8,128)(2,1)S(1)}, bf16[128,512]{1,0:T(8,128)(2,1)S(1)}, u32[]{:S(2)}, u32[]{:S(2)}) collective-permute-start(bf16[128,512]{1,0:T(8,128)(2,1)S(1)} %constant_dynamic-slice_fusion.refs_0_), channel_id=1, source_target_pairs={{0,12},{2,14},{4,0},{6,2},{8,4},{10,6},{12,8},{14,10},{1,13},{3,15... | collective-permute-start | bytes 393224 | tf_op jit(solution)/shard_map/ppermute | solution.py:190
  8.9 1.6 %collective-permute-start = (bf16[128,512]{1,0:T(8,128)(2,1)S(1)}, bf16[128,512]{1,0:T(8,128)(2,1)S(1)}, u32[]{:S(2)}, u32[]{:S(2)}) collective-permute-start(bf16[128,512]{1,0:T(8,128)(2,1)S(1)} %shard_map.92), channel_id=1, source_target_pairs={{0,2},{2,0},{4,6},{6,4},{8,10},{10,8},{12,14},{14,12},{1,3},{3,1},... | collective-permute-start | bytes 393224 | tf_op jit(solution)/shard_map/ppermute | solution.py:190
  11.1 0.7 %shard_map.94 = (bf16[128,512]{1,0:T(8,128)(2,1)S(1)}, f32[128,512]{1,0:T(8,128)S(1)}) custom-call(bf16[128,512]{1,0:T(8,128)(2,1)S(1)} %copy-done.1, bf16[128,512]{1,0:T(8,128)(2,1)S(1)} %copy-done.2, bf16[128,512]{1,0:T(8,128)(2,1)S(1)} %copy-done.3), custom_call_target="tpu_custom_call" | custom-call | flops 3000000000 | bytes 1048576 | tf_op jit(solution)/shard_map/pallas_call | solution.py:149
  11.8 4.3 %collective-permute-done.1.refs_4_ = bf16[128,512]{1,0:T(8,128)(2,1)S(1)} collective-permute-done((bf16[128,512]{1,0:T(8,128)(2,1)S(1)}, bf16[128,512]{1,0:T(8,128)(2,1)S(1)}, u32[]{:S(2)}, u32[]{:S(2)}) %collective-permute-start.1) | collective-permute-done | bytes 131104 | tf_op jit(solution)/shard_map/ppermute | solution.py:190
  16.1 1.5 %collective-permute-start.3 = (bf16[128,1024]{1,0:T(8,128)(2,1)S(1)}, bf16[128,1024]{1,0:T(8,128)(2,1)S(1)}, u32[]{:S(2)}, u32[]{:S(2)}) collective-permute-start(bf16[128,1024]{1,0:T(8,128)(2,1)S(1)} %get-tuple-element.59), channel_id=1, source_target_pairs={{0,16},{16,0},{1,17},{17,1},{2,18},{18,2},{3,19},{19,3},{4,20},{20... | collective-permute-start | bytes 786440 | tf_op jit(solution)/shard_map/ppermute | solution.py:199
  17.7 0.7 %collective-permute-start.4 = (bf16[128,512]{1,0:T(8,128)(2,1)S(1)}, bf16[128,512]{1,0:T(8,128)(2,1)S(1)}, u32[]{:S(2)}, u32[]{:S(2)}) collective-permute-start(bf16[128,512]{1,0:T(8,128)(2,1)S(1)} %get-tuple-element.60), channel_id=1, source_target_pairs={{0,4},{2,6},{4,0},{6,2},{8,12},{10,14},{12,8},{14,10},{1,5},{3,7},... | collective-permute-start | bytes 393224 | tf_op jit(solution)/shard_map/ppermute | solution.py:190
  18.4 1.4 %collective-permute-start.2 = (bf16[128,512]{1,0:T(8,128)(2,1)S(1)}, bf16[128,512]{1,0:T(8,128)(2,1)S(1)}, u32[]{:S(2)}, u32[]{:S(2)}) collective-permute-start(bf16[128,512]{1,0:T(8,128)(2,1)S(1)} %add_convert_fusion.3), channel_id=1, source_target_pairs={{0,4},{2,6},{4,0},{6,2},{8,12},{10,14},{12,8},{14,10},{1,5},{3,7},... | collective-permute-start | bytes 393224 | tf_op jit(solution)/shard_map/ppermute | solution.py:190
  19.8 1.6 %collective-permute-start.9 = (bf16[384,512]{1,0:T(8,128)(2,1)S(1)}, bf16[384,512]{1,0:T(8,128)(2,1)S(1)}, u32[]{:S(2)}, u32[]{:S(2)}) collective-permute-start(bf16[384,512]{1,0:T(8,128)(2,1)S(1)} %pad_maximum_fusion), channel_id=1, source_target_pairs={{0,2},{2,0},{4,6},{6,4},{8,10},{10,8},{12,14},{14,12},{1,3},{3,1},... | collective-permute-start | bytes 1179656 | tf_op jit(solution)/shard_map/ppermute | solution.py:190
  21.4 1.2 %collective-permute-done.4.cols_ref = bf16[128,512]{1,0:T(8,128)(2,1)S(1)} collective-permute-done((bf16[128,512]{1,0:T(8,128)(2,1)S(1)}, bf16[128,512]{1,0:T(8,128)(2,1)S(1)}, u32[]{:S(2)}, u32[]{:S(2)}) %collective-permute-start.4) | collective-permute-done | bytes 131104 | tf_op jit(solution)/shard_map/ppermute | solution.py:190
  22.6 1.4 %collective-permute-done.2.near_ref = bf16[128,512]{1,0:T(8,128)(2,1)S(1)} collective-permute-done((bf16[128,512]{1,0:T(8,128)(2,1)S(1)}, bf16[128,512]{1,0:T(8,128)(2,1)S(1)}, u32[]{:S(2)}, u32[]{:S(2)}) %collective-permute-start.2) | collective-permute-done | bytes 131104 | tf_op jit(solution)/shard_map/ppermute | solution.py:190
  24.6 3.5 %collective-permute-done.9.refs_5_ = bf16[384,512]{1,0:T(8,128)(2,1)S(1)} collective-permute-done((bf16[384,512]{1,0:T(8,128)(2,1)S(1)}, bf16[384,512]{1,0:T(8,128)(2,1)S(1)}, u32[]{:S(2)}, u32[]{:S(2)}) %collective-permute-start.9) | collective-permute-done | bytes 393248 | tf_op jit(solution)/shard_map/ppermute | solution.py:190
  29.1 2.5 %collective-permute-done.8.far_ref = bf16[128,512]{1,0:T(8,128)(2,1)S(1)} collective-permute-done((bf16[128,512]{1,0:T(8,128)(2,1)S(1)}, bf16[128,512]{1,0:T(8,128)(2,1)S(1)}, u32[]{:S(2)}, u32[]{:S(2)}) %collective-permute-start.8) | collective-permute-done | bytes 131104 | tf_op jit(solution)/shard_map/ppermute | solution.py:190
  32.5 1.4 %collective-permute-start.14 = (bf16[128,512]{1,0:T(8,128)(2,1)S(1)}, bf16[128,512]{1,0:T(8,128)(2,1)S(1)}, u32[]{:S(2)}, u32[]{:S(2)}) collective-permute-start(bf16[128,512]{1,0:T(8,128)(2,1)S(1)} %get-tuple-element.73.n_ref), channel_id=1, source_target_pairs={{0,16},{16,0},{1,17},{17,1},{2,18},{18,2},{3,19},{19,3},{4,20},{20... | collective-permute-start | bytes 393224 | tf_op jit(solution)/shard_map/ppermute | solution.py:199
  34.0 1.7 %collective-permute-start.12 = (bf16[128,512]{1,0:T(8,128)(2,1)S(1)}, bf16[128,512]{1,0:T(8,128)(2,1)S(1)}, u32[]{:S(2)}, u32[]{:S(2)}) collective-permute-start(bf16[128,512]{1,0:T(8,128)(2,1)S(1)} %get-tuple-element.73.n_ref), channel_id=1, source_target_pairs={{0,4},{2,6},{4,0},{6,2},{8,12},{10,14},{12,8},{14,10},{1,5},{3,7},... | collective-permute-start | bytes 393224 | tf_op jit(solution)/shard_map/ppermute | solution.py:190
  35.6 0.8 %collective-permute-done.10.other_ref = f32[128,512]{1,0:T(8,128)S(1)} collective-permute-done((f32[128,512]{1,0:T(8,128)S(1)}, f32[128,512]{1,0:T(8,128)S(1)}, u32[]{:S(2)}, u32[]{:S(2)}) %collective-permute-start.10) | collective-permute-done | bytes 262176 | tf_op jit(solution)/shard_map/ppermute | solution.py:199
  36.8 1.5 %collective-permute-start.11 = (bf16[128,512]{1,0:T(8,128)(2,1)S(1)}, bf16[128,512]{1,0:T(8,128)(2,1)S(1)}, u32[]{:S(2)}, u32[]{:S(2)}) collective-permute-start(bf16[128,512]{1,0:T(8,128)(2,1)S(1)} %get-tuple-element.72), channel_id=1, source_target_pairs={{0,2},{2,0},{4,6},{6,4},{8,10},{10,8},{12,14},{14,12},{1,3},{3,1},... | collective-permute-start | bytes 393224 | tf_op jit(solution)/shard_map/ppermute | solution.py:190
  38.4 0.7 %shard_map.99 = (bf16[128,1024]{1,0:T(8,128)(2,1)S(1)}, bf16[128,1024]{1,0:T(8,128)(2,1)S(1)}) custom-call(bf16[128,512]{1,0:T(8,128)(2,1)S(1)} %get-tuple-element.73.n_ref, bf16[128,512]{1,0:T(8,128)(2,1)S(1)} %collective-permute-done.14.yn_ref, bf16[128,512]{1,0:T(8,128)(2,1)S(1)} %constant_dynamic-slice_fusion.refs_0_, ...), custom_call_target="tpu_custom_call" | custom-call | flops 3000000000 | bytes 1048576 | tf_op jit(solution)/shard_map/pallas_call | solution.py:149
  39.1 0.6 %collective-permute-start.15 = (bf16[128,1024]{1,0:T(8,128)(2,1)S(1)}, bf16[128,1024]{1,0:T(8,128)(2,1)S(1)}, u32[]{:S(2)}, u32[]{:S(2)}) collective-permute-start(bf16[128,1024]{1,0:T(8,128)(2,1)S(1)} %get-tuple-element.75), channel_id=1, source_target_pairs={{0,16},{16,0},{1,17},{17,1},{2,18},{18,2},{3,19},{19,3},{4,20},{20... | collective-permute-start | bytes 786440 | tf_op jit(solution)/shard_map/ppermute | solution.py:199
  40.2 1.6 %collective-permute-done.11.x_ref = bf16[128,512]{1,0:T(8,128)(2,1)S(1)} collective-permute-done((bf16[128,512]{1,0:T(8,128)(2,1)S(1)}, bf16[128,512]{1,0:T(8,128)(2,1)S(1)}, u32[]{:S(2)}, u32[]{:S(2)}) %collective-permute-start.11) | collective-permute-done | bytes 131104 | tf_op jit(solution)/shard_map/ppermute | solution.py:190
  41.9 2.7 %collective-permute-start.13 = (bf16[128,512]{1,0:T(8,128)(2,1)S(1)}, bf16[128,512]{1,0:T(8,128)(2,1)S(1)}, u32[]{:S(2)}, u32[]{:S(2)}) collective-permute-start(bf16[128,512]{1,0:T(8,128)(2,1)S(1)} %add_convert_fusion.1), channel_id=1, source_target_pairs={{0,4},{2,6},{4,0},{6,2},{8,12},{10,14},{12,8},{14,10},{1,5},{3,7},... | collective-permute-start | bytes 393224 | tf_op jit(solution)/shard_map/ppermute | solution.py:190
  44.9 1.4 %shard_map.100 = (bf16[128,512]{1,0:T(8,128)(2,1)}, f32[128,512]{1,0:T(8,128)S(1)}, f32[128,512]{1,0:T(8,128)S(1)}) custom-call(bf16[128,512]{1,0:T(8,128)(2,1)S(1)} %get-tuple-element.76.go_ref, bf16[128,512]{1,0:T(8,128)(2,1)S(1)} %copy-done.1, bf16[128,512]{1,0:T(8,128)(2,1)S(1)} %copy-done.2, bf16[128,512]{1,0:T(8,128)(2,1)S(1)} %copy-done.3, ...), custom_call_target="tpu_custom_call" | custom-call | flops 1048576 | bytes 1048576 | tf_op jit(solution)/shard_map/pallas_call | solution.py:149
  46.3 2.7 %collective-permute-done.13.near_ref = bf16[128,512]{1,0:T(8,128)(2,1)S(1)} collective-permute-done((bf16[128,512]{1,0:T(8,128)(2,1)S(1)}, bf16[128,512]{1,0:T(8,128)(2,1)S(1)}, u32[]{:S(2)}, u32[]{:S(2)}) %collective-permute-start.13) | collective-permute-done | bytes 131104 | tf_op jit(solution)/shard_map/ppermute | solution.py:190
  49.0 1.7 %collective-permute-start.16 = (bf16[128,512]{1,0:T(8,128)(2,1)S(1)}, bf16[128,512]{1,0:T(8,128)(2,1)S(1)}, u32[]{:S(2)}, u32[]{:S(2)}) collective-permute-start(bf16[128,512]{1,0:T(8,128)(2,1)S(1)} %add_convert_fusion), channel_id=1, source_target_pairs={{0,8},{2,10},{4,12},{6,14},{8,0},{10,2},{12,4},{14,6},{1,9},{3,11}... | collective-permute-start | bytes 393224 | tf_op jit(solution)/shard_map/ppermute | solution.py:190
  50.8 0.7 %shard_map.102 = (f32[256,512]{1,0:T(8,128)S(1)}, bf16[256,512]{1,0:T(8,128)(2,1)S(1)}) custom-call(bf16[128,2048]{1,0:T(8,128)(2,1)S(1)} %copy-done.5, bf16[128,768]{1,0:T(8,128)(2,1)S(1)} %pad_maximum_fusion.1.c_ref, bf16[128,768]{1,0:T(8,128)(2,1)S(1)} %collective-permute-done.20.o_ref, bf16[128,512]{1,0:T(8,128)(2,1)S(1)} %get-tuple-element.73.n_ref, ...), custom_call_target="tpu_custom_call" | custom-call | flops 600000000 | bytes 1048576 | tf_op jit(solution)/shard_map/pallas_call | solution.py:149
  51.5 1.5 %collective-permute-start.22 = (bf16[256,512]{1,0:T(8,128)(2,1)S(1)}, bf16[256,512]{1,0:T(8,128)(2,1)S(1)}, u32[]{:S(2)}, u32[]{:S(2)}) collective-permute-start(bf16[256,512]{1,0:T(8,128)(2,1)S(1)} %get-tuple-element.88), channel_id=1, source_target_pairs={{0,2},{2,0},{4,6},{6,4},{8,10},{10,8},{12,14},{14,12},{1,3},{3,1},... | collective-permute-start | bytes 786440 | tf_op jit(solution)/shard_map/ppermute | solution.py:190
  53.0 1.0 %shard_map.101 = bf16[128,2048]{1,0:T(8,128)(2,1)} custom-call(bf16[128,1024]{1,0:T(8,128)(2,1)S(1)} %get-tuple-element.81.a_ref, bf16[128,1024]{1,0:T(8,128)(2,1)S(1)} %collective-permute-done.17.b_ref, bf16[128,1024]{1,0:T(8,128)(2,1)S(1)} %collective-permute-done.15.c_ref, bf16[128,1024]{1,0:T(8,128)(2,1)S(1)} %collective-permute-done.18.d_ref), custom_call_target="tpu_custom_call" | custom-call | flops 1048576 | bytes 1048576 | tf_op jit(solution)/shard_map/pallas_call | solution.py:149
  54.0 4.7 %collective-permute-done.16.far_ref = bf16[128,512]{1,0:T(8,128)(2,1)S(1)} collective-permute-done((bf16[128,512]{1,0:T(8,128)(2,1)S(1)}, bf16[128,512]{1,0:T(8,128)(2,1)S(1)}, u32[]{:S(2)}, u32[]{:S(2)}) %collective-permute-start.16) | collective-permute-done | bytes 131104 | tf_op jit(solution)/shard_map/ppermute | solution.py:190
  58.7 1.0 %shard_map.103 = (bf16[128,512]{1,0:T(8,128)(2,1)}, bf16[128,512]{1,0:T(8,128)(2,1)}) custom-call(f32[128,512]{1,0:T(8,128)S(1)} %get-tuple-element.89.gk_ref, f32[128,512]{1,0:T(8,128)S(1)} %get-tuple-element.90.gv_ref, bf16[128,512]{1,0:T(8,128)(2,1)S(1)} %copy-done.2, bf16[128,512]{1,0:T(8,128)(2,1)S(1)} %copy-done.3, ...), custom_call_target="tpu_custom_call" | custom-call | flops 3000000000 | bytes 1048576 | tf_op jit(solution)/shard_map/pallas_call | solution.py:149
  60.0 0.9 %convert_add_fusion = f32[256,512]{1,0:T(8,128)} fusion(f32[256,512]{1,0:T(8,128)S(1)} %get-tuple-element.95, bf16[256,512]{1,0:T(8,128)(2,1)S(1)} %collective-permute-done.22), kind=kLoop, calls=%fused_computation | loop fusion | flops 262144 | bytes 1310720 | tf_op jit(solution)/shard_map/add | solution.py:454
  (49 shorter events, 4.9 us)
Async XLA Ops:
  0.6 1.0 %copy-start = (bf16[256,512]{1,0:T(8,128)(2,1)S(1)}, bf16[256,512]{1,0:T(8,128)(2,1)}, u32[]{:S(2)}) copy-start(bf16[256,512]{1,0:T(8,128)(2,1)} %param.8) | copy-start | bytes 786436
  1.6 7.0 %copy-start.2 = (bf16[128,512]{1,0:T(8,128)(2,1)S(1)}, bf16[128,512]{1,0:T(8,128)(2,1)}, u32[]{:S(2)}) copy-start(bf16[128,512]{1,0:T(8,128)(2,1)} %k_ref.7) | copy-start | bytes 393220
  1.6 7.0 %copy-start.3 = (bf16[128,512]{1,0:T(8,128)(2,1)S(1)}, bf16[128,512]{1,0:T(8,128)(2,1)}, u32[]{:S(2)}) copy-start(bf16[128,512]{1,0:T(8,128)(2,1)} %v_ref.6) | copy-start | bytes 393220
  1.6 9.4 %copy-start.5 = (bf16[128,2048]{1,0:T(8,128)(2,1)S(1)}, bf16[128,2048]{1,0:T(8,128)(2,1)}, u32[]{:S(2)}) copy-start(bf16[128,2048]{1,0:T(8,128)(2,1)} %gy_ref.6) | copy-start | bytes 1572868
  1.6 16.8 %collective-permute-start.5 = (bf16[128,512]{1,0:T(8,128)(2,1)S(1)}, bf16[128,512]{1,0:T(8,128)(2,1)S(1)}, u32[]{:S(2)}, u32[]{:S(2)}) collective-permute-start(bf16[128,512]{1,0:T(8,128)(2,1)S(1)} %constant_dynamic-slice_fusion.refs_0_), channel_id=1, source_target_pairs={{0,4},{2,6},{4,8},{6,10},{8,12},{10,14},{12,0},{14,2},{1,5},{3,7},... | collective-permute-start | bytes 393224 | tf_op jit(solution)/shard_map/ppermute | solution.py:190
  4.7 15.1 %collective-permute-start.6 = (bf16[128,512]{1,0:T(8,128)(2,1)S(1)}, bf16[128,512]{1,0:T(8,128)(2,1)S(1)}, u32[]{:S(2)}, u32[]{:S(2)}) collective-permute-start(bf16[128,512]{1,0:T(8,128)(2,1)S(1)} %constant_dynamic-slice_fusion.refs_0_), channel_id=1, source_target_pairs={{0,8},{2,10},{4,12},{6,14},{8,0},{10,2},{12,4},{14,6},{1,9},{3,11}... | collective-permute-start | bytes 393224 | tf_op jit(solution)/shard_map/ppermute | solution.py:190
  7.3 12.5 %collective-permute-start.7 = (bf16[128,512]{1,0:T(8,128)(2,1)S(1)}, bf16[128,512]{1,0:T(8,128)(2,1)S(1)}, u32[]{:S(2)}, u32[]{:S(2)}) collective-permute-start(bf16[128,512]{1,0:T(8,128)(2,1)S(1)} %constant_dynamic-slice_fusion.refs_0_), channel_id=1, source_target_pairs={{0,12},{2,14},{4,0},{6,2},{8,4},{10,6},{12,8},{14,10},{1,13},{3,15... | collective-permute-start | bytes 393224 | tf_op jit(solution)/shard_map/ppermute | solution.py:190
  8.9 2.2 %copy-start.1 = (bf16[128,512]{1,0:T(8,128)(2,1)S(1)}, bf16[128,512]{1,0:T(8,128)(2,1)}, u32[]{:S(2)}) copy-start(bf16[128,512]{1,0:T(8,128)(2,1)} %q_ref.7) | copy-start | bytes 393220
  8.9 8.8 %collective-permute-start = (bf16[128,512]{1,0:T(8,128)(2,1)S(1)}, bf16[128,512]{1,0:T(8,128)(2,1)S(1)}, u32[]{:S(2)}, u32[]{:S(2)}) collective-permute-start(bf16[128,512]{1,0:T(8,128)(2,1)S(1)} %shard_map.92), channel_id=1, source_target_pairs={{0,2},{2,0},{4,6},{6,4},{8,10},{10,8},{12,14},{14,12},{1,3},{3,1},... | collective-permute-start | bytes 393224 | tf_op jit(solution)/shard_map/ppermute | solution.py:190
  10.4 5.7 %collective-permute-start.1 = (bf16[128,512]{1,0:T(8,128)(2,1)S(1)}, bf16[128,512]{1,0:T(8,128)(2,1)S(1)}, u32[]{:S(2)}, u32[]{:S(2)}) collective-permute-start(bf16[128,512]{1,0:T(8,128)(2,1)S(1)} %constant_dynamic-slice_fusion.refs_0_), channel_id=1, source_target_pairs={{0,2},{2,0},{4,6},{6,4},{8,10},{10,8},{12,14},{14,12},{1,3},{3,1},... | collective-permute-start | bytes 393224 | tf_op jit(solution)/shard_map/ppermute | solution.py:190
  16.1 7.9 %collective-permute-start.3 = (bf16[128,1024]{1,0:T(8,128)(2,1)S(1)}, bf16[128,1024]{1,0:T(8,128)(2,1)S(1)}, u32[]{:S(2)}, u32[]{:S(2)}) collective-permute-start(bf16[128,1024]{1,0:T(8,128)(2,1)S(1)} %get-tuple-element.59), channel_id=1, source_target_pairs={{0,16},{16,0},{1,17},{17,1},{2,18},{18,2},{3,19},{19,3},{4,20},{20... | collective-permute-start | bytes 786440 | tf_op jit(solution)/shard_map/ppermute | solution.py:199
  17.7 5.0 %collective-permute-start.4 = (bf16[128,512]{1,0:T(8,128)(2,1)S(1)}, bf16[128,512]{1,0:T(8,128)(2,1)S(1)}, u32[]{:S(2)}, u32[]{:S(2)}) collective-permute-start(bf16[128,512]{1,0:T(8,128)(2,1)S(1)} %get-tuple-element.60), channel_id=1, source_target_pairs={{0,4},{2,6},{4,0},{6,2},{8,12},{10,14},{12,8},{14,10},{1,5},{3,7},... | collective-permute-start | bytes 393224 | tf_op jit(solution)/shard_map/ppermute | solution.py:190
  18.4 5.6 %collective-permute-start.2 = (bf16[128,512]{1,0:T(8,128)(2,1)S(1)}, bf16[128,512]{1,0:T(8,128)(2,1)S(1)}, u32[]{:S(2)}, u32[]{:S(2)}) collective-permute-start(bf16[128,512]{1,0:T(8,128)(2,1)S(1)} %add_convert_fusion.3), channel_id=1, source_target_pairs={{0,4},{2,6},{4,0},{6,2},{8,12},{10,14},{12,8},{14,10},{1,5},{3,7},... | collective-permute-start | bytes 393224 | tf_op jit(solution)/shard_map/ppermute | solution.py:190
  19.8 8.3 %collective-permute-start.9 = (bf16[384,512]{1,0:T(8,128)(2,1)S(1)}, bf16[384,512]{1,0:T(8,128)(2,1)S(1)}, u32[]{:S(2)}, u32[]{:S(2)}) collective-permute-start(bf16[384,512]{1,0:T(8,128)(2,1)S(1)} %pad_maximum_fusion), channel_id=1, source_target_pairs={{0,2},{2,0},{4,6},{6,4},{8,10},{10,8},{12,14},{14,12},{1,3},{3,1},... | collective-permute-start | bytes 1179656 | tf_op jit(solution)/shard_map/ppermute | solution.py:190
  22.6 9.0 %copy-start.4 = (bf16[128,512]{1,0:T(8,128)(2,1)}, bf16[128,512]{1,0:T(8,128)(2,1)S(1)}, u32[]{:S(2)}) copy-start(bf16[128,512]{1,0:T(8,128)(2,1)S(1)} %collective-permute-done.4.cols_ref) | copy-start | bytes 393220
  24.1 7.6 %collective-permute-start.8 = (bf16[128,512]{1,0:T(8,128)(2,1)S(1)}, bf16[128,512]{1,0:T(8,128)(2,1)S(1)}, u32[]{:S(2)}, u32[]{:S(2)}) collective-permute-start(bf16[128,512]{1,0:T(8,128)(2,1)S(1)} %add_convert_fusion.2), channel_id=1, source_target_pairs={{0,8},{2,10},{4,12},{6,14},{8,0},{10,2},{12,4},{14,6},{1,9},{3,11}... | collective-permute-start | bytes 393224 | tf_op jit(solution)/shard_map/ppermute | solution.py:190
  28.6 7.8 %collective-permute-start.10 = (f32[128,512]{1,0:T(8,128)S(1)}, f32[128,512]{1,0:T(8,128)S(1)}, u32[]{:S(2)}, u32[]{:S(2)}) collective-permute-start(f32[128,512]{1,0:T(8,128)S(1)} %shard_map.97), channel_id=1, source_target_pairs={{0,16},{16,0},{1,17},{17,1},{2,18},{18,2},{3,19},{19,3},{4,20},{20... | collective-permute-start | bytes 786440 | tf_op jit(solution)/shard_map/ppermute | solution.py:199
  32.0 12.6 %collective-permute-start.19 = (bf16[256,512]{1,0:T(8,128)(2,1)S(1)}, bf16[256,512]{1,0:T(8,128)(2,1)S(1)}, u32[]{:S(2)}, u32[]{:S(2)}) collective-permute-start(bf16[256,512]{1,0:T(8,128)(2,1)S(1)} %get-tuple-element.85), channel_id=1, source_target_pairs={{0,8},{2,10},{4,12},{6,14},{8,0},{10,2},{12,4},{14,6},{1,9},{3,11}... | collective-permute-start | bytes 786440 | tf_op jit(solution)/shard_map/ppermute | solution.py:190
  32.5 5.9 %collective-permute-start.14 = (bf16[128,512]{1,0:T(8,128)(2,1)S(1)}, bf16[128,512]{1,0:T(8,128)(2,1)S(1)}, u32[]{:S(2)}, u32[]{:S(2)}) collective-permute-start(bf16[128,512]{1,0:T(8,128)(2,1)S(1)} %get-tuple-element.73.n_ref), channel_id=1, source_target_pairs={{0,16},{16,0},{1,17},{17,1},{2,18},{18,2},{3,19},{19,3},{4,20},{20... | collective-permute-start | bytes 393224 | tf_op jit(solution)/shard_map/ppermute | solution.py:199
  34.0 6.3 %collective-permute-start.12 = (bf16[128,512]{1,0:T(8,128)(2,1)S(1)}, bf16[128,512]{1,0:T(8,128)(2,1)S(1)}, u32[]{:S(2)}, u32[]{:S(2)}) collective-permute-start(bf16[128,512]{1,0:T(8,128)(2,1)S(1)} %get-tuple-element.73.n_ref), channel_id=1, source_target_pairs={{0,4},{2,6},{4,0},{6,2},{8,12},{10,14},{12,8},{14,10},{1,5},{3,7},... | collective-permute-start | bytes 393224 | tf_op jit(solution)/shard_map/ppermute | solution.py:190
  36.8 5.0 %collective-permute-start.11 = (bf16[128,512]{1,0:T(8,128)(2,1)S(1)}, bf16[128,512]{1,0:T(8,128)(2,1)S(1)}, u32[]{:S(2)}, u32[]{:S(2)}) collective-permute-start(bf16[128,512]{1,0:T(8,128)(2,1)S(1)} %get-tuple-element.72), channel_id=1, source_target_pairs={{0,2},{2,0},{4,6},{6,4},{8,10},{10,8},{12,14},{14,12},{1,3},{3,1},... | collective-permute-start | bytes 393224 | tf_op jit(solution)/shard_map/ppermute | solution.py:190
  39.1 7.2 %collective-permute-start.15 = (bf16[128,1024]{1,0:T(8,128)(2,1)S(1)}, bf16[128,1024]{1,0:T(8,128)(2,1)S(1)}, u32[]{:S(2)}, u32[]{:S(2)}) collective-permute-start(bf16[128,1024]{1,0:T(8,128)(2,1)S(1)} %get-tuple-element.75), channel_id=1, source_target_pairs={{0,16},{16,0},{1,17},{17,1},{2,18},{18,2},{3,19},{19,3},{4,20},{20... | collective-permute-start | bytes 786440 | tf_op jit(solution)/shard_map/ppermute | solution.py:199
  39.7 13.3 %collective-permute-start.17 = (bf16[128,1024]{1,0:T(8,128)(2,1)S(1)}, bf16[128,1024]{1,0:T(8,128)(2,1)S(1)}, u32[]{:S(2)}, u32[]{:S(2)}) collective-permute-start(bf16[128,1024]{1,0:T(8,128)(2,1)S(1)} %get-tuple-element.81.a_ref), channel_id=1, source_target_pairs={{0,1},{1,0},{2,3},{3,2},{4,5},{5,4},{6,7},{7,6},{8,9},{9,8},{10,11... | collective-permute-start | bytes 786440 | tf_op jit(solution)/shard_map/ppermute | solution.py:202
  41.9 2.9 %slice-start = ((bf16[128,512]{1,0:T(8,128)(2,1)}), bf16[128,256]{1,0:T(8,128)(2,1)S(1)}, s32[]{:S(2)}) async-start(bf16[128,512]{1,0:T(8,128)(2,1)} %copy-done.4), calls=%async_computation | async-start | bytes 131072 | tf_op jit(solution)/shard_map/slice | solution.py:389
  41.9 7.1 %collective-permute-start.13 = (bf16[128,512]{1,0:T(8,128)(2,1)S(1)}, bf16[128,512]{1,0:T(8,128)(2,1)S(1)}, u32[]{:S(2)}, u32[]{:S(2)}) collective-permute-start(bf16[128,512]{1,0:T(8,128)(2,1)S(1)} %add_convert_fusion.1), channel_id=1, source_target_pairs={{0,4},{2,6},{4,0},{6,2},{8,12},{10,14},{12,8},{14,10},{1,5},{3,7},... | collective-permute-start | bytes 393224 | tf_op jit(solution)/shard_map/ppermute | solution.py:190
  44.7 6.1 %collective-permute-start.21 = (bf16[128,512]{1,0:T(8,128)(2,1)S(1)}, bf16[128,512]{1,0:T(8,128)(2,1)S(1)}, u32[]{:S(2)}, u32[]{:S(2)}) collective-permute-start(bf16[128,512]{1,0:T(8,128)(2,1)S(1)} %get-tuple-element.97), channel_id=1, source_target_pairs={{0,4},{2,6},{4,0},{6,2},{8,12},{10,14},{12,8},{14,10},{1,5},{3,7},... | collective-permute-start | bytes 393224 | tf_op jit(solution)/shard_map/ppermute | solution.py:190
  44.8 6.0 %collective-permute-start.20 = (bf16[128,768]{1,0:T(8,128)(2,1)S(1)}, bf16[128,768]{1,0:T(8,128)(2,1)S(1)}, u32[]{:S(2)}, u32[]{:S(2)}) collective-permute-start(bf16[128,768]{1,0:T(8,128)(2,1)S(1)} %pad_maximum_fusion.1.c_ref), channel_id=1, source_target_pairs={{0,1},{1,0},{2,3},{3,2},{4,5},{5,4},{6,7},{7,6},{8,9},{9,8},{10,11... | collective-permute-start | bytes 589832 | tf_op jit(solution)/shard_map/ppermute | solution.py:202
  49.0 4.0 %collective-permute-start.18 = (bf16[128,1024]{1,0:T(8,128)(2,1)S(1)}, bf16[128,1024]{1,0:T(8,128)(2,1)S(1)}, u32[]{:S(2)}, u32[]{:S(2)}) collective-permute-start(bf16[128,1024]{1,0:T(8,128)(2,1)S(1)} %collective-permute-done.15.c_ref), channel_id=1, source_target_pairs={{0,1},{1,0},{2,3},{3,2},{4,5},{5,4},{6,7},{7,6},{8,9},{9,8},{10,11... | collective-permute-start | bytes 786440 | tf_op jit(solution)/shard_map/ppermute | solution.py:202
  49.0 9.7 %collective-permute-start.16 = (bf16[128,512]{1,0:T(8,128)(2,1)S(1)}, bf16[128,512]{1,0:T(8,128)(2,1)S(1)}, u32[]{:S(2)}, u32[]{:S(2)}) collective-permute-start(bf16[128,512]{1,0:T(8,128)(2,1)S(1)} %add_convert_fusion), channel_id=1, source_target_pairs={{0,8},{2,10},{4,12},{6,14},{8,0},{10,2},{12,4},{14,6},{1,9},{3,11}... | collective-permute-start | bytes 393224 | tf_op jit(solution)/shard_map/ppermute | solution.py:190
  51.5 8.5 %collective-permute-start.22 = (bf16[256,512]{1,0:T(8,128)(2,1)S(1)}, bf16[256,512]{1,0:T(8,128)(2,1)S(1)}, u32[]{:S(2)}, u32[]{:S(2)}) collective-permute-start(bf16[256,512]{1,0:T(8,128)(2,1)S(1)} %get-tuple-element.88), channel_id=1, source_target_pairs={{0,2},{2,0},{4,6},{6,4},{8,10},{10,8},{12,14},{14,12},{1,3},{3,1},... | collective-permute-start | bytes 786440 | tf_op jit(solution)/shard_map/ppermute | solution.py:190

commit v11 on v10

--- a/solution.py
+++ b/solution.py
@@ -209,7 +209,8 @@
 
     g = lax.axis_index("groups")
     my_weight = lax.dynamic_slice_in_dim(out_weight, g * half, half, 0)
-    z_weight = [rotate(my_weight, k) for k in turns]
+    hops = [*turns[1:], turns[0]]
+    z_weight = [rotate(my_weight, k) for k in hops]
 
     def own_state(k_ref, v_ref, out_ref):
         for i in range(heads):
@@ -269,13 +270,13 @@
         own, *others, x_own, x_others = refs
         g, z, x, h = place()
         blocks = []
-        for k in range(line):
+        for i, k in enumerate((0, *hops)):
             zk = lax.rem(z - k + line, line)
-            blocks.append((zk * 2 + x, (own, *others)[k][...]))
-            if k == 0:
+            blocks.append((zk * 2 + x, (own, *others)[i][...]))
+            if i == 0:
                 block = x_own[...]
             else:
-                block = x_others[(k - 1) * half : k * half, :]
+                block = x_others[(i - 1) * half : i * half, :]
             blocks.append((zk * 2 + 1 - x, block))
         return blocks
 

time: 61 us -> 62.8 us (1.030)
  starting transfers between devices: 26.9 us -> 31.7 us
  waiting for transfers between devices: 23.8 us -> 20.7 us
    ppermute x16, starting transfers between devices: 22.7 us -> 28.2 us  [permute(): return lax.ppermute(array, 'seq', pairs)]
    ppermute x16, waiting for transfers between devices: 23 us -> 18 us  [permute(): return lax.ppermute(array, 'seq', pairs)]
    ppermute x4, waiting for transfers between devices: 0.8 us -> 2.68 us  [swap_y(): return lax.ppermute(array, 'groups', [(0, 1), (1, 0)])]
    ppermute x4, starting transfers between devices: 4.15 us -> 3.47 us  [swap_y(): return lax.ppermute(array, 'groups', [(0, 1), (1, 0)])]
where the time goes in v11:
time: 62.8 us; the launch traced here: 62.6 us
  starting transfers between devices  31.7 us (50%)
  waiting for transfers between devices  20.7 us (33%)
  Pallas kernels  7.37 us (12%)
  other arithmetic  1.04 us (2%)
  local copies, waits for them, and re-layouts  1 us (2%)
  between operations  0.82 us (1%)
    ppermute x16, starting transfers between devices, permute(): return lax.ppermute(array, 'seq', pairs)  28.2 us
    ppermute x16, waiting for transfers between devices, permute(): return lax.ppermute(array, 'seq', pairs)  18 us
    pallas_call x12, Pallas kernels, call(): pl.pallas_call(body, out_shape=[jax.ShapeDtypeStruct(s, d) for s, d in sh...  7.37 us
    ppermute x4, starting transfers between devices, swap_y(): return lax.ppermute(array, 'groups', [(0, 1), (1, 0)])  3.47 us
    ppermute x4, waiting for transfers between devices, swap_y(): return lax.ppermute(array, 'groups', [(0, 1), (1, 0)])  2.68 us
  transfers between devices with their start and end apart: 23, of which 11 were waited for; matrix products, arithmetic and copies ran while one was open for 0% of the time, Pallas kernels for 12%

profile of v11, /device:TPU:0, one launch (start us, length us, event | category | flops | bytes accessed | tf_op | source)
XLA Modules:
  0.0 62.6 jit_solution(3699112968086399733)
XLA Ops:
  0.7 0.9 %copy-done = bf16[256,512]{1,0:T(8,128)(2,1)S(1)} copy-done((bf16[256,512]{1,0:T(8,128)(2,1)S(1)}, bf16[256,512]{1,0:T(8,128)(2,1)}, u32[]{:S(2)}) %copy-start) | copy-done | bytes 262168
  1.6 4.1 %collective-permute-start.5 = (bf16[128,512]{1,0:T(8,128)(2,1)S(1)}, bf16[128,512]{1,0:T(8,128)(2,1)S(1)}, u32[]{:S(2)}, u32[]{:S(2)}) collective-permute-start(bf16[128,512]{1,0:T(8,128)(2,1)S(1)} %constant_dynamic-slice_fusion.refs_0_), channel_id=1, source_target_pairs={{0,8},{2,10},{4,12},{6,14},{8,0},{10,2},{12,4},{14,6},{1,9},{3,11}... | collective-permute-start | bytes 393224 | tf_op jit(solution)/shard_map/ppermute | solution.py:190
  5.7 1.3 %collective-permute-start.6 = (bf16[128,512]{1,0:T(8,128)(2,1)S(1)}, bf16[128,512]{1,0:T(8,128)(2,1)S(1)}, u32[]{:S(2)}, u32[]{:S(2)}) collective-permute-start(bf16[128,512]{1,0:T(8,128)(2,1)S(1)} %constant_dynamic-slice_fusion.refs_0_), channel_id=1, source_target_pairs={{0,12},{2,14},{4,0},{6,2},{8,4},{10,6},{12,8},{14,10},{1,13},{3,15... | collective-permute-start | bytes 393224 | tf_op jit(solution)/shard_map/ppermute | solution.py:190
  8.0 1.6 %collective-permute-start = (bf16[128,512]{1,0:T(8,128)(2,1)S(1)}, bf16[128,512]{1,0:T(8,128)(2,1)S(1)}, u32[]{:S(2)}, u32[]{:S(2)}) collective-permute-start(bf16[128,512]{1,0:T(8,128)(2,1)S(1)} %shard_map.92), channel_id=1, source_target_pairs={{0,2},{2,0},{4,6},{6,4},{8,10},{10,8},{12,14},{14,12},{1,3},{3,1},... | collective-permute-start | bytes 393224 | tf_op jit(solution)/shard_map/ppermute | solution.py:190
  10.2 0.7 %shard_map.94 = (bf16[128,512]{1,0:T(8,128)(2,1)S(1)}, f32[128,512]{1,0:T(8,128)S(1)}) custom-call(bf16[128,512]{1,0:T(8,128)(2,1)S(1)} %copy-done.1, bf16[128,512]{1,0:T(8,128)(2,1)S(1)} %copy-done.2, bf16[128,512]{1,0:T(8,128)(2,1)S(1)} %copy-done.3), custom_call_target="tpu_custom_call" | custom-call | flops 3000000000 | bytes 1048576 | tf_op jit(solution)/shard_map/pallas_call | solution.py:149
  10.9 4.3 %collective-permute-done.1.refs_4_ = bf16[128,512]{1,0:T(8,128)(2,1)S(1)} collective-permute-done((bf16[128,512]{1,0:T(8,128)(2,1)S(1)}, bf16[128,512]{1,0:T(8,128)(2,1)S(1)}, u32[]{:S(2)}, u32[]{:S(2)}) %collective-permute-start.1) | collective-permute-done | bytes 131104 | tf_op jit(solution)/shard_map/ppermute | solution.py:190
  15.3 1.5 %collective-permute-start.3 = (bf16[128,1024]{1,0:T(8,128)(2,1)S(1)}, bf16[128,1024]{1,0:T(8,128)(2,1)S(1)}, u32[]{:S(2)}, u32[]{:S(2)}) collective-permute-start(bf16[128,1024]{1,0:T(8,128)(2,1)S(1)} %get-tuple-element.59), channel_id=1, source_target_pairs={{0,16},{16,0},{1,17},{17,1},{2,18},{18,2},{3,19},{19,3},{4,20},{20... | collective-permute-start | bytes 786440 | tf_op jit(solution)/shard_map/ppermute | solution.py:199
  16.8 1.6 %collective-permute-start.4 = (bf16[128,512]{1,0:T(8,128)(2,1)S(1)}, bf16[128,512]{1,0:T(8,128)(2,1)S(1)}, u32[]{:S(2)}, u32[]{:S(2)}) collective-permute-start(bf16[128,512]{1,0:T(8,128)(2,1)S(1)} %get-tuple-element.60), channel_id=1, source_target_pairs={{0,4},{2,6},{4,0},{6,2},{8,12},{10,14},{12,8},{14,10},{1,5},{3,7},... | collective-permute-start | bytes 393224 | tf_op jit(solution)/shard_map/ppermute | solution.py:190
  19.0 1.6 %collective-permute-start.9 = (bf16[384,512]{1,0:T(8,128)(2,1)S(1)}, bf16[384,512]{1,0:T(8,128)(2,1)S(1)}, u32[]{:S(2)}, u32[]{:S(2)}) collective-permute-start(bf16[384,512]{1,0:T(8,128)(2,1)S(1)} %pad_maximum_fusion), channel_id=1, source_target_pairs={{0,2},{2,0},{4,6},{6,4},{8,10},{10,8},{12,14},{14,12},{1,3},{3,1},... | collective-permute-start | bytes 1179656 | tf_op jit(solution)/shard_map/ppermute | solution.py:190
  20.5 1.2 %collective-permute-done.4.cols_ref = bf16[128,512]{1,0:T(8,128)(2,1)S(1)} collective-permute-done((bf16[128,512]{1,0:T(8,128)(2,1)S(1)}, bf16[128,512]{1,0:T(8,128)(2,1)S(1)}, u32[]{:S(2)}, u32[]{:S(2)}) %collective-permute-start.4) | collective-permute-done | bytes 131104 | tf_op jit(solution)/shard_map/ppermute | solution.py:190
  21.7 1.7 %collective-permute-done.2.near_ref = bf16[128,512]{1,0:T(8,128)(2,1)S(1)} collective-permute-done((bf16[128,512]{1,0:T(8,128)(2,1)S(1)}, bf16[128,512]{1,0:T(8,128)(2,1)S(1)}, u32[]{:S(2)}, u32[]{:S(2)}) %collective-permute-start.2) | collective-permute-done | bytes 131104 | tf_op jit(solution)/shard_map/ppermute | solution.py:190
  23.5 2.5 %collective-permute-start.8 = (bf16[128,512]{1,0:T(8,128)(2,1)S(1)}, bf16[128,512]{1,0:T(8,128)(2,1)S(1)}, u32[]{:S(2)}, u32[]{:S(2)}) collective-permute-start(bf16[128,512]{1,0:T(8,128)(2,1)S(1)} %add_convert_fusion.2), channel_id=1, source_target_pairs={{0,8},{2,10},{4,12},{6,14},{8,0},{10,2},{12,4},{14,6},{1,9},{3,11}... | collective-permute-start | bytes 393224 | tf_op jit(solution)/shard_map/ppermute | solution.py:190
  26.0 1.3 %collective-permute-done.9.refs_5_ = bf16[384,512]{1,0:T(8,128)(2,1)S(1)} collective-permute-done((bf16[384,512]{1,0:T(8,128)(2,1)S(1)}, bf16[384,512]{1,0:T(8,128)(2,1)S(1)}, u32[]{:S(2)}, u32[]{:S(2)}) %collective-permute-start.9) | collective-permute-done | bytes 393248 | tf_op jit(solution)/shard_map/ppermute | solution.py:190
  27.7 0.8 %collective-permute-start.10 = (f32[128,512]{1,0:T(8,128)S(1)}, f32[128,512]{1,0:T(8,128)S(1)}, u32[]{:S(2)}, u32[]{:S(2)}) collective-permute-start(f32[128,512]{1,0:T(8,128)S(1)} %shard_map.97), channel_id=1, source_target_pairs={{0,16},{16,0},{1,17},{17,1},{2,18},{18,2},{3,19},{19,3},{4,20},{20... | collective-permute-start | bytes 786440 | tf_op jit(solution)/shard_map/ppermute | solution.py:199
  28.5 2.3 %collective-permute-done.8.far_ref = bf16[128,512]{1,0:T(8,128)(2,1)S(1)} collective-permute-done((bf16[128,512]{1,0:T(8,128)(2,1)S(1)}, bf16[128,512]{1,0:T(8,128)(2,1)S(1)}, u32[]{:S(2)}, u32[]{:S(2)}) %collective-permute-start.8) | collective-permute-done | bytes 131104 | tf_op jit(solution)/shard_map/ppermute | solution.py:190
  31.2 2.7 %collective-permute-start.19 = (bf16[256,512]{1,0:T(8,128)(2,1)S(1)}, bf16[256,512]{1,0:T(8,128)(2,1)S(1)}, u32[]{:S(2)}, u32[]{:S(2)}) collective-permute-start(bf16[256,512]{1,0:T(8,128)(2,1)S(1)} %get-tuple-element.85), channel_id=1, source_target_pairs={{0,8},{2,10},{4,12},{6,14},{8,0},{10,2},{12,4},{14,6},{1,9},{3,11}... | collective-permute-start | bytes 786440 | tf_op jit(solution)/shard_map/ppermute | solution.py:190
  34.9 0.8 %collective-permute-start.12 = (bf16[128,512]{1,0:T(8,128)(2,1)S(1)}, bf16[128,512]{1,0:T(8,128)(2,1)S(1)}, u32[]{:S(2)}, u32[]{:S(2)}) collective-permute-start(bf16[128,512]{1,0:T(8,128)(2,1)S(1)} %get-tuple-element.73.n_ref), channel_id=1, source_target_pairs={{0,4},{2,6},{4,0},{6,2},{8,12},{10,14},{12,8},{14,10},{1,5},{3,7},... | collective-permute-start | bytes 393224 | tf_op jit(solution)/shard_map/ppermute | solution.py:190
  36.1 1.6 %collective-permute-start.11 = (bf16[128,512]{1,0:T(8,128)(2,1)S(1)}, bf16[128,512]{1,0:T(8,128)(2,1)S(1)}, u32[]{:S(2)}, u32[]{:S(2)}) collective-permute-start(bf16[128,512]{1,0:T(8,128)(2,1)S(1)} %get-tuple-element.72), channel_id=1, source_target_pairs={{0,2},{2,0},{4,6},{6,4},{8,10},{10,8},{12,14},{14,12},{1,3},{3,1},... | collective-permute-start | bytes 393224 | tf_op jit(solution)/shard_map/ppermute | solution.py:190
  37.6 1.7 %collective-permute-done.14.yn_ref = bf16[128,512]{1,0:T(8,128)(2,1)S(1)} collective-permute-done((bf16[128,512]{1,0:T(8,128)(2,1)S(1)}, bf16[128,512]{1,0:T(8,128)(2,1)S(1)}, u32[]{:S(2)}, u32[]{:S(2)}) %collective-permute-start.14) | collective-permute-done | bytes 131104 | tf_op jit(solution)/shard_map/ppermute | solution.py:199
  40.6 0.7 %collective-permute-done.12.near_ref = bf16[128,512]{1,0:T(8,128)(2,1)S(1)} collective-permute-done((bf16[128,512]{1,0:T(8,128)(2,1)S(1)}, bf16[128,512]{1,0:T(8,128)(2,1)S(1)}, u32[]{:S(2)}, u32[]{:S(2)}) %collective-permute-start.12) | collective-permute-done | bytes 131104 | tf_op jit(solution)/shard_map/ppermute | solution.py:190
  41.4 2.5 %collective-permute-start.13 = (bf16[128,512]{1,0:T(8,128)(2,1)S(1)}, bf16[128,512]{1,0:T(8,128)(2,1)S(1)}, u32[]{:S(2)}, u32[]{:S(2)}) collective-permute-start(bf16[128,512]{1,0:T(8,128)(2,1)S(1)} %add_convert_fusion.1), channel_id=1, source_target_pairs={{0,4},{2,6},{4,0},{6,2},{8,12},{10,14},{12,8},{14,10},{1,5},{3,7},... | collective-permute-start | bytes 393224 | tf_op jit(solution)/shard_map/ppermute | solution.py:190
  44.2 1.4 %shard_map.100 = (bf16[128,512]{1,0:T(8,128)(2,1)}, f32[128,512]{1,0:T(8,128)S(1)}, f32[128,512]{1,0:T(8,128)S(1)}) custom-call(bf16[128,512]{1,0:T(8,128)(2,1)S(1)} %get-tuple-element.76.go_ref, bf16[128,512]{1,0:T(8,128)(2,1)S(1)} %copy-done.1, bf16[128,512]{1,0:T(8,128)(2,1)S(1)} %copy-done.2, bf16[128,512]{1,0:T(8,128)(2,1)S(1)} %copy-done.3, ...), custom_call_target="tpu_custom_call" | custom-call | flops 1048576 | bytes 1048576 | tf_op jit(solution)/shard_map/pallas_call | solution.py:149
  45.6 0.9 %collective-permute-done.15.c_ref = bf16[128,1024]{1,0:T(8,128)(2,1)S(1)} collective-permute-done((bf16[128,1024]{1,0:T(8,128)(2,1)S(1)}, bf16[128,1024]{1,0:T(8,128)(2,1)S(1)}, u32[]{:S(2)}, u32[]{:S(2)}) %collective-permute-start.15) | collective-permute-done | bytes 262176 | tf_op jit(solution)/shard_map/ppermute | solution.py:199
  46.5 0.9 %collective-permute-done.13.near_ref = bf16[128,512]{1,0:T(8,128)(2,1)S(1)} collective-permute-done((bf16[128,512]{1,0:T(8,128)(2,1)S(1)}, bf16[128,512]{1,0:T(8,128)(2,1)S(1)}, u32[]{:S(2)}, u32[]{:S(2)}) %collective-permute-start.13) | collective-permute-done | bytes 131104 | tf_op jit(solution)/shard_map/ppermute | solution.py:190
  47.4 5.1 %collective-permute-start.16 = (bf16[128,512]{1,0:T(8,128)(2,1)S(1)}, bf16[128,512]{1,0:T(8,128)(2,1)S(1)}, u32[]{:S(2)}, u32[]{:S(2)}) collective-permute-start(bf16[128,512]{1,0:T(8,128)(2,1)S(1)} %add_convert_fusion), channel_id=1, source_target_pairs={{0,8},{2,10},{4,12},{6,14},{8,0},{10,2},{12,4},{14,6},{1,9},{3,11}... | collective-permute-start | bytes 393224 | tf_op jit(solution)/shard_map/ppermute | solution.py:190
  52.5 0.7 %shard_map.102 = (f32[256,512]{1,0:T(8,128)S(1)}, bf16[256,512]{1,0:T(8,128)(2,1)S(1)}) custom-call(bf16[128,2048]{1,0:T(8,128)(2,1)S(1)} %copy-done.5, bf16[128,768]{1,0:T(8,128)(2,1)S(1)} %pad_maximum_fusion.1.c_ref, bf16[128,768]{1,0:T(8,128)(2,1)S(1)} %collective-permute-done.20.o_ref, bf16[128,512]{1,0:T(8,128)(2,1)S(1)} %get-tuple-element.73.n_ref, ...), custom_call_target="tpu_custom_call" | custom-call | flops 600000000 | bytes 1048576 | tf_op jit(solution)/shard_map/pallas_call | solution.py:149
  53.3 1.0 %collective-permute-start.22 = (bf16[256,512]{1,0:T(8,128)(2,1)S(1)}, bf16[256,512]{1,0:T(8,128)(2,1)S(1)}, u32[]{:S(2)}, u32[]{:S(2)}) collective-permute-start(bf16[256,512]{1,0:T(8,128)(2,1)S(1)} %get-tuple-element.88), channel_id=1, source_target_pairs={{0,2},{2,0},{4,6},{6,4},{8,10},{10,8},{12,14},{14,12},{1,3},{3,1},... | collective-permute-start | bytes 786440 | tf_op jit(solution)/shard_map/ppermute | solution.py:190
  54.3 1.0 %shard_map.101 = bf16[128,2048]{1,0:T(8,128)(2,1)} custom-call(bf16[128,1024]{1,0:T(8,128)(2,1)S(1)} %get-tuple-element.81.a_ref, bf16[128,1024]{1,0:T(8,128)(2,1)S(1)} %collective-permute-done.17.b_ref, bf16[128,1024]{1,0:T(8,128)(2,1)S(1)} %collective-permute-done.15.c_ref, bf16[128,1024]{1,0:T(8,128)(2,1)S(1)} %collective-permute-done.18.d_ref), custom_call_target="tpu_custom_call" | custom-call | flops 1048576 | bytes 1048576 | tf_op jit(solution)/shard_map/pallas_call | solution.py:149
  55.3 3.7 %collective-permute-done.16.far_ref = bf16[128,512]{1,0:T(8,128)(2,1)S(1)} collective-permute-done((bf16[128,512]{1,0:T(8,128)(2,1)S(1)}, bf16[128,512]{1,0:T(8,128)(2,1)S(1)}, u32[]{:S(2)}, u32[]{:S(2)}) %collective-permute-start.16) | collective-permute-done | bytes 131104 | tf_op jit(solution)/shard_map/ppermute | solution.py:190
  59.0 1.0 %shard_map.103 = (bf16[128,512]{1,0:T(8,128)(2,1)}, bf16[128,512]{1,0:T(8,128)(2,1)}) custom-call(f32[128,512]{1,0:T(8,128)S(1)} %get-tuple-element.89.gk_ref, f32[128,512]{1,0:T(8,128)S(1)} %get-tuple-element.90.gv_ref, bf16[128,512]{1,0:T(8,128)(2,1)S(1)} %copy-done.2, bf16[128,512]{1,0:T(8,128)(2,1)S(1)} %copy-done.3, ...), custom_call_target="tpu_custom_call" | custom-call | flops 3000000000 | bytes 1048576 | tf_op jit(solution)/shard_map/pallas_call | solution.py:149
  59.9 1.8 %collective-permute-done.22 = bf16[256,512]{1,0:T(8,128)(2,1)S(1)} collective-permute-done((bf16[256,512]{1,0:T(8,128)(2,1)S(1)}, bf16[256,512]{1,0:T(8,128)(2,1)S(1)}, u32[]{:S(2)}, u32[]{:S(2)}) %collective-permute-start.22) | collective-permute-done | bytes 262176 | tf_op jit(solution)/shard_map/ppermute | solution.py:190
  61.8 0.9 %convert_add_fusion = f32[256,512]{1,0:T(8,128)} fusion(f32[256,512]{1,0:T(8,128)S(1)} %get-tuple-element.95, bf16[256,512]{1,0:T(8,128)(2,1)S(1)} %collective-permute-done.22), kind=kLoop, calls=%fused_computation | loop fusion | flops 262144 | bytes 1310720 | tf_op jit(solution)/shard_map/add | solution.py:455
  (49 shorter events, 5.9 us)
Async XLA Ops:
  0.6 1.0 %copy-start = (bf16[256,512]{1,0:T(8,128)(2,1)S(1)}, bf16[256,512]{1,0:T(8,128)(2,1)}, u32[]{:S(2)}) copy-start(bf16[256,512]{1,0:T(8,128)(2,1)} %param.8) | copy-start | bytes 786436
  1.6 6.2 %copy-start.2 = (bf16[128,512]{1,0:T(8,128)(2,1)S(1)}, bf16[128,512]{1,0:T(8,128)(2,1)}, u32[]{:S(2)}) copy-start(bf16[128,512]{1,0:T(8,128)(2,1)} %k_ref.7) | copy-start | bytes 393220
  1.6 6.2 %copy-start.3 = (bf16[128,512]{1,0:T(8,128)(2,1)S(1)}, bf16[128,512]{1,0:T(8,128)(2,1)}, u32[]{:S(2)}) copy-start(bf16[128,512]{1,0:T(8,128)(2,1)} %v_ref.6) | copy-start | bytes 393220
  1.6 8.5 %copy-start.5 = (bf16[128,2048]{1,0:T(8,128)(2,1)S(1)}, bf16[128,2048]{1,0:T(8,128)(2,1)}, u32[]{:S(2)}) copy-start(bf16[128,2048]{1,0:T(8,128)(2,1)} %gy_ref.6) | copy-start | bytes 1572868
  1.6 16.8 %collective-permute-start.5 = (bf16[128,512]{1,0:T(8,128)(2,1)S(1)}, bf16[128,512]{1,0:T(8,128)(2,1)S(1)}, u32[]{:S(2)}, u32[]{:S(2)}) collective-permute-start(bf16[128,512]{1,0:T(8,128)(2,1)S(1)} %constant_dynamic-slice_fusion.refs_0_), channel_id=1, source_target_pairs={{0,8},{2,10},{4,12},{6,14},{8,0},{10,2},{12,4},{14,6},{1,9},{3,11}... | collective-permute-start | bytes 393224 | tf_op jit(solution)/shard_map/ppermute | solution.py:190
  5.7 13.2 %collective-permute-start.6 = (bf16[128,512]{1,0:T(8,128)(2,1)S(1)}, bf16[128,512]{1,0:T(8,128)(2,1)S(1)}, u32[]{:S(2)}, u32[]{:S(2)}) collective-permute-start(bf16[128,512]{1,0:T(8,128)(2,1)S(1)} %constant_dynamic-slice_fusion.refs_0_), channel_id=1, source_target_pairs={{0,12},{2,14},{4,0},{6,2},{8,4},{10,6},{12,8},{14,10},{1,13},{3,15... | collective-permute-start | bytes 393224 | tf_op jit(solution)/shard_map/ppermute | solution.py:190
  7.1 11.9 %collective-permute-start.7 = (bf16[128,512]{1,0:T(8,128)(2,1)S(1)}, bf16[128,512]{1,0:T(8,128)(2,1)S(1)}, u32[]{:S(2)}, u32[]{:S(2)}) collective-permute-start(bf16[128,512]{1,0:T(8,128)(2,1)S(1)} %constant_dynamic-slice_fusion.refs_0_), channel_id=1, source_target_pairs={{0,4},{2,6},{4,8},{6,10},{8,12},{10,14},{12,0},{14,2},{1,5},{3,7},... | collective-permute-start | bytes 393224 | tf_op jit(solution)/shard_map/ppermute | solution.py:190
  8.0 2.2 %copy-start.1 = (bf16[128,512]{1,0:T(8,128)(2,1)S(1)}, bf16[128,512]{1,0:T(8,128)(2,1)}, u32[]{:S(2)}) copy-start(bf16[128,512]{1,0:T(8,128)(2,1)} %q_ref.7) | copy-start | bytes 393220
  8.0 8.8 %collective-permute-start = (bf16[128,512]{1,0:T(8,128)(2,1)S(1)}, bf16[128,512]{1,0:T(8,128)(2,1)S(1)}, u32[]{:S(2)}, u32[]{:S(2)}) collective-permute-start(bf16[128,512]{1,0:T(8,128)(2,1)S(1)} %shard_map.92), channel_id=1, source_target_pairs={{0,2},{2,0},{4,6},{6,4},{8,10},{10,8},{12,14},{14,12},{1,3},{3,1},... | collective-permute-start | bytes 393224 | tf_op jit(solution)/shard_map/ppermute | solution.py:190
  9.5 5.7 %collective-permute-start.1 = (bf16[128,512]{1,0:T(8,128)(2,1)S(1)}, bf16[128,512]{1,0:T(8,128)(2,1)S(1)}, u32[]{:S(2)}, u32[]{:S(2)}) collective-permute-start(bf16[128,512]{1,0:T(8,128)(2,1)S(1)} %constant_dynamic-slice_fusion.refs_0_), channel_id=1, source_target_pairs={{0,2},{2,0},{4,6},{6,4},{8,10},{10,8},{12,14},{14,12},{1,3},{3,1},... | collective-permute-start | bytes 393224 | tf_op jit(solution)/shard_map/ppermute | solution.py:190
  15.3 8.2 %collective-permute-start.3 = (bf16[128,1024]{1,0:T(8,128)(2,1)S(1)}, bf16[128,1024]{1,0:T(8,128)(2,1)S(1)}, u32[]{:S(2)}, u32[]{:S(2)}) collective-permute-start(bf16[128,1024]{1,0:T(8,128)(2,1)S(1)} %get-tuple-element.59), channel_id=1, source_target_pairs={{0,16},{16,0},{1,17},{17,1},{2,18},{18,2},{3,19},{19,3},{4,20},{20... | collective-permute-start | bytes 786440 | tf_op jit(solution)/shard_map/ppermute | solution.py:199
  16.8 5.0 %collective-permute-start.4 = (bf16[128,512]{1,0:T(8,128)(2,1)S(1)}, bf16[128,512]{1,0:T(8,128)(2,1)S(1)}, u32[]{:S(2)}, u32[]{:S(2)}) collective-permute-start(bf16[128,512]{1,0:T(8,128)(2,1)S(1)} %get-tuple-element.60), channel_id=1, source_target_pairs={{0,4},{2,6},{4,0},{6,2},{8,12},{10,14},{12,8},{14,10},{1,5},{3,7},... | collective-permute-start | bytes 393224 | tf_op jit(solution)/shard_map/ppermute | solution.py:190
  18.4 5.0 %collective-permute-start.2 = (bf16[128,512]{1,0:T(8,128)(2,1)S(1)}, bf16[128,512]{1,0:T(8,128)(2,1)S(1)}, u32[]{:S(2)}, u32[]{:S(2)}) collective-permute-start(bf16[128,512]{1,0:T(8,128)(2,1)S(1)} %add_convert_fusion.3), channel_id=1, source_target_pairs={{0,4},{2,6},{4,0},{6,2},{8,12},{10,14},{12,8},{14,10},{1,5},{3,7},... | collective-permute-start | bytes 393224 | tf_op jit(solution)/shard_map/ppermute | solution.py:190
  19.0 8.3 %collective-permute-start.9 = (bf16[384,512]{1,0:T(8,128)(2,1)S(1)}, bf16[384,512]{1,0:T(8,128)(2,1)S(1)}, u32[]{:S(2)}, u32[]{:S(2)}) collective-permute-start(bf16[384,512]{1,0:T(8,128)(2,1)S(1)} %pad_maximum_fusion), channel_id=1, source_target_pairs={{0,2},{2,0},{4,6},{6,4},{8,10},{10,8},{12,14},{14,12},{1,3},{3,1},... | collective-permute-start | bytes 1179656 | tf_op jit(solution)/shard_map/ppermute | solution.py:190
  21.7 9.1 %copy-start.4 = (bf16[128,512]{1,0:T(8,128)(2,1)}, bf16[128,512]{1,0:T(8,128)(2,1)S(1)}, u32[]{:S(2)}) copy-start(bf16[128,512]{1,0:T(8,128)(2,1)S(1)} %collective-permute-done.4.cols_ref) | copy-start | bytes 393220
  23.5 7.3 %collective-permute-start.8 = (bf16[128,512]{1,0:T(8,128)(2,1)S(1)}, bf16[128,512]{1,0:T(8,128)(2,1)S(1)}, u32[]{:S(2)}, u32[]{:S(2)}) collective-permute-start(bf16[128,512]{1,0:T(8,128)(2,1)S(1)} %add_convert_fusion.2), channel_id=1, source_target_pairs={{0,8},{2,10},{4,12},{6,14},{8,0},{10,2},{12,4},{14,6},{1,9},{3,11}... | collective-permute-start | bytes 393224 | tf_op jit(solution)/shard_map/ppermute | solution.py:190
  27.7 8.0 %collective-permute-start.10 = (f32[128,512]{1,0:T(8,128)S(1)}, f32[128,512]{1,0:T(8,128)S(1)}, u32[]{:S(2)}, u32[]{:S(2)}) collective-permute-start(f32[128,512]{1,0:T(8,128)S(1)} %shard_map.97), channel_id=1, source_target_pairs={{0,16},{16,0},{1,17},{17,1},{2,18},{18,2},{3,19},{19,3},{4,20},{20... | collective-permute-start | bytes 786440 | tf_op jit(solution)/shard_map/ppermute | solution.py:199
  31.2 12.8 %collective-permute-start.19 = (bf16[256,512]{1,0:T(8,128)(2,1)S(1)}, bf16[256,512]{1,0:T(8,128)(2,1)S(1)}, u32[]{:S(2)}, u32[]{:S(2)}) collective-permute-start(bf16[256,512]{1,0:T(8,128)(2,1)S(1)} %get-tuple-element.85), channel_id=1, source_target_pairs={{0,8},{2,10},{4,12},{6,14},{8,0},{10,2},{12,4},{14,6},{1,9},{3,11}... | collective-permute-start | bytes 786440 | tf_op jit(solution)/shard_map/ppermute | solution.py:190
  34.3 5.0 %collective-permute-start.14 = (bf16[128,512]{1,0:T(8,128)(2,1)S(1)}, bf16[128,512]{1,0:T(8,128)(2,1)S(1)}, u32[]{:S(2)}, u32[]{:S(2)}) collective-permute-start(bf16[128,512]{1,0:T(8,128)(2,1)S(1)} %get-tuple-element.73.n_ref), channel_id=1, source_target_pairs={{0,16},{16,0},{1,17},{17,1},{2,18},{18,2},{3,19},{19,3},{4,20},{20... | collective-permute-start | bytes 393224 | tf_op jit(solution)/shard_map/ppermute | solution.py:199
  34.9 6.4 %collective-permute-start.12 = (bf16[128,512]{1,0:T(8,128)(2,1)S(1)}, bf16[128,512]{1,0:T(8,128)(2,1)S(1)}, u32[]{:S(2)}, u32[]{:S(2)}) collective-permute-start(bf16[128,512]{1,0:T(8,128)(2,1)S(1)} %get-tuple-element.73.n_ref), channel_id=1, source_target_pairs={{0,4},{2,6},{4,0},{6,2},{8,12},{10,14},{12,8},{14,10},{1,5},{3,7},... | collective-permute-start | bytes 393224 | tf_op jit(solution)/shard_map/ppermute | solution.py:190
  36.1 5.3 %collective-permute-start.11 = (bf16[128,512]{1,0:T(8,128)(2,1)S(1)}, bf16[128,512]{1,0:T(8,128)(2,1)S(1)}, u32[]{:S(2)}, u32[]{:S(2)}) collective-permute-start(bf16[128,512]{1,0:T(8,128)(2,1)S(1)} %get-tuple-element.72), channel_id=1, source_target_pairs={{0,2},{2,0},{4,6},{6,4},{8,10},{10,8},{12,14},{14,12},{1,3},{3,1},... | collective-permute-start | bytes 393224 | tf_op jit(solution)/shard_map/ppermute | solution.py:190
  40.1 6.4 %collective-permute-start.15 = (bf16[128,1024]{1,0:T(8,128)(2,1)S(1)}, bf16[128,1024]{1,0:T(8,128)(2,1)S(1)}, u32[]{:S(2)}, u32[]{:S(2)}) collective-permute-start(bf16[128,1024]{1,0:T(8,128)(2,1)S(1)} %get-tuple-element.75), channel_id=1, source_target_pairs={{0,16},{16,0},{1,17},{17,1},{2,18},{18,2},{3,19},{19,3},{4,20},{20... | collective-permute-start | bytes 786440 | tf_op jit(solution)/shard_map/ppermute | solution.py:199
  40.6 13.6 %collective-permute-start.17 = (bf16[128,1024]{1,0:T(8,128)(2,1)S(1)}, bf16[128,1024]{1,0:T(8,128)(2,1)S(1)}, u32[]{:S(2)}, u32[]{:S(2)}) collective-permute-start(bf16[128,1024]{1,0:T(8,128)(2,1)S(1)} %get-tuple-element.81.a_ref), channel_id=1, source_target_pairs={{0,1},{1,0},{2,3},{3,2},{4,5},{5,4},{6,7},{7,6},{8,9},{9,8},{10,11... | collective-permute-start | bytes 786440 | tf_op jit(solution)/shard_map/ppermute | solution.py:202
  41.4 2.7 %slice-start = ((bf16[128,512]{1,0:T(8,128)(2,1)}), bf16[128,256]{1,0:T(8,128)(2,1)S(1)}, s32[]{:S(2)}) async-start(bf16[128,512]{1,0:T(8,128)(2,1)} %copy-done.4), calls=%async_computation | async-start | bytes 131072 | tf_op jit(solution)/shard_map/slice | solution.py:390
  41.4 6.0 %collective-permute-start.13 = (bf16[128,512]{1,0:T(8,128)(2,1)S(1)}, bf16[128,512]{1,0:T(8,128)(2,1)S(1)}, u32[]{:S(2)}, u32[]{:S(2)}) collective-permute-start(bf16[128,512]{1,0:T(8,128)(2,1)S(1)} %add_convert_fusion.1), channel_id=1, source_target_pairs={{0,4},{2,6},{4,0},{6,2},{8,12},{10,14},{12,8},{14,10},{1,5},{3,7},... | collective-permute-start | bytes 393224 | tf_op jit(solution)/shard_map/ppermute | solution.py:190
  44.0 8.6 %collective-permute-start.21 = (bf16[128,512]{1,0:T(8,128)(2,1)S(1)}, bf16[128,512]{1,0:T(8,128)(2,1)S(1)}, u32[]{:S(2)}, u32[]{:S(2)}) collective-permute-start(bf16[128,512]{1,0:T(8,128)(2,1)S(1)} %get-tuple-element.97), channel_id=1, source_target_pairs={{0,4},{2,6},{4,0},{6,2},{8,12},{10,14},{12,8},{14,10},{1,5},{3,7},... | collective-permute-start | bytes 393224 | tf_op jit(solution)/shard_map/ppermute | solution.py:190
  44.1 8.5 %collective-permute-start.20 = (bf16[128,768]{1,0:T(8,128)(2,1)S(1)}, bf16[128,768]{1,0:T(8,128)(2,1)S(1)}, u32[]{:S(2)}, u32[]{:S(2)}) collective-permute-start(bf16[128,768]{1,0:T(8,128)(2,1)S(1)} %pad_maximum_fusion.1.c_ref), channel_id=1, source_target_pairs={{0,1},{1,0},{2,3},{3,2},{4,5},{5,4},{6,7},{7,6},{8,9},{9,8},{10,11... | collective-permute-start | bytes 589832 | tf_op jit(solution)/shard_map/ppermute | solution.py:202
  47.4 6.9 %collective-permute-start.18 = (bf16[128,1024]{1,0:T(8,128)(2,1)S(1)}, bf16[128,1024]{1,0:T(8,128)(2,1)S(1)}, u32[]{:S(2)}, u32[]{:S(2)}) collective-permute-start(bf16[128,1024]{1,0:T(8,128)(2,1)S(1)} %collective-permute-done.15.c_ref), channel_id=1, source_target_pairs={{0,1},{1,0},{2,3},{3,2},{4,5},{5,4},{6,7},{7,6},{8,9},{9,8},{10,11... | collective-permute-start | bytes 786440 | tf_op jit(solution)/shard_map/ppermute | solution.py:202
  47.4 11.6 %collective-permute-start.16 = (bf16[128,512]{1,0:T(8,128)(2,1)S(1)}, bf16[128,512]{1,0:T(8,128)(2,1)S(1)}, u32[]{:S(2)}, u32[]{:S(2)}) collective-permute-start(bf16[128,512]{1,0:T(8,128)(2,1)S(1)} %add_convert_fusion), channel_id=1, source_target_pairs={{0,8},{2,10},{4,12},{6,14},{8,0},{10,2},{12,4},{14,6},{1,9},{3,11}... | collective-permute-start | bytes 393224 | tf_op jit(solution)/shard_map/ppermute | solution.py:190
  53.3 8.5 %collective-permute-start.22 = (bf16[256,512]{1,0:T(8,128)(2,1)S(1)}, bf16[256,512]{1,0:T(8,128)(2,1)S(1)}, u32[]{:S(2)}, u32[]{:S(2)}) collective-permute-start(bf16[256,512]{1,0:T(8,128)(2,1)S(1)} %get-tuple-element.88), channel_id=1, source_target_pairs={{0,2},{2,0},{4,6},{6,4},{8,10},{10,8},{12,14},{14,12},{1,3},{3,1},... | collective-permute-start | bytes 786440 | tf_op jit(solution)/shard_map/ppermute | solution.py:190
